TPU v7x, 32 devices: a whole 2x2x4 slice. The times are simulated.
32 devices in a mesh: blocks: 2 (over x), mode: 16 (over z, y, core).
Axes of the slice: x: 2, y: 2, z: 4, core: 2. Of those that a mesh axis runs over, the one named last changes fastest.
Arguments:
- right_side: float32 [2, 8, 1024, 1024], P(None, 'blocks', 'mode'), parts along dimension 1, may hold values from -6 to 6
- classes: int32 [8, 1024, 1024], P('blocks', 'mode'), parts along dimension 0, may hold values from 0 to 7
- noise_table: float32 [8], replicated, may hold values from 0.05 to 1
- kernel_first: bfloat16 [1024, 1024], replicated, may hold values from -1 to 3, as said below
- kernel_second: bfloat16 [1024, 1024], replicated, may hold values from -1 to 3, as said below
- basis_first: bfloat16 [1024, 1024], replicated, may hold values from -1 to 2, as said below
- basis_second: bfloat16 [1024, 1024], replicated, may hold values from -1 to 2, as said below
- eigen_first: float32 [1024], replicated, may hold values from 0.5 to 4
- eigen_second: float32 [1024], P('mode'), may hold values from 0.5 to 4
Outputs:
- solution_field: float32 [2, 8, 1024, 1024], P(None, 'blocks', 'mode'), parts along dimension 1
- residual: float32 [2, 8, 1024, 1024], P(None, 'blocks', 'mode'), parts along dimension 1
There are 2 independent parts, one for each index of `blocks`. A program takes and returns all parts, laid end to end along the dimension named above; an argument that names none is the same for every part. Nothing has to cross between parts.
Inputs may be any that keep to these rules, and one draw needn't show every extreme that they name: `kernel_first`: symmetric positive definite. `kernel_second`: symmetric positive definite. `basis_first`: nonsingular. `basis_second`: nonsingular.
All inputs are finite; a program needn't handle non-finite values.
Results may differ from a plain program's by a relative error of at most 0.0003.
Values sent between devices are 32-bit elements; how exact they have to be, the bound alone decides.
No kernel may reach another device: no remote copies, remote signals or barrier semaphores. Data moves between devices by JAX's collectives and lax.ppermute only.
A program may use at most 128 MiB of HBM per device.

v0:
```python
import jax
import jax.numpy as jnp
from jax import lax
from jax.sharding import PartitionSpec as P

NCLASS = 8
ITERS = 2


def along_rows(matrix, field):
    return jnp.einsum("jk,sprk->sprj", matrix, field, precision=lax.Precision.HIGHEST)


def rows_to_send(matrix, field, groups):
    result = jnp.einsum("kj,sprk->jspr", matrix, field, precision=lax.Precision.HIGHEST)
    return result.reshape(groups, -1)


def received_to_columns(matrix, received, shape5):
    groups, cols, samples, planes, rows = shape5
    block = received.reshape(shape5)
    reshaped = matrix.reshape(groups, rows, matrix.shape[1])
    return jnp.einsum("mri,mcspr->cspi", reshaped, block, precision=lax.Precision.HIGHEST)


def along_columns(matrix, columns):
    return jnp.einsum("ik,cspk->cspi", matrix, columns, precision=lax.Precision.HIGHEST)


def columns_to_send(matrix, columns, groups, rows):
    reshaped = matrix.reshape(groups, rows, matrix.shape[1])
    result = jnp.einsum("mrk,cspk->mcspr", reshaped, columns, precision=lax.Precision.HIGHEST)
    return result.reshape(groups, -1)


def received_to_rows(matrix, received, shape5):
    groups, cols, samples, planes, rows = shape5
    block = received.reshape(shape5)
    reshaped = matrix.reshape(matrix.shape[0], groups, cols)
    return jnp.einsum("jmc,mcspr->sprj", reshaped, block, precision=lax.Precision.HIGHEST)


def body(
    right_side,
    classes,
    noise_table,
    kernel_first,
    kernel_second,
    basis_first,
    basis_second,
    eigen_first,
    eigen_second,
):
    groups = lax.axis_size("mode")
    samples, planes, rows, width_two = right_side.shape
    cols = eigen_second.shape[0]
    shape5 = (groups, cols, samples, planes, rows)
    kern_one = kernel_first.astype(jnp.float32)
    kern_two = kernel_second.astype(jnp.float32)
    base_one = basis_first.astype(jnp.float32)
    base_two = basis_second.astype(jnp.float32)
    noise = jnp.zeros(classes.shape, jnp.float32)
    for level in range(NCLASS):
        noise = noise + jnp.where(classes == level, noise_table[level], 0.0)
    noise = noise[None]
    mean_noise = jnp.mean(noise_table)
    col_weights = 1.0 / (eigen_second[:, None] * eigen_first[None, :] + mean_noise)
    col_weights = col_weights[:, None, None, :]

    def spectral(field):
        outgoing = rows_to_send(base_two, field, groups)
        incoming = lax.all_to_all(outgoing, "mode", split_axis=0, concat_axis=0, tiled=True)
        return received_to_columns(base_one, incoming, shape5) * col_weights

    def precond_apply(field):
        weighted = spectral(field)
        columns = along_columns(base_one, weighted)
        outgoing = columns_to_send(base_one, weighted, groups, rows)
        kernel_send = columns_to_send(kern_one, columns, groups, rows)
        back, kernel_back = (
            lax.all_to_all(outgoing, "mode", split_axis=0, concat_axis=0, tiled=True),
            lax.all_to_all(kernel_send, "mode", split_axis=0, concat_axis=0, tiled=True),
        )
        z_field = received_to_rows(base_two, back, shape5)
        image = (
            along_rows(kern_two, received_to_rows(base_two, kernel_back, shape5)) + noise * z_field
        )
        return (z_field, image)

    def residual_inner(residual, z_field):
        return lax.psum(jnp.sum(residual * z_field), "mode")

    solution_field = jnp.zeros_like(right_side)
    residual = right_side
    z_field, image = precond_apply(residual)
    direction, along = (z_field, image)
    gamma = residual_inner(residual, z_field)
    for step in range(ITERS):
        curvature = lax.psum(jnp.sum(direction * along), "mode")
        alpha = gamma / curvature
        solution_field = solution_field + alpha * direction
        residual = residual - alpha * along
        if step + 1 < ITERS:
            z_field, image = precond_apply(residual)
            gamma_new = residual_inner(residual, z_field)
            ratio = gamma_new / gamma
            direction = z_field + ratio * direction
            along = image + ratio * along
            gamma = gamma_new
    return (solution_field, residual)


def solution(mesh):
    in_specs = (
        P(None, "blocks", "mode", None),
        P("blocks", "mode", None),
        P(),
        P(),
        P(),
        P(),
        P(),
        P(),
        P("mode"),
    )
    out_specs = (P(None, "blocks", "mode", None), P(None, "blocks", "mode", None))
    return jax.shard_map(body, mesh=mesh, in_specs=in_specs, out_specs=out_specs, check_vma=False)
```

profile of v0, /device:TPU:0, one launch (start us, length us, event | category | flops | bytes accessed | tf_op | source)
XLA Modules:
  0.0 580.7 jit_solution(399112543989142584)
XLA Ops:
  0.6 7.1 %fusion.30 = f32[1024,2,4,64]{0,3,2,1:T(8,128)} fusion(f32[2,4,64,1024]{3,2,1,0:T(8,128)} %param.9, bf16[1024,1024]{1,0:T(8,128)(2,1)} %param.15), kind=kOutput, calls=%fused_computation.38 | convolution fusion | flops 6442450944 | bytes 6291456 | tf_op jit(solution)/shard_map/kj,sprk->jspr/dot_general | solution.py:15
  19.0 7.9 %all-to-all-start = ((f32[16,1,32768]{2,1,0:T(1,128)}), f32[16,1,32768]{2,1,0:T(1,128)}, u32[]{:S(2)}, u32[]{:S(2)}) async-start(f32[16,1,32768]{2,1,0:T(1,128)} %all_to_all.48), calls=%async_computation | async-start | bytes 4194304 | tf_op jit(solution)/shard_map/all_to_all | solution.py:72
  28.3 39.6 %all-to-all-done = f32[16,1,32768]{2,1,0:T(1,128)} async-done(((f32[16,1,32768]{2,1,0:T(1,128)}), f32[16,1,32768]{2,1,0:T(1,128)}, u32[]{:S(2)}, u32[]{:S(2)}) %all-to-all-start) | async-done | bytes 2097184 | tf_op jit(solution)/shard_map/all_to_all | solution.py:72
  67.9 8.0 %reduce = f32[16,32768]{1,0:T(8,128)} reduce(f32[16,1,32768]{2,1,0:T(1,128)} %all-to-all-done, f32[]{:T(128)} %constant.23), dimensions={1}, to_apply=%all_to_all.37.reduce_sub_computation | reduce | bytes 4194308 | tf_op jit(solution)/shard_map/all_to_all | solution.py:72
  81.3 7.0 %fusion.10 = f32[64,2,4,1024,1]{3,0,4,2,1:T(8,128)S(1)} fusion(bf16[16,64,1024,1,1]{2,1,0,4,3:T(8,128)(2,1)S(1)} %bitcast.162, f32[16,64,2,4,64]{4,3,2,1,0:T(4,128)} %reshape.94), kind=kOutput, calls=%fused_computation.10 | convolution fusion | flops 6442450944 | bytes 6291456 | tf_op jit(solution)/shard_map/mri,mcspr->cspi/dot_general | solution.py:23
  89.6 6.7 %convolution_bitcast_fusion.3 = f32[16,64,2,4,64]{4,1,0,3,2:T(8,128)S(1)} fusion(bf16[16,64,1024,1,1]{2,1,0,4,3:T(8,128)(2,1)S(1)} %bitcast.163, f32[64,2,4,1024,1]{3,0,4,2,1:T(8,128)S(1)} %fusion.10, f32[64,1024]{1,0:T(8,128)S(1)} %add_divide_fusion), kind=kOutput, calls=%fused_computation.15 | convolution fusion | flops 6442975232 | bytes 6553600 | tf_op jit(solution)/shard_map/mrk,cspk->mcspr/dot_general | solution.py:32
  107.6 11.4 %all-to-all-start.1 = ((f32[16,1,32768]{2,1,0:T(1,128)}), f32[16,1,32768]{2,1,0:T(1,128)}, u32[]{:S(2)}, u32[]{:S(2)}) async-start(f32[16,1,32768]{2,1,0:T(1,128)} %all_to_all.49), calls=%async_computation.1 | async-start | bytes 4194304 | tf_op jit(solution)/shard_map/all_to_all | solution.py:81
  124.2 6.8 %convolution_bitcast_fusion.2 = f32[16,64,2,4,64]{4,1,0,3,2:T(8,128)S(1)} fusion(bf16[16,64,1024,1,1]{2,1,0,4,3:T(8,128)(2,1)S(1)} %bitcast.170, f32[64,2,4,1024]{3,0,2,1:T(8,128)S(1)} %fusion.23), kind=kOutput, calls=%fused_computation.14 | convolution fusion | flops 6442450944 | bytes 6291456 | tf_op jit(solution)/shard_map/mrk,cspk->mcspr/dot_general | solution.py:32
  135.9 6.5 %all_to_all.50 = f32[16,1,32768]{2,1,0:T(1,128)} reshape(f32[16,64,2,4,64]{4,3,2,1,0:T(4,128)} %copy.48) | data formatting | bytes 4194304 | tf_op jit(solution)/shard_map/all_to_all | solution.py:82
  142.4 17.4 %all-to-all-done.1 = f32[16,1,32768]{2,1,0:T(1,128)} async-done(((f32[16,1,32768]{2,1,0:T(1,128)}), f32[16,1,32768]{2,1,0:T(1,128)}, u32[]{:S(2)}, u32[]{:S(2)}) %all-to-all-start.1) | async-done | bytes 2097184 | tf_op jit(solution)/shard_map/all_to_all | solution.py:81
  159.8 11.3 %all-to-all-start.2 = ((f32[16,1,32768]{2,1,0:T(1,128)}), f32[16,1,32768]{2,1,0:T(1,128)}, u32[]{:S(2)}, u32[]{:S(2)}) async-start(f32[16,1,32768]{2,1,0:T(1,128)} %all_to_all.50), calls=%async_computation.2 | async-start | bytes 4194304 | tf_op jit(solution)/shard_map/all_to_all | solution.py:82
  175.7 6.9 %select_add_fusion = f32[4,64,1024]{2,1,0:T(8,128)S(1)} fusion(s32[4,64,1024]{2,1,0:T(8,128)} %param.10, f32[]{:T(128)} %bitcast.36, f32[]{:T(128)} %bitcast.35, f32[]{:T(128)} %bitcast.34, f32[]{:T(128)} %bitcast.33, f32[]{:T(128)} %bitcast.32, f32[]{:T(128)} %bitcast.31, f32[]{:T(128)} %bitcast.30, f32[]{:T(128)} %bitcast.29), kind=kLoop, calls=%fused_computation.55 | loop fusion | flops 6029312 | bytes 2097184 | tf_op jit(solution)/shard_map/add | solution.py:64
  182.7 8.0 %reduce.1 = f32[16,32768]{1,0:T(8,128)} reduce(f32[16,1,32768]{2,1,0:T(1,128)} %all-to-all-done.1, f32[]{:T(128)} %constant.23), dimensions={1}, to_apply=%all_to_all.39.reduce_sub_computation | reduce | bytes 4194308 | tf_op jit(solution)/shard_map/all_to_all | solution.py:81
  196.4 15.7 %all-to-all-done.2 = f32[16,1,32768]{2,1,0:T(1,128)} async-done(((f32[16,1,32768]{2,1,0:T(1,128)}), f32[16,1,32768]{2,1,0:T(1,128)}, u32[]{:S(2)}, u32[]{:S(2)}) %all-to-all-start.2) | async-done | bytes 2097184 | tf_op jit(solution)/shard_map/all_to_all | solution.py:82
  212.2 8.0 %reduce.2 = f32[16,32768]{1,0:T(8,128)} reduce(f32[16,1,32768]{2,1,0:T(1,128)} %all-to-all-done.2, f32[]{:T(128)} %constant.23), dimensions={1}, to_apply=%all_to_all.41.reduce_sub_computation | reduce | bytes 4194308 | tf_op jit(solution)/shard_map/all_to_all | solution.py:82
  225.5 6.7 %fusion.8 = f32[2,4,64,1024,1]{3,2,4,1,0:T(8,128)S(1)} fusion(bf16[1024,16,64,1,1]{0,2,1,4,3:T(8,128)(2,1)} %bitcast.166, f32[16,64,2,4,64]{4,3,2,1,0:T(4,128)} %reshape.96), kind=kOutput, calls=%fused_computation.8 | convolution fusion | flops 6442450944 | bytes 6291456 | tf_op jit(solution)/shard_map/jmc,mcspr->sprj/dot_general | solution.py:40
  241.8 40.0 %all-reduce = (f32[]{:T(128)}, f32[]{:T(128)}) all-reduce(f32[]{:T(128)} %get-tuple-element.3, f32[]{:T(128)} %get-tuple-element.2), channel_id=1, replica_groups=mesh['blocks'=2,'mode'=16] {'mode'}, use_global_device_ids=true, to_apply=%region_2.3 | all-reduce | flops 2 | bytes 16 | tf_op jit(solution)/shard_map/psum | solution.py:91
  303.2 51.8 %all_to_all.60 = f32[16,1,32768]{2,1,0:T(1,128)} all-to-all(f32[16,1,32768]{2,1,0:T(1,128)} %all_to_all.51), channel_id=1, replica_groups=mesh['blocks'=2,'mode'=16] {'mode'}, dimensions={0} | all-to-all | bytes 4194304 | tf_op jit(solution)/shard_map/all_to_all | solution.py:72
  355.0 8.0 %reduce.3 = f32[16,32768]{1,0:T(8,128)} reduce(f32[16,1,32768]{2,1,0:T(1,128)} %all_to_all.60, f32[]{:T(128)} %constant.23), dimensions={1}, to_apply=%all_to_all.43.reduce_sub_computation | reduce | bytes 4194308 | tf_op jit(solution)/shard_map/all_to_all | solution.py:72
  368.4 6.8 %fusion.4 = f32[64,2,4,1024,1]{3,0,4,2,1:T(8,128)S(1)} fusion(bf16[16,64,1024,1,1]{2,1,0,4,3:T(8,128)(2,1)S(1)} %bitcast.164, f32[16,64,2,4,64]{4,3,2,1,0:T(4,128)} %reshape.100), kind=kOutput, calls=%fused_computation.4 | convolution fusion | flops 6442450944 | bytes 6291456 | tf_op jit(solution)/shard_map/mri,mcspr->cspi/dot_general | solution.py:23
  376.6 6.7 %convolution_bitcast_fusion.1 = f32[16,64,2,4,64]{4,1,0,3,2:T(8,128)S(1)} fusion(bf16[16,64,1024,1,1]{2,1,0,4,3:T(8,128)(2,1)S(1)} %bitcast.165, f32[64,2,4,1024,1]{3,0,4,2,1:T(8,128)S(1)} %fusion.4, f32[64,1024]{1,0:T(8,128)S(1)} %add_divide_fusion), kind=kOutput, calls=%fused_computation.13 | convolution fusion | flops 6442975232 | bytes 6553600 | tf_op jit(solution)/shard_map/mrk,cspk->mcspr/dot_general | solution.py:32
  404.9 6.8 %convolution_bitcast_fusion = f32[16,64,2,4,64]{4,1,0,3,2:T(8,128)S(1)} fusion(bf16[16,64,1024,1,1]{2,1,0,4,3:T(8,128)(2,1)S(1)} %bitcast.171, f32[64,2,4,1024]{3,0,2,1:T(8,128)S(1)} %fusion.21), kind=kOutput, calls=%fused_computation.12 | convolution fusion | flops 6442450944 | bytes 6291456 | tf_op jit(solution)/shard_map/mrk,cspk->mcspr/dot_general | solution.py:32
  416.6 6.5 %all_to_all.53 = f32[16,1,32768]{2,1,0:T(1,128)} reshape(f32[16,64,2,4,64]{4,3,2,1,0:T(4,128)} %copy.57) | data formatting | bytes 4194304 | tf_op jit(solution)/shard_map/all_to_all | solution.py:82
  423.1 17.4 %all-to-all-done.4 = f32[16,1,32768]{2,1,0:T(1,128)} async-done(((f32[16,1,32768]{2,1,0:T(1,128)}), f32[16,1,32768]{2,1,0:T(1,128)}, u32[]{:S(2)}, u32[]{:S(2)}) %all-to-all-start.4) | async-done | bytes 2097184 | tf_op jit(solution)/shard_map/all_to_all | solution.py:81
  440.6 11.3 %all-to-all-start.5 = ((f32[16,1,32768]{2,1,0:T(1,128)}), f32[16,1,32768]{2,1,0:T(1,128)}, u32[]{:S(2)}, u32[]{:S(2)}) async-start(f32[16,1,32768]{2,1,0:T(1,128)} %all_to_all.53), calls=%async_computation.5 | async-start | bytes 4194304 | tf_op jit(solution)/shard_map/all_to_all | solution.py:82
  451.8 8.0 %reduce.4 = f32[16,32768]{1,0:T(8,128)} reduce(f32[16,1,32768]{2,1,0:T(1,128)} %all-to-all-done.4, f32[]{:T(128)} %constant.23), dimensions={1}, to_apply=%all_to_all.45.reduce_sub_computation | reduce | bytes 4194308 | tf_op jit(solution)/shard_map/all_to_all | solution.py:81
  465.2 9.3 %fusion.25 = (f32[]{:T(128)}, f32[2,4,64,1024,1]{3,2,4,1,0:T(8,128)}) fusion(f32[2,4,64,1024]{3,2,1,0:T(8,128)} %copy-done.4, bf16[1024,16,64,1,1]{0,2,1,4,3:T(8,128)(2,1)} %bitcast.167, f32[16,64,2,4,64]{4,3,2,1,0:T(4,128)} %reshape.101), kind=kOutput, calls=%fused_computation.32 | convolution fusion | flops 6443499520 | bytes 8388612 | tf_op jit(solution)/shard_map/jmc,mcspr->sprj/dot_general | solution.py:40
  474.5 40.3 %psum.30 = f32[]{:T(128)} all-reduce(f32[]{:T(128)} %get-tuple-element.15), channel_id=1, replica_groups=mesh['blocks'=2,'mode'=16] {'mode'}, use_global_device_ids=true, to_apply=%region_6.7 | all-reduce | flops 1 | bytes 8 | tf_op jit(solution)/shard_map/psum | solution.py:91
  516.0 7.9 %reduce.5 = f32[16,32768]{1,0:T(8,128)} reduce(f32[16,1,32768]{2,1,0:T(1,128)} %all-to-all-done.5, f32[]{:T(128)} %constant.23), dimensions={1}, to_apply=%all_to_all.47.reduce_sub_computation | reduce | bytes 4194308 | tf_op jit(solution)/shard_map/all_to_all | solution.py:82
  529.4 6.7 %fusion = f32[2,4,64,1024,1]{3,2,4,1,0:T(8,128)S(1)} fusion(bf16[1024,16,64,1,1]{0,2,1,4,3:T(8,128)(2,1)} %bitcast.168, f32[16,64,2,4,64]{4,3,2,1,0:T(4,128)} %reshape.102), kind=kOutput, calls=%fused_computation | convolution fusion | flops 6442450944 | bytes 6291456 | tf_op jit(solution)/shard_map/jmc,mcspr->sprj/dot_general | solution.py:40
  542.0 30.2 %psum.31 = f32[]{:T(128)} all-reduce(f32[]{:T(128)} %get-tuple-element.17), channel_id=1, replica_groups=mesh['blocks'=2,'mode'=16] {'mode'}, use_global_device_ids=true, to_apply=%region_8.9 | all-reduce | flops 1 | bytes 8 | tf_op jit(solution)/shard_map/psum | solution.py:99
  573.5 7.0 %fusion.36 = (f32[2,4,64,1024]{3,2,1,0:T(8,128)}, f32[2,4,64,1024]{3,2,1,0:T(8,128)}) fusion(f32[2,4,64,1024,1]{3,2,4,1,0:T(8,128)} %copy-done.2, f32[]{:T(128)S(6)} %div.27, f32[]{:T(128)S(6)} %div.26, f32[2,4,64,1024,1]{3,2,4,1,0:T(8,128)} %get-tuple-element.16, f32[]{:T(128)S(6)} %div.25, f32[2,4,64,1024]{3,2,1,0:T(8,128)} %copy-done.4, ...), kind=kLoop, calls=%fused_computation.49 | loop fusion | flops 3670016 | bytes 12582924 | tf_op jit(solution)/shard_map/add | solution.py:101
  (67 shorter events, 135.4 us)
Async XLA Ops:
  0.6 80.7 %copy-start = (bf16[1024,1024]{1,0:T(8,128)(2,1)S(1)}, bf16[1024,1024]{1,0:T(8,128)(2,1)}, u32[]{:S(2)}) copy-start(bf16[1024,1024]{1,0:T(8,128)(2,1)} %param.14) | copy-start | bytes 6291460
  19.0 7.9 %copy-start.12 = (f32[8]{0:T(128)S(1)}, f32[8]{0:T(128)}, u32[]{:S(2)}) copy-start(f32[8]{0:T(128)} %param.11) | copy-start | bytes 100
  19.0 9.2 %copy-start.13 = (f32[1024]{0:T(1024)S(1)}, f32[1024]{0:T(1024)}, u32[]{:S(2)}) copy-start(f32[1024]{0:T(1024)} %param.16) | copy-start | bytes 12292
  19.0 9.2 %copy-start.14 = (f32[64]{0:T(128)S(1)}, f32[64]{0:T(128)}, u32[]{:S(2)}) copy-start(f32[64]{0:T(128)} %param.17) | copy-start | bytes 772
  19.0 48.9 %all-to-all-start = ((f32[16,1,32768]{2,1,0:T(1,128)}), f32[16,1,32768]{2,1,0:T(1,128)}, u32[]{:S(2)}, u32[]{:S(2)}) async-start(f32[16,1,32768]{2,1,0:T(1,128)} %all_to_all.48), calls=%async_computation | async-start | bytes 4194304 | tf_op jit(solution)/shard_map/all_to_all | solution.py:72
  88.3 1.3 copy-start.18
  107.6 52.3 %all-to-all-start.1 = ((f32[16,1,32768]{2,1,0:T(1,128)}), f32[16,1,32768]{2,1,0:T(1,128)}, u32[]{:S(2)}, u32[]{:S(2)}) async-start(f32[16,1,32768]{2,1,0:T(1,128)} %all_to_all.49), calls=%async_computation.1 | async-start | bytes 4194304 | tf_op jit(solution)/shard_map/all_to_all | solution.py:81
  119.0 5.2 copy-start.15
  159.8 52.3 %all-to-all-start.2 = ((f32[16,1,32768]{2,1,0:T(1,128)}), f32[16,1,32768]{2,1,0:T(1,128)}, u32[]{:S(2)}, u32[]{:S(2)}) async-start(f32[16,1,32768]{2,1,0:T(1,128)} %all_to_all.50), calls=%async_computation.2 | async-start | bytes 4194304 | tf_op jit(solution)/shard_map/all_to_all | solution.py:82
  225.5 6.7 %copy-start.1 = (bf16[1024,1024]{0,1:T(8,128)(2,1)S(1)}, bf16[1024,1024]{0,1:T(8,128)(2,1)}, u32[]{:S(2)}) copy-start(bf16[1024,1024]{0,1:T(8,128)(2,1)} %copy.46) | copy-start | bytes 6291460
  225.5 6.7 %copy-start.7 = (f32[16,64,2,4,64]{4,3,2,1,0:T(4,128)S(1)}, f32[16,64,2,4,64]{4,3,2,1,0:T(4,128)}, u32[]{:S(2)}) copy-start(f32[16,64,2,4,64]{4,3,2,1,0:T(4,128)} %reshape.99) | copy-start | bytes 6291460
  232.3 3.9 copy-start.2
  232.3 3.9 copy-start.8
  232.3 3.9 copy-start.9
  283.0 4.2 copy-start.11
  285.8 1.3 copy-start.4
  375.3 1.3 copy-start.17
  394.5 46.0 %all-to-all-start.4 = ((f32[16,1,32768]{2,1,0:T(1,128)}), f32[16,1,32768]{2,1,0:T(1,128)}, u32[]{:S(2)}, u32[]{:S(2)}) async-start(f32[16,1,32768]{2,1,0:T(1,128)} %all_to_all.52), calls=%async_computation.4 | async-start | bytes 4194304 | tf_op jit(solution)/shard_map/all_to_all | solution.py:81
  399.7 5.2 copy-start.16
  440.6 75.5 %all-to-all-start.5 = ((f32[16,1,32768]{2,1,0:T(1,128)}), f32[16,1,32768]{2,1,0:T(1,128)}, u32[]{:S(2)}, u32[]{:S(2)}) async-start(f32[16,1,32768]{2,1,0:T(1,128)} %all_to_all.53), calls=%async_computation.5 | async-start | bytes 4194304 | tf_op jit(solution)/shard_map/all_to_all | solution.py:82
  529.4 6.7 %copy-start.3 = (f32[2,4,64,1024,1]{3,2,4,1,0:T(8,128)S(1)}, f32[2,4,64,1024,1]{3,2,4,1,0:T(8,128)}, u32[]{:S(2)}) copy-start(f32[2,4,64,1024,1]{3,2,4,1,0:T(8,128)} %copy-done.2) | copy-start | bytes 6291460
  529.4 6.7 %copy-start.5 = (f32[2,4,64,1024]{3,2,1,0:T(8,128)S(1)}, f32[2,4,64,1024]{3,2,1,0:T(8,128)}, u32[]{:S(2)}) copy-start(f32[2,4,64,1024]{3,2,1,0:T(8,128)} %get-tuple-element.14) | copy-start | bytes 6291460
  529.4 6.7 %copy-start.6 = (f32[2,4,64,1024,1]{3,2,4,1,0:T(8,128)S(1)}, f32[2,4,64,1024,1]{3,2,4,1,0:T(8,128)}, u32[]{:S(2)}) copy-start(f32[2,4,64,1024,1]{3,2,4,1,0:T(8,128)} %get-tuple-element.16) | copy-start | bytes 6291460
  529.4 6.7 %copy-start.10 = (bf16[1024,1024]{1,0:T(8,128)(2,1)S(1)}, bf16[1024,1024]{1,0:T(8,128)(2,1)}, u32[]{:S(2)}) copy-start(bf16[1024,1024]{1,0:T(8,128)(2,1)} %param.13) | copy-start | bytes 6291460
where the time goes:
time: 586 us; the launch traced here: 581 us
  blocking collectives  162 us (28%)
  local copies, waits for them, and re-layouts  109 us (19%)
  matrix products  101 us (17%)
  waiting for transfers between devices  90.2 us (15%)
  other arithmetic  65.3 us (11%)
  starting transfers between devices  47 us (8%)
    psum x2, blocking collectives, residual_inner(): return lax.psum(jnp.sum(residual * z_field), 'mode')  80.3 us
    all_to_all x1, blocking collectives, spectral(): lax.all_to_all(outgoing, 'mode', split_axis=0, concat_axis=0, tiled=True)  51.8 us
    all_to_all x1, waiting for transfers between devices, spectral(): lax.all_to_all(outgoing, 'mode', split_axis=0, concat_axis=0, tiled=True)  39.6 us
    all_to_all x2, waiting for transfers between devices, precond_apply(): lax.all_to_all(outgoing, 'mode', split_axis=0, concat_axis=0, tiled=True)  34.8 us
    psum x1, blocking collectives, body(): curvature = lax.psum(jnp.sum(direction * along), 'mode')  30.2 us
    dot_general x4, matrix products, columns_to_send(): jnp.einsum('mrk,cspk->mcspr', reshaped, columns, precision=lax.Precision....  27 us
    dot_general x4, matrix products, received_to_rows(): jnp.einsum('jmc,mcspr->sprj', reshaped, block, precision=lax.Precision.HI...  26.5 us
    all_to_all x2, starting transfers between devices, precond_apply(): lax.all_to_all(kernel_send, 'mode', split_axis=0, concat_axis=0, tiled=True)  22.5 us
  transfers between devices with their start and end apart: 5, of which 4 were waited for; matrix products, arithmetic and copies ran while one was open for 14% of the time, Pallas kernels for 0%

commit v1 on v0

v1 whole, which is shorter than its diff:
```python
import functools

import jax
import jax.numpy as jnp
from jax import lax
from jax.experimental import pallas as pl
from jax.experimental.pallas import tpu as pltpu
from jax.sharding import PartitionSpec as P

NCLASS = 8
ITERS = 2
F32 = jnp.float32
BF16 = jnp.bfloat16


def along_rows(matrix, field):
    return jnp.einsum("jk,sprk->sprj", matrix, field, precision=lax.Precision.HIGHEST)


def rows_to_send(matrix, field, groups):
    result = jnp.einsum("kj,sprk->jspr", matrix, field, precision=lax.Precision.HIGHEST)
    return result.reshape(groups, -1)


def received_to_columns(matrix, received, shape5):
    groups, cols, samples, planes, rows = shape5
    block = received.reshape(shape5)
    reshaped = matrix.reshape(groups, rows, matrix.shape[1])
    return jnp.einsum("mri,mcspr->cspi", reshaped, block, precision=lax.Precision.HIGHEST)


def along_columns(matrix, columns):
    return jnp.einsum("ik,cspk->cspi", matrix, columns, precision=lax.Precision.HIGHEST)


def columns_to_send(matrix, columns, groups, rows):
    reshaped = matrix.reshape(groups, rows, matrix.shape[1])
    result = jnp.einsum("mrk,cspk->mcspr", reshaped, columns, precision=lax.Precision.HIGHEST)
    return result.reshape(groups, -1)


def received_to_rows(matrix, received, shape5):
    groups, cols, samples, planes, rows = shape5
    block = received.reshape(shape5)
    reshaped = matrix.reshape(matrix.shape[0], groups, cols)
    return jnp.einsum("jmc,mcspr->sprj", reshaped, block, precision=lax.Precision.HIGHEST)


def general_body(
    right_side,
    classes,
    noise_table,
    kernel_first,
    kernel_second,
    basis_first,
    basis_second,
    eigen_first,
    eigen_second,
):
    groups = lax.axis_size("mode")
    samples, planes, rows, width_two = right_side.shape
    cols = eigen_second.shape[0]
    shape5 = (groups, cols, samples, planes, rows)
    kern_one = kernel_first.astype(F32)
    kern_two = kernel_second.astype(F32)
    base_one = basis_first.astype(F32)
    base_two = basis_second.astype(F32)
    noise = jnp.zeros(classes.shape, F32)
    for level in range(NCLASS):
        noise = noise + jnp.where(classes == level, noise_table[level], 0.0)
    noise = noise[None]
    mean_noise = jnp.mean(noise_table)
    col_weights = 1.0 / (eigen_second[:, None] * eigen_first[None, :] + mean_noise)
    col_weights = col_weights[:, None, None, :]

    def exchange(outgoing):
        return lax.all_to_all(outgoing, "mode", split_axis=0, concat_axis=0, tiled=True)

    def precond_apply(field):
        incoming = exchange(rows_to_send(base_two, field, groups))
        weighted = received_to_columns(base_one, incoming, shape5) * col_weights
        columns = along_columns(base_one, weighted)
        back = exchange(columns_to_send(base_one, weighted, groups, rows))
        kernel_back = exchange(columns_to_send(kern_one, columns, groups, rows))
        z_field = received_to_rows(base_two, back, shape5)
        image = (
            along_rows(kern_two, received_to_rows(base_two, kernel_back, shape5)) + noise * z_field
        )
        return (z_field, image)

    def inner(left, right):
        return lax.psum(jnp.sum(left * right), "mode")

    solution_field = jnp.zeros_like(right_side)
    residual = right_side
    z_field, image = precond_apply(residual)
    direction, along = (z_field, image)
    gamma = inner(residual, z_field)
    for step in range(ITERS):
        alpha = gamma / inner(direction, along)
        solution_field = solution_field + alpha * direction
        residual = residual - alpha * along
        if step + 1 < ITERS:
            z_field, image = precond_apply(residual)
            gamma_new = inner(residual, z_field)
            ratio = gamma_new / gamma
            direction = z_field + ratio * direction
            along = image + ratio * along
            gamma = gamma_new
    return (solution_field, residual)


def split(value):
    high = value.astype(BF16)
    low = (value - high.astype(F32)).astype(BF16)
    return high, low


def times_right(value, matrix, contract):
    high, low = split(value)
    dims = (((1,), (contract,)), ((), ()))
    both = jnp.concatenate([high, low], axis=0)
    result = lax.dot_general(both, matrix, dims, preferred_element_type=F32)
    return result[: value.shape[0]] + result[value.shape[0] :]


def times_left(matrix, value):
    high, low = split(value)
    dims = (((1,), (0,)), ((), ()))
    return lax.dot_general(matrix, high, dims, preferred_element_type=F32) + lax.dot_general(
        matrix, low, dims, preferred_element_type=F32
    )


def fold(value):
    total = jnp.sum(value, axis=0, keepdims=True)
    return functools.reduce(
        jnp.add, [total[:, at : at + 128] for at in range(0, total.shape[1], 128)]
    )


def params(dims):
    return pltpu.CompilerParams(
        dimension_semantics=("arbitrary",) * dims, vmem_limit_bytes=56 * 1024 * 1024
    )


def outgoing_kernel(table_ref, right_ref, class_ref, basis_ref, out_ref):
    samples, _, rows, width = right_ref.shape
    cores = out_ref.shape[1] // samples
    half = width // cores
    field = right_ref[...].reshape(samples * rows, width)
    mapped = times_right(field, basis_ref[...], 0)
    level = class_ref[0]
    noise = jnp.full(level.shape, table_ref[0], F32)
    for index in range(1, NCLASS):
        noise = jnp.where(level == index, table_ref[index], noise)
    share = rows // cores
    for sample in range(samples):
        for core in range(cores):
            out_ref[0, sample * cores + core, :rows, :] = mapped[
                sample * rows : (sample + 1) * rows, core * half : (core + 1) * half
            ]
            out_ref[0, sample * cores + core, rows:, :] = noise[
                core * share : (core + 1) * share, sample * half : (sample + 1) * half
            ]


def column_kernel(first_call, place_ref, *refs):
    if first_call:
        (field_ref, weight_ref, turned_ref, basis_ref, kernel_ref) = refs[:5]
        (spectral_ref, keep_ref, send_ref, sum_ref, scratch_ref) = refs[5:]
    else:
        (held_ref, got_ref, before_ref, weight_ref, turned_ref, basis_ref, kernel_ref) = refs[:7]
        (keep_ref, send_ref, sum_ref, scratch_ref) = refs[7:]
    groups, rows, chunk = scratch_ref.shape
    share = rows // 2
    core = place_ref[0]
    mine = pl.ds(pl.multiple_of(core * share, share), share)
    theirs = pl.ds(pl.multiple_of((1 - core) * share, share), share)
    if first_call:
        field = field_ref[...].reshape(groups * rows, chunk)
    else:
        scratch_ref[:, mine, :] = held_ref[...]
        scratch_ref[:, theirs, :] = got_ref[...]
        field = scratch_ref[...].reshape(groups * rows, chunk)
    spectral = times_left(turned_ref[...], field)
    weighted = spectral * weight_ref[...]
    if first_call:
        spectral_ref[...] = spectral
        sums = [fold(spectral * weighted)]
    else:
        sums = [fold(before_ref[...] * weighted), fold(spectral * weighted)]
    block = jnp.concatenate(sums + [jnp.zeros((8 - len(sums), 128), F32)], axis=0)

    @pl.when(pl.program_id(0) == 0)
    def _():
        sum_ref[...] = block

    @pl.when(pl.program_id(0) != 0)
    def _():
        sum_ref[...] += block

    column = times_left(basis_ref[...], weighted)
    scratch_ref[...] = column.reshape(groups, rows, chunk)
    keep_ref[0] = scratch_ref[:, mine, :]
    send_ref[0] = scratch_ref[:, theirs, :]
    image = times_left(kernel_ref[...], column)
    scratch_ref[...] = image.reshape(groups, rows, chunk)
    keep_ref[1] = scratch_ref[:, mine, :]
    send_ref[1] = scratch_ref[:, theirs, :]


def row_kernel(first_call, place_ref, keep_ref, got_ref, near_ref, far_ref, basis_ref, kernel_ref, *refs):
    if first_call:
        (z_ref, image_ref, back_keep_ref, back_send_ref, scratch_ref) = refs
    else:
        (one_ref, two_ref, z_ref, image_ref, sum_ref, scratch_ref) = refs
    height, width = scratch_ref.shape
    half = width // 2
    groups, share = z_ref.shape[:2]
    core = place_ref[0]
    sample = place_ref[1]
    mine = pl.ds(pl.multiple_of(core * half, half), half)
    theirs = pl.ds(pl.multiple_of((1 - core) * half, half), half)

    def whole(index):
        scratch_ref[:, mine] = keep_ref[index].reshape(height, half)
        scratch_ref[:, theirs] = got_ref[index].reshape(height, half)
        return scratch_ref[...]

    basis = basis_ref[...]
    z_field = times_right(whole(0), basis, 1)
    image = times_right(times_right(whole(1), basis, 1), kernel_ref[...], 1)
    scratch_ref[:, pl.ds(pl.multiple_of(sample * half, half), half)] = near_ref[...].reshape(
        height, half
    )
    scratch_ref[:, pl.ds(pl.multiple_of((1 - sample) * half, half), half)] = far_ref[
        ...
    ].reshape(height, half)
    image = image + scratch_ref[...] * z_field
    z_ref[...] = z_field.reshape(z_ref.shape)
    image_ref[...] = image.reshape(image_ref.shape)
    if first_call:
        scratch_ref[...] = times_right(image, basis, 0)
        back_keep_ref[...] = scratch_ref[:, mine].reshape(back_keep_ref.shape)
        back_send_ref[...] = scratch_ref[:, theirs].reshape(back_send_ref.shape)
    else:

        @pl.when(pl.program_id(0) == 0)
        def _():
            first = jnp.concatenate(
                [one_ref[0:1], two_ref[0:2], jnp.zeros((5, 128), F32)], axis=0
            )
            sum_ref[...] = jnp.broadcast_to(first[None], sum_ref.shape)

        last = jnp.concatenate(
            [jnp.zeros((3, 128), F32), fold(z_field * image), jnp.zeros((4, 128), F32)], axis=0
        )
        sum_ref[...] += jnp.broadcast_to(last[None], sum_ref.shape)


def combine_kernel(sum_ref, z_ref, image_ref, f_ref, f_image_ref, out_ref):
    total = jnp.sum(sum_ref[...], axis=0)
    total = jnp.sum(total, axis=1, keepdims=True)
    g00, g01, g11, h11 = (total[at : at + 1] for at in range(4))
    alpha = g00 / g01
    turn = alpha * g11 / g01
    gamma = alpha * alpha * g11 - g00
    curvature = alpha * alpha * h11 - turn * turn * g01
    step = gamma / curvature
    on_z = alpha + step * turn
    on_f = -(alpha * step)
    share = z_ref.shape[1]
    out_ref[:, :share, :] = on_z[None] * z_ref[...] + on_f[None] * f_ref[...]
    out_ref[:, share:, :] = on_z[None] * image_ref[...] + on_f[None] * f_image_ref[...]


def finish_kernel(got_ref, right_ref, solution_ref, residual_ref):
    cores, double = got_ref.shape[:2]
    share = double // 2
    for core in range(cores):
        at = slice(core * share, (core + 1) * share)
        solution_ref[0, 0, at, :] = got_ref[core, :share, :]
        residual_ref[0, 0, at, :] = right_ref[0, 0, at, :] - got_ref[core, share:, :]


def paired_body(
    right_side,
    classes,
    noise_table,
    kernel_first,
    kernel_second,
    basis_first,
    basis_second,
    eigen_first,
    eigen_second,
):
    groups = lax.axis_size("mode")
    samples, planes, rows, width = right_side.shape
    height = groups * rows
    cores = 2
    half = width // cores
    share = rows // cores
    tall = rows + share
    index = lax.axis_index("mode")
    core = index % cores
    sample = (index // cores) % samples
    place = jnp.stack([core, sample]).astype(jnp.int32)

    def shape_of(*shape):
        return jax.ShapeDtypeStruct(shape, F32)

    smem = pl.BlockSpec(memory_space=pltpu.SMEM)

    def full(*shape):
        return pl.BlockSpec(shape, lambda *at: (0,) * len(shape))

    core_swap = [(at, at ^ 1) for at in range(groups)]
    sample_swap = [(at, at ^ cores) for at in range(groups)]

    outgoing = pl.pallas_call(
        outgoing_kernel,
        grid=(planes,),
        in_specs=[
            smem,
            pl.BlockSpec((samples, 1, rows, width), lambda p: (0, p, 0, 0)),
            pl.BlockSpec((1, rows, width), lambda p: (p, 0, 0)),
            full(width, width),
        ],
        out_specs=pl.BlockSpec((1, samples * cores, tall, half), lambda p: (p, 0, 0, 0)),
        out_shape=shape_of(planes, samples * cores, tall, half),
        compiler_params=params(1),
        name="outgoing",
    )(noise_table, right_side, classes, basis_second)
    arrived = lax.all_to_all(
        outgoing.reshape(groups, tall, half), "mode", split_axis=0, concat_axis=0, tiled=True
    )

    eigen = eigen_second.reshape(1, -1)
    reach = 1
    while reach < groups:
        other = lax.ppermute(eigen, "mode", [(at, at ^ reach) for at in range(groups)])
        low = (index // reach) % 2 == 0
        eigen = jnp.where(
            low,
            jnp.concatenate([eigen, other], axis=1),
            jnp.concatenate([other, eigen], axis=1),
        )
        reach *= 2
    eigen = lax.dynamic_slice(eigen, (0, core * half), (1, half))
    weights = 1.0 / (eigen_first[:, None] * eigen + jnp.mean(noise_table))
    turned = basis_first.T

    near = arrived[:, rows:, :]
    far = lax.ppermute(near, "mode", sample_swap)

    chunk = half // 2
    steps = half // chunk
    tile = pl.BlockSpec((height, chunk), lambda j: (0, j))
    piece = pl.BlockSpec((groups, share, chunk), lambda j: (0, 0, j))
    pieces = pl.BlockSpec((2, groups, share, chunk), lambda j: (0, 0, 0, j))
    square = full(height, height)
    row_square = full(width, width)
    scratch = [pltpu.VMEM((groups, rows, chunk), F32)]
    spectral, keep, send, sum_one = pl.pallas_call(
        functools.partial(column_kernel, True),
        grid=(steps,),
        in_specs=[
            smem,
            pl.BlockSpec((groups, rows, chunk), lambda j: (0, 0, j)),
            tile,
            square,
            square,
            square,
        ],
        out_specs=[tile, pieces, pieces, full(8, 128)],
        out_shape=[
            shape_of(height, half),
            shape_of(2, groups, share, half),
            shape_of(2, groups, share, half),
            shape_of(8, 128),
        ],
        scratch_shapes=scratch,
        compiler_params=params(1),
        name="columns_one",
    )(place, arrived, weights, turned, basis_first, kernel_first)
    got = lax.ppermute(send, "mode", core_swap)

    part = groups // 2
    row_pieces = pl.BlockSpec((2, part, share, half), lambda i: (0, i, 0, 0))
    row_piece = pl.BlockSpec((part, share, half), lambda i: (i, 0, 0))
    row_whole = pl.BlockSpec((part, share, width), lambda i: (i, 0, 0))
    row_scratch = [pltpu.VMEM((part * share, width), F32)]
    row_specs = [smem, row_pieces, row_pieces, row_piece, row_piece, row_square, row_square]
    z_field, image, back_keep, back_send = pl.pallas_call(
        functools.partial(row_kernel, True),
        grid=(2,),
        in_specs=row_specs,
        out_specs=[row_whole, row_whole, row_piece, row_piece],
        out_shape=[
            shape_of(groups, share, width),
            shape_of(groups, share, width),
            shape_of(groups, share, half),
            shape_of(groups, share, half),
        ],
        scratch_shapes=row_scratch,
        compiler_params=params(1),
        name="rows_one",
    )(place, keep, got, near, far, basis_second, kernel_second)
    back_got = lax.ppermute(back_send, "mode", core_swap)

    keep, send, sum_two = pl.pallas_call(
        functools.partial(column_kernel, False),
        grid=(steps,),
        in_specs=[smem, piece, piece, tile, tile, square, square, square],
        out_specs=[pieces, pieces, full(8, 128)],
        out_shape=[
            shape_of(2, groups, share, half),
            shape_of(2, groups, share, half),
            shape_of(8, 128),
        ],
        scratch_shapes=scratch,
        compiler_params=params(1),
        name="columns_two",
    )(place, back_keep, back_got, spectral, weights, turned, basis_first, kernel_first)
    got = lax.ppermute(send, "mode", core_swap)

    f_field, f_image, sums = pl.pallas_call(
        functools.partial(row_kernel, False),
        grid=(2,),
        in_specs=row_specs + [full(8, 128), full(8, 128)],
        out_specs=[row_whole, row_whole, full(groups, 8, 128)],
        out_shape=[
            shape_of(groups, share, width),
            shape_of(groups, share, width),
            shape_of(groups, 8, 128),
        ],
        scratch_shapes=row_scratch,
        compiler_params=params(1),
        name="rows_two",
    )(place, keep, got, near, far, basis_second, kernel_second, sum_one, sum_two)
    sums = lax.all_to_all(sums, "mode", split_axis=0, concat_axis=0, tiled=True)

    few = groups // 8
    few_spec = pl.BlockSpec((few, share, width), lambda i: (i, 0, 0))
    answer = pl.pallas_call(
        combine_kernel,
        grid=(8,),
        in_specs=[full(groups, 8, 128)] + [few_spec] * 4,
        out_specs=pl.BlockSpec((few, rows, width), lambda i: (i, 0, 0)),
        out_shape=shape_of(groups, rows, width),
        compiler_params=params(1),
        name="combine",
    )(sums, z_field, image, f_field, f_image)
    answer = lax.all_to_all(answer, "mode", split_axis=0, concat_axis=0, tiled=True)

    block = pl.BlockSpec((1, 1, rows, width), lambda p, s: (s, p, 0, 0))
    return tuple(
        pl.pallas_call(
            finish_kernel,
            grid=(planes, samples),
            in_specs=[
                pl.BlockSpec((cores, rows, width), lambda p, s: (p * samples + s, 0, 0)),
                block,
            ],
            out_specs=[block, block],
            out_shape=[shape_of(*right_side.shape)] * 2,
            compiler_params=params(2),
            name="finish",
        )(answer, right_side)
    )


def body(right_side, classes, *rest):
    groups = lax.axis_size("mode")
    samples, planes, rows, width = right_side.shape
    paired = (
        groups == 2 * samples * planes
        and samples == 2
        and rows % 16 == 0
        and width % 512 == 0
        and groups % 8 == 0
    )
    chosen = paired_body if paired else general_body
    return chosen(right_side, classes, *rest)


def solution(mesh):
    in_specs = (
        P(None, "blocks", "mode", None),
        P("blocks", "mode", None),
        P(),
        P(),
        P(),
        P(),
        P(),
        P(),
        P("mode"),
    )
    out_specs = (P(None, "blocks", "mode", None), P(None, "blocks", "mode", None))
    return jax.shard_map(body, mesh=mesh, in_specs=in_specs, out_specs=out_specs, check_vma=False)
```

time: 586 us -> 310 us (0.53)
  local copies, waits for them, and re-layouts: 109 us -> 7.95 us
  matrix products: 101 us -> 0 us
  Pallas kernels: 0 us -> 81.4 us
  other arithmetic: 65.3 us -> 3.04 us
  blocking collectives: 162 us -> 108 us
  starting transfers between devices: 47 us -> 16.1 us
    psum x3 -> x0, blocking collectives: 110 us -> none  [the longest x2 80.3 us: residual_inner(): return lax.psum(jnp.sum(residual * z_field), 'mode')]
    dot_general x16 -> x0, matrix products: 101 us -> none  [the longest x4 27 us: columns_to_send(): jnp.einsum('mrk,cspk->mcspr', reshaped, columns, precision=lax.Precision....]
    ppermute x0 -> x8, waiting for transfers between devices: none -> 91.4 us  [the longest x4 60.3 us: paired_body(): lax.ppermute(eigen, 'mode', [(at, at ^ reach) for at in range(groups)])]
    all_to_all x5 -> x1, waiting for transfers between devices: 90.2 us -> 0.01 us  [paired_body(): lax.all_to_all(outgoing.reshape(groups, tall, half), 'mode', split_axis=0...]
    pallas_call x0 -> x7, Pallas kernels: none -> 81.4 us  [the longest x1 17 us: paired_body(): pl.pallas_call(functools.partial(column_kernel, False), grid=(steps,), in...]
    all_to_all x1 -> x2, blocking collectives: 51.8 us -> 108 us  [the longest x1 96.6 us: paired_body(): lax.all_to_all(answer, 'mode', split_axis=0, concat_axis=0, tiled=True)]
    all_to_all x6 -> x0, other arithmetic: 47.8 us -> none  [the longest x2 16 us: spectral(): lax.all_to_all(outgoing, 'mode', split_axis=0, concat_axis=0, tiled=True)]
    all_to_all x5 -> x1, starting transfers between devices: 47 us -> 7.6 us  [paired_body(): lax.all_to_all(outgoing.reshape(groups, tall, half), 'mode', split_axis=0...]
  transfers between devices with their start and end apart: 5 -> 9, of which waited for: 4 -> 6; matrix products, arithmetic and copies ran while one was open for 14% -> 2% of each run, Pallas kernels for 0% -> 0%
where the time goes in v1:
time: 310 us; the launch traced here: 309 us
  blocking collectives  108 us (35%)
  waiting for transfers between devices  91.5 us (30%)
  Pallas kernels  81.4 us (26%)
  starting transfers between devices  16.1 us (5%)
  local copies, waits for them, and re-layouts  7.95 us (3%)
    all_to_all x1, blocking collectives, paired_body(): lax.all_to_all(answer, 'mode', split_axis=0, concat_axis=0, tiled=True)  96.6 us
    ppermute x4, waiting for transfers between devices, paired_body(): lax.ppermute(eigen, 'mode', [(at, at ^ reach) for at in range(groups)])  60.3 us
    ppermute x1, waiting for transfers between devices, paired_body(): far = lax.ppermute(near, 'mode', sample_swap)  24.1 us
    pallas_call x1, Pallas kernels, paired_body(): pl.pallas_call(functools.partial(column_kernel, False), grid=(steps,), in...  17 us
    pallas_call x1, Pallas kernels, paired_body(): pl.pallas_call(functools.partial(column_kernel, True), grid=(steps,), in_...  16.4 us
    pallas_call x1, Pallas kernels, paired_body(): pl.pallas_call(functools.partial(row_kernel, True), grid=(2,), in_specs=r...  14 us
    pallas_call x1, Pallas kernels, paired_body(): pl.pallas_call(functools.partial(row_kernel, False), grid=(2,), in_specs=...  12.1 us
    all_to_all x1, blocking collectives, paired_body(): sums = lax.all_to_all(sums, 'mode', split_axis=0, concat_axis=0, tiled=True)  11 us
  transfers between devices with their start and end apart: 9, of which 6 were waited for; matrix products, arithmetic and copies ran while one was open for 2% of the time, Pallas kernels for 0%

profile of v1, /device:TPU:0, one launch (start us, length us, event | category | flops | bytes accessed | tf_op | source)
XLA Modules:
  0.0 308.9 jit_solution(8689968503570779187)
XLA Ops:
  0.6 6.7 %outgoing.1 = f32[4,4,96,512]{3,2,1,0:T(8,128)} custom-call(f32[8]{0:T(128)} %table_ref.1, f32[2,4,64,1024]{3,2,1,0:T(8,128)} %right_ref.3, s32[4,64,1024]{2,1,0:T(8,128)} %class_ref.1, bf16[1024,1024]{1,0:T(8,128)(2,1)} %basis_ref.5), custom_call_target="tpu_custom_call" | custom-call | tf_op jit(solution)/shard_map/outgoing/pallas_call | solution.py:322
  7.4 7.6 %all-to-all-start = ((f32[16,96,512]{2,1,0:T(8,128)}), f32[16,96,512]{2,1,0:T(8,128)}, u32[]{:S(2)}, u32[]{:S(2)}) async-start(f32[16,96,512]{2,1,0:T(8,128)} %bitcast.14), calls=%async_computation | async-start | bytes 6291456 | tf_op jit(solution)/shard_map/all_to_all | solution.py:336
  15.0 0.4 collective-permute-start
  15.4 0.6 reduce_sum.9
  16.0 0.6 pad_add_fusion.place_ref
  16.6 2.5 copy.11
  19.7 0.1 broadcast_select_fusion.3
  19.8 1.6 collective-permute-start.1
  21.5 10.2 %collective-permute-done.1 = f32[1,128]{1,0:T(1,128)S(1)} collective-permute-done((f32[1,128]{1,0:T(1,128)S(1)}, f32[1,128]{1,0:T(1,128)S(1)}, u32[]{:S(2)}, u32[]{:S(2)}) %collective-permute-start.1) | collective-permute-done | bytes 544 | tf_op jit(solution)/shard_map/ppermute | solution.py:343
  31.7 0.4 collective-permute-start.2
  32.2 34.6 %collective-permute-done.2 = f32[1,256]{1,0:T(1,128)S(1)} collective-permute-done((f32[1,256]{1,0:T(1,128)S(1)}, f32[1,256]{1,0:T(1,128)S(1)}, u32[]{:S(2)}, u32[]{:S(2)}) %collective-permute-start.2) | collective-permute-done | bytes 1056 | tf_op jit(solution)/shard_map/ppermute | solution.py:343
  66.8 4.4 %collective-permute-start.3 = (f32[1,512]{1,0:T(1,128)S(1)}, f32[1,512]{1,0:T(1,128)S(1)}, u32[]{:S(2)}, u32[]{:S(2)}) collective-permute-start(f32[1,512]{1,0:T(1,128)S(1)} %broadcast_select_fusion.1), channel_id=1, source_target_pairs={{0,8},{1,9},{2,10},{3,11},{4,12},{5,13},{6,14},{7,15},{8,0},{9,1},... | collective-permute-start | bytes 6152 | tf_op jit(solution)/shard_map/ppermute | solution.py:343
  71.2 15.4 %collective-permute-done.3 = f32[1,512]{1,0:T(1,128)S(1)} collective-permute-done((f32[1,512]{1,0:T(1,128)S(1)}, f32[1,512]{1,0:T(1,128)S(1)}, u32[]{:S(2)}, u32[]{:S(2)}) %collective-permute-start.3) | collective-permute-done | bytes 2080 | tf_op jit(solution)/shard_map/ppermute | solution.py:343
  86.6 1.7 add_divide_fusion.refs_1_.refs_3_
  88.3 16.4 %columns_one.1 = (f32[1024,512]{1,0:T(8,128)}, f32[2,16,32,512]{3,2,1,0:T(8,128)}, f32[2,16,32,512]{3,2,1,0:T(8,128)}, f32[8,128]{1,0:T(8,128)}) custom-call(s32[2]{0:T(128)} %pad_add_fusion.place_ref, f32[16,96,512]{2,1,0:T(8,128)} %all-to-all-done.refs_0_, f32[1024,512]{1,0:T(8,128)} %add_divide_fusion.refs_1_.refs_3_, bf16[1024,1024]{1,0:T(8,128)(2,1)} %bitcast.12, ...), custom_call_target="tpu_custom_call" | custom-call | tf_op jit(solution)/shard_map/columns_one/pallas_call | solution.py:366
  104.7 1.3 slice.4.near_ref
  106.0 1.5 collective-permute-start.5
  107.5 24.1 %collective-permute-done.5.far_ref = f32[16,32,512]{2,1,0:T(8,128)S(1)} collective-permute-done((f32[16,32,512]{2,1,0:T(8,128)S(1)}, f32[16,32,512]{2,1,0:T(8,128)S(1)}, u32[]{:S(2)}, u32[]{:S(2)}) %collective-permute-start.5) | collective-permute-done | bytes 1048608 | tf_op jit(solution)/shard_map/ppermute | solution.py:356
  131.6 1.0 copy-done.2
  132.6 0.8 copy-done.3
  133.4 14.0 %rows_one.1 = (f32[16,32,1024]{2,1,0:T(8,128)}, f32[16,32,1024]{2,1,0:T(8,128)}, f32[16,32,512]{2,1,0:T(8,128)}, f32[16,32,512]{2,1,0:T(8,128)}) custom-call(s32[2]{0:T(128)} %pad_add_fusion.place_ref, f32[2,16,32,512]{3,2,1,0:T(8,128)} %get-tuple-element.16.keep_ref, f32[2,16,32,512]{3,2,1,0:T(8,128)} %copy-done.3, f32[16,32,512]{2,1,0:T(8,128)} %copy-done.1, ...), custom_call_target="tpu_custom_call" | custom-call | tf_op jit(solution)/shard_map/rows_one/pallas_call | solution.py:396
  147.4 2.9 collective-permute-done.6.refs_1_
  150.2 1.0 copy-done.5
  151.2 17.0 %columns_two.1 = (f32[2,16,32,512]{3,2,1,0:T(8,128)}, f32[2,16,32,512]{3,2,1,0:T(8,128)}, f32[8,128]{1,0:T(8,128)}) custom-call(s32[2]{0:T(128)} %pad_add_fusion.place_ref, f32[16,32,512]{2,1,0:T(8,128)} %get-tuple-element.18.refs_0_, f32[16,32,512]{2,1,0:T(8,128)} %copy-done.5, f32[1024,512]{1,0:T(8,128)} %get-tuple-element.20.refs_2_, ...), custom_call_target="tpu_custom_call" | custom-call | tf_op jit(solution)/shard_map/columns_two/pallas_call | solution.py:413
  168.2 0.1 collective-permute-start.7
  168.4 4.2 %collective-permute-done.7.got_ref = f32[2,16,32,512]{3,2,1,0:T(8,128)S(1)} collective-permute-done((f32[2,16,32,512]{3,2,1,0:T(8,128)}, f32[2,16,32,512]{3,2,1,0:T(8,128)S(1)}, u32[]{:S(2)}, u32[]{:S(2)}) %collective-permute-start.7) | collective-permute-done | bytes 2097184 | tf_op jit(solution)/shard_map/ppermute | solution.py:427
  172.6 1.3 copy-done.4
  173.9 12.1 %rows_two.1 = (f32[16,32,1024]{2,1,0:T(8,128)}, f32[16,32,1024]{2,1,0:T(8,128)}, f32[16,8,128]{2,1,0:T(8,128)}) custom-call(s32[2]{0:T(128)} %pad_add_fusion.place_ref, f32[2,16,32,512]{3,2,1,0:T(8,128)} %get-tuple-element.21.keep_ref, f32[2,16,32,512]{3,2,1,0:T(8,128)} %copy-done.4, f32[16,32,512]{2,1,0:T(8,128)} %copy-done.1, f32[16,32,512]{2,1,0:T(8,128)} %copy-done.2, ...), custom_call_target="tpu_custom_call" | custom-call | tf_op jit(solution)/shard_map/rows_two/pallas_call | solution.py:429
  186.1 11.0 %all_to_all.15.sum_ref = f32[16,8,128]{2,1,0:T(8,128)} all-to-all(f32[16,8,128]{2,1,0:T(8,128)} %get-tuple-element.25), channel_id=1, replica_groups=mesh['blocks'=2,'mode'=16] {'mode'}, dimensions={0} | all-to-all | bytes 131072 | tf_op jit(solution)/shard_map/all_to_all | solution.py:443
  197.1 8.2 %combine.1 = f32[16,64,1024]{2,1,0:T(8,128)} custom-call(f32[16,8,128]{2,1,0:T(8,128)} %all_to_all.15.sum_ref, f32[16,32,1024]{2,1,0:T(8,128)} %get-tuple-element.26.z_ref, f32[16,32,1024]{2,1,0:T(8,128)} %get-tuple-element.27.image_ref, f32[16,32,1024]{2,1,0:T(8,128)} %get-tuple-element.28.f_ref, f32[16,32,1024]{2,1,0:T(8,128)} %get-tuple-element.29.f_image_ref), custom_call_target="tpu_custom_call" | custom-call | tf_op jit(solution)/shard_map/combine/pallas_call | solution.py:447
  205.3 96.6 %all_to_all.16.got_ref = f32[16,64,1024]{2,1,0:T(8,128)} all-to-all(f32[16,64,1024]{2,1,0:T(8,128)} %combine.1), channel_id=1, replica_groups=mesh['blocks'=2,'mode'=16] {'mode'}, dimensions={0} | all-to-all | bytes 8388608 | tf_op jit(solution)/shard_map/all_to_all | solution.py:456
  301.9 7.0 %finish.1 = (f32[2,4,64,1024]{3,2,1,0:T(8,128)}, f32[2,4,64,1024]{3,2,1,0:T(8,128)}) custom-call(f32[16,64,1024]{2,1,0:T(8,128)} %all_to_all.16.got_ref, f32[2,4,64,1024]{3,2,1,0:T(8,128)} %right_ref.3), custom_call_target="tpu_custom_call" | custom-call | tf_op jit(solution)/shard_map/finish/pallas_call | solution.py:460
  (25 shorter events, 0.2 us)
Async XLA Ops:
  7.4 7.6 %copy-start.7 = (f32[64]{0:T(128)S(1)}, f32[64]{0:T(128)}, u32[]{:S(2)}) copy-start(f32[64]{0:T(128)} %param.17) | copy-start | bytes 772
  7.4 8.1 %copy-start.8 = (f32[8]{0:T(128)S(1)}, f32[8]{0:T(128)}, u32[]{:S(2)}) copy-start(f32[8]{0:T(128)} %table_ref.1) | copy-start | bytes 100
  7.4 9.2 %copy-start = (bf16[1024,1024]{1,0:T(8,128)(2,1)S(1)}, bf16[1024,1024]{1,0:T(8,128)(2,1)}, u32[]{:S(2)}) copy-start(bf16[1024,1024]{1,0:T(8,128)(2,1)} %refs_5_.1) | copy-start | bytes 6291460
  7.4 80.9 %all-to-all-start = ((f32[16,96,512]{2,1,0:T(8,128)}), f32[16,96,512]{2,1,0:T(8,128)}, u32[]{:S(2)}, u32[]{:S(2)}) async-start(f32[16,96,512]{2,1,0:T(8,128)} %bitcast.14), calls=%async_computation | async-start | bytes 6291456 | tf_op jit(solution)/shard_map/all_to_all | solution.py:336
  15.0 4.7 %collective-permute-start = (f32[1,64]{1,0:T(1,128)S(1)}, f32[1,64]{1,0:T(1,128)S(1)}, u32[]{:S(2)}, u32[]{:S(2)}) collective-permute-start(f32[1,64]{1,0:T(1,128)S(1)} %bitcast.21), channel_id=1, source_target_pairs={{0,1},{1,0},{2,3},{3,2},{4,5},{5,4},{6,7},{7,6},{8,9},{9,8},{10,11... | collective-permute-start | bytes 776 | tf_op jit(solution)/shard_map/ppermute | solution.py:343
  16.6 70.0 %copy-start.6 = (f32[1024]{0:T(1024)S(1)}, f32[1024]{0:T(1024)}, u32[]{:S(2)}) copy-start(f32[1024]{0:T(1024)} %param.16) | copy-start | bytes 12292
  19.8 11.9 %collective-permute-start.1 = (f32[1,128]{1,0:T(1,128)S(1)}, f32[1,128]{1,0:T(1,128)S(1)}, u32[]{:S(2)}, u32[]{:S(2)}) collective-permute-start(f32[1,128]{1,0:T(1,128)S(1)} %broadcast_select_fusion.3), channel_id=1, source_target_pairs={{0,2},{1,3},{2,0},{3,1},{4,6},{5,7},{6,4},{7,5},{8,10},{9,11},{10,... | collective-permute-start | bytes 1544 | tf_op jit(solution)/shard_map/ppermute | solution.py:343
  31.7 35.1 %collective-permute-start.2 = (f32[1,256]{1,0:T(1,128)S(1)}, f32[1,256]{1,0:T(1,128)S(1)}, u32[]{:S(2)}, u32[]{:S(2)}) collective-permute-start(f32[1,256]{1,0:T(1,128)S(1)} %broadcast_select_fusion.2), channel_id=1, source_target_pairs={{0,4},{1,5},{2,6},{3,7},{4,0},{5,1},{6,2},{7,3},{8,12},{9,13},{10,... | collective-permute-start | bytes 3080 | tf_op jit(solution)/shard_map/ppermute | solution.py:343
  66.8 19.8 %collective-permute-start.3 = (f32[1,512]{1,0:T(1,128)S(1)}, f32[1,512]{1,0:T(1,128)S(1)}, u32[]{:S(2)}, u32[]{:S(2)}) collective-permute-start(f32[1,512]{1,0:T(1,128)S(1)} %broadcast_select_fusion.1), channel_id=1, source_target_pairs={{0,8},{1,9},{2,10},{3,11},{4,12},{5,13},{6,14},{7,15},{8,0},{9,1},... | collective-permute-start | bytes 6152 | tf_op jit(solution)/shard_map/ppermute | solution.py:343
  104.7 27.0 %collective-permute-start.4 = (f32[2,16,32,512]{3,2,1,0:T(8,128)}, f32[2,16,32,512]{3,2,1,0:T(8,128)S(1)}, u32[]{:S(2)}, u32[]{:S(2)}) collective-permute-start(f32[2,16,32,512]{3,2,1,0:T(8,128)} %get-tuple-element.17), channel_id=1, source_target_pairs={{0,1},{1,0},{2,3},{3,2},{4,5},{5,4},{6,7},{7,6},{8,9},{9,8},{10,11... | collective-permute-start | bytes 6291464 | tf_op jit(solution)/shard_map/ppermute | solution.py:388
  106.0 25.6 %copy-start.1 = (f32[16,32,512]{2,1,0:T(8,128)}, f32[16,32,512]{2,1,0:T(8,128)S(1)}, u32[]{:S(2)}) copy-start(f32[16,32,512]{2,1,0:T(8,128)S(1)} %slice.4.near_ref) | copy-start | bytes 3145732
  106.0 25.6 %collective-permute-start.5 = (f32[16,32,512]{2,1,0:T(8,128)S(1)}, f32[16,32,512]{2,1,0:T(8,128)S(1)}, u32[]{:S(2)}, u32[]{:S(2)}) collective-permute-start(f32[16,32,512]{2,1,0:T(8,128)S(1)} %slice.4.near_ref), channel_id=1, source_target_pairs={{0,2},{1,3},{2,0},{3,1},{4,6},{5,7},{6,4},{7,5},{8,10},{9,11},{10,... | collective-permute-start | bytes 3145736 | tf_op jit(solution)/shard_map/ppermute | solution.py:356
  131.6 1.0 copy-start.2
  131.6 1.8 copy-start.3
  147.4 2.9 collective-permute-start.6
  150.2 1.0 copy-start.5
  168.2 4.4 %collective-permute-start.7 = (f32[2,16,32,512]{3,2,1,0:T(8,128)}, f32[2,16,32,512]{3,2,1,0:T(8,128)S(1)}, u32[]{:S(2)}, u32[]{:S(2)}) collective-permute-start(f32[2,16,32,512]{3,2,1,0:T(8,128)} %get-tuple-element.22), channel_id=1, source_target_pairs={{0,1},{1,0},{2,3},{3,2},{4,5},{5,4},{6,7},{7,6},{8,9},{9,8},{10,11... | collective-permute-start | bytes 6291464 | tf_op jit(solution)/shard_map/ppermute | solution.py:427
  172.6 1.3 copy-start.4

commit v2 on v1

--- a/solution.py
+++ b/solution.py
@@ -7,6 +7,7 @@
 from jax.experimental.pallas import tpu as pltpu
 from jax.sharding import PartitionSpec as P
 
+
 NCLASS = 8
 ITERS = 2
 F32 = jnp.float32
@@ -23,7 +24,7 @@
 
 
 def received_to_columns(matrix, received, shape5):
-    groups, cols, samples, planes, rows = shape5
+    groups, _, _, _, rows = shape5
     block = received.reshape(shape5)
     reshaped = matrix.reshape(groups, rows, matrix.shape[1])
     return jnp.einsum("mri,mcspr->cspi", reshaped, block, precision=lax.Precision.HIGHEST)
@@ -40,7 +41,7 @@
 
 
 def received_to_rows(matrix, received, shape5):
-    groups, cols, samples, planes, rows = shape5
+    groups, cols, _, _, _ = shape5
     block = received.reshape(shape5)
     reshaped = matrix.reshape(matrix.shape[0], groups, cols)
     return jnp.einsum("jmc,mcspr->sprj", reshaped, block, precision=lax.Precision.HIGHEST)
@@ -58,7 +59,7 @@
     eigen_second,
 ):
     groups = lax.axis_size("mode")
-    samples, planes, rows, width_two = right_side.shape
+    samples, planes, rows, _ = right_side.shape
     cols = eigen_second.shape[0]
     shape5 = (groups, cols, samples, planes, rows)
     kern_one = kernel_first.astype(F32)
@@ -127,9 +128,9 @@
 def times_left(matrix, value):
     high, low = split(value)
     dims = (((1,), (0,)), ((), ()))
-    return lax.dot_general(matrix, high, dims, preferred_element_type=F32) + lax.dot_general(
-        matrix, low, dims, preferred_element_type=F32
-    )
+    both = jnp.concatenate([high, low], axis=1)
+    result = lax.dot_general(matrix, both, dims, preferred_element_type=F32)
+    return result[:, : value.shape[1]] + result[:, value.shape[1] :]
 
 
 def fold(value):
@@ -139,9 +140,9 @@
     )
 
 
-def params(dims):
+def params(dims, mebibytes):
     return pltpu.CompilerParams(
-        dimension_semantics=("arbitrary",) * dims, vmem_limit_bytes=56 * 1024 * 1024
+        dimension_semantics=("arbitrary",) * dims, vmem_limit_bytes=mebibytes * 1024 * 1024
     )
 
 
@@ -218,7 +219,6 @@
         (one_ref, two_ref, z_ref, image_ref, sum_ref, scratch_ref) = refs
     height, width = scratch_ref.shape
     half = width // 2
-    groups, share = z_ref.shape[:2]
     core = place_ref[0]
     sample = place_ref[1]
     mine = pl.ds(pl.multiple_of(core * half, half), half)
@@ -277,12 +277,18 @@
 
 
 def finish_kernel(got_ref, right_ref, solution_ref, residual_ref):
-    cores, double = got_ref.shape[:2]
-    share = double // 2
-    for core in range(cores):
-        at = slice(core * share, (core + 1) * share)
-        solution_ref[0, 0, at, :] = got_ref[core, :share, :]
-        residual_ref[0, 0, at, :] = right_ref[0, 0, at, :] - got_ref[core, share:, :]
+    count, rows = got_ref.shape[:2]
+    samples = right_ref.shape[0]
+    cores = count // samples
+    share = rows // cores
+    for sample in range(samples):
+        for core in range(cores):
+            at = slice(core * share, (core + 1) * share)
+            block = sample * cores + core
+            solution_ref[sample, 0, at, :] = got_ref[block, :share, :]
+            residual_ref[sample, 0, at, :] = (
+                right_ref[sample, 0, at, :] - got_ref[block, share:, :]
+            )
 
 
 def paired_body(
@@ -314,6 +320,11 @@
     smem = pl.BlockSpec(memory_space=pltpu.SMEM)
 
     def full(*shape):
+        return pl.BlockSpec(
+            shape, lambda *at: (0,) * len(shape), pipeline_mode=pl.Buffered(1)
+        )
+
+    def whole_out(*shape):
         return pl.BlockSpec(shape, lambda *at: (0,) * len(shape))
 
     core_swap = [(at, at ^ 1) for at in range(groups)]
@@ -330,7 +341,7 @@
         ],
         out_specs=pl.BlockSpec((1, samples * cores, tall, half), lambda p: (p, 0, 0, 0)),
         out_shape=shape_of(planes, samples * cores, tall, half),
-        compiler_params=params(1),
+        compiler_params=params(1, 16),
         name="outgoing",
     )(noise_table, right_side, classes, basis_second)
     arrived = lax.all_to_all(
@@ -374,7 +385,7 @@
             square,
             square,
         ],
-        out_specs=[tile, pieces, pieces, full(8, 128)],
+        out_specs=[tile, pieces, pieces, whole_out(8, 128)],
         out_shape=[
             shape_of(height, half),
             shape_of(2, groups, share, half),
@@ -382,7 +393,7 @@
             shape_of(8, 128),
         ],
         scratch_shapes=scratch,
-        compiler_params=params(1),
+        compiler_params=params(1, 32),
         name="columns_one",
     )(place, arrived, weights, turned, basis_first, kernel_first)
     got = lax.ppermute(send, "mode", core_swap)
@@ -405,7 +416,7 @@
             shape_of(groups, share, half),
         ],
         scratch_shapes=row_scratch,
-        compiler_params=params(1),
+        compiler_params=params(1, 32),
         name="rows_one",
     )(place, keep, got, near, far, basis_second, kernel_second)
     back_got = lax.ppermute(back_send, "mode", core_swap)
@@ -414,14 +425,14 @@
         functools.partial(column_kernel, False),
         grid=(steps,),
         in_specs=[smem, piece, piece, tile, tile, square, square, square],
-        out_specs=[pieces, pieces, full(8, 128)],
+        out_specs=[pieces, pieces, whole_out(8, 128)],
         out_shape=[
             shape_of(2, groups, share, half),
             shape_of(2, groups, share, half),
             shape_of(8, 128),
         ],
         scratch_shapes=scratch,
-        compiler_params=params(1),
+        compiler_params=params(1, 32),
         name="columns_two",
     )(place, back_keep, back_got, spectral, weights, turned, basis_first, kernel_first)
     got = lax.ppermute(send, "mode", core_swap)
@@ -430,43 +441,43 @@
         functools.partial(row_kernel, False),
         grid=(2,),
         in_specs=row_specs + [full(8, 128), full(8, 128)],
-        out_specs=[row_whole, row_whole, full(groups, 8, 128)],
+        out_specs=[row_whole, row_whole, whole_out(groups, 8, 128)],
         out_shape=[
             shape_of(groups, share, width),
             shape_of(groups, share, width),
             shape_of(groups, 8, 128),
         ],
         scratch_shapes=row_scratch,
-        compiler_params=params(1),
+        compiler_params=params(1, 32),
         name="rows_two",
     )(place, keep, got, near, far, basis_second, kernel_second, sum_one, sum_two)
     sums = lax.all_to_all(sums, "mode", split_axis=0, concat_axis=0, tiled=True)
 
-    few = groups // 8
+    few = groups // 4
     few_spec = pl.BlockSpec((few, share, width), lambda i: (i, 0, 0))
     answer = pl.pallas_call(
         combine_kernel,
-        grid=(8,),
+        grid=(4,),
         in_specs=[full(groups, 8, 128)] + [few_spec] * 4,
         out_specs=pl.BlockSpec((few, rows, width), lambda i: (i, 0, 0)),
         out_shape=shape_of(groups, rows, width),
-        compiler_params=params(1),
+        compiler_params=params(1, 20),
         name="combine",
     )(sums, z_field, image, f_field, f_image)
     answer = lax.all_to_all(answer, "mode", split_axis=0, concat_axis=0, tiled=True)
 
-    block = pl.BlockSpec((1, 1, rows, width), lambda p, s: (s, p, 0, 0))
+    block = pl.BlockSpec((samples, 1, rows, width), lambda p: (0, p, 0, 0))
     return tuple(
         pl.pallas_call(
             finish_kernel,
-            grid=(planes, samples),
+            grid=(planes,),
             in_specs=[
-                pl.BlockSpec((cores, rows, width), lambda p, s: (p * samples + s, 0, 0)),
+                pl.BlockSpec((samples * cores, rows, width), lambda p: (p, 0, 0)),
                 block,
             ],
             out_specs=[block, block],
             out_shape=[shape_of(*right_side.shape)] * 2,
-            compiler_params=params(2),
+            compiler_params=params(1, 20),
             name="finish",
         )(answer, right_side)
     )

time: 310 us -> 289 us (0.932)
  Pallas kernels: 81.4 us -> 53.2 us
  local copies, waits for them, and re-layouts: 7.95 us -> 18.2 us
    pallas_call x2, Pallas kernels: 15.2 us -> 4.04 us  [the longest x1 2.59 us: paired_body(): pl.pallas_call(finish_kernel, grid=(planes,), in_specs=[pl.BlockSpec((sam...]
    unnamed x19 -> x45, local copies, waits for them, and re-layouts: 6.63 us -> 16.8 us
    pallas_call x1, Pallas kernels: 17 us -> 13 us  [paired_body(): pl.pallas_call(functools.partial(column_kernel, False), grid=(steps,), in...]
    pallas_call x1, Pallas kernels: 12.1 us -> 8.39 us  [paired_body(): pl.pallas_call(functools.partial(row_kernel, False), grid=(2,), in_specs=...]
    pallas_call x1, Pallas kernels: 14 us -> 10.4 us  [paired_body(): pl.pallas_call(functools.partial(row_kernel, True), grid=(2,), in_specs=r...]
where the time goes in v2:
time: 289 us; the launch traced here: 288 us
  blocking collectives  105 us (36%)
  waiting for transfers between devices  91.3 us (32%)
  Pallas kernels  53.2 us (18%)
  local copies, waits for them, and re-layouts  18.2 us (6%)
  starting transfers between devices  16.2 us (6%)
    all_to_all x1, blocking collectives, paired_body(): lax.all_to_all(answer, 'mode', split_axis=0, concat_axis=0, tiled=True)  94.9 us
    ppermute x4, waiting for transfers between devices, paired_body(): lax.ppermute(eigen, 'mode', [(at, at ^ reach) for at in range(groups)])  60.6 us
    ppermute x1, waiting for transfers between devices, paired_body(): far = lax.ppermute(near, 'mode', sample_swap)  24 us
    unnamed x45, local copies, waits for them, and re-layouts  16.8 us
    pallas_call x1, Pallas kernels, paired_body(): pl.pallas_call(functools.partial(column_kernel, True), grid=(steps,), in_...  13.4 us
    pallas_call x1, Pallas kernels, paired_body(): pl.pallas_call(functools.partial(column_kernel, False), grid=(steps,), in...  13 us
    pallas_call x1, Pallas kernels, paired_body(): pl.pallas_call(functools.partial(row_kernel, True), grid=(2,), in_specs=r...  10.4 us
    all_to_all x1, blocking collectives, paired_body(): sums = lax.all_to_all(sums, 'mode', split_axis=0, concat_axis=0, tiled=True)  10.3 us
  transfers between devices with their start and end apart: 9, of which 6 were waited for; matrix products, arithmetic and copies ran while one was open for 2% of the time, Pallas kernels for 0%

profile of v2, /device:TPU:0, one launch (start us, length us, event | category | flops | bytes accessed | tf_op | source)
XLA Modules:
  0.0 288.2 jit_solution(10182676024211656357)
XLA Ops:
  0.6 1.6 copy-done.5
  2.2 1.6 copy-done.10
  3.8 1.2 copy-done.17
  5.7 3.9 %outgoing.1 = f32[4,4,96,512]{3,2,1,0:T(8,128)S(1)} custom-call(f32[8]{0:T(128)S(1)} %copy-done.18, f32[2,4,64,1024]{3,2,1,0:T(8,128)S(1)} %copy-done.10, s32[4,64,1024]{2,1,0:T(8,128)S(1)} %copy-done.17, bf16[1024,1024]{1,0:T(8,128)(2,1)S(1)} %copy-done.5), custom_call_target="tpu_custom_call" | custom-call | tf_op jit(solution)/shard_map/outgoing/pallas_call | solution.py:333
  9.6 1.7 copy-done.7
  11.3 7.6 %all-to-all-start = ((f32[16,96,512]{2,1,0:T(8,128)}), f32[16,96,512]{2,1,0:T(8,128)}, u32[]{:S(2)}, u32[]{:S(2)}) async-start(f32[16,96,512]{2,1,0:T(8,128)} %bitcast.14), calls=%async_computation | async-start | bytes 6291456 | tf_op jit(solution)/shard_map/all_to_all | solution.py:347
  19.4 0.7 reduce_sum.9
  20.1 2.5 copy.11
  23.4 1.6 collective-permute-start.1
  25.1 10.6 %collective-permute-done.1 = f32[1,128]{1,0:T(1,128)S(1)} collective-permute-done((f32[1,128]{1,0:T(1,128)S(1)}, f32[1,128]{1,0:T(1,128)S(1)}, u32[]{:S(2)}, u32[]{:S(2)}) %collective-permute-start.1) | collective-permute-done | bytes 544 | tf_op jit(solution)/shard_map/ppermute | solution.py:354
  36.1 34.6 %collective-permute-done.2 = f32[1,256]{1,0:T(1,128)S(1)} collective-permute-done((f32[1,256]{1,0:T(1,128)S(1)}, f32[1,256]{1,0:T(1,128)S(1)}, u32[]{:S(2)}, u32[]{:S(2)}) %collective-permute-start.2) | collective-permute-done | bytes 1056 | tf_op jit(solution)/shard_map/ppermute | solution.py:354
  70.8 4.4 %collective-permute-start.3 = (f32[1,512]{1,0:T(1,128)S(1)}, f32[1,512]{1,0:T(1,128)S(1)}, u32[]{:S(2)}, u32[]{:S(2)}) collective-permute-start(f32[1,512]{1,0:T(1,128)S(1)} %broadcast_select_fusion.1), channel_id=1, source_target_pairs={{0,8},{1,9},{2,10},{3,11},{4,12},{5,13},{6,14},{7,15},{8,0},{9,1},... | collective-permute-start | bytes 6152 | tf_op jit(solution)/shard_map/ppermute | solution.py:354
  75.1 15.4 %collective-permute-done.3 = f32[1,512]{1,0:T(1,128)S(1)} collective-permute-done((f32[1,512]{1,0:T(1,128)S(1)}, f32[1,512]{1,0:T(1,128)S(1)}, u32[]{:S(2)}, u32[]{:S(2)}) %collective-permute-start.3) | collective-permute-done | bytes 2080 | tf_op jit(solution)/shard_map/ppermute | solution.py:354
  90.6 1.7 add_divide_fusion.refs_1_.refs_3_
  92.2 1.6 copy-done.1
  93.8 1.6 copy-done.3
  95.4 1.6 copy-done.8
  97.0 13.4 %columns_one.1 = (f32[1024,512]{1,0:T(8,128)S(1)}, f32[2,16,32,512]{3,2,1,0:T(8,128)S(1)}, f32[2,16,32,512]{3,2,1,0:T(8,128)S(1)}, f32[8,128]{1,0:T(8,128)S(1)}) custom-call(s32[2]{0:T(128)S(1)} %pad_add_fusion.place_ref, f32[16,96,512]{2,1,0:T(8,128)} %all-to-all-done.refs_0_, f32[1024,512]{1,0:T(8,128)S(1)} %copy-done.3, bf16[1024,1024]{1,0:T(8,128)(2,1)S(1)} %bitcast.12, ...), custom_call_target="tpu_custom_call" | custom-call | tf_op jit(solution)/shard_map/columns_one/pallas_call | solution.py:377
  110.5 1.4 slice.4.near_ref
  112.0 1.5 collective-permute-start.5
  113.5 24.0 %collective-permute-done.5.far_ref = f32[16,32,512]{2,1,0:T(8,128)S(1)} collective-permute-done((f32[16,32,512]{2,1,0:T(8,128)S(1)}, f32[16,32,512]{2,1,0:T(8,128)S(1)}, u32[]{:S(2)}, u32[]{:S(2)}) %collective-permute-start.5) | collective-permute-done | bytes 1048608 | tf_op jit(solution)/shard_map/ppermute | solution.py:367
  137.5 10.4 %rows_one.1 = (f32[16,32,1024]{2,1,0:T(8,128)S(1)}, f32[16,32,1024]{2,1,0:T(8,128)S(1)}, f32[16,32,512]{2,1,0:T(8,128)S(1)}, f32[16,32,512]{2,1,0:T(8,128)S(1)}) custom-call(s32[2]{0:T(128)S(1)} %pad_add_fusion.place_ref, f32[2,16,32,512]{3,2,1,0:T(8,128)S(1)} %get-tuple-element.16.keep_ref, f32[2,16,32,512]{3,2,1,0:T(8,128)S(1)} %collective-permute-done.4.got_ref, ...), custom_call_target="tpu_custom_call" | custom-call | tf_op jit(solution)/shard_map/rows_one/pallas_call | solution.py:407
  148.0 1.3 copy-done.13
  149.3 1.3 copy-done.15
  150.7 2.7 collective-permute-done.6.refs_1_
  153.3 13.0 %columns_two.1 = (f32[2,16,32,512]{3,2,1,0:T(8,128)S(1)}, f32[2,16,32,512]{3,2,1,0:T(8,128)S(1)}, f32[8,128]{1,0:T(8,128)S(1)}) custom-call(s32[2]{0:T(128)S(1)} %pad_add_fusion.place_ref, f32[16,32,512]{2,1,0:T(8,128)S(1)} %get-tuple-element.18.refs_0_, f32[16,32,512]{2,1,0:T(8,128)S(1)} %collective-permute-done.6.refs_1_, ...), custom_call_target="tpu_custom_call" | custom-call | tf_op jit(solution)/shard_map/columns_two/pallas_call | solution.py:424
  166.5 4.0 %collective-permute-done.7.got_ref = f32[2,16,32,512]{3,2,1,0:T(8,128)S(1)} collective-permute-done((f32[2,16,32,512]{3,2,1,0:T(8,128)S(1)}, f32[2,16,32,512]{3,2,1,0:T(8,128)S(1)}, u32[]{:S(2)}, u32[]{:S(2)}) %collective-permute-start.7) | collective-permute-done | bytes 2097184 | tf_op jit(solution)/shard_map/ppermute | solution.py:438
  170.5 8.4 %rows_two.1 = (f32[16,32,1024]{2,1,0:T(8,128)S(1)}, f32[16,32,1024]{2,1,0:T(8,128)S(1)}, f32[16,8,128]{2,1,0:T(8,128)S(1)}) custom-call(s32[2]{0:T(128)S(1)} %pad_add_fusion.place_ref, f32[2,16,32,512]{3,2,1,0:T(8,128)S(1)} %get-tuple-element.21.keep_ref, f32[2,16,32,512]{3,2,1,0:T(8,128)S(1)} %collective-permute-done.7.got_ref, ...), custom_call_target="tpu_custom_call" | custom-call | tf_op jit(solution)/shard_map/rows_two/pallas_call | solution.py:440
  178.9 10.3 %all_to_all.15.sum_ref = f32[16,8,128]{2,1,0:T(8,128)S(1)} all-to-all(f32[16,8,128]{2,1,0:T(8,128)S(1)} %get-tuple-element.25), channel_id=1, replica_groups=mesh['blocks'=2,'mode'=16] {'mode'}, dimensions={0} | all-to-all | bytes 131072 | tf_op jit(solution)/shard_map/all_to_all | solution.py:454
  189.3 1.5 combine.1
  190.8 94.9 %all_to_all.16.got_ref = f32[16,64,1024]{2,1,0:T(8,128)S(1)} all-to-all(f32[16,64,1024]{2,1,0:T(8,128)S(1)} %combine.1), channel_id=1, replica_groups=mesh['blocks'=2,'mode'=16] {'mode'}, dimensions={0} | all-to-all | bytes 8388608 | tf_op jit(solution)/shard_map/all_to_all | solution.py:467
  285.6 2.6 finish.1
  (51 shorter events, 2.1 us)
Async XLA Ops:
  0.6 1.6 copy-start.5
  2.2 1.6 copy-start.10
  3.8 1.2 copy-start.17
  5.0 0.7 copy-start.18
  9.6 1.7 copy-start.7
  11.3 7.6 %copy-start.21 = (f32[64]{0:T(128)S(1)}, f32[64]{0:T(128)}, u32[]{:S(2)}) copy-start(f32[64]{0:T(128)} %param.17) | copy-start | bytes 772
  11.3 8.0 %copy-start.19 = (f32[8]{0:T(128)S(1)}, f32[8]{0:T(128)}, u32[]{:S(2)}) copy-start(f32[8]{0:T(128)} %table_ref.1) | copy-start | bytes 100
  11.3 8.8 %copy-start = (bf16[1024,1024]{1,0:T(8,128)(2,1)S(1)}, bf16[1024,1024]{1,0:T(8,128)(2,1)}, u32[]{:S(2)}) copy-start(bf16[1024,1024]{1,0:T(8,128)(2,1)} %refs_5_.1) | copy-start | bytes 6291460
  11.3 80.9 %all-to-all-start = ((f32[16,96,512]{2,1,0:T(8,128)}), f32[16,96,512]{2,1,0:T(8,128)}, u32[]{:S(2)}, u32[]{:S(2)}) async-start(f32[16,96,512]{2,1,0:T(8,128)} %bitcast.14), calls=%async_computation | async-start | bytes 6291456 | tf_op jit(solution)/shard_map/all_to_all | solution.py:347
  18.9 4.3 %collective-permute-start = (f32[1,64]{1,0:T(1,128)S(1)}, f32[1,64]{1,0:T(1,128)S(1)}, u32[]{:S(2)}, u32[]{:S(2)}) collective-permute-start(f32[1,64]{1,0:T(1,128)S(1)} %bitcast.21), channel_id=1, source_target_pairs={{0,1},{1,0},{2,3},{3,2},{4,5},{5,4},{6,7},{7,6},{8,9},{9,8},{10,11... | collective-permute-start | bytes 776 | tf_op jit(solution)/shard_map/ppermute | solution.py:354
  20.1 70.4 %copy-start.20 = (f32[1024]{0:T(1024)S(1)}, f32[1024]{0:T(1024)}, u32[]{:S(2)}) copy-start(f32[1024]{0:T(1024)} %param.16) | copy-start | bytes 12292
  23.4 12.3 %collective-permute-start.1 = (f32[1,128]{1,0:T(1,128)S(1)}, f32[1,128]{1,0:T(1,128)S(1)}, u32[]{:S(2)}, u32[]{:S(2)}) collective-permute-start(f32[1,128]{1,0:T(1,128)S(1)} %broadcast_select_fusion.3), channel_id=1, source_target_pairs={{0,2},{1,3},{2,0},{3,1},{4,6},{5,7},{6,4},{7,5},{8,10},{9,11},{10,... | collective-permute-start | bytes 1544 | tf_op jit(solution)/shard_map/ppermute | solution.py:354
  35.7 35.1 %collective-permute-start.2 = (f32[1,256]{1,0:T(1,128)S(1)}, f32[1,256]{1,0:T(1,128)S(1)}, u32[]{:S(2)}, u32[]{:S(2)}) collective-permute-start(f32[1,256]{1,0:T(1,128)S(1)} %broadcast_select_fusion.2), channel_id=1, source_target_pairs={{0,4},{1,5},{2,6},{3,7},{4,0},{5,1},{6,2},{7,3},{8,12},{9,13},{10,... | collective-permute-start | bytes 3080 | tf_op jit(solution)/shard_map/ppermute | solution.py:354
  70.8 19.8 %collective-permute-start.3 = (f32[1,512]{1,0:T(1,128)S(1)}, f32[1,512]{1,0:T(1,128)S(1)}, u32[]{:S(2)}, u32[]{:S(2)}) collective-permute-start(f32[1,512]{1,0:T(1,128)S(1)} %broadcast_select_fusion.1), channel_id=1, source_target_pairs={{0,8},{1,9},{2,10},{3,11},{4,12},{5,13},{6,14},{7,15},{8,0},{9,1},... | collective-permute-start | bytes 6152 | tf_op jit(solution)/shard_map/ppermute | solution.py:354
  92.2 1.6 copy-start.1
  93.8 1.6 copy-start.3
  95.4 1.6 copy-start.8
  97.0 40.5 %copy-start.12 = (bf16[1024,1024]{1,0:T(8,128)(2,1)S(1)}, bf16[1024,1024]{1,0:T(8,128)(2,1)}, u32[]{:S(2)}) copy-start(bf16[1024,1024]{1,0:T(8,128)(2,1)} %kernel_ref.3) | copy-start | bytes 6291460
  110.4 27.0 %copy-start.6 = (bf16[1024,1024]{1,0:T(8,128)(2,1)S(1)}, bf16[1024,1024]{1,0:T(8,128)(2,1)}, u32[]{:S(2)}) copy-start(bf16[1024,1024]{1,0:T(8,128)(2,1)} %basis_ref.5) | copy-start | bytes 6291460
  110.4 27.0 %collective-permute-start.4 = (f32[2,16,32,512]{3,2,1,0:T(8,128)S(1)}, f32[2,16,32,512]{3,2,1,0:T(8,128)S(1)}, u32[]{:S(2)}, u32[]{:S(2)}) collective-permute-start(f32[2,16,32,512]{3,2,1,0:T(8,128)S(1)} %get-tuple-element.17), channel_id=1, source_target_pairs={{0,1},{1,0},{2,3},{3,2},{4,5},{5,4},{6,7},{7,6},{8,9},{9,8},{10,11... | collective-permute-start | bytes 6291464 | tf_op jit(solution)/shard_map/ppermute | solution.py:399
  112.0 25.5 %collective-permute-start.5 = (f32[16,32,512]{2,1,0:T(8,128)S(1)}, f32[16,32,512]{2,1,0:T(8,128)S(1)}, u32[]{:S(2)}, u32[]{:S(2)}) collective-permute-start(f32[16,32,512]{2,1,0:T(8,128)S(1)} %slice.4.near_ref), channel_id=1, source_target_pairs={{0,2},{1,3},{2,0},{3,1},{4,6},{5,7},{6,4},{7,5},{8,10},{9,11},{10,... | collective-permute-start | bytes 3145736 | tf_op jit(solution)/shard_map/ppermute | solution.py:367
  137.5 15.8 %copy-start.2 = (bf16[1024,1024]{0,1:T(8,128)(2,1)S(1)}, bf16[1024,1024]{0,1:T(8,128)(2,1)}, u32[]{:S(2)}) copy-start(bf16[1024,1024]{0,1:T(8,128)(2,1)} %copy.11) | copy-start | bytes 6291460
  137.5 15.8 %copy-start.4 = (f32[1024,512]{1,0:T(8,128)S(1)}, f32[1024,512]{1,0:T(8,128)}, u32[]{:S(2)}) copy-start(f32[1024,512]{1,0:T(8,128)} %add_divide_fusion.refs_1_.refs_3_) | copy-start | bytes 6291460
  137.5 15.8 %copy-start.9 = (bf16[1024,1024]{1,0:T(8,128)(2,1)S(1)}, bf16[1024,1024]{1,0:T(8,128)(2,1)}, u32[]{:S(2)}) copy-start(bf16[1024,1024]{1,0:T(8,128)(2,1)} %refs_6_.1) | copy-start | bytes 6291460
  148.0 1.4 copy-start.13
  149.3 1.3 copy-start.15
  150.7 2.7 collective-permute-start.6
  166.3 4.2 %collective-permute-start.7 = (f32[2,16,32,512]{3,2,1,0:T(8,128)S(1)}, f32[2,16,32,512]{3,2,1,0:T(8,128)S(1)}, u32[]{:S(2)}, u32[]{:S(2)}) collective-permute-start(f32[2,16,32,512]{3,2,1,0:T(8,128)S(1)} %get-tuple-element.22), channel_id=1, source_target_pairs={{0,1},{1,0},{2,3},{3,2},{4,5},{5,4},{6,7},{7,6},{8,9},{9,8},{10,11... | collective-permute-start | bytes 6291464 | tf_op jit(solution)/shard_map/ppermute | solution.py:438
  170.5 18.8 %copy-start.14 = (f32[16,32,1024]{2,1,0:T(8,128)S(1)}, f32[16,32,1024]{2,1,0:T(8,128)}, u32[]{:S(2)}) copy-start(f32[16,32,1024]{2,1,0:T(8,128)} %copy-done.13) | copy-start | bytes 6291460
  170.5 18.8 %copy-start.16 = (f32[16,32,1024]{2,1,0:T(8,128)S(1)}, f32[16,32,1024]{2,1,0:T(8,128)}, u32[]{:S(2)}) copy-start(f32[16,32,1024]{2,1,0:T(8,128)} %copy-done.15) | copy-start | bytes 6291460
  190.8 94.9 %copy-start.11 = (f32[2,4,64,1024]{3,2,1,0:T(8,128)S(1)}, f32[2,4,64,1024]{3,2,1,0:T(8,128)}, u32[]{:S(2)}) copy-start(f32[2,4,64,1024]{3,2,1,0:T(8,128)} %right_ref.3) | copy-start | bytes 6291460

commit v3 on v2

--- a/solution.py
+++ b/solution.py
@@ -341,7 +341,7 @@
         ],
         out_specs=pl.BlockSpec((1, samples * cores, tall, half), lambda p: (p, 0, 0, 0)),
         out_shape=shape_of(planes, samples * cores, tall, half),
-        compiler_params=params(1, 16),
+        compiler_params=params(1, 58),
         name="outgoing",
     )(noise_table, right_side, classes, basis_second)
     arrived = lax.all_to_all(
@@ -349,8 +349,8 @@
     )
 
     eigen = eigen_second.reshape(1, -1)
-    reach = 1
-    while reach < groups:
+    plane = index // (cores * samples)
+    for reach in (1, cores):
         other = lax.ppermute(eigen, "mode", [(at, at ^ reach) for at in range(groups)])
         low = (index // reach) % 2 == 0
         eigen = jnp.where(
@@ -358,15 +358,32 @@
             jnp.concatenate([eigen, other], axis=1),
             jnp.concatenate([other, eigen], axis=1),
         )
-        reach *= 2
-    eigen = lax.dynamic_slice(eigen, (0, core * half), (1, half))
+    unit = cores * samples
+    shifted = [eigen] + [
+        lax.ppermute(eigen, "mode", [(at, (at + by * unit) % groups) for at in range(groups)])
+        for by in range(1, planes)
+    ]
+    per_core = planes // cores
+    eigen = jnp.concatenate(
+        [
+            functools.reduce(
+                jnp.add,
+                [
+                    jnp.where((plane - by) % planes == core * per_core + at, shifted[by], 0.0)
+                    for by in range(planes)
+                ],
+            )
+            for at in range(per_core)
+        ],
+        axis=1,
+    )
     weights = 1.0 / (eigen_first[:, None] * eigen + jnp.mean(noise_table))
     turned = basis_first.T
 
     near = arrived[:, rows:, :]
     far = lax.ppermute(near, "mode", sample_swap)
 
-    chunk = half // 2
+    chunk = half
     steps = half // chunk
     tile = pl.BlockSpec((height, chunk), lambda j: (0, j))
     piece = pl.BlockSpec((groups, share, chunk), lambda j: (0, 0, j))
@@ -393,12 +410,12 @@
             shape_of(8, 128),
         ],
         scratch_shapes=scratch,
-        compiler_params=params(1, 32),
+        compiler_params=params(1, 14),
         name="columns_one",
     )(place, arrived, weights, turned, basis_first, kernel_first)
     got = lax.ppermute(send, "mode", core_swap)
 
-    part = groups // 2
+    part = groups
     row_pieces = pl.BlockSpec((2, part, share, half), lambda i: (0, i, 0, 0))
     row_piece = pl.BlockSpec((part, share, half), lambda i: (i, 0, 0))
     row_whole = pl.BlockSpec((part, share, width), lambda i: (i, 0, 0))
@@ -406,7 +423,7 @@
     row_specs = [smem, row_pieces, row_pieces, row_piece, row_piece, row_square, row_square]
     z_field, image, back_keep, back_send = pl.pallas_call(
         functools.partial(row_kernel, True),
-        grid=(2,),
+        grid=(groups // part,),
         in_specs=row_specs,
         out_specs=[row_whole, row_whole, row_piece, row_piece],
         out_shape=[
@@ -416,7 +433,7 @@
             shape_of(groups, share, half),
         ],
         scratch_shapes=row_scratch,
-        compiler_params=params(1, 32),
+        compiler_params=params(1, 12),
         name="rows_one",
     )(place, keep, got, near, far, basis_second, kernel_second)
     back_got = lax.ppermute(back_send, "mode", core_swap)
@@ -432,14 +449,14 @@
             shape_of(8, 128),
         ],
         scratch_shapes=scratch,
-        compiler_params=params(1, 32),
+        compiler_params=params(1, 14),
         name="columns_two",
     )(place, back_keep, back_got, spectral, weights, turned, basis_first, kernel_first)
     got = lax.ppermute(send, "mode", core_swap)
 
     f_field, f_image, sums = pl.pallas_call(
         functools.partial(row_kernel, False),
-        grid=(2,),
+        grid=(groups // part,),
         in_specs=row_specs + [full(8, 128), full(8, 128)],
         out_specs=[row_whole, row_whole, whole_out(groups, 8, 128)],
         out_shape=[
@@ -448,7 +465,7 @@
             shape_of(groups, 8, 128),
         ],
         scratch_shapes=row_scratch,
-        compiler_params=params(1, 32),
+        compiler_params=params(1, 12),
         name="rows_two",
     )(place, keep, got, near, far, basis_second, kernel_second, sum_one, sum_two)
     sums = lax.all_to_all(sums, "mode", split_axis=0, concat_axis=0, tiled=True)
@@ -461,7 +478,7 @@
         in_specs=[full(groups, 8, 128)] + [few_spec] * 4,
         out_specs=pl.BlockSpec((few, rows, width), lambda i: (i, 0, 0)),
         out_shape=shape_of(groups, rows, width),
-        compiler_params=params(1, 20),
+        compiler_params=params(1, 6),
         name="combine",
     )(sums, z_field, image, f_field, f_image)
     answer = lax.all_to_all(answer, "mode", split_axis=0, concat_axis=0, tiled=True)
@@ -477,7 +494,7 @@
             ],
             out_specs=[block, block],
             out_shape=[shape_of(*right_side.shape)] * 2,
-            compiler_params=params(1, 20),
+            compiler_params=params(1, 10),
             name="finish",
         )(answer, right_side)
     )
@@ -492,6 +509,7 @@
         and rows % 16 == 0
         and width % 512 == 0
         and groups % 8 == 0
+        and planes % 2 == 0
     )
     chosen = paired_body if paired else general_body
     return chosen(right_side, classes, *rest)

time: 289 us -> 272 us (0.941)
  local copies, waits for them, and re-layouts: 18.2 us -> 8.81 us
  Pallas kernels: 53.2 us -> 45.7 us
    ppermute x4 -> x2, waiting for transfers between devices: 60.6 us -> 14.4 us  [paired_body(): lax.ppermute(eigen, 'mode', [(at, at ^ reach) for at in range(groups)])]
    ppermute x0 -> x3, waiting for transfers between devices: none -> 43.6 us  [paired_body(): lax.ppermute(eigen, 'mode', [(at, (at + by * unit) % groups) for at in ra...]
    unnamed x45 -> x27, local copies, waits for them, and re-layouts: 16.8 us -> 7.36 us
    ppermute x0 -> x3, starting transfers between devices: none -> 7.41 us  [paired_body(): lax.ppermute(eigen, 'mode', [(at, (at + by * unit) % groups) for at in ra...]
    pallas_call x1, Pallas kernels: 13 us -> 8.12 us  [paired_body(): pl.pallas_call(functools.partial(column_kernel, False), grid=(steps,), in...]
    ppermute x4 -> x2, starting transfers between devices: 6.84 us -> 2.08 us  [paired_body(): lax.ppermute(eigen, 'mode', [(at, at ^ reach) for at in range(groups)])]
    pallas_call x1, Pallas kernels: 13.4 us -> 8.86 us  [paired_body(): pl.pallas_call(functools.partial(column_kernel, True), grid=(steps,), in_...]
  transfers between devices with their start and end apart: 9 -> 10, of which waited for: 6 -> 7; matrix products, arithmetic and copies ran while one was open for 2% -> 2% of each run, Pallas kernels for 0% -> 0%
where the time goes in v3:
time: 272 us; the launch traced here: 271 us
  blocking collectives  105 us (39%)
  waiting for transfers between devices  88.7 us (33%)
  Pallas kernels  45.7 us (17%)
  starting transfers between devices  18.9 us (7%)
  local copies, waits for them, and re-layouts  8.81 us (3%)
    all_to_all x1, blocking collectives, paired_body(): lax.all_to_all(answer, 'mode', split_axis=0, concat_axis=0, tiled=True)  94.9 us
    ppermute x3, waiting for transfers between devices, paired_body(): lax.ppermute(eigen, 'mode', [(at, (at + by * unit) % groups) for at in ra...  43.6 us
    ppermute x1, waiting for transfers between devices, paired_body(): far = lax.ppermute(near, 'mode', sample_swap)  24 us
    ppermute x2, waiting for transfers between devices, paired_body(): lax.ppermute(eigen, 'mode', [(at, at ^ reach) for at in range(groups)])  14.4 us
    all_to_all x1, blocking collectives, paired_body(): sums = lax.all_to_all(sums, 'mode', split_axis=0, concat_axis=0, tiled=True)  10.3 us
    pallas_call x1, Pallas kernels, paired_body(): pl.pallas_call(functools.partial(row_kernel, True), grid=(groups // part,...  10.2 us
    pallas_call x1, Pallas kernels, paired_body(): pl.pallas_call(functools.partial(column_kernel, True), grid=(steps,), in_...  8.86 us
    pallas_call x1, Pallas kernels, paired_body(): pl.pallas_call(functools.partial(column_kernel, False), grid=(steps,), in...  8.12 us
  transfers between devices with their start and end apart: 10, of which 7 were waited for; matrix products, arithmetic and copies ran while one was open for 2% of the time, Pallas kernels for 0%

profile of v3, /device:TPU:0, one launch (start us, length us, event | category | flops | bytes accessed | tf_op | source)
XLA Modules:
  0.0 271.3 jit_solution(11479045434705186851)
XLA Ops:
  0.6 6.7 %outgoing.1 = f32[4,4,96,512]{3,2,1,0:T(8,128)} custom-call(f32[8]{0:T(128)} %table_ref.1, f32[2,4,64,1024]{3,2,1,0:T(8,128)} %right_ref.3, s32[4,64,1024]{2,1,0:T(8,128)} %class_ref.1, bf16[1024,1024]{1,0:T(8,128)(2,1)} %basis_ref.5), custom_call_target="tpu_custom_call" | custom-call | tf_op jit(solution)/shard_map/outgoing/pallas_call | solution.py:333
  7.4 7.6 %all-to-all-start = ((f32[16,96,512]{2,1,0:T(8,128)}), f32[16,96,512]{2,1,0:T(8,128)}, u32[]{:S(2)}, u32[]{:S(2)}) async-start(f32[16,96,512]{2,1,0:T(8,128)} %bitcast.11), calls=%async_computation | async-start | bytes 6291456 | tf_op jit(solution)/shard_map/all_to_all | solution.py:347
  15.0 0.4 collective-permute-start
  15.5 1.1 collective-permute-done
  16.6 0.1 broadcast_select_fusion.9
  16.7 1.7 collective-permute-start.1
  18.4 0.1 fusion.6
  18.4 13.3 %collective-permute-done.1 = f32[1,128]{1,0:T(1,128)S(1)} collective-permute-done((f32[1,128]{1,0:T(1,128)S(1)}, f32[1,128]{1,0:T(1,128)S(1)}, u32[]{:S(2)}, u32[]{:S(2)}) %collective-permute-start.1) | collective-permute-done | bytes 544 | tf_op jit(solution)/shard_map/ppermute | solution.py:354
  31.7 6.8 %collective-permute-start.4 = (f32[1,256]{1,0:T(1,128)S(1)}, f32[1,256]{1,0:T(1,128)S(1)}, u32[]{:S(2)}, u32[]{:S(2)}) collective-permute-start(f32[1,256]{1,0:T(1,128)S(1)} %broadcast_select_fusion.7), channel_id=1, source_target_pairs={{0,12},{1,13},{2,14},{3,15},{4,0},{5,1},{6,2},{7,3},{8,4},{9,5},{1... | collective-permute-start | bytes 3080 | tf_op jit(solution)/shard_map/ppermute | solution.py:363
  38.5 0.6 collective-permute-start.2
  39.2 0.6 reduce_sum.9
  39.8 2.5 copy.11
  43.0 23.9 %collective-permute-done.4 = f32[1,256]{1,0:T(1,128)S(1)} collective-permute-done((f32[1,256]{1,0:T(1,128)S(1)}, f32[1,256]{1,0:T(1,128)S(1)}, u32[]{:S(2)}, u32[]{:S(2)}) %collective-permute-start.4) | collective-permute-done | bytes 1056 | tf_op jit(solution)/shard_map/ppermute | solution.py:363
  66.8 19.8 %collective-permute-done.3 = f32[1,256]{1,0:T(1,128)S(1)} collective-permute-done((f32[1,256]{1,0:T(1,128)S(1)}, f32[1,256]{1,0:T(1,128)S(1)}, u32[]{:S(2)}, u32[]{:S(2)}) %collective-permute-start.3) | collective-permute-done | bytes 1056 | tf_op jit(solution)/shard_map/ppermute | solution.py:363
  86.6 1.7 add_divide_fusion.refs_1_.refs_3_
  88.3 1.6 copy-done.1
  89.9 1.6 copy-done.3
  91.5 1.6 copy-done.6
  93.1 8.9 %columns_one.1 = (f32[1024,512]{1,0:T(8,128)S(1)}, f32[2,16,32,512]{3,2,1,0:T(8,128)S(1)}, f32[2,16,32,512]{3,2,1,0:T(8,128)S(1)}, f32[8,128]{1,0:T(8,128)S(1)}) custom-call(s32[2]{0:T(128)S(1)} %pad_add_fusion.place_ref, f32[16,96,512]{2,1,0:T(8,128)} %all-to-all-done.refs_0_, f32[1024,512]{1,0:T(8,128)S(1)} %copy-done.3, bf16[1024,1024]{1,0:T(8,128)(2,1)S(1)} %bitcast.9, ...), custom_call_target="tpu_custom_call" | custom-call | tf_op jit(solution)/shard_map/columns_one/pallas_call | solution.py:394
  102.0 1.4 slice.4.near_ref
  103.5 1.5 collective-permute-start.6
  105.0 24.0 %collective-permute-done.6.far_ref = f32[16,32,512]{2,1,0:T(8,128)S(1)} collective-permute-done((f32[16,32,512]{2,1,0:T(8,128)S(1)}, f32[16,32,512]{2,1,0:T(8,128)S(1)}, u32[]{:S(2)}, u32[]{:S(2)}) %collective-permute-start.6) | collective-permute-done | bytes 1048608 | tf_op jit(solution)/shard_map/ppermute | solution.py:384
  129.0 10.2 %rows_one.1 = (f32[16,32,1024]{2,1,0:T(8,128)S(1)}, f32[16,32,1024]{2,1,0:T(8,128)S(1)}, f32[16,32,512]{2,1,0:T(8,128)S(1)}, f32[16,32,512]{2,1,0:T(8,128)S(1)}) custom-call(s32[2]{0:T(128)S(1)} %pad_add_fusion.place_ref, f32[2,16,32,512]{3,2,1,0:T(8,128)S(1)} %get-tuple-element.16.keep_ref, f32[2,16,32,512]{3,2,1,0:T(8,128)S(1)} %collective-permute-done.5.got_ref, ...), custom_call_target="tpu_custom_call" | custom-call | tf_op jit(solution)/shard_map/rows_one/pallas_call | solution.py:424
  139.3 2.6 collective-permute-done.7.refs_1_
  142.0 8.1 %columns_two.1 = (f32[2,16,32,512]{3,2,1,0:T(8,128)S(1)}, f32[2,16,32,512]{3,2,1,0:T(8,128)S(1)}, f32[8,128]{1,0:T(8,128)S(1)}) custom-call(s32[2]{0:T(128)S(1)} %pad_add_fusion.place_ref, f32[16,32,512]{2,1,0:T(8,128)S(1)} %get-tuple-element.18.refs_0_, f32[16,32,512]{2,1,0:T(8,128)S(1)} %collective-permute-done.7.refs_1_, ...), custom_call_target="tpu_custom_call" | custom-call | tf_op jit(solution)/shard_map/columns_two/pallas_call | solution.py:441
  150.1 0.2 collective-permute-start.8
  150.3 4.0 %collective-permute-done.8.got_ref = f32[2,16,32,512]{3,2,1,0:T(8,128)S(1)} collective-permute-done((f32[2,16,32,512]{3,2,1,0:T(8,128)S(1)}, f32[2,16,32,512]{3,2,1,0:T(8,128)S(1)}, u32[]{:S(2)}, u32[]{:S(2)}) %collective-permute-start.8) | collective-permute-done | bytes 2097184 | tf_op jit(solution)/shard_map/ppermute | solution.py:455
  154.4 7.7 %rows_two.1 = (f32[16,32,1024]{2,1,0:T(8,128)S(1)}, f32[16,32,1024]{2,1,0:T(8,128)S(1)}, f32[16,8,128]{2,1,0:T(8,128)S(1)}) custom-call(s32[2]{0:T(128)S(1)} %pad_add_fusion.place_ref, f32[2,16,32,512]{3,2,1,0:T(8,128)S(1)} %get-tuple-element.21.keep_ref, f32[2,16,32,512]{3,2,1,0:T(8,128)S(1)} %collective-permute-done.8.got_ref, ...), custom_call_target="tpu_custom_call" | custom-call | tf_op jit(solution)/shard_map/rows_two/pallas_call | solution.py:457
  162.1 10.3 %all_to_all.15.sum_ref = f32[16,8,128]{2,1,0:T(8,128)S(1)} all-to-all(f32[16,8,128]{2,1,0:T(8,128)S(1)} %get-tuple-element.25), channel_id=1, replica_groups=mesh['blocks'=2,'mode'=16] {'mode'}, dimensions={0} | all-to-all | bytes 131072 | tf_op jit(solution)/shard_map/all_to_all | solution.py:471
  172.4 1.5 combine.1
  173.9 94.9 %all_to_all.16.got_ref = f32[16,64,1024]{2,1,0:T(8,128)S(1)} all-to-all(f32[16,64,1024]{2,1,0:T(8,128)S(1)} %combine.1), channel_id=1, replica_groups=mesh['blocks'=2,'mode'=16] {'mode'}, dimensions={0} | all-to-all | bytes 8388608 | tf_op jit(solution)/shard_map/all_to_all | solution.py:484
  268.8 2.6 finish.1
  (33 shorter events, 0.3 us)
Async XLA Ops:
  7.4 7.6 %copy-start.11 = (f32[64]{0:T(128)S(1)}, f32[64]{0:T(128)}, u32[]{:S(2)}) copy-start(f32[64]{0:T(128)} %param.17) | copy-start | bytes 772
  7.4 31.8 %copy-start.12 = (f32[8]{0:T(128)S(1)}, f32[8]{0:T(128)}, u32[]{:S(2)}) copy-start(f32[8]{0:T(128)} %table_ref.1) | copy-start | bytes 100
  7.4 32.4 %copy-start = (bf16[1024,1024]{1,0:T(8,128)(2,1)S(1)}, bf16[1024,1024]{1,0:T(8,128)(2,1)}, u32[]{:S(2)}) copy-start(bf16[1024,1024]{1,0:T(8,128)(2,1)} %refs_5_.1) | copy-start | bytes 6291460
  7.4 80.9 %all-to-all-start = ((f32[16,96,512]{2,1,0:T(8,128)}), f32[16,96,512]{2,1,0:T(8,128)}, u32[]{:S(2)}, u32[]{:S(2)}) async-start(f32[16,96,512]{2,1,0:T(8,128)} %bitcast.11), calls=%async_computation | async-start | bytes 6291456 | tf_op jit(solution)/shard_map/all_to_all | solution.py:347
  15.0 1.6 collective-permute-start
  16.7 15.0 %collective-permute-start.1 = (f32[1,128]{1,0:T(1,128)S(1)}, f32[1,128]{1,0:T(1,128)S(1)}, u32[]{:S(2)}, u32[]{:S(2)}) collective-permute-start(f32[1,128]{1,0:T(1,128)S(1)} %broadcast_select_fusion.9), channel_id=1, source_target_pairs={{0,2},{1,3},{2,0},{3,1},{4,6},{5,7},{6,4},{7,5},{8,10},{9,11},{10,... | collective-permute-start | bytes 1544 | tf_op jit(solution)/shard_map/ppermute | solution.py:354
  31.7 35.1 %collective-permute-start.4 = (f32[1,256]{1,0:T(1,128)S(1)}, f32[1,256]{1,0:T(1,128)S(1)}, u32[]{:S(2)}, u32[]{:S(2)}) collective-permute-start(f32[1,256]{1,0:T(1,128)S(1)} %broadcast_select_fusion.7), channel_id=1, source_target_pairs={{0,12},{1,13},{2,14},{3,15},{4,0},{5,1},{6,2},{7,3},{8,4},{9,5},{1... | collective-permute-start | bytes 3080 | tf_op jit(solution)/shard_map/ppermute | solution.py:363
  38.5 48.1 %collective-permute-start.3 = (f32[1,256]{1,0:T(1,128)S(1)}, f32[1,256]{1,0:T(1,128)S(1)}, u32[]{:S(2)}, u32[]{:S(2)}) collective-permute-start(f32[1,256]{1,0:T(1,128)S(1)} %broadcast_select_fusion.7), channel_id=1, source_target_pairs={{0,8},{1,9},{2,10},{3,11},{4,12},{5,13},{6,14},{7,15},{8,0},{9,1},... | collective-permute-start | bytes 3080 | tf_op jit(solution)/shard_map/ppermute | solution.py:363
  38.5 48.1 %collective-permute-start.2 = (f32[1,256]{1,0:T(1,128)S(1)}, f32[1,256]{1,0:T(1,128)S(1)}, u32[]{:S(2)}, u32[]{:S(2)}) collective-permute-start(f32[1,256]{1,0:T(1,128)S(1)} %broadcast_select_fusion.7), channel_id=1, source_target_pairs={{0,4},{1,5},{2,6},{3,7},{4,8},{5,9},{6,10},{7,11},{8,12},{9,13},{1... | collective-permute-start | bytes 3080 | tf_op jit(solution)/shard_map/ppermute | solution.py:363
  39.8 46.9 %copy-start.10 = (f32[1024]{0:T(1024)S(1)}, f32[1024]{0:T(1024)}, u32[]{:S(2)}) copy-start(f32[1024]{0:T(1024)} %param.16) | copy-start | bytes 12292
  88.3 1.6 copy-start.1
  89.9 1.6 copy-start.3
  91.5 1.6 copy-start.6
  93.1 35.9 %copy-start.9 = (bf16[1024,1024]{1,0:T(8,128)(2,1)S(1)}, bf16[1024,1024]{1,0:T(8,128)(2,1)}, u32[]{:S(2)}) copy-start(bf16[1024,1024]{1,0:T(8,128)(2,1)} %kernel_ref.3) | copy-start | bytes 6291460
  101.9 27.0 %copy-start.5 = (bf16[1024,1024]{1,0:T(8,128)(2,1)S(1)}, bf16[1024,1024]{1,0:T(8,128)(2,1)}, u32[]{:S(2)}) copy-start(bf16[1024,1024]{1,0:T(8,128)(2,1)} %basis_ref.5) | copy-start | bytes 6291460
  102.0 27.0 %collective-permute-start.5 = (f32[2,16,32,512]{3,2,1,0:T(8,128)S(1)}, f32[2,16,32,512]{3,2,1,0:T(8,128)S(1)}, u32[]{:S(2)}, u32[]{:S(2)}) collective-permute-start(f32[2,16,32,512]{3,2,1,0:T(8,128)S(1)} %get-tuple-element.17), channel_id=1, source_target_pairs={{0,1},{1,0},{2,3},{3,2},{4,5},{5,4},{6,7},{7,6},{8,9},{9,8},{10,11... | collective-permute-start | bytes 6291464 | tf_op jit(solution)/shard_map/ppermute | solution.py:416
  103.5 25.5 %collective-permute-start.6 = (f32[16,32,512]{2,1,0:T(8,128)S(1)}, f32[16,32,512]{2,1,0:T(8,128)S(1)}, u32[]{:S(2)}, u32[]{:S(2)}) collective-permute-start(f32[16,32,512]{2,1,0:T(8,128)S(1)} %slice.4.near_ref), channel_id=1, source_target_pairs={{0,2},{1,3},{2,0},{3,1},{4,6},{5,7},{6,4},{7,5},{8,10},{9,11},{10,... | collective-permute-start | bytes 3145736 | tf_op jit(solution)/shard_map/ppermute | solution.py:384
  129.0 13.0 %copy-start.2 = (bf16[1024,1024]{0,1:T(8,128)(2,1)S(1)}, bf16[1024,1024]{0,1:T(8,128)(2,1)}, u32[]{:S(2)}) copy-start(bf16[1024,1024]{0,1:T(8,128)(2,1)} %copy.11) | copy-start | bytes 6291460
  129.0 13.0 %copy-start.4 = (f32[1024,512]{1,0:T(8,128)S(1)}, f32[1024,512]{1,0:T(8,128)}, u32[]{:S(2)}) copy-start(f32[1024,512]{1,0:T(8,128)} %add_divide_fusion.refs_1_.refs_3_) | copy-start | bytes 6291460
  129.0 13.0 %copy-start.7 = (bf16[1024,1024]{1,0:T(8,128)(2,1)S(1)}, bf16[1024,1024]{1,0:T(8,128)(2,1)}, u32[]{:S(2)}) copy-start(bf16[1024,1024]{1,0:T(8,128)(2,1)} %refs_6_.1) | copy-start | bytes 6291460
  139.3 2.7 %collective-permute-start.7 = (f32[16,32,512]{2,1,0:T(8,128)S(1)}, f32[16,32,512]{2,1,0:T(8,128)S(1)}, u32[]{:S(2)}, u32[]{:S(2)}) collective-permute-start(f32[16,32,512]{2,1,0:T(8,128)S(1)} %get-tuple-element.19), channel_id=1, source_target_pairs={{0,1},{1,0},{2,3},{3,2},{4,5},{5,4},{6,7},{7,6},{8,9},{9,8},{10,11... | collective-permute-start | bytes 3145736 | tf_op jit(solution)/shard_map/ppermute | solution.py:439
  150.1 4.2 %collective-permute-start.8 = (f32[2,16,32,512]{3,2,1,0:T(8,128)S(1)}, f32[2,16,32,512]{3,2,1,0:T(8,128)S(1)}, u32[]{:S(2)}, u32[]{:S(2)}) collective-permute-start(f32[2,16,32,512]{3,2,1,0:T(8,128)S(1)} %get-tuple-element.22), channel_id=1, source_target_pairs={{0,1},{1,0},{2,3},{3,2},{4,5},{5,4},{6,7},{7,6},{8,9},{9,8},{10,11... | collective-permute-start | bytes 6291464 | tf_op jit(solution)/shard_map/ppermute | solution.py:455
  173.9 94.9 %copy-start.8 = (f32[2,4,64,1024]{3,2,1,0:T(8,128)S(1)}, f32[2,4,64,1024]{3,2,1,0:T(8,128)}, u32[]{:S(2)}) copy-start(f32[2,4,64,1024]{3,2,1,0:T(8,128)} %right_ref.3) | copy-start | bytes 6291460

commit v4 on v3

--- a/solution.py
+++ b/solution.py
@@ -167,97 +167,165 @@
             ]
 
 
-def column_kernel(first_call, place_ref, *refs):
-    if first_call:
-        (field_ref, weight_ref, turned_ref, basis_ref, kernel_ref) = refs[:5]
-        (spectral_ref, keep_ref, send_ref, sum_ref, scratch_ref) = refs[5:]
-    else:
-        (held_ref, got_ref, before_ref, weight_ref, turned_ref, basis_ref, kernel_ref) = refs[:7]
-        (keep_ref, send_ref, sum_ref, scratch_ref) = refs[7:]
-    groups, rows, chunk = scratch_ref.shape
-    share = rows // 2
+def both_shares(place_ref, share):
     core = place_ref[0]
     mine = pl.ds(pl.multiple_of(core * share, share), share)
     theirs = pl.ds(pl.multiple_of((1 - core) * share, share), share)
-    if first_call:
-        field = field_ref[...].reshape(groups * rows, chunk)
-    else:
-        scratch_ref[:, mine, :] = held_ref[...]
-        scratch_ref[:, theirs, :] = got_ref[...]
-        field = scratch_ref[...].reshape(groups * rows, chunk)
-    spectral = times_left(turned_ref[...], field)
+    return mine, theirs
+
+
+def split_rows(place_ref, value, scratch_ref, keep_ref, send_ref):
+    mine, theirs = both_shares(place_ref, scratch_ref.shape[1] // 2)
+    scratch_ref[...] = value.reshape(scratch_ref.shape)
+    keep_ref[...] = scratch_ref[:, mine, :]
+    send_ref[...] = scratch_ref[:, theirs, :]
+
+
+def store_sums(sum_ref, sums):
+    rows = sum_ref.shape[0]
+    sum_ref[...] = jnp.concatenate(sums + [jnp.zeros((rows - len(sums), 128), F32)], axis=0)
+
+
+def first_column_kernel(
+    place_ref,
+    table_ref,
+    field_ref,
+    tall_ref,
+    wide_ref,
+    turned_ref,
+    basis_ref,
+    spectral_ref,
+    weight_ref,
+    column_ref,
+    keep_ref,
+    send_ref,
+    sum_ref,
+    scratch_ref,
+):
+    mean = functools.reduce(jnp.add, [table_ref[at] for at in range(NCLASS)]) * (1.0 / NCLASS)
+    height, width = spectral_ref.shape
+    for at in range(0, width, 128):
+        lanes = slice(at, at + 128)
+        weight_ref[:, lanes] = 1.0 / (tall_ref[...] * wide_ref[:, lanes] + mean)
+    spectral = times_left(turned_ref[...], field_ref[...].reshape(height, width))
     weighted = spectral * weight_ref[...]
-    if first_call:
-        spectral_ref[...] = spectral
-        sums = [fold(spectral * weighted)]
-    else:
-        sums = [fold(before_ref[...] * weighted), fold(spectral * weighted)]
-    block = jnp.concatenate(sums + [jnp.zeros((8 - len(sums), 128), F32)], axis=0)
-
-    @pl.when(pl.program_id(0) == 0)
-    def _():
-        sum_ref[...] = block
-
-    @pl.when(pl.program_id(0) != 0)
-    def _():
-        sum_ref[...] += block
-
+    spectral_ref[...] = spectral
+    store_sums(sum_ref, [fold(spectral * weighted)])
     column = times_left(basis_ref[...], weighted)
-    scratch_ref[...] = column.reshape(groups, rows, chunk)
-    keep_ref[0] = scratch_ref[:, mine, :]
-    send_ref[0] = scratch_ref[:, theirs, :]
-    image = times_left(kernel_ref[...], column)
-    scratch_ref[...] = image.reshape(groups, rows, chunk)
-    keep_ref[1] = scratch_ref[:, mine, :]
-    send_ref[1] = scratch_ref[:, theirs, :]
-
-
-def row_kernel(first_call, place_ref, keep_ref, got_ref, near_ref, far_ref, basis_ref, kernel_ref, *refs):
-    if first_call:
-        (z_ref, image_ref, back_keep_ref, back_send_ref, scratch_ref) = refs
-    else:
-        (one_ref, two_ref, z_ref, image_ref, sum_ref, scratch_ref) = refs
+    column_ref[...] = column
+    split_rows(place_ref, column, scratch_ref, keep_ref, send_ref)
+
+
+def next_column_kernel(
+    place_ref,
+    held_ref,
+    got_ref,
+    before_ref,
+    weight_ref,
+    turned_ref,
+    basis_ref,
+    column_ref,
+    keep_ref,
+    send_ref,
+    sum_ref,
+    scratch_ref,
+):
+    mine, theirs = both_shares(place_ref, scratch_ref.shape[1] // 2)
+    scratch_ref[:, mine, :] = held_ref[...]
+    scratch_ref[:, theirs, :] = got_ref[...]
+    spectral = times_left(turned_ref[...], scratch_ref[...].reshape(column_ref.shape))
+    weighted = spectral * weight_ref[...]
+    store_sums(sum_ref, [fold(before_ref[...] * weighted), fold(spectral * weighted)])
+    column = times_left(basis_ref[...], weighted)
+    column_ref[...] = column
+    split_rows(place_ref, column, scratch_ref, keep_ref, send_ref)
+
+
+def column_image_kernel(place_ref, column_ref, kernel_ref, keep_ref, send_ref, scratch_ref):
+    image = times_left(kernel_ref[...], column_ref[...])
+    split_rows(place_ref, image, scratch_ref, keep_ref, send_ref)
+
+
+def join_columns(place_ref, scratch_ref, keep_ref, got_ref):
+    height, width = scratch_ref.shape
+    mine, theirs = both_shares(place_ref, width // 2)
+    scratch_ref[:, mine] = keep_ref[...].reshape(height, width // 2)
+    scratch_ref[:, theirs] = got_ref[...].reshape(height, width // 2)
+    return scratch_ref[...]
+
+
+def row_kernel(place_ref, keep_ref, got_ref, basis_ref, z_ref, scratch_ref):
+    field = join_columns(place_ref, scratch_ref, keep_ref, got_ref)
+    z_ref[...] = times_right(field, basis_ref[...], 1).reshape(z_ref.shape)
+
+
+def row_image(place_ref, keep_ref, got_ref, basis_ref, kernel_ref, scratch_ref):
+    field = join_columns(place_ref, scratch_ref, keep_ref, got_ref)
+    return times_right(times_right(field, basis_ref[...], 1), kernel_ref[...], 1)
+
+
+def add_noise(place_ref, image, z_ref, near_ref, far_ref, scratch_ref):
     height, width = scratch_ref.shape
     half = width // 2
-    core = place_ref[0]
     sample = place_ref[1]
-    mine = pl.ds(pl.multiple_of(core * half, half), half)
-    theirs = pl.ds(pl.multiple_of((1 - core) * half, half), half)
-
-    def whole(index):
-        scratch_ref[:, mine] = keep_ref[index].reshape(height, half)
-        scratch_ref[:, theirs] = got_ref[index].reshape(height, half)
-        return scratch_ref[...]
-
-    basis = basis_ref[...]
-    z_field = times_right(whole(0), basis, 1)
-    image = times_right(times_right(whole(1), basis, 1), kernel_ref[...], 1)
-    scratch_ref[:, pl.ds(pl.multiple_of(sample * half, half), half)] = near_ref[...].reshape(
-        height, half
-    )
-    scratch_ref[:, pl.ds(pl.multiple_of((1 - sample) * half, half), half)] = far_ref[
-        ...
-    ].reshape(height, half)
-    image = image + scratch_ref[...] * z_field
-    z_ref[...] = z_field.reshape(z_ref.shape)
+    near = pl.ds(pl.multiple_of(sample * half, half), half)
+    far = pl.ds(pl.multiple_of((1 - sample) * half, half), half)
+    scratch_ref[:, near] = near_ref[...].reshape(height, half)
+    scratch_ref[:, far] = far_ref[...].reshape(height, half)
+    return image + scratch_ref[...] * z_ref[...].reshape(height, width)
+
+
+def first_image_kernel(
+    place_ref, keep_ref, got_ref, basis_ref, kernel_ref, image_ref, scratch_ref
+):
+    image = row_image(place_ref, keep_ref, got_ref, basis_ref, kernel_ref, scratch_ref)
     image_ref[...] = image.reshape(image_ref.shape)
-    if first_call:
-        scratch_ref[...] = times_right(image, basis, 0)
-        back_keep_ref[...] = scratch_ref[:, mine].reshape(back_keep_ref.shape)
-        back_send_ref[...] = scratch_ref[:, theirs].reshape(back_send_ref.shape)
-    else:
-
-        @pl.when(pl.program_id(0) == 0)
-        def _():
-            first = jnp.concatenate(
-                [one_ref[0:1], two_ref[0:2], jnp.zeros((5, 128), F32)], axis=0
-            )
-            sum_ref[...] = jnp.broadcast_to(first[None], sum_ref.shape)
-
-        last = jnp.concatenate(
-            [jnp.zeros((3, 128), F32), fold(z_field * image), jnp.zeros((4, 128), F32)], axis=0
-        )
-        sum_ref[...] += jnp.broadcast_to(last[None], sum_ref.shape)
+
+
+def return_kernel(
+    place_ref,
+    part_ref,
+    z_ref,
+    near_ref,
+    far_ref,
+    basis_ref,
+    image_ref,
+    keep_ref,
+    send_ref,
+    scratch_ref,
+):
+    image = part_ref[...].reshape(scratch_ref.shape)
+    image = add_noise(place_ref, image, z_ref, near_ref, far_ref, scratch_ref)
+    image_ref[...] = image.reshape(image_ref.shape)
+    mine, theirs = both_shares(place_ref, scratch_ref.shape[1] // 2)
+    scratch_ref[...] = times_right(image, basis_ref[...], 0)
+    keep_ref[...] = scratch_ref[:, mine].reshape(keep_ref.shape)
+    send_ref[...] = scratch_ref[:, theirs].reshape(send_ref.shape)
+
+
+def last_image_kernel(
+    place_ref,
+    keep_ref,
+    got_ref,
+    z_ref,
+    near_ref,
+    far_ref,
+    basis_ref,
+    kernel_ref,
+    one_ref,
+    two_ref,
+    image_ref,
+    sum_ref,
+    scratch_ref,
+):
+    image = row_image(place_ref, keep_ref, got_ref, basis_ref, kernel_ref, scratch_ref)
+    image = add_noise(place_ref, image, z_ref, near_ref, far_ref, scratch_ref)
+    image_ref[...] = image.reshape(image_ref.shape)
+    last = fold(z_ref[...].reshape(image.shape) * image)
+    total = jnp.concatenate(
+        [one_ref[0:1], two_ref[0:2], last, jnp.zeros((4, 128), F32)], axis=0
+    )
+    sum_ref[...] = jnp.broadcast_to(total[None], sum_ref.shape)
 
 
 def combine_kernel(sum_ref, z_ref, image_ref, f_ref, f_image_ref, out_ref):
@@ -377,97 +445,87 @@
         ],
         axis=1,
     )
-    weights = 1.0 / (eigen_first[:, None] * eigen + jnp.mean(noise_table))
+    tall_eigen = jnp.broadcast_to(eigen_first[:, None], (height, 128))
     turned = basis_first.T
 
     near = arrived[:, rows:, :]
     far = lax.ppermute(near, "mode", sample_swap)
 
-    chunk = half
-    steps = half // chunk
-    tile = pl.BlockSpec((height, chunk), lambda j: (0, j))
-    piece = pl.BlockSpec((groups, share, chunk), lambda j: (0, 0, j))
-    pieces = pl.BlockSpec((2, groups, share, chunk), lambda j: (0, 0, 0, j))
-    square = full(height, height)
-    row_square = full(width, width)
-    scratch = [pltpu.VMEM((groups, rows, chunk), F32)]
-    spectral, keep, send, sum_one = pl.pallas_call(
-        functools.partial(column_kernel, True),
-        grid=(steps,),
-        in_specs=[
-            smem,
-            pl.BlockSpec((groups, rows, chunk), lambda j: (0, 0, j)),
-            tile,
-            square,
-            square,
-            square,
-        ],
-        out_specs=[tile, pieces, pieces, whole_out(8, 128)],
-        out_shape=[
-            shape_of(height, half),
-            shape_of(2, groups, share, half),
-            shape_of(2, groups, share, half),
-            shape_of(8, 128),
-        ],
-        scratch_shapes=scratch,
-        compiler_params=params(1, 14),
-        name="columns_one",
-    )(place, arrived, weights, turned, basis_first, kernel_first)
-    got = lax.ppermute(send, "mode", core_swap)
-
-    part = groups
-    row_pieces = pl.BlockSpec((2, part, share, half), lambda i: (0, i, 0, 0))
-    row_piece = pl.BlockSpec((part, share, half), lambda i: (i, 0, 0))
-    row_whole = pl.BlockSpec((part, share, width), lambda i: (i, 0, 0))
-    row_scratch = [pltpu.VMEM((part * share, width), F32)]
-    row_specs = [smem, row_pieces, row_pieces, row_piece, row_piece, row_square, row_square]
-    z_field, image, back_keep, back_send = pl.pallas_call(
-        functools.partial(row_kernel, True),
-        grid=(groups // part,),
-        in_specs=row_specs,
-        out_specs=[row_whole, row_whole, row_piece, row_piece],
-        out_shape=[
-            shape_of(groups, share, width),
-            shape_of(groups, share, width),
-            shape_of(groups, share, half),
-            shape_of(groups, share, half),
-        ],
-        scratch_shapes=row_scratch,
-        compiler_params=params(1, 12),
-        name="rows_one",
-    )(place, keep, got, near, far, basis_second, kernel_second)
-    back_got = lax.ppermute(back_send, "mode", core_swap)
-
-    keep, send, sum_two = pl.pallas_call(
-        functools.partial(column_kernel, False),
-        grid=(steps,),
-        in_specs=[smem, piece, piece, tile, tile, square, square, square],
-        out_specs=[pieces, pieces, whole_out(8, 128)],
-        out_shape=[
-            shape_of(2, groups, share, half),
-            shape_of(2, groups, share, half),
-            shape_of(8, 128),
-        ],
-        scratch_shapes=scratch,
-        compiler_params=params(1, 14),
-        name="columns_two",
-    )(place, back_keep, back_got, spectral, weights, turned, basis_first, kernel_first)
-    got = lax.ppermute(send, "mode", core_swap)
-
-    f_field, f_image, sums = pl.pallas_call(
-        functools.partial(row_kernel, False),
-        grid=(groups // part,),
-        in_specs=row_specs + [full(8, 128), full(8, 128)],
-        out_specs=[row_whole, row_whole, whole_out(groups, 8, 128)],
-        out_shape=[
-            shape_of(groups, share, width),
-            shape_of(groups, share, width),
-            shape_of(groups, 8, 128),
-        ],
-        scratch_shapes=row_scratch,
-        compiler_params=params(1, 12),
-        name="rows_two",
-    )(place, keep, got, near, far, basis_second, kernel_second, sum_one, sum_two)
+    def swap(value):
+        return lax.ppermute(value, "mode", core_swap)
+
+    def call(kernel, inputs, shapes, scratch_shape, specs=None):
+        return pl.pallas_call(
+            kernel,
+            grid=(1,),
+            in_specs=specs or [smem] + [full(*value.shape) for value in inputs[1:]],
+            out_specs=[whole_out(*shape) for shape in shapes],
+            out_shape=[shape_of(*shape) for shape in shapes],
+            scratch_shapes=[pltpu.VMEM(scratch_shape, F32)],
+            compiler_params=params(1, 12),
+        )(*inputs)
+
+    tile = (height, half)
+    piece = (groups, share, half)
+    whole = (groups, share, width)
+    by_rows = (groups, rows, half)
+    flat = (groups * share, width)
+    sums_shape = (8, 128)
+
+    spectral, weights, column, keep, send, sum_one = call(
+        first_column_kernel,
+        (place, noise_table, arrived, tall_eigen, eigen, turned, basis_first),
+        (tile, tile, tile, piece, piece, sums_shape),
+        by_rows,
+        [smem, smem, full(groups, rows, half), full(height, 128), full(1, half)]
+        + [full(height, height)] * 2,
+    )
+    got = swap(send)
+    image_keep, image_send = call(
+        column_image_kernel, (place, column, kernel_first), (piece, piece), by_rows
+    )
+    image_got = swap(image_send)
+    (z_field,) = call(row_kernel, (place, keep, got, basis_second), (whole,), flat)
+    (part,) = call(
+        first_image_kernel,
+        (place, image_keep, image_got, basis_second, kernel_second),
+        (whole,),
+        flat,
+    )
+    image, back_keep, back_send = call(
+        return_kernel, (place, part, z_field, near, far, basis_second), (whole, piece, piece), flat
+    )
+    back_got = swap(back_send)
+
+    column, keep, send, sum_two = call(
+        next_column_kernel,
+        (place, back_keep, back_got, spectral, weights, turned, basis_first),
+        (tile, piece, piece, sums_shape),
+        by_rows,
+    )
+    got = swap(send)
+    image_keep, image_send = call(
+        column_image_kernel, (place, column, kernel_first), (piece, piece), by_rows
+    )
+    image_got = swap(image_send)
+    (f_field,) = call(row_kernel, (place, keep, got, basis_second), (whole,), flat)
+    f_image, sums = call(
+        last_image_kernel,
+        (
+            place,
+            image_keep,
+            image_got,
+            f_field,
+            near,
+            far,
+            basis_second,
+            kernel_second,
+            sum_one,
+            sum_two,
+        ),
+        (whole, (groups, 8, 128)),
+        flat,
+    )
     sums = lax.all_to_all(sums, "mode", split_axis=0, concat_axis=0, tiled=True)
 
     few = groups // 4

time: 272 us -> 259 us (0.952)
  waiting for transfers between devices: 88.7 us -> 77.4 us
  local copies, waits for them, and re-layouts: 8.81 us -> 5.75 us
  Pallas kernels: 45.7 us -> 48.7 us
    ppermute x1, waiting for transfers between devices: 24 us -> 15.5 us  [paired_body(): far = lax.ppermute(near, 'mode', sample_swap)]
    ppermute x3 -> x5, waiting for transfers between devices: 6.68 us -> 2.66 us  [swap(): return lax.ppermute(value, 'mode', core_swap)]
    unnamed x27 -> x21, local copies, waits for them, and re-layouts: 7.36 us -> 4.18 us
    pallas_call x4 -> x9, Pallas kernels: 34.9 us -> 38 us  [call(): pl.pallas_call(kernel, grid=(1,), in_specs=specs or [smem] + [full(*value...]
  transfers between devices with their start and end apart: 10 -> 12, of which waited for: 7 -> 6; matrix products, arithmetic and copies ran while one was open for 2% -> 2% of each run, Pallas kernels for 0% -> 7%
where the time goes in v4:
time: 259 us; the launch traced here: 258 us
  blocking collectives  105 us (41%)
  waiting for transfers between devices  77.4 us (30%)
  Pallas kernels  48.7 us (19%)
  starting transfers between devices  19.9 us (8%)
  local copies, waits for them, and re-layouts  5.75 us (2%)
    all_to_all x1, blocking collectives, paired_body(): lax.all_to_all(answer, 'mode', split_axis=0, concat_axis=0, tiled=True)  94.9 us
    ppermute x3, waiting for transfers between devices, paired_body(): lax.ppermute(eigen, 'mode', [(at, (at + by * unit) % groups) for at in ra...  44.9 us
    pallas_call x9, Pallas kernels, call(): pl.pallas_call(kernel, grid=(1,), in_specs=specs or [smem] + [full(*value...  38 us
    ppermute x1, waiting for transfers between devices, paired_body(): far = lax.ppermute(near, 'mode', sample_swap)  15.5 us
    ppermute x2, waiting for transfers between devices, paired_body(): lax.ppermute(eigen, 'mode', [(at, at ^ reach) for at in range(groups)])  14.4 us
    all_to_all x1, blocking collectives, paired_body(): sums = lax.all_to_all(sums, 'mode', split_axis=0, concat_axis=0, tiled=True)  10.3 us
    all_to_all x1, starting transfers between devices, paired_body(): lax.all_to_all(outgoing.reshape(groups, tall, half), 'mode', split_axis=0...  7.6 us
    ppermute x3, starting transfers between devices, paired_body(): lax.ppermute(eigen, 'mode', [(at, (at + by * unit) % groups) for at in ra...  7.41 us
  transfers between devices with their start and end apart: 12, of which 6 were waited for; matrix products, arithmetic and copies ran while one was open for 2% of the time, Pallas kernels for 7%

profile of v4, /device:TPU:0, one launch (start us, length us, event | category | flops | bytes accessed | tf_op | source)
XLA Modules:
  0.0 258.1 jit_solution(8437279729371009959)
XLA Ops:
  0.6 6.7 %outgoing.1 = f32[4,4,96,512]{3,2,1,0:T(8,128)} custom-call(f32[8]{0:T(128)} %table_ref.3, f32[2,4,64,1024]{3,2,1,0:T(8,128)} %right_ref.3, s32[4,64,1024]{2,1,0:T(8,128)} %class_ref.1, bf16[1024,1024]{1,0:T(8,128)(2,1)} %basis_ref.15), custom_call_target="tpu_custom_call" | custom-call | tf_op jit(solution)/shard_map/outgoing/pallas_call | solution.py:401
  7.4 7.6 %all-to-all-start = ((f32[16,96,512]{2,1,0:T(8,128)}), f32[16,96,512]{2,1,0:T(8,128)}, u32[]{:S(2)}, u32[]{:S(2)}) async-start(f32[16,96,512]{2,1,0:T(8,128)} %bitcast.10), calls=%async_computation | async-start | bytes 6291456 | tf_op jit(solution)/shard_map/all_to_all | solution.py:415
  15.0 0.4 collective-permute-start
  15.5 1.1 collective-permute-done
  16.7 1.7 collective-permute-start.1
  18.4 13.3 %collective-permute-done.1 = f32[1,128]{1,0:T(1,128)S(1)} collective-permute-done((f32[1,128]{1,0:T(1,128)S(1)}, f32[1,128]{1,0:T(1,128)S(1)}, u32[]{:S(2)}, u32[]{:S(2)}) %collective-permute-start.1) | collective-permute-done | bytes 544 | tf_op jit(solution)/shard_map/ppermute | solution.py:422
  31.7 6.8 %collective-permute-start.4 = (f32[1,256]{1,0:T(1,128)S(1)}, f32[1,256]{1,0:T(1,128)S(1)}, u32[]{:S(2)}, u32[]{:S(2)}) collective-permute-start(f32[1,256]{1,0:T(1,128)S(1)} %broadcast_select_fusion.7), channel_id=1, source_target_pairs={{0,12},{1,13},{2,14},{3,15},{4,0},{5,1},{6,2},{7,3},{8,4},{9,5},{1... | collective-permute-start | bytes 3080 | tf_op jit(solution)/shard_map/ppermute | solution.py:431
  38.5 0.6 collective-permute-start.2
  39.1 2.6 copy.11
  41.7 25.1 %collective-permute-done.4 = f32[1,256]{1,0:T(1,128)S(1)} collective-permute-done((f32[1,256]{1,0:T(1,128)S(1)}, f32[1,256]{1,0:T(1,128)S(1)}, u32[]{:S(2)}, u32[]{:S(2)}) %collective-permute-start.4) | collective-permute-done | bytes 1056 | tf_op jit(solution)/shard_map/ppermute | solution.py:431
  66.8 19.8 %collective-permute-done.3 = f32[1,256]{1,0:T(1,128)S(1)} collective-permute-done((f32[1,256]{1,0:T(1,128)S(1)}, f32[1,256]{1,0:T(1,128)S(1)}, u32[]{:S(2)}, u32[]{:S(2)}) %collective-permute-start.3) | collective-permute-done | bytes 1056 | tf_op jit(solution)/shard_map/ppermute | solution.py:431
  86.8 1.6 copy-done.2
  88.4 6.5 %shard_map.104 = (f32[1024,512]{1,0:T(8,128)S(1)}, f32[1024,512]{1,0:T(8,128)S(1)}, f32[1024,512]{1,0:T(8,128)S(1)}, f32[16,32,512]{2,1,0:T(8,128)S(1)}, f32[16,...) custom-call(s32[2]{0:T(128)S(1)} %pad_add_fusion.place_ref, f32[8]{0:T(128)S(1)} %copy-done.7, ...), custom_call_target="tpu_custom_call" | custom-call | tf_op jit(solution)/shard_map/pallas_call | solution.py:458
  95.0 3.0 %shard_map.105 = (f32[16,32,512]{2,1,0:T(8,128)S(1)}, f32[16,32,512]{2,1,0:T(8,128)S(1)}) custom-call(s32[2]{0:T(128)S(1)} %pad_add_fusion.place_ref, f32[1024,512]{1,0:T(8,128)S(1)} %get-tuple-element.21.column_ref, bf16[1024,1024]{1,0:T(8,128)(2,1)S(1)} %copy-done.4), custom_call_target="tpu_custom_call" | custom-call | tf_op jit(solution)/shard_map/pallas_call | solution.py:458
  98.0 0.6 collective-permute-start.5
  98.6 1.4 slice.4.near_ref
  100.0 1.5 collective-permute-start.7
  101.5 3.0 %shard_map.107.z_ref = f32[16,32,1024]{2,1,0:T(8,128)S(1)} custom-call(s32[2]{0:T(128)S(1)} %pad_add_fusion.place_ref, f32[16,32,512]{2,1,0:T(8,128)S(1)} %get-tuple-element.24.keep_ref, f32[16,32,512]{2,1,0:T(8,128)S(1)} %collective-permute-done.6.got_ref, bf16[1024,1024]{1,0:T(8,128)(2,1)S(1)} %copy-done), custom_call_target="tpu_custom_call" | custom-call | tf_op jit(solution)/shard_map/pallas_call | solution.py:458
  104.5 5.2 %shard_map.106.part_ref = f32[16,32,1024]{2,1,0:T(8,128)S(1)} custom-call(s32[2]{0:T(128)S(1)} %pad_add_fusion.place_ref, f32[16,32,512]{2,1,0:T(8,128)S(1)} %get-tuple-element.22.keep_ref, f32[16,32,512]{2,1,0:T(8,128)S(1)} %collective-permute-done.5.got_ref, bf16[1024,1024]{1,0:T(8,128)(2,1)S(1)} %copy-done, bf16[1024,1024]{1,0:T(8,128)(2,1)S(1)} %copy-done.6), custom_call_target="tpu_custom_call" | custom-call | tf_op jit(solution)/shard_map/pallas_call | solution.py:458
  109.7 15.5 %collective-permute-done.7.far_ref = f32[16,32,512]{2,1,0:T(8,128)S(1)} collective-permute-done((f32[16,32,512]{2,1,0:T(8,128)S(1)}, f32[16,32,512]{2,1,0:T(8,128)S(1)}, u32[]{:S(2)}, u32[]{:S(2)}) %collective-permute-start.7) | collective-permute-done | bytes 1048608 | tf_op jit(solution)/shard_map/ppermute | solution.py:452
  125.2 3.4 %shard_map.108 = (f32[16,32,1024]{2,1,0:T(8,128)S(1)}, f32[16,32,512]{2,1,0:T(8,128)S(1)}, f32[16,32,512]{2,1,0:T(8,128)S(1)}) custom-call(s32[2]{0:T(128)S(1)} %pad_add_fusion.place_ref, f32[16,32,1024]{2,1,0:T(8,128)S(1)} %shard_map.106.part_ref, f32[16,32,1024]{2,1,0:T(8,128)S(1)} %shard_map.107.z_ref, f32[16,32,512]{2,1,0:T(8,128)S(1)} %slice.4.near_ref, ...), custom_call_target="tpu_custom_call" | custom-call | tf_op jit(solution)/shard_map/pallas_call | solution.py:458
  128.7 2.6 %collective-permute-done.8.got_ref = f32[16,32,512]{2,1,0:T(8,128)S(1)} collective-permute-done((f32[16,32,512]{2,1,0:T(8,128)S(1)}, f32[16,32,512]{2,1,0:T(8,128)S(1)}, u32[]{:S(2)}, u32[]{:S(2)}) %collective-permute-start.8) | collective-permute-done | bytes 1048608 | tf_op jit(solution)/shard_map/ppermute | solution.py:455
  131.4 5.5 %shard_map.109 = (f32[1024,512]{1,0:T(8,128)S(1)}, f32[16,32,512]{2,1,0:T(8,128)S(1)}, f32[16,32,512]{2,1,0:T(8,128)S(1)}, f32[8,128]{1,0:T(8,128)S(1)}) custom-call(s32[2]{0:T(128)S(1)} %pad_add_fusion.place_ref, f32[16,32,512]{2,1,0:T(8,128)S(1)} %get-tuple-element.26.held_ref, f32[16,32,512]{2,1,0:T(8,128)S(1)} %collective-permute-done.8.got_ref, ...), custom_call_target="tpu_custom_call" | custom-call | tf_op jit(solution)/shard_map/pallas_call | solution.py:458
  136.9 0.2 collective-permute-start.10
  137.1 3.0 %shard_map.110 = (f32[16,32,512]{2,1,0:T(8,128)S(1)}, f32[16,32,512]{2,1,0:T(8,128)S(1)}) custom-call(s32[2]{0:T(128)S(1)} %pad_add_fusion.place_ref, f32[1024,512]{1,0:T(8,128)S(1)} %get-tuple-element.30.column_ref, bf16[1024,1024]{1,0:T(8,128)(2,1)S(1)} %copy-done.4), custom_call_target="tpu_custom_call" | custom-call | tf_op jit(solution)/shard_map/pallas_call | solution.py:458
  140.1 0.4 collective-permute-start.9
  140.6 3.0 %shard_map.111.z_ref.f_ref = f32[16,32,1024]{2,1,0:T(8,128)S(1)} custom-call(s32[2]{0:T(128)S(1)} %pad_add_fusion.place_ref, f32[16,32,512]{2,1,0:T(8,128)S(1)} %get-tuple-element.33.keep_ref, f32[16,32,512]{2,1,0:T(8,128)S(1)} %collective-permute-done.10.got_ref, bf16[1024,1024]{1,0:T(8,128)(2,1)S(1)} %copy-done), custom_call_target="tpu_custom_call" | custom-call | tf_op jit(solution)/shard_map/pallas_call | solution.py:458
  143.6 5.3 %shard_map.112 = (f32[16,32,1024]{2,1,0:T(8,128)S(1)}, f32[16,8,128]{2,1,0:T(8,128)S(1)}) custom-call(s32[2]{0:T(128)S(1)} %pad_add_fusion.place_ref, f32[16,32,512]{2,1,0:T(8,128)S(1)} %get-tuple-element.31.keep_ref, f32[16,32,512]{2,1,0:T(8,128)S(1)} %collective-permute-done.9.got_ref, f32[16,32,1024]{2,1,0:T(8,128)S(1)} %shard_map.111.z_ref.f_ref, ...), custom_call_target="tpu_custom_call" | custom-call | tf_op jit(solution)/shard_map/pallas_call | solution.py:458
  148.9 10.3 %all_to_all.15.sum_ref = f32[16,8,128]{2,1,0:T(8,128)S(1)} all-to-all(f32[16,8,128]{2,1,0:T(8,128)S(1)} %get-tuple-element.37), channel_id=1, replica_groups=mesh['blocks'=2,'mode'=16] {'mode'}, dimensions={0} | all-to-all | bytes 131072 | tf_op jit(solution)/shard_map/all_to_all | solution.py:529
  159.2 1.5 combine.1
  160.7 94.9 %all_to_all.16.got_ref = f32[16,64,1024]{2,1,0:T(8,128)S(1)} all-to-all(f32[16,64,1024]{2,1,0:T(8,128)S(1)} %combine.1), channel_id=1, replica_groups=mesh['blocks'=2,'mode'=16] {'mode'}, dimensions={0} | all-to-all | bytes 8388608 | tf_op jit(solution)/shard_map/all_to_all | solution.py:542
  255.6 2.6 %finish.1 = (f32[2,4,64,1024]{3,2,1,0:T(8,128)}, f32[2,4,64,1024]{3,2,1,0:T(8,128)}) custom-call(f32[16,64,1024]{2,1,0:T(8,128)S(1)} %all_to_all.16.got_ref, f32[2,4,64,1024]{3,2,1,0:T(8,128)S(1)} %copy-done.5), custom_call_target="tpu_custom_call" | custom-call | tf_op jit(solution)/shard_map/finish/pallas_call | solution.py:546
  (35 shorter events, 0.6 us)
Async XLA Ops:
  7.4 7.6 %copy-start.9 = (f32[64]{0:T(128)S(1)}, f32[64]{0:T(128)}, u32[]{:S(2)}) copy-start(f32[64]{0:T(128)} %param.17) | copy-start | bytes 772
  7.4 31.8 %copy-start.1 = (bf16[1024,1024]{1,0:T(8,128)(2,1)S(1)}, bf16[1024,1024]{1,0:T(8,128)(2,1)}, u32[]{:S(2)}) copy-start(bf16[1024,1024]{1,0:T(8,128)(2,1)} %basis_ref.13) | copy-start | bytes 6291460
  7.4 79.2 %all-to-all-start = ((f32[16,96,512]{2,1,0:T(8,128)}), f32[16,96,512]{2,1,0:T(8,128)}, u32[]{:S(2)}, u32[]{:S(2)}) async-start(f32[16,96,512]{2,1,0:T(8,128)} %bitcast.10), calls=%async_computation | async-start | bytes 6291456 | tf_op jit(solution)/shard_map/all_to_all | solution.py:415
  15.0 1.6 collective-permute-start
  16.7 15.0 %collective-permute-start.1 = (f32[1,128]{1,0:T(1,128)S(1)}, f32[1,128]{1,0:T(1,128)S(1)}, u32[]{:S(2)}, u32[]{:S(2)}) collective-permute-start(f32[1,128]{1,0:T(1,128)S(1)} %broadcast_select_fusion.9), channel_id=1, source_target_pairs={{0,2},{1,3},{2,0},{3,1},{4,6},{5,7},{6,4},{7,5},{8,10},{9,11},{10,... | collective-permute-start | bytes 1544 | tf_op jit(solution)/shard_map/ppermute | solution.py:422
  31.7 35.1 %collective-permute-start.4 = (f32[1,256]{1,0:T(1,128)S(1)}, f32[1,256]{1,0:T(1,128)S(1)}, u32[]{:S(2)}, u32[]{:S(2)}) collective-permute-start(f32[1,256]{1,0:T(1,128)S(1)} %broadcast_select_fusion.7), channel_id=1, source_target_pairs={{0,12},{1,13},{2,14},{3,15},{4,0},{5,1},{6,2},{7,3},{8,4},{9,5},{1... | collective-permute-start | bytes 3080 | tf_op jit(solution)/shard_map/ppermute | solution.py:431
  38.5 48.1 %collective-permute-start.3 = (f32[1,256]{1,0:T(1,128)S(1)}, f32[1,256]{1,0:T(1,128)S(1)}, u32[]{:S(2)}, u32[]{:S(2)}) collective-permute-start(f32[1,256]{1,0:T(1,128)S(1)} %broadcast_select_fusion.7), channel_id=1, source_target_pairs={{0,8},{1,9},{2,10},{3,11},{4,12},{5,13},{6,14},{7,15},{8,0},{9,1},... | collective-permute-start | bytes 3080 | tf_op jit(solution)/shard_map/ppermute | solution.py:431
  38.5 48.1 %collective-permute-start.2 = (f32[1,256]{1,0:T(1,128)S(1)}, f32[1,256]{1,0:T(1,128)S(1)}, u32[]{:S(2)}, u32[]{:S(2)}) collective-permute-start(f32[1,256]{1,0:T(1,128)S(1)} %broadcast_select_fusion.7), channel_id=1, source_target_pairs={{0,4},{1,5},{2,6},{3,7},{4,8},{5,9},{6,10},{7,11},{8,12},{9,13},{1... | collective-permute-start | bytes 3080 | tf_op jit(solution)/shard_map/ppermute | solution.py:431
  39.1 47.5 %copy-start.8 = (f32[1024]{0:T(1024)S(1)}, f32[1024]{0:T(1024)}, u32[]{:S(2)}) copy-start(f32[1024]{0:T(1024)} %param.16) | copy-start | bytes 12292
  39.1 47.7 %copy-start.7 = (f32[8]{0:T(128)S(1)}, f32[8]{0:T(128)}, u32[]{:S(2)}) copy-start(f32[8]{0:T(128)} %table_ref.3) | copy-start | bytes 100
  86.8 1.6 copy-start.2
  88.4 6.6 %copy-start.4 = (bf16[1024,1024]{1,0:T(8,128)(2,1)S(1)}, bf16[1024,1024]{1,0:T(8,128)(2,1)}, u32[]{:S(2)}) copy-start(bf16[1024,1024]{1,0:T(8,128)(2,1)} %kernel_ref.6) | copy-start | bytes 6291460
  94.9 6.6 %collective-permute-start.6 = (f32[16,32,512]{2,1,0:T(8,128)S(1)}, f32[16,32,512]{2,1,0:T(8,128)S(1)}, u32[]{:S(2)}, u32[]{:S(2)}) collective-permute-start(f32[16,32,512]{2,1,0:T(8,128)S(1)} %get-tuple-element.25), channel_id=1, source_target_pairs={{0,1},{1,0},{2,3},{3,2},{4,5},{5,4},{6,7},{7,6},{8,9},{9,8},{10,11... | collective-permute-start | bytes 3145736 | tf_op jit(solution)/shard_map/ppermute | solution.py:455
  98.0 3.5 %copy-start = (bf16[1024,1024]{1,0:T(8,128)(2,1)S(1)}, bf16[1024,1024]{1,0:T(8,128)(2,1)}, u32[]{:S(2)}) copy-start(bf16[1024,1024]{1,0:T(8,128)(2,1)} %basis_ref.15) | copy-start | bytes 6291460
  98.0 6.5 %collective-permute-start.5 = (f32[16,32,512]{2,1,0:T(8,128)S(1)}, f32[16,32,512]{2,1,0:T(8,128)S(1)}, u32[]{:S(2)}, u32[]{:S(2)}) collective-permute-start(f32[16,32,512]{2,1,0:T(8,128)S(1)} %get-tuple-element.23), channel_id=1, source_target_pairs={{0,1},{1,0},{2,3},{3,2},{4,5},{5,4},{6,7},{7,6},{8,9},{9,8},{10,11... | collective-permute-start | bytes 3145736 | tf_op jit(solution)/shard_map/ppermute | solution.py:455
  100.0 25.2 %collective-permute-start.7 = (f32[16,32,512]{2,1,0:T(8,128)S(1)}, f32[16,32,512]{2,1,0:T(8,128)S(1)}, u32[]{:S(2)}, u32[]{:S(2)}) collective-permute-start(f32[16,32,512]{2,1,0:T(8,128)S(1)} %slice.4.near_ref), channel_id=1, source_target_pairs={{0,2},{1,3},{2,0},{3,1},{4,6},{5,7},{6,4},{7,5},{8,10},{9,11},{10,... | collective-permute-start | bytes 3145736 | tf_op jit(solution)/shard_map/ppermute | solution.py:452
  101.5 3.0 %copy-start.6 = (bf16[1024,1024]{1,0:T(8,128)(2,1)S(1)}, bf16[1024,1024]{1,0:T(8,128)(2,1)}, u32[]{:S(2)}) copy-start(bf16[1024,1024]{1,0:T(8,128)(2,1)} %kernel_ref.7) | copy-start | bytes 6291460
  109.7 21.7 %copy-start.3 = (bf16[1024,1024]{0,1:T(8,128)(2,1)S(1)}, bf16[1024,1024]{0,1:T(8,128)(2,1)}, u32[]{:S(2)}) copy-start(bf16[1024,1024]{0,1:T(8,128)(2,1)} %copy.11) | copy-start | bytes 6291460
  128.6 2.7 %collective-permute-start.8 = (f32[16,32,512]{2,1,0:T(8,128)S(1)}, f32[16,32,512]{2,1,0:T(8,128)S(1)}, u32[]{:S(2)}, u32[]{:S(2)}) collective-permute-start(f32[16,32,512]{2,1,0:T(8,128)S(1)} %get-tuple-element.27), channel_id=1, source_target_pairs={{0,1},{1,0},{2,3},{3,2},{4,5},{5,4},{6,7},{7,6},{8,9},{9,8},{10,11... | collective-permute-start | bytes 3145736 | tf_op jit(solution)/shard_map/ppermute | solution.py:455
  136.9 3.7 %collective-permute-start.10 = (f32[16,32,512]{2,1,0:T(8,128)S(1)}, f32[16,32,512]{2,1,0:T(8,128)S(1)}, u32[]{:S(2)}, u32[]{:S(2)}) collective-permute-start(f32[16,32,512]{2,1,0:T(8,128)S(1)} %get-tuple-element.34), channel_id=1, source_target_pairs={{0,1},{1,0},{2,3},{3,2},{4,5},{5,4},{6,7},{7,6},{8,9},{9,8},{10,11... | collective-permute-start | bytes 3145736 | tf_op jit(solution)/shard_map/ppermute | solution.py:455
  140.1 3.5 %collective-permute-start.9 = (f32[16,32,512]{2,1,0:T(8,128)S(1)}, f32[16,32,512]{2,1,0:T(8,128)S(1)}, u32[]{:S(2)}, u32[]{:S(2)}) collective-permute-start(f32[16,32,512]{2,1,0:T(8,128)S(1)} %get-tuple-element.32), channel_id=1, source_target_pairs={{0,1},{1,0},{2,3},{3,2},{4,5},{5,4},{6,7},{7,6},{8,9},{9,8},{10,11... | collective-permute-start | bytes 3145736 | tf_op jit(solution)/shard_map/ppermute | solution.py:455
  160.7 94.9 %copy-start.5 = (f32[2,4,64,1024]{3,2,1,0:T(8,128)S(1)}, f32[2,4,64,1024]{3,2,1,0:T(8,128)}, u32[]{:S(2)}) copy-start(f32[2,4,64,1024]{3,2,1,0:T(8,128)} %right_ref.3) | copy-start | bytes 6291460

commit v5 on v4

--- a/solution.py
+++ b/solution.py
@@ -146,24 +146,30 @@
     )
 
 
-def outgoing_kernel(table_ref, right_ref, class_ref, basis_ref, out_ref):
+def noise_kernel(place_ref, table_ref, class_ref, *out_refs):
+    planes = class_ref.shape[0]
+    for by, out_ref in enumerate(out_refs):
+        level = class_ref[(place_ref[2] + by) % planes]
+        noise = jnp.full(level.shape, table_ref[0], F32)
+        for index in range(1, NCLASS):
+            noise = jnp.where(level == index, table_ref[index], noise)
+        out_ref[...] = noise
+
+
+def follow_kernel(value_ref, *refs):
+    refs[-1][...] = value_ref[...]
+
+
+def outgoing_kernel(right_ref, basis_ref, out_ref):
     samples, _, rows, width = right_ref.shape
-    cores = out_ref.shape[1] // samples
+    cores = out_ref.shape[2]
     half = width // cores
     field = right_ref[...].reshape(samples * rows, width)
     mapped = times_right(field, basis_ref[...], 0)
-    level = class_ref[0]
-    noise = jnp.full(level.shape, table_ref[0], F32)
-    for index in range(1, NCLASS):
-        noise = jnp.where(level == index, table_ref[index], noise)
-    share = rows // cores
     for sample in range(samples):
         for core in range(cores):
-            out_ref[0, sample * cores + core, :rows, :] = mapped[
+            out_ref[0, sample, core] = mapped[
                 sample * rows : (sample + 1) * rows, core * half : (core + 1) * half
-            ]
-            out_ref[0, sample * cores + core, rows:, :] = noise[
-                core * share : (core + 1) * share, sample * half : (sample + 1) * half
             ]
 
 
@@ -175,10 +181,10 @@
 
 
 def split_rows(place_ref, value, scratch_ref, keep_ref, send_ref):
-    mine, theirs = both_shares(place_ref, scratch_ref.shape[1] // 2)
+    core = place_ref[0]
     scratch_ref[...] = value.reshape(scratch_ref.shape)
-    keep_ref[...] = scratch_ref[:, mine, :]
-    send_ref[...] = scratch_ref[:, theirs, :]
+    keep_ref[...] = scratch_ref[:, core]
+    send_ref[...] = scratch_ref[:, 1 - core]
 
 
 def store_sums(sum_ref, sums):
@@ -230,9 +236,9 @@
     sum_ref,
     scratch_ref,
 ):
-    mine, theirs = both_shares(place_ref, scratch_ref.shape[1] // 2)
-    scratch_ref[:, mine, :] = held_ref[...]
-    scratch_ref[:, theirs, :] = got_ref[...]
+    core = place_ref[0]
+    scratch_ref[:, core] = held_ref[...]
+    scratch_ref[:, 1 - core] = got_ref[...]
     spectral = times_left(turned_ref[...], scratch_ref[...].reshape(column_ref.shape))
     weighted = spectral * weight_ref[...]
     store_sums(sum_ref, [fold(before_ref[...] * weighted), fold(spectral * weighted)])
@@ -264,15 +270,16 @@
     return times_right(times_right(field, basis_ref[...], 1), kernel_ref[...], 1)
 
 
-def add_noise(place_ref, image, z_ref, near_ref, far_ref, scratch_ref):
-    height, width = scratch_ref.shape
-    half = width // 2
-    sample = place_ref[1]
-    near = pl.ds(pl.multiple_of(sample * half, half), half)
-    far = pl.ds(pl.multiple_of((1 - sample) * half, half), half)
-    scratch_ref[:, near] = near_ref[...].reshape(height, half)
-    scratch_ref[:, far] = far_ref[...].reshape(height, half)
-    return image + scratch_ref[...] * z_ref[...].reshape(height, width)
+def add_noise(place_ref, image, z_ref, noise_refs, image_ref):
+    image_ref[...] = image.reshape(image_ref.shape)
+    planes = len(noise_refs) // 2
+    samples = image_ref.shape[0] // planes
+    for by in range(planes):
+        row = (place_ref[2] + planes - by) % planes
+        for at, noise_ref in enumerate((noise_refs[by], noise_refs[planes + by])):
+            sample = (place_ref[1] + at) % samples
+            block = row * samples + sample
+            image_ref[block] += noise_ref[...] * z_ref[block]
 
 
 def first_image_kernel(
@@ -282,46 +289,22 @@
     image_ref[...] = image.reshape(image_ref.shape)
 
 
-def return_kernel(
-    place_ref,
-    part_ref,
-    z_ref,
-    near_ref,
-    far_ref,
-    basis_ref,
-    image_ref,
-    keep_ref,
-    send_ref,
-    scratch_ref,
-):
-    image = part_ref[...].reshape(scratch_ref.shape)
-    image = add_noise(place_ref, image, z_ref, near_ref, far_ref, scratch_ref)
-    image_ref[...] = image.reshape(image_ref.shape)
+def return_kernel(place_ref, part_ref, z_ref, basis_ref, *refs):
+    noise_refs, (image_ref, keep_ref, send_ref, scratch_ref) = refs[:-4], refs[-4:]
+    add_noise(place_ref, part_ref[...], z_ref, noise_refs, image_ref)
     mine, theirs = both_shares(place_ref, scratch_ref.shape[1] // 2)
-    scratch_ref[...] = times_right(image, basis_ref[...], 0)
+    scratch_ref[...] = times_right(image_ref[...].reshape(scratch_ref.shape), basis_ref[...], 0)
     keep_ref[...] = scratch_ref[:, mine].reshape(keep_ref.shape)
     send_ref[...] = scratch_ref[:, theirs].reshape(send_ref.shape)
 
 
 def last_image_kernel(
-    place_ref,
-    keep_ref,
-    got_ref,
-    z_ref,
-    near_ref,
-    far_ref,
-    basis_ref,
-    kernel_ref,
-    one_ref,
-    two_ref,
-    image_ref,
-    sum_ref,
-    scratch_ref,
+    place_ref, keep_ref, got_ref, z_ref, basis_ref, kernel_ref, one_ref, two_ref, *refs
 ):
+    noise_refs, (image_ref, sum_ref, scratch_ref) = refs[:-3], refs[-3:]
     image = row_image(place_ref, keep_ref, got_ref, basis_ref, kernel_ref, scratch_ref)
-    image = add_noise(place_ref, image, z_ref, near_ref, far_ref, scratch_ref)
-    image_ref[...] = image.reshape(image_ref.shape)
-    last = fold(z_ref[...].reshape(image.shape) * image)
+    add_noise(place_ref, image, z_ref, noise_refs, image_ref)
+    last = fold((z_ref[...] * image_ref[...]).reshape(scratch_ref.shape))
     total = jnp.concatenate(
         [one_ref[0:1], two_ref[0:2], last, jnp.zeros((4, 128), F32)], axis=0
     )
@@ -345,18 +328,11 @@
 
 
 def finish_kernel(got_ref, right_ref, solution_ref, residual_ref):
-    count, rows = got_ref.shape[:2]
-    samples = right_ref.shape[0]
-    cores = count // samples
-    share = rows // cores
+    samples = got_ref.shape[0]
+    rows = got_ref.shape[1] // 2
     for sample in range(samples):
-        for core in range(cores):
-            at = slice(core * share, (core + 1) * share)
-            block = sample * cores + core
-            solution_ref[sample, 0, at, :] = got_ref[block, :share, :]
-            residual_ref[sample, 0, at, :] = (
-                right_ref[sample, 0, at, :] - got_ref[block, share:, :]
-            )
+        solution_ref[sample, 0] = got_ref[sample, :rows, :]
+        residual_ref[sample, 0] = right_ref[sample, 0] - got_ref[sample, rows:, :]
 
 
 def paired_body(
@@ -375,12 +351,13 @@
     height = groups * rows
     cores = 2
     half = width // cores
-    share = rows // cores
-    tall = rows + share
+    blocks = groups // cores
+    unit = cores * samples
     index = lax.axis_index("mode")
     core = index % cores
     sample = (index // cores) % samples
-    place = jnp.stack([core, sample]).astype(jnp.int32)
+    plane = index // unit
+    place = jnp.stack([core, sample, plane]).astype(jnp.int32)
 
     def shape_of(*shape):
         return jax.ShapeDtypeStruct(shape, F32)
@@ -398,26 +375,39 @@
     core_swap = [(at, at ^ 1) for at in range(groups)]
     sample_swap = [(at, at ^ cores) for at in range(groups)]
 
+    noise = pl.pallas_call(
+        noise_kernel,
+        grid=(1,),
+        in_specs=[smem, smem, full(planes, rows, width)],
+        out_specs=[whole_out(rows, width)] * planes,
+        out_shape=[shape_of(rows, width)] * planes,
+        compiler_params=params(1, 8),
+        name="noise",
+    )(place, noise_table, classes)
+    near = [noise[0]] + [
+        lax.ppermute(noise[by], "mode", [(at, (at + by * unit) % groups) for at in range(groups)])
+        for by in range(1, planes)
+    ]
+    far = [lax.ppermute(value, "mode", sample_swap) for value in near]
+    noise = (*near, *far)
+
     outgoing = pl.pallas_call(
         outgoing_kernel,
         grid=(planes,),
         in_specs=[
-            smem,
             pl.BlockSpec((samples, 1, rows, width), lambda p: (0, p, 0, 0)),
-            pl.BlockSpec((1, rows, width), lambda p: (p, 0, 0)),
             full(width, width),
         ],
-        out_specs=pl.BlockSpec((1, samples * cores, tall, half), lambda p: (p, 0, 0, 0)),
-        out_shape=shape_of(planes, samples * cores, tall, half),
-        compiler_params=params(1, 58),
+        out_specs=pl.BlockSpec((1, samples, cores, rows, half), lambda p: (p, 0, 0, 0, 0)),
+        out_shape=shape_of(planes, samples, cores, rows, half),
+        compiler_params=params(1, 56),
         name="outgoing",
-    )(noise_table, right_side, classes, basis_second)
+    )(right_side, basis_second)
     arrived = lax.all_to_all(
-        outgoing.reshape(groups, tall, half), "mode", split_axis=0, concat_axis=0, tiled=True
+        outgoing.reshape(groups, rows, half), "mode", split_axis=0, concat_axis=0, tiled=True
     )
 
     eigen = eigen_second.reshape(1, -1)
-    plane = index // (cores * samples)
     for reach in (1, cores):
         other = lax.ppermute(eigen, "mode", [(at, at ^ reach) for at in range(groups)])
         low = (index // reach) % 2 == 0
@@ -426,7 +416,15 @@
             jnp.concatenate([eigen, other], axis=1),
             jnp.concatenate([other, eigen], axis=1),
         )
-    unit = cores * samples
+    eigen = pl.pallas_call(
+        follow_kernel,
+        in_specs=[pl.BlockSpec(memory_space=pltpu.VMEM)]
+        + [pl.BlockSpec(memory_space=pl.ANY)] * (planes - 1),
+        out_specs=pl.BlockSpec(memory_space=pltpu.VMEM),
+        out_shape=shape_of(*eigen.shape),
+        compiler_params=pltpu.CompilerParams(vmem_limit_bytes=1024 * 1024),
+        name="follow",
+    )(eigen, *near[1:])
     shifted = [eigen] + [
         lax.ppermute(eigen, "mode", [(at, (at + by * unit) % groups) for at in range(groups)])
         for by in range(1, planes)
@@ -448,9 +446,6 @@
     tall_eigen = jnp.broadcast_to(eigen_first[:, None], (height, 128))
     turned = basis_first.T
 
-    near = arrived[:, rows:, :]
-    far = lax.ppermute(near, "mode", sample_swap)
-
     def swap(value):
         return lax.ppermute(value, "mode", core_swap)
 
@@ -466,10 +461,10 @@
         )(*inputs)
 
     tile = (height, half)
-    piece = (groups, share, half)
-    whole = (groups, share, width)
-    by_rows = (groups, rows, half)
-    flat = (groups * share, width)
+    piece = (blocks, rows, half)
+    whole = (blocks, rows, width)
+    by_rows = (blocks, cores, rows, half)
+    flat = (blocks * rows, width)
     sums_shape = (8, 128)
 
     spectral, weights, column, keep, send, sum_one = call(
@@ -493,7 +488,7 @@
         flat,
     )
     image, back_keep, back_send = call(
-        return_kernel, (place, part, z_field, near, far, basis_second), (whole, piece, piece), flat
+        return_kernel, (place, part, z_field, basis_second, *noise), (whole, piece, piece), flat
     )
     back_got = swap(back_send)
 
@@ -516,30 +511,36 @@
             image_keep,
             image_got,
             f_field,
-            near,
-            far,
             basis_second,
             kernel_second,
             sum_one,
             sum_two,
+            *noise,
         ),
         (whole, (groups, 8, 128)),
         flat,
     )
     sums = lax.all_to_all(sums, "mode", split_axis=0, concat_axis=0, tiled=True)
 
-    few = groups // 4
-    few_spec = pl.BlockSpec((few, share, width), lambda i: (i, 0, 0))
+    few = blocks // 4
+    few_spec = pl.BlockSpec((few, rows, width), lambda i: (i, 0, 0))
     answer = pl.pallas_call(
         combine_kernel,
         grid=(4,),
         in_specs=[full(groups, 8, 128)] + [few_spec] * 4,
-        out_specs=pl.BlockSpec((few, rows, width), lambda i: (i, 0, 0)),
-        out_shape=shape_of(groups, rows, width),
+        out_specs=pl.BlockSpec((few, 2 * rows, width), lambda i: (i, 0, 0)),
+        out_shape=shape_of(blocks, 2 * rows, width),
         compiler_params=params(1, 6),
         name="combine",
     )(sums, z_field, image, f_field, f_image)
-    answer = lax.all_to_all(answer, "mode", split_axis=0, concat_axis=0, tiled=True)
+    answer = lax.all_to_all(
+        answer,
+        "mode",
+        split_axis=0,
+        concat_axis=0,
+        axis_index_groups=[list(range(at, groups, cores)) for at in range(cores)],
+        tiled=True,
+    )
 
     block = pl.BlockSpec((samples, 1, rows, width), lambda p: (0, p, 0, 0))
     return tuple(
@@ -547,7 +548,7 @@
             finish_kernel,
             grid=(planes,),
             in_specs=[
-                pl.BlockSpec((samples * cores, rows, width), lambda p: (p, 0, 0)),
+                pl.BlockSpec((samples, 2 * rows, width), lambda p: (p, 0, 0)),
                 block,
             ],
             out_specs=[block, block],
@@ -564,9 +565,8 @@
     paired = (
         groups == 2 * samples * planes
         and samples == 2
-        and rows % 16 == 0
+        and rows % 8 == 0
         and width % 512 == 0
-        and groups % 8 == 0
         and planes % 2 == 0
     )
     chosen = paired_body if paired else general_body

time: 259 us -> 265 us (1.023)
  starting transfers between devices: 19.9 us -> 27.5 us
  waiting for transfers between devices: 77.4 us -> 74.2 us
    ppermute x1 -> x7, waiting for transfers between devices: 15.5 us -> 66.7 us  [the longest x3 53.9 us: paired_body(): lax.ppermute(noise[by], 'mode', [(at, (at + by * unit) % groups) for at i...]
    ppermute x3, waiting for transfers between devices: 44.9 us -> 2.76 us  [paired_body(): lax.ppermute(eigen, 'mode', [(at, (at + by * unit) % groups) for at in ra...]
    ppermute x2, waiting for transfers between devices: 14.4 us -> 2.1 us  [paired_body(): lax.ppermute(eigen, 'mode', [(at, at ^ reach) for at in range(groups)])]
    ppermute x1 -> x7, starting transfers between devices: 1.53 us -> 9.51 us  [the longest x3 5.46 us: paired_body(): lax.ppermute(noise[by], 'mode', [(at, (at + by * unit) % groups) for at i...]
    unnamed x21 -> x23, local copies, waits for them, and re-layouts: 4.18 us -> 5.4 us
    pallas_call x1 -> x3, Pallas kernels: 6.73 us -> 7.64 us  [the longest x1 6.02 us: paired_body(): pl.pallas_call(outgoing_kernel, grid=(planes,), in_specs=[pl.BlockSpec((s...]
  transfers between devices with their start and end apart: 12 -> 18, of which waited for: 6 -> 9; matrix products, arithmetic and copies ran while one was open for 2% -> 1% of each run, Pallas kernels for 7% -> 7%
where the time goes in v5:
time: 265 us
  blocking collectives  106 us (40%)
  waiting for transfers between devices  74.2 us (28%)
  Pallas kernels  50.6 us (19%)
  starting transfers between devices  27.5 us (10%)
  local copies, waits for them, and re-layouts  5.58 us (2%)
    all_to_all x1, blocking collectives, paired_body(): lax.all_to_all(answer, 'mode', split_axis=0, concat_axis=0, axis_index_gr...  95.8 us
    ppermute x3, waiting for transfers between devices, paired_body(): lax.ppermute(noise[by], 'mode', [(at, (at + by * unit) % groups) for at i...  53.9 us
    pallas_call x9, Pallas kernels, call(): pl.pallas_call(kernel, grid=(1,), in_specs=specs or [smem] + [full(*value...  38.8 us
    ppermute x4, waiting for transfers between devices, paired_body(): far = [lax.ppermute(value, 'mode', sample_swap) for value in near]  12.9 us
    all_to_all x1, blocking collectives, paired_body(): sums = lax.all_to_all(sums, 'mode', split_axis=0, concat_axis=0, tiled=True)  10 us
    all_to_all x1, starting transfers between devices, paired_body(): lax.all_to_all(outgoing.reshape(groups, rows, half), 'mode', split_axis=0...  7.61 us
    ppermute x3, starting transfers between devices, paired_body(): lax.ppermute(eigen, 'mode', [(at, (at + by * unit) % groups) for at in ra...  7.14 us
    pallas_call x1, Pallas kernels, paired_body(): pl.pallas_call(outgoing_kernel, grid=(planes,), in_specs=[pl.BlockSpec((s...  6.02 us
  transfers between devices with their start and end apart: 18, of which 9 were waited for; matrix products, arithmetic and copies ran while one was open for 1% of the time, Pallas kernels for 7%

profile of v5, /device:TPU:0, one launch (start us, length us, event | category | flops | bytes accessed | tf_op | source)
XLA Modules:
  0.0 264.8 jit_solution(17532559435712304685)
XLA Ops:
  0.6 6.0 %outgoing.1 = f32[4,2,2,64,512]{4,3,2,1,0:T(8,128)} custom-call(f32[2,4,64,1024]{3,2,1,0:T(8,128)} %right_ref.3, bf16[1024,1024]{1,0:T(8,128)(2,1)} %basis_ref.15), custom_call_target="tpu_custom_call" | custom-call | tf_op jit(solution)/shard_map/outgoing/pallas_call | solution.py:394
  6.7 7.6 %all-to-all-start = ((f32[16,64,512]{2,1,0:T(8,128)}), f32[16,64,512]{2,1,0:T(8,128)}, u32[]{:S(2)}, u32[]{:S(2)}) async-start(f32[16,64,512]{2,1,0:T(8,128)} %bitcast.11), calls=%async_computation | async-start | bytes 4194304 | tf_op jit(solution)/shard_map/all_to_all | solution.py:406
  16.0 1.6 noise.1
  17.6 1.6 collective-permute-start.2
  19.3 2.4 collective-permute-start.3
  21.6 1.5 collective-permute-start.4
  23.2 1.5 collective-permute-start.1
  24.7 2.1 collective-permute-done.1
  26.8 32.4 %collective-permute-done.2.refs_0_.refs_1_ = f32[64,1024]{1,0:T(8,128)S(1)} collective-permute-done((f32[64,1024]{1,0:T(8,128)}, f32[64,1024]{1,0:T(8,128)S(1)}, u32[]{:S(2)}, u32[]{:S(2)}) %collective-permute-start.2) | collective-permute-done | bytes 262176 | tf_op jit(solution)/shard_map/ppermute | solution.py:388
  59.3 21.4 %collective-permute-done.3.refs_1_.refs_2_ = f32[64,1024]{1,0:T(8,128)S(1)} collective-permute-done((f32[64,1024]{1,0:T(8,128)}, f32[64,1024]{1,0:T(8,128)S(1)}, u32[]{:S(2)}, u32[]{:S(2)}) %collective-permute-start.3) | collective-permute-done | bytes 262176 | tf_op jit(solution)/shard_map/ppermute | solution.py:388
  80.7 6.5 %collective-permute-start.7 = (f32[1,256]{1,0:T(1,128)S(1)}, f32[1,256]{1,0:T(1,128)S(1)}, u32[]{:S(2)}, u32[]{:S(2)}) collective-permute-start(f32[1,256]{1,0:T(1,128)S(1)} %follow.1), channel_id=1, source_target_pairs={{0,12},{1,13},{2,14},{3,15},{4,0},{5,1},{6,2},{7,3},{8,4},{9,5},{1... | collective-permute-start | bytes 3080 | tf_op jit(solution)/shard_map/ppermute | solution.py:429
  87.8 2.5 copy.11
  91.7 1.5 collective-permute-done.5
  93.4 1.6 copy-done.2
  95.0 6.5 %shard_map.104 = (f32[1024,512]{1,0:T(8,128)S(1)}, f32[1024,512]{1,0:T(8,128)S(1)}, f32[1024,512]{1,0:T(8,128)S(1)}, f32[8,64,512]{2,1,0:T(8,128)S(1)}, f32[8,64,512]{2,1,0:T(8,128)S(1)}, /*index=5*/f32[8,128]{1,0:T(8,128)S(1)}) custom-call(s32[3]{0:T(128)S(1)} %pad_add_fusion.place_ref, f32[8]{0:T(128)S(1)} %copy-done.8, ...), custom_call_target="tpu_custom_call" | custom-call | tf_op jit(solution)/shard_map/pallas_call | solution.py:453
  101.6 3.0 %shard_map.105 = (f32[8,64,512]{2,1,0:T(8,128)S(1)}, f32[8,64,512]{2,1,0:T(8,128)S(1)}) custom-call(s32[3]{0:T(128)S(1)} %pad_add_fusion.place_ref, f32[1024,512]{1,0:T(8,128)S(1)} %get-tuple-element.28.column_ref, bf16[1024,1024]{1,0:T(8,128)(2,1)S(1)} %copy-done.5), custom_call_target="tpu_custom_call" | custom-call | tf_op jit(solution)/shard_map/pallas_call | solution.py:453
  105.1 1.5 collective-permute-start.10
  107.2 1.5 collective-permute-start.12
  109.2 3.0 %shard_map.107.z_ref = f32[8,64,1024]{2,1,0:T(8,128)S(1)} custom-call(s32[3]{0:T(128)S(1)} %pad_add_fusion.place_ref, f32[8,64,512]{2,1,0:T(8,128)S(1)} %get-tuple-element.31.keep_ref, f32[8,64,512]{2,1,0:T(8,128)S(1)} %collective-permute-done.9.got_ref, bf16[1024,1024]{1,0:T(8,128)(2,1)S(1)} %copy-done), custom_call_target="tpu_custom_call" | custom-call | tf_op jit(solution)/shard_map/pallas_call | solution.py:453
  112.2 5.2 %shard_map.106.part_ref = f32[8,64,1024]{2,1,0:T(8,128)S(1)} custom-call(s32[3]{0:T(128)S(1)} %pad_add_fusion.place_ref, f32[8,64,512]{2,1,0:T(8,128)S(1)} %get-tuple-element.29.keep_ref, f32[8,64,512]{2,1,0:T(8,128)S(1)} %collective-permute-done.8.got_ref, bf16[1024,1024]{1,0:T(8,128)(2,1)S(1)} %copy-done, bf16[1024,1024]{1,0:T(8,128)(2,1)S(1)} %copy-done.6), custom_call_target="tpu_custom_call" | custom-call | tf_op jit(solution)/shard_map/pallas_call | solution.py:453
  117.4 2.5 collective-permute-done.11.refs_5_
  119.9 5.6 %collective-permute-done.12.refs_6_ = f32[64,1024]{1,0:T(8,128)S(1)} collective-permute-done((f32[64,1024]{1,0:T(8,128)S(1)}, f32[64,1024]{1,0:T(8,128)S(1)}, u32[]{:S(2)}, u32[]{:S(2)}) %collective-permute-start.12) | collective-permute-done | bytes 262176 | tf_op jit(solution)/shard_map/ppermute | solution.py:391
  125.5 4.7 %collective-permute-done.13.refs_7_ = f32[64,1024]{1,0:T(8,128)S(1)} collective-permute-done((f32[64,1024]{1,0:T(8,128)S(1)}, f32[64,1024]{1,0:T(8,128)S(1)}, u32[]{:S(2)}, u32[]{:S(2)}) %collective-permute-start.13) | collective-permute-done | bytes 262176 | tf_op jit(solution)/shard_map/ppermute | solution.py:391
  130.3 3.7 %shard_map.108 = (f32[8,64,1024]{2,1,0:T(8,128)S(1)}, f32[8,64,512]{2,1,0:T(8,128)S(1)}, f32[8,64,512]{2,1,0:T(8,128)S(1)}) custom-call(s32[3]{0:T(128)S(1)} %pad_add_fusion.place_ref, f32[8,64,1024]{2,1,0:T(8,128)S(1)} %shard_map.106.part_ref, f32[8,64,1024]{2,1,0:T(8,128)S(1)} %shard_map.107.z_ref, bf16[1024,1024]{1,0:T(8,128)(2,1)S(1)} %copy-done, ...), custom_call_target="tpu_custom_call" | custom-call | tf_op jit(solution)/shard_map/pallas_call | solution.py:453
  134.0 2.6 collective-permute-done.14.got_ref
  136.7 5.5 %shard_map.109 = (f32[1024,512]{1,0:T(8,128)S(1)}, f32[8,64,512]{2,1,0:T(8,128)S(1)}, f32[8,64,512]{2,1,0:T(8,128)S(1)}, f32[8,128]{1,0:T(8,128)S(1)}) custom-call(s32[3]{0:T(128)S(1)} %pad_add_fusion.place_ref, f32[8,64,512]{2,1,0:T(8,128)S(1)} %get-tuple-element.34.held_ref, f32[8,64,512]{2,1,0:T(8,128)S(1)} %collective-permute-done.14.got_ref, ...), custom_call_target="tpu_custom_call" | custom-call | tf_op jit(solution)/shard_map/pallas_call | solution.py:453
  142.4 3.0 %shard_map.110 = (f32[8,64,512]{2,1,0:T(8,128)S(1)}, f32[8,64,512]{2,1,0:T(8,128)S(1)}) custom-call(s32[3]{0:T(128)S(1)} %pad_add_fusion.place_ref, f32[1024,512]{1,0:T(8,128)S(1)} %get-tuple-element.38.column_ref, bf16[1024,1024]{1,0:T(8,128)(2,1)S(1)} %copy-done.5), custom_call_target="tpu_custom_call" | custom-call | tf_op jit(solution)/shard_map/pallas_call | solution.py:453
  145.9 3.0 %shard_map.111.z_ref.f_ref = f32[8,64,1024]{2,1,0:T(8,128)S(1)} custom-call(s32[3]{0:T(128)S(1)} %pad_add_fusion.place_ref, f32[8,64,512]{2,1,0:T(8,128)S(1)} %get-tuple-element.41.keep_ref, f32[8,64,512]{2,1,0:T(8,128)S(1)} %collective-permute-done.16.got_ref, bf16[1024,1024]{1,0:T(8,128)(2,1)S(1)} %copy-done), custom_call_target="tpu_custom_call" | custom-call | tf_op jit(solution)/shard_map/pallas_call | solution.py:453
  148.9 6.0 %shard_map.112 = (f32[8,64,1024]{2,1,0:T(8,128)S(1)}, f32[16,8,128]{2,1,0:T(8,128)S(1)}) custom-call(s32[3]{0:T(128)S(1)} %pad_add_fusion.place_ref, f32[8,64,512]{2,1,0:T(8,128)S(1)} %get-tuple-element.39.keep_ref, f32[8,64,512]{2,1,0:T(8,128)S(1)} %collective-permute-done.15.got_ref, f32[8,64,1024]{2,1,0:T(8,128)S(1)} %shard_map.111.z_ref.f_ref, ...), custom_call_target="tpu_custom_call" | custom-call | tf_op jit(solution)/shard_map/pallas_call | solution.py:453
  154.8 10.0 %all_to_all.15.sum_ref = f32[16,8,128]{2,1,0:T(8,128)S(1)} all-to-all(f32[16,8,128]{2,1,0:T(8,128)S(1)} %get-tuple-element.45), channel_id=1, replica_groups=mesh['blocks'=2,'mode'=16] {'mode'}, dimensions={0} | all-to-all | bytes 131072 | tf_op jit(solution)/shard_map/all_to_all | solution.py:523
  166.4 95.8 %all_to_all.16.got_ref = f32[8,128,1024]{2,1,0:T(8,128)S(1)} all-to-all(f32[8,128,1024]{2,1,0:T(8,128)S(1)} %combine.1), channel_id=1, replica_groups={{0,2,4,6,8,10,12,14},{1,3,5,7,9,11,13,15},{16,18,20,22,24,26,28,30},{17..., dimensions={0} | all-to-all | bytes 8388608 | tf_op jit(solution)/shard_map/all_to_all | solution.py:536
  262.2 2.7 %finish.1 = (f32[2,4,64,1024]{3,2,1,0:T(8,128)}, f32[2,4,64,1024]{3,2,1,0:T(8,128)}) custom-call(f32[8,128,1024]{2,1,0:T(8,128)S(1)} %all_to_all.16.got_ref, f32[2,4,64,1024]{3,2,1,0:T(8,128)S(1)} %copy-done.4), custom_call_target="tpu_custom_call" | custom-call | tf_op jit(solution)/shard_map/finish/pallas_call | solution.py:547
  (50 shorter events, 7.9 us)
Async XLA Ops:
  6.6 7.6 %copy-start.10 = (f32[64]{0:T(128)S(1)}, f32[64]{0:T(128)}, u32[]{:S(2)}) copy-start(f32[64]{0:T(128)} %param.17) | copy-start | bytes 772
  6.7 8.1 %copy-start.8 = (f32[8]{0:T(128)S(1)}, f32[8]{0:T(128)}, u32[]{:S(2)}) copy-start(f32[8]{0:T(128)} %table_ref.3) | copy-start | bytes 100
  6.7 81.2 %copy-start.1 = (bf16[1024,1024]{1,0:T(8,128)(2,1)S(1)}, bf16[1024,1024]{1,0:T(8,128)(2,1)}, u32[]{:S(2)}) copy-start(bf16[1024,1024]{1,0:T(8,128)(2,1)} %basis_ref.13) | copy-start | bytes 6291460
  6.7 86.5 %all-to-all-start = ((f32[16,64,512]{2,1,0:T(8,128)}), f32[16,64,512]{2,1,0:T(8,128)}, u32[]{:S(2)}, u32[]{:S(2)}) async-start(f32[16,64,512]{2,1,0:T(8,128)} %bitcast.11), calls=%async_computation | async-start | bytes 4194304 | tf_op jit(solution)/shard_map/all_to_all | solution.py:406
  14.3 8.8 %collective-permute-start = (f32[1,64]{1,0:T(1,128)S(1)}, f32[1,64]{1,0:T(1,128)S(1)}, u32[]{:S(2)}, u32[]{:S(2)}) collective-permute-start(f32[1,64]{1,0:T(1,128)S(1)} %bitcast.12), channel_id=1, source_target_pairs={{0,1},{1,0},{2,3},{3,2},{4,5},{5,4},{6,7},{7,6},{8,9},{9,8},{10,11... | collective-permute-start | bytes 776 | tf_op jit(solution)/shard_map/ppermute | solution.py:412
  14.8 1.2 copy-start.7
  17.6 41.6 %collective-permute-start.2 = (f32[64,1024]{1,0:T(8,128)}, f32[64,1024]{1,0:T(8,128)S(1)}, u32[]{:S(2)}, u32[]{:S(2)}) collective-permute-start(f32[64,1024]{1,0:T(8,128)} %get-tuple-element.25), channel_id=1, source_target_pairs={{0,4},{1,5},{2,6},{3,7},{4,8},{5,9},{6,10},{7,11},{8,12},{9,13},{1... | collective-permute-start | bytes 786440 | tf_op jit(solution)/shard_map/ppermute | solution.py:388
  19.3 61.4 %collective-permute-start.3 = (f32[64,1024]{1,0:T(8,128)}, f32[64,1024]{1,0:T(8,128)S(1)}, u32[]{:S(2)}, u32[]{:S(2)}) collective-permute-start(f32[64,1024]{1,0:T(8,128)} %get-tuple-element.26), channel_id=1, source_target_pairs={{0,8},{1,9},{2,10},{3,11},{4,12},{5,13},{6,14},{7,15},{8,0},{9,1},... | collective-permute-start | bytes 786440 | tf_op jit(solution)/shard_map/ppermute | solution.py:388
  21.6 59.1 %collective-permute-start.4 = (f32[64,1024]{1,0:T(8,128)S(1)}, f32[64,1024]{1,0:T(8,128)S(1)}, u32[]{:S(2)}, u32[]{:S(2)}) collective-permute-start(f32[64,1024]{1,0:T(8,128)S(1)} %get-tuple-element.27), channel_id=1, source_target_pairs={{0,12},{1,13},{2,14},{3,15},{4,0},{5,1},{6,2},{7,3},{8,4},{9,5},{1... | collective-permute-start | bytes 786440 | tf_op jit(solution)/shard_map/ppermute | solution.py:388
  23.2 3.6 %collective-permute-start.1 = (f32[1,128]{1,0:T(1,128)S(1)}, f32[1,128]{1,0:T(1,128)S(1)}, u32[]{:S(2)}, u32[]{:S(2)}) collective-permute-start(f32[1,128]{1,0:T(1,128)S(1)} %broadcast_select_fusion.9), channel_id=1, source_target_pairs={{0,2},{1,3},{2,0},{3,1},{4,6},{5,7},{6,4},{7,5},{8,10},{9,11},{10,... | collective-permute-start | bytes 1544 | tf_op jit(solution)/shard_map/ppermute | solution.py:412
  80.7 9.7 %collective-permute-start.7 = (f32[1,256]{1,0:T(1,128)S(1)}, f32[1,256]{1,0:T(1,128)S(1)}, u32[]{:S(2)}, u32[]{:S(2)}) collective-permute-start(f32[1,256]{1,0:T(1,128)S(1)} %follow.1), channel_id=1, source_target_pairs={{0,12},{1,13},{2,14},{3,15},{4,0},{5,1},{6,2},{7,3},{8,4},{9,5},{1... | collective-permute-start | bytes 3080 | tf_op jit(solution)/shard_map/ppermute | solution.py:429
  87.2 4.5 %collective-permute-start.6 = (f32[1,256]{1,0:T(1,128)S(1)}, f32[1,256]{1,0:T(1,128)S(1)}, u32[]{:S(2)}, u32[]{:S(2)}) collective-permute-start(f32[1,256]{1,0:T(1,128)S(1)} %follow.1), channel_id=1, source_target_pairs={{0,8},{1,9},{2,10},{3,11},{4,12},{5,13},{6,14},{7,15},{8,0},{9,1},... | collective-permute-start | bytes 3080 | tf_op jit(solution)/shard_map/ppermute | solution.py:429
  87.8 5.4 %collective-permute-start.5 = (f32[1,256]{1,0:T(1,128)S(1)}, f32[1,256]{1,0:T(1,128)S(1)}, u32[]{:S(2)}, u32[]{:S(2)}) collective-permute-start(f32[1,256]{1,0:T(1,128)S(1)} %follow.1), channel_id=1, source_target_pairs={{0,4},{1,5},{2,6},{3,7},{4,8},{5,9},{6,10},{7,11},{8,12},{9,13},{1... | collective-permute-start | bytes 3080 | tf_op jit(solution)/shard_map/ppermute | solution.py:429
  87.8 5.3 %copy-start.9 = (f32[1024]{0:T(1024)S(1)}, f32[1024]{0:T(1024)}, u32[]{:S(2)}) copy-start(f32[1024]{0:T(1024)} %param.16) | copy-start | bytes 12292
  93.4 1.6 copy-start.2
  95.0 6.6 %copy-start.5 = (bf16[1024,1024]{1,0:T(8,128)(2,1)S(1)}, bf16[1024,1024]{1,0:T(8,128)(2,1)}, u32[]{:S(2)}) copy-start(bf16[1024,1024]{1,0:T(8,128)(2,1)} %kernel_ref.6) | copy-start | bytes 6291460
  101.5 7.2 %collective-permute-start.9 = (f32[8,64,512]{2,1,0:T(8,128)S(1)}, f32[8,64,512]{2,1,0:T(8,128)S(1)}, u32[]{:S(2)}, u32[]{:S(2)}) collective-permute-start(f32[8,64,512]{2,1,0:T(8,128)S(1)} %get-tuple-element.32), channel_id=1, source_target_pairs={{0,1},{1,0},{2,3},{3,2},{4,5},{5,4},{6,7},{7,6},{8,9},{9,8},{10,11... | collective-permute-start | bytes 3145736 | tf_op jit(solution)/shard_map/ppermute | solution.py:450
  101.5 7.6 %copy-start = (bf16[1024,1024]{1,0:T(8,128)(2,1)S(1)}, bf16[1024,1024]{1,0:T(8,128)(2,1)}, u32[]{:S(2)}) copy-start(bf16[1024,1024]{1,0:T(8,128)(2,1)} %basis_ref.15) | copy-start | bytes 6291460
  104.6 7.6 %collective-permute-start.8 = (f32[8,64,512]{2,1,0:T(8,128)S(1)}, f32[8,64,512]{2,1,0:T(8,128)S(1)}, u32[]{:S(2)}, u32[]{:S(2)}) collective-permute-start(f32[8,64,512]{2,1,0:T(8,128)S(1)} %get-tuple-element.30), channel_id=1, source_target_pairs={{0,1},{1,0},{2,3},{3,2},{4,5},{5,4},{6,7},{7,6},{8,9},{9,8},{10,11... | collective-permute-start | bytes 3145736 | tf_op jit(solution)/shard_map/ppermute | solution.py:450
  105.1 12.3 %collective-permute-start.10 = (f32[64,1024]{1,0:T(8,128)S(1)}, f32[64,1024]{1,0:T(8,128)S(1)}, u32[]{:S(2)}, u32[]{:S(2)}) collective-permute-start(f32[64,1024]{1,0:T(8,128)S(1)} %get-tuple-element.33.refs_0_), channel_id=1, source_target_pairs={{0,2},{1,3},{2,0},{3,1},{4,6},{5,7},{6,4},{7,5},{8,10},{9,11},{10,... | collective-permute-start | bytes 786440 | tf_op jit(solution)/shard_map/ppermute | solution.py:391
  106.6 13.3 %collective-permute-start.11 = (f32[64,1024]{1,0:T(8,128)S(1)}, f32[64,1024]{1,0:T(8,128)S(1)}, u32[]{:S(2)}, u32[]{:S(2)}) collective-permute-start(f32[64,1024]{1,0:T(8,128)S(1)} %collective-permute-done.2.refs_0_.refs_1_), channel_id=1, source_target_pairs={{0,2},{1,3},{2,0},{3,1},{4,6},{5,7},{6,4},{7,5},{8,10},{9,11},{10,... | collective-permute-start | bytes 786440 | tf_op jit(solution)/shard_map/ppermute | solution.py:391
  107.2 18.4 %collective-permute-start.12 = (f32[64,1024]{1,0:T(8,128)S(1)}, f32[64,1024]{1,0:T(8,128)S(1)}, u32[]{:S(2)}, u32[]{:S(2)}) collective-permute-start(f32[64,1024]{1,0:T(8,128)S(1)} %collective-permute-done.3.refs_1_.refs_2_), channel_id=1, source_target_pairs={{0,2},{1,3},{2,0},{3,1},{4,6},{5,7},{6,4},{7,5},{8,10},{9,11},{10,... | collective-permute-start | bytes 786440 | tf_op jit(solution)/shard_map/ppermute | solution.py:391
  108.7 21.6 %collective-permute-start.13 = (f32[64,1024]{1,0:T(8,128)S(1)}, f32[64,1024]{1,0:T(8,128)S(1)}, u32[]{:S(2)}, u32[]{:S(2)}) collective-permute-start(f32[64,1024]{1,0:T(8,128)S(1)} %collective-permute-done.4.refs_2_.refs_3_), channel_id=1, source_target_pairs={{0,2},{1,3},{2,0},{3,1},{4,6},{5,7},{6,4},{7,5},{8,10},{9,11},{10,... | collective-permute-start | bytes 786440 | tf_op jit(solution)/shard_map/ppermute | solution.py:391
  109.2 3.0 %copy-start.6 = (bf16[1024,1024]{1,0:T(8,128)(2,1)S(1)}, bf16[1024,1024]{1,0:T(8,128)(2,1)}, u32[]{:S(2)}) copy-start(bf16[1024,1024]{1,0:T(8,128)(2,1)} %kernel_ref.7) | copy-start | bytes 6291460
  117.4 19.3 %copy-start.3 = (bf16[1024,1024]{0,1:T(8,128)(2,1)S(1)}, bf16[1024,1024]{0,1:T(8,128)(2,1)}, u32[]{:S(2)}) copy-start(bf16[1024,1024]{0,1:T(8,128)(2,1)} %copy.11) | copy-start | bytes 6291460
  133.9 2.7 %collective-permute-start.14 = (f32[8,64,512]{2,1,0:T(8,128)S(1)}, f32[8,64,512]{2,1,0:T(8,128)S(1)}, u32[]{:S(2)}, u32[]{:S(2)}) collective-permute-start(f32[8,64,512]{2,1,0:T(8,128)S(1)} %get-tuple-element.35), channel_id=1, source_target_pairs={{0,1},{1,0},{2,3},{3,2},{4,5},{5,4},{6,7},{7,6},{8,9},{9,8},{10,11... | collective-permute-start | bytes 3145736 | tf_op jit(solution)/shard_map/ppermute | solution.py:450
  142.2 3.7 %collective-permute-start.16 = (f32[8,64,512]{2,1,0:T(8,128)S(1)}, f32[8,64,512]{2,1,0:T(8,128)S(1)}, u32[]{:S(2)}, u32[]{:S(2)}) collective-permute-start(f32[8,64,512]{2,1,0:T(8,128)S(1)} %get-tuple-element.42), channel_id=1, source_target_pairs={{0,1},{1,0},{2,3},{3,2},{4,5},{5,4},{6,7},{7,6},{8,9},{9,8},{10,11... | collective-permute-start | bytes 3145736 | tf_op jit(solution)/shard_map/ppermute | solution.py:450
  145.4 3.5 %collective-permute-start.15 = (f32[8,64,512]{2,1,0:T(8,128)S(1)}, f32[8,64,512]{2,1,0:T(8,128)S(1)}, u32[]{:S(2)}, u32[]{:S(2)}) collective-permute-start(f32[8,64,512]{2,1,0:T(8,128)S(1)} %get-tuple-element.40), channel_id=1, source_target_pairs={{0,1},{1,0},{2,3},{3,2},{4,5},{5,4},{6,7},{7,6},{8,9},{9,8},{10,11... | collective-permute-start | bytes 3145736 | tf_op jit(solution)/shard_map/ppermute | solution.py:450
  166.4 95.8 %copy-start.4 = (f32[2,4,64,1024]{3,2,1,0:T(8,128)S(1)}, f32[2,4,64,1024]{3,2,1,0:T(8,128)}, u32[]{:S(2)}) copy-start(f32[2,4,64,1024]{3,2,1,0:T(8,128)} %right_ref.3) | copy-start | bytes 6291460

commit v6 on v5

--- a/solution.py
+++ b/solution.py
@@ -146,9 +146,9 @@
     )
 
 
-def noise_kernel(place_ref, table_ref, class_ref, *out_refs):
+def noise_kernel(shifts, place_ref, table_ref, class_ref, *out_refs):
     planes = class_ref.shape[0]
-    for by, out_ref in enumerate(out_refs):
+    for by, out_ref in zip(shifts, out_refs):
         level = class_ref[(place_ref[2] + by) % planes]
         noise = jnp.full(level.shape, table_ref[0], F32)
         for index in range(1, NCLASS):
@@ -158,6 +158,18 @@
 
 def follow_kernel(value_ref, *refs):
     refs[-1][...] = value_ref[...]
+
+
+def prepare_kernel(
+    first_ref, second_ref, kernel_ref, eigen_ref, _, turned_ref, high_ref, low_ref, tall_ref
+):
+    turned_ref[...] = first_ref[...].T
+    tall_ref[...] = jnp.broadcast_to(eigen_ref[...], tall_ref.shape[::-1]).T
+    dims = (((1,), (0,)), ((), ()))
+    product = lax.dot_general(
+        kernel_ref[...], second_ref[...], dims, preferred_element_type=F32
+    )
+    high_ref[...], low_ref[...] = split(product)
 
 
 def outgoing_kernel(right_ref, basis_ref, out_ref):
@@ -195,28 +207,42 @@
 def first_column_kernel(
     place_ref,
     table_ref,
-    field_ref,
+    field_hbm,
+    turned_hbm,
+    basis_hbm,
     tall_ref,
-    wide_ref,
-    turned_ref,
-    basis_ref,
-    spectral_ref,
-    weight_ref,
-    column_ref,
-    keep_ref,
-    send_ref,
-    sum_ref,
-    scratch_ref,
+    *refs,
 ):
+    wide_refs, refs, local = refs[:-11], refs[-11:-4], refs[-4:]
+    spectral_ref, weight_ref, column_ref, keep_ref, send_ref, sum_ref, scratch_ref = refs
+    field_ref, turned_ref, basis_ref, done = local
+    pairs = ((field_hbm, field_ref), (turned_hbm, turned_ref), (basis_hbm, basis_ref))
+    copies = [
+        pltpu.make_async_copy(source, target, done.at[at])
+        for at, (source, target) in enumerate(pairs)
+    ]
+    for copy in copies:
+        copy.start()
     mean = functools.reduce(jnp.add, [table_ref[at] for at in range(NCLASS)]) * (1.0 / NCLASS)
     height, width = spectral_ref.shape
-    for at in range(0, width, 128):
-        lanes = slice(at, at + 128)
-        weight_ref[:, lanes] = 1.0 / (tall_ref[...] * wide_ref[:, lanes] + mean)
+    planes = len(wide_refs)
+    part = wide_refs[0].shape[1]
+    for block in range(width // part):
+        wanted = place_ref[0] * (width // part) + block
+        wide = jnp.zeros((1, part), F32)
+        for by, wide_ref in enumerate(wide_refs):
+            here = (place_ref[2] + planes - by) % planes == wanted
+            wide = jnp.where(here, wide_ref[...], wide)
+        for at in range(0, part, 128):
+            lanes = slice(block * part + at, block * part + at + 128)
+            weight_ref[:, lanes] = 1.0 / (tall_ref[...] * wide[:, at : at + 128] + mean)
+    copies[0].wait()
+    copies[1].wait()
     spectral = times_left(turned_ref[...], field_ref[...].reshape(height, width))
     weighted = spectral * weight_ref[...]
     spectral_ref[...] = spectral
     store_sums(sum_ref, [fold(spectral * weighted)])
+    copies[2].wait()
     column = times_left(basis_ref[...], weighted)
     column_ref[...] = column
     split_rows(place_ref, column, scratch_ref, keep_ref, send_ref)
@@ -265,48 +291,62 @@
     z_ref[...] = times_right(field, basis_ref[...], 1).reshape(z_ref.shape)
 
 
-def row_image(place_ref, keep_ref, got_ref, basis_ref, kernel_ref, scratch_ref):
+def row_image(place_ref, keep_ref, got_ref, high_ref, low_ref, scratch_ref):
     field = join_columns(place_ref, scratch_ref, keep_ref, got_ref)
-    return times_right(times_right(field, basis_ref[...], 1), kernel_ref[...], 1)
-
-
-def add_noise(place_ref, image, z_ref, noise_refs, image_ref):
+    high, low = split(field)
+    dims = (((1,), (1,)), ((), ()))
+    both = jnp.concatenate([high, low], axis=0)
+    result = lax.dot_general(both, high_ref[...], dims, preferred_element_type=F32)
+    small = lax.dot_general(high, low_ref[...], dims, preferred_element_type=F32)
+    return result[: field.shape[0]] + (result[field.shape[0] :] + small)
+
+
+def first_image_kernel(place_ref, keep_ref, got_ref, high_ref, low_ref, image_ref, scratch_ref):
+    image = row_image(place_ref, keep_ref, got_ref, high_ref, low_ref, scratch_ref)
     image_ref[...] = image.reshape(image_ref.shape)
+
+
+def noise_image_kernel(place_ref, part_ref, z_ref, basis_ref, *refs):
+    noise_refs, (noise_ref, image_ref, send_ref) = refs[:-3], refs[-3:]
     planes = len(noise_refs) // 2
     samples = image_ref.shape[0] // planes
     for by in range(planes):
         row = (place_ref[2] + planes - by) % planes
-        for at, noise_ref in enumerate((noise_refs[by], noise_refs[planes + by])):
-            sample = (place_ref[1] + at) % samples
-            block = row * samples + sample
-            image_ref[block] += noise_ref[...] * z_ref[block]
-
-
-def first_image_kernel(
-    place_ref, keep_ref, got_ref, basis_ref, kernel_ref, image_ref, scratch_ref
+        for at, part in enumerate((noise_refs[by], noise_refs[planes + by])):
+            noise_ref[row * samples + (place_ref[1] + at) % samples] = part[...]
+    image_ref[...] = part_ref[...] + noise_ref[...] * z_ref[...]
+    half = send_ref.shape[2]
+    _, theirs = both_shares(place_ref, half)
+    image = image_ref[...].reshape(-1, basis_ref.shape[0])
+    send_ref[...] = times_right(image, basis_ref[:, theirs], 0).reshape(send_ref.shape)
+
+
+def keep_kernel(place_ref, image_ref, basis_ref, keep_ref):
+    mine, _ = both_shares(place_ref, keep_ref.shape[2])
+    image = image_ref[...].reshape(-1, basis_ref.shape[0])
+    keep_ref[...] = times_right(image, basis_ref[:, mine], 0).reshape(keep_ref.shape)
+
+
+def last_image_kernel(
+    place_ref,
+    keep_ref,
+    got_ref,
+    z_ref,
+    noise_ref,
+    high_ref,
+    low_ref,
+    one_ref,
+    two_ref,
+    image_ref,
+    sum_ref,
+    scratch_ref,
 ):
-    image = row_image(place_ref, keep_ref, got_ref, basis_ref, kernel_ref, scratch_ref)
+    image = row_image(place_ref, keep_ref, got_ref, high_ref, low_ref, scratch_ref)
+    field = z_ref[...].reshape(image.shape)
+    image = image + noise_ref[...].reshape(image.shape) * field
     image_ref[...] = image.reshape(image_ref.shape)
-
-
-def return_kernel(place_ref, part_ref, z_ref, basis_ref, *refs):
-    noise_refs, (image_ref, keep_ref, send_ref, scratch_ref) = refs[:-4], refs[-4:]
-    add_noise(place_ref, part_ref[...], z_ref, noise_refs, image_ref)
-    mine, theirs = both_shares(place_ref, scratch_ref.shape[1] // 2)
-    scratch_ref[...] = times_right(image_ref[...].reshape(scratch_ref.shape), basis_ref[...], 0)
-    keep_ref[...] = scratch_ref[:, mine].reshape(keep_ref.shape)
-    send_ref[...] = scratch_ref[:, theirs].reshape(send_ref.shape)
-
-
-def last_image_kernel(
-    place_ref, keep_ref, got_ref, z_ref, basis_ref, kernel_ref, one_ref, two_ref, *refs
-):
-    noise_refs, (image_ref, sum_ref, scratch_ref) = refs[:-3], refs[-3:]
-    image = row_image(place_ref, keep_ref, got_ref, basis_ref, kernel_ref, scratch_ref)
-    add_noise(place_ref, image, z_ref, noise_refs, image_ref)
-    last = fold((z_ref[...] * image_ref[...]).reshape(scratch_ref.shape))
     total = jnp.concatenate(
-        [one_ref[0:1], two_ref[0:2], last, jnp.zeros((4, 128), F32)], axis=0
+        [one_ref[0:1], two_ref[0:2], fold(field * image), jnp.zeros((4, 128), F32)], axis=0
     )
     sum_ref[...] = jnp.broadcast_to(total[None], sum_ref.shape)
 
@@ -375,19 +415,27 @@
     core_swap = [(at, at ^ 1) for at in range(groups)]
     sample_swap = [(at, at ^ cores) for at in range(groups)]
 
-    noise = pl.pallas_call(
-        noise_kernel,
-        grid=(1,),
-        in_specs=[smem, smem, full(planes, rows, width)],
-        out_specs=[whole_out(rows, width)] * planes,
-        out_shape=[shape_of(rows, width)] * planes,
-        compiler_params=params(1, 8),
-        name="noise",
-    )(place, noise_table, classes)
-    near = [noise[0]] + [
-        lax.ppermute(noise[by], "mode", [(at, (at + by * unit) % groups) for at in range(groups)])
-        for by in range(1, planes)
-    ]
+    def noise_of(shifts):
+        return pl.pallas_call(
+            functools.partial(noise_kernel, shifts),
+            grid=(1,),
+            in_specs=[smem, smem, full(planes, rows, width)],
+            out_specs=[whole_out(rows, width)] * len(shifts),
+            out_shape=[shape_of(rows, width)] * len(shifts),
+            compiler_params=params(1, 56),
+        )(place, noise_table, classes)
+
+    def plane_shift(value, by):
+        pairs = [(at, (at + by * unit) % groups) for at in range(groups)]
+        return lax.ppermute(value, "mode", pairs)
+
+    ahead = planes // 2
+    others = [by for by in range(planes) if by != ahead]
+    near = [None] * planes
+    near[ahead] = plane_shift(noise_of([ahead])[0], ahead)
+    rest = noise_of(others)
+    for by, value in zip(others, rest):
+        near[by] = plane_shift(value, by) if by else value
     far = [lax.ppermute(value, "mode", sample_swap) for value in near]
     noise = (*near, *far)
 
@@ -429,35 +477,30 @@
         lax.ppermute(eigen, "mode", [(at, (at + by * unit) % groups) for at in range(groups)])
         for by in range(1, planes)
     ]
-    per_core = planes // cores
-    eigen = jnp.concatenate(
-        [
-            functools.reduce(
-                jnp.add,
-                [
-                    jnp.where((plane - by) % planes == core * per_core + at, shifted[by], 0.0)
-                    for by in range(planes)
-                ],
-            )
-            for at in range(per_core)
-        ],
-        axis=1,
-    )
-    tall_eigen = jnp.broadcast_to(eigen_first[:, None], (height, 128))
-    turned = basis_first.T
+    bf16_square = jax.ShapeDtypeStruct((height, height), BF16)
+    turned, high, low, tall_eigen = pl.pallas_call(
+        prepare_kernel,
+        grid=(1,),
+        in_specs=[full(height, height), full(width, width), full(width, width), full(1, height)]
+        + [pl.BlockSpec(memory_space=pl.ANY)],
+        out_specs=[whole_out(height, height)] * 3 + [whole_out(height, 128)],
+        out_shape=[bf16_square] * 3 + [shape_of(height, 128)],
+        compiler_params=params(1, 24),
+        name="prepare",
+    )(basis_first, basis_second, kernel_second, eigen_first.reshape(1, -1), eigen)
 
     def swap(value):
         return lax.ppermute(value, "mode", core_swap)
 
-    def call(kernel, inputs, shapes, scratch_shape, specs=None):
+    def call(kernel, inputs, shapes, scratch_shape, specs=None, more=(), mebibytes=12):
         return pl.pallas_call(
             kernel,
             grid=(1,),
             in_specs=specs or [smem] + [full(*value.shape) for value in inputs[1:]],
             out_specs=[whole_out(*shape) for shape in shapes],
             out_shape=[shape_of(*shape) for shape in shapes],
-            scratch_shapes=[pltpu.VMEM(scratch_shape, F32)],
-            compiler_params=params(1, 12),
+            scratch_shapes=[*([pltpu.VMEM(scratch_shape, F32)] if scratch_shape else []), *more],
+            compiler_params=params(1, mebibytes),
         )(*inputs)
 
     tile = (height, half)
@@ -469,11 +512,28 @@
 
     spectral, weights, column, keep, send, sum_one = call(
         first_column_kernel,
-        (place, noise_table, arrived, tall_eigen, eigen, turned, basis_first),
+        (
+            place,
+            noise_table,
+            pltpu.with_memory_space_constraint(arrived, pltpu.HBM),
+            pltpu.with_memory_space_constraint(turned, pltpu.HBM),
+            pltpu.with_memory_space_constraint(basis_first, pltpu.HBM),
+            tall_eigen,
+            *shifted,
+        ),
         (tile, tile, tile, piece, piece, sums_shape),
         by_rows,
-        [smem, smem, full(groups, rows, half), full(height, 128), full(1, half)]
-        + [full(height, height)] * 2,
+        [smem, smem]
+        + [pl.BlockSpec(memory_space=pltpu.HBM)] * 3
+        + [full(height, 128)]
+        + [full(*value.shape) for value in shifted],
+        [
+            pltpu.VMEM((groups, rows, half), F32),
+            pltpu.VMEM((height, height), BF16),
+            pltpu.VMEM((height, height), BF16),
+            pltpu.SemaphoreType.DMA((3,)),
+        ],
+        18,
     )
     got = swap(send)
     image_keep, image_send = call(
@@ -481,15 +541,14 @@
     )
     image_got = swap(image_send)
     (z_field,) = call(row_kernel, (place, keep, got, basis_second), (whole,), flat)
-    (part,) = call(
-        first_image_kernel,
-        (place, image_keep, image_got, basis_second, kernel_second),
-        (whole,),
-        flat,
-    )
-    image, back_keep, back_send = call(
-        return_kernel, (place, part, z_field, basis_second, *noise), (whole, piece, piece), flat
-    )
+    (part,) = call(first_image_kernel, (place, image_keep, image_got, high, low), (whole,), flat)
+    noise, image, back_send = call(
+        noise_image_kernel,
+        (place, part, z_field, basis_second, *noise),
+        (whole, whole, piece),
+        None,
+    )
+    (back_keep,) = call(keep_kernel, (place, image, basis_second), (piece,), None)
     back_got = swap(back_send)
 
     column, keep, send, sum_two = call(
@@ -511,11 +570,11 @@
             image_keep,
             image_got,
             f_field,
-            basis_second,
-            kernel_second,
+            noise,
+            high,
+            low,
             sum_one,
             sum_two,
-            *noise,
         ),
         (whole, (groups, 8, 128)),
         flat,

time: 265 us -> 269 us (1.015)
  waiting for transfers between devices: 74.2 us -> 67.7 us
  Pallas kernels: 50.6 us -> 54.4 us
    pallas_call x1 -> x3, Pallas kernels: 1.61 us -> 6.77 us  [the longest x2 4.39 us: noise_of(): pl.pallas_call(functools.partial(noise_kernel, shifts), grid=(1,), in_spe...]
    ppermute x3, waiting for transfers between devices: 53.9 us -> 50.8 us  [plane_shift(): return lax.ppermute(value, 'mode', pairs)]
    ppermute x3, waiting for transfers between devices: 2.76 us -> 0.01 us  [paired_body(): lax.ppermute(eigen, 'mode', [(at, (at + by * unit) % groups) for at in ra...]
    unnamed x23 -> x34, local copies, waits for them, and re-layouts: 5.4 us -> 7.27 us
    pallas_call x9 -> x10, Pallas kernels: 38.8 us -> 37.6 us  [call(): pl.pallas_call(kernel, grid=(1,), in_specs=specs or [smem] + [full(*value...]
  transfers between devices with their start and end apart: 18 -> 18, of which waited for: 9 -> 6; matrix products, arithmetic and copies ran while one was open for 1% -> 0% of each run, Pallas kernels for 7% -> 9%
where the time goes in v6:
time: 269 us; the launch traced here: 268 us
  blocking collectives  108 us (40%)
  waiting for transfers between devices  67.7 us (25%)
  Pallas kernels  54.4 us (20%)
  starting transfers between devices  28.9 us (11%)
  local copies, waits for them, and re-layouts  7.27 us (3%)
    all_to_all x1, blocking collectives, paired_body(): lax.all_to_all(answer, 'mode', split_axis=0, concat_axis=0, axis_index_gr...  95.8 us
    ppermute x3, waiting for transfers between devices, plane_shift(): return lax.ppermute(value, 'mode', pairs)  50.8 us
    pallas_call x10, Pallas kernels, call(): pl.pallas_call(kernel, grid=(1,), in_specs=specs or [smem] + [full(*value...  37.6 us
    ppermute x4, waiting for transfers between devices, paired_body(): far = [lax.ppermute(value, 'mode', sample_swap) for value in near]  14 us
    all_to_all x1, blocking collectives, paired_body(): sums = lax.all_to_all(sums, 'mode', split_axis=0, concat_axis=0, tiled=True)  12.3 us
    ppermute x3, starting transfers between devices, paired_body(): lax.ppermute(eigen, 'mode', [(at, (at + by * unit) % groups) for at in ra...  7.63 us
    all_to_all x1, starting transfers between devices, paired_body(): lax.all_to_all(outgoing.reshape(groups, rows, half), 'mode', split_axis=0...  7.6 us
    unnamed x34, local copies, waits for them, and re-layouts  7.27 us
  transfers between devices with their start and end apart: 18, of which 6 were waited for; matrix products, arithmetic and copies ran while one was open for 0% of the time, Pallas kernels for 9%

profile of v6, /device:TPU:0, one launch (start us, length us, event | category | flops | bytes accessed | tf_op | source)
XLA Modules:
  0.0 268.1 jit_solution(11774304970168191649)
XLA Ops:
  0.6 6.0 %outgoing.1 = f32[4,2,2,64,512]{4,3,2,1,0:T(8,128)} custom-call(f32[2,4,64,1024]{3,2,1,0:T(8,128)} %right_ref.3, bf16[1024,1024]{1,0:T(8,128)(2,1)} %basis_ref.11), custom_call_target="tpu_custom_call" | custom-call | tf_op jit(solution)/shard_map/outgoing/pallas_call | solution.py:442
  6.7 7.6 %all-to-all-start = ((f32[16,64,512]{2,1,0:T(8,128)}), f32[16,64,512]{2,1,0:T(8,128)}, u32[]{:S(2)}, u32[]{:S(2)}) async-start(f32[16,64,512]{2,1,0:T(8,128)} %bitcast.10), calls=%async_computation | async-start | bytes 4194304 | tf_op jit(solution)/shard_map/all_to_all | solution.py:454
  15.4 2.1 shard_map.105
  17.4 2.5 collective-permute-start.3
  20.0 2.3 shard_map.104
  22.3 1.5 collective-permute-start.2
  23.8 2.4 collective-permute-start.4
  26.2 1.5 collective-permute-start.1
  27.7 2.1 collective-permute-done.1
  29.8 50.8 %collective-permute-done.3.refs_1_.refs_2_ = f32[64,1024]{1,0:T(8,128)S(1)} collective-permute-done((f32[64,1024]{1,0:T(8,128)}, f32[64,1024]{1,0:T(8,128)S(1)}, u32[]{:S(2)}, u32[]{:S(2)}) %collective-permute-start.3) | collective-permute-done | bytes 262176 | tf_op jit(solution)/shard_map/ppermute | solution.py:430
  80.7 1.5 collective-permute-start.7
  82.2 5.6 %collective-permute-start.6 = (f32[1,256]{1,0:T(1,128)S(1)}, f32[1,256]{1,0:T(1,128)S(1)}, u32[]{:S(2)}, u32[]{:S(2)}) collective-permute-start(f32[1,256]{1,0:T(1,128)S(1)} %follow.1._.refs_0_), channel_id=1, source_target_pairs={{0,8},{1,9},{2,10},{3,11},{4,12},{5,13},{6,14},{7,15},{8,0},{9,1},... | collective-permute-start | bytes 3080 | tf_op jit(solution)/shard_map/ppermute | solution.py:477
  88.3 1.6 copy-done.1
  89.9 1.6 copy-done.11
  91.5 2.4 prepare.1
  98.0 7.7 %shard_map.106 = (f32[1024,512]{1,0:T(8,128)S(1)}, f32[1024,512]{1,0:T(8,128)S(1)}, f32[1024,512]{1,0:T(8,128)S(1)}, f32[8,64,512]{2,1,0:T(8,128)S(1)}, f32[8,64,512]{2,1,0:T(8,128)S(1)}, /*index=5*/f32[8,128]{1,0:T(8,128)S(1)}) custom-call(s32[3]{0:T(128)S(1)} %copy-done.13, f32[8]{0:T(128)S(1)} %copy-done.14, f32[16,64,512]{2,1,0:T(8,128)} %all-to-all-done.field_hbm, ...), custom_call_target="tpu_custom_call" | custom-call | tf_op jit(solution)/shard_map/pallas_call | solution.py:496
  105.8 3.0 %shard_map.107 = (f32[8,64,512]{2,1,0:T(8,128)S(1)}, f32[8,64,512]{2,1,0:T(8,128)S(1)}) custom-call(s32[3]{0:T(128)S(1)} %copy-done.13, f32[1024,512]{1,0:T(8,128)S(1)} %get-tuple-element.32.column_ref, bf16[1024,1024]{1,0:T(8,128)(2,1)S(1)} %copy-done.4), custom_call_target="tpu_custom_call" | custom-call | tf_op jit(solution)/shard_map/pallas_call | solution.py:496
  113.4 3.0 %shard_map.109.z_ref = f32[8,64,1024]{2,1,0:T(8,128)S(1)} custom-call(s32[3]{0:T(128)S(1)} %copy-done.13, f32[8,64,512]{2,1,0:T(8,128)S(1)} %get-tuple-element.37.keep_ref, f32[8,64,512]{2,1,0:T(8,128)S(1)} %collective-permute-done.9.got_ref, bf16[1024,1024]{1,0:T(8,128)(2,1)S(1)} %copy-done), custom_call_target="tpu_custom_call" | custom-call | tf_op jit(solution)/shard_map/pallas_call | solution.py:496
  116.4 4.1 %shard_map.108.part_ref = f32[8,64,1024]{2,1,0:T(8,128)S(1)} custom-call(s32[3]{0:T(128)S(1)} %copy-done.13, f32[8,64,512]{2,1,0:T(8,128)S(1)} %get-tuple-element.33.keep_ref, f32[8,64,512]{2,1,0:T(8,128)S(1)} %collective-permute-done.8.got_ref, bf16[1024,1024]{1,0:T(8,128)(2,1)S(1)} %copy-done.8, bf16[1024,1024]{1,0:T(8,128)(2,1)S(1)} %copy-done.10), custom_call_target="tpu_custom_call" | custom-call | tf_op jit(solution)/shard_map/pallas_call | solution.py:496
  120.5 3.6 %collective-permute-done.12.refs_6_ = f32[64,1024]{1,0:T(8,128)S(1)} collective-permute-done((f32[64,1024]{1,0:T(8,128)S(1)}, f32[64,1024]{1,0:T(8,128)S(1)}, u32[]{:S(2)}, u32[]{:S(2)}) %collective-permute-start.12) | collective-permute-done | bytes 262176 | tf_op jit(solution)/shard_map/ppermute | solution.py:439
  124.2 5.6 %collective-permute-done.11.refs_5_ = f32[64,1024]{1,0:T(8,128)S(1)} collective-permute-done((f32[64,1024]{1,0:T(8,128)S(1)}, f32[64,1024]{1,0:T(8,128)S(1)}, u32[]{:S(2)}, u32[]{:S(2)}) %collective-permute-start.11) | collective-permute-done | bytes 262176 | tf_op jit(solution)/shard_map/ppermute | solution.py:439
  129.8 4.7 %collective-permute-done.13.refs_7_ = f32[64,1024]{1,0:T(8,128)S(1)} collective-permute-done((f32[64,1024]{1,0:T(8,128)S(1)}, f32[64,1024]{1,0:T(8,128)S(1)}, u32[]{:S(2)}, u32[]{:S(2)}) %collective-permute-start.13) | collective-permute-done | bytes 262176 | tf_op jit(solution)/shard_map/ppermute | solution.py:439
  134.5 2.3 shard_map.110
  136.9 1.8 shard_map.111.held_ref
  139.5 5.5 %shard_map.112 = (f32[1024,512]{1,0:T(8,128)S(1)}, f32[8,64,512]{2,1,0:T(8,128)S(1)}, f32[8,64,512]{2,1,0:T(8,128)S(1)}, f32[8,128]{1,0:T(8,128)S(1)}) custom-call(s32[3]{0:T(128)S(1)} %copy-done.13, f32[8,64,512]{2,1,0:T(8,128)S(1)} %shard_map.111.held_ref, f32[8,64,512]{2,1,0:T(8,128)S(1)} %collective-permute-done.14.got_ref, ...), custom_call_target="tpu_custom_call" | custom-call | tf_op jit(solution)/shard_map/pallas_call | solution.py:496
  145.3 3.0 %shard_map.113 = (f32[8,64,512]{2,1,0:T(8,128)S(1)}, f32[8,64,512]{2,1,0:T(8,128)S(1)}) custom-call(s32[3]{0:T(128)S(1)} %copy-done.13, f32[1024,512]{1,0:T(8,128)S(1)} %get-tuple-element.44.column_ref, bf16[1024,1024]{1,0:T(8,128)(2,1)S(1)} %copy-done.4), custom_call_target="tpu_custom_call" | custom-call | tf_op jit(solution)/shard_map/pallas_call | solution.py:496
  148.7 3.0 %shard_map.114.z_ref.f_ref = f32[8,64,1024]{2,1,0:T(8,128)S(1)} custom-call(s32[3]{0:T(128)S(1)} %copy-done.13, f32[8,64,512]{2,1,0:T(8,128)S(1)} %get-tuple-element.47.keep_ref, f32[8,64,512]{2,1,0:T(8,128)S(1)} %collective-permute-done.16.got_ref, bf16[1024,1024]{1,0:T(8,128)(2,1)S(1)} %copy-done), custom_call_target="tpu_custom_call" | custom-call | tf_op jit(solution)/shard_map/pallas_call | solution.py:496
  151.7 4.2 %shard_map.115 = (f32[8,64,1024]{2,1,0:T(8,128)S(1)}, f32[16,8,128]{2,1,0:T(8,128)S(1)}) custom-call(s32[3]{0:T(128)S(1)} %copy-done.13, f32[8,64,512]{2,1,0:T(8,128)S(1)} %get-tuple-element.45.keep_ref, f32[8,64,512]{2,1,0:T(8,128)S(1)} %collective-permute-done.15.got_ref, f32[8,64,1024]{2,1,0:T(8,128)S(1)} %shard_map.114.z_ref.f_ref, ...), custom_call_target="tpu_custom_call" | custom-call | tf_op jit(solution)/shard_map/pallas_call | solution.py:496
  155.9 12.3 %all_to_all.15.sum_ref = f32[16,8,128]{2,1,0:T(8,128)S(1)} all-to-all(f32[16,8,128]{2,1,0:T(8,128)S(1)} %get-tuple-element.52), channel_id=1, replica_groups=mesh['blocks'=2,'mode'=16] {'mode'}, dimensions={0} | all-to-all | bytes 131072 | tf_op jit(solution)/shard_map/all_to_all | solution.py:582
  168.2 1.5 combine.1
  169.7 95.8 %all_to_all.16.got_ref = f32[8,128,1024]{2,1,0:T(8,128)S(1)} all-to-all(f32[8,128,1024]{2,1,0:T(8,128)S(1)} %combine.1), channel_id=1, replica_groups={{0,2,4,6,8,10,12,14},{1,3,5,7,9,11,13,15},{16,18,20,22,24,26,28,30},{17..., dimensions={0} | all-to-all | bytes 8388608 | tf_op jit(solution)/shard_map/all_to_all | solution.py:595
  265.5 2.6 finish.1
  (61 shorter events, 12.1 us)
Async XLA Ops:
  6.6 7.6 %copy-start.16 = (f32[64]{0:T(128)S(1)}, f32[64]{0:T(128)}, u32[]{:S(2)}) copy-start(f32[64]{0:T(128)} %param.17) | copy-start | bytes 772
  6.7 91.3 %all-to-all-start = ((f32[16,64,512]{2,1,0:T(8,128)}), f32[16,64,512]{2,1,0:T(8,128)}, u32[]{:S(2)}, u32[]{:S(2)}) async-start(f32[16,64,512]{2,1,0:T(8,128)} %bitcast.10), calls=%async_computation | async-start | bytes 4194304 | tf_op jit(solution)/shard_map/all_to_all | solution.py:454
  14.3 74.1 %copy-start = (bf16[1024,1024]{1,0:T(8,128)(2,1)S(1)}, bf16[1024,1024]{1,0:T(8,128)(2,1)}, u32[]{:S(2)}) copy-start(bf16[1024,1024]{1,0:T(8,128)(2,1)} %basis_ref.11) | copy-start | bytes 6291460
  14.3 74.0 %copy-start.15 = (f32[1024]{0:T(1024)S(1)}, f32[1024]{0:T(1024)}, u32[]{:S(2)}) copy-start(f32[1024]{0:T(1024)} %param.16) | copy-start | bytes 12292
  14.3 11.8 %collective-permute-start = (f32[1,64]{1,0:T(1,128)S(1)}, f32[1,64]{1,0:T(1,128)S(1)}, u32[]{:S(2)}, u32[]{:S(2)}) collective-permute-start(f32[1,64]{1,0:T(1,128)S(1)} %bitcast.11), channel_id=1, source_target_pairs={{0,1},{1,0},{2,3},{3,2},{4,5},{5,4},{6,7},{7,6},{8,9},{9,8},{10,11... | collective-permute-start | bytes 776 | tf_op jit(solution)/shard_map/ppermute | solution.py:460
  17.4 63.2 %collective-permute-start.3 = (f32[64,1024]{1,0:T(8,128)}, f32[64,1024]{1,0:T(8,128)S(1)}, u32[]{:S(2)}, u32[]{:S(2)}) collective-permute-start(f32[64,1024]{1,0:T(8,128)} %shard_map.105), channel_id=1, source_target_pairs={{0,8},{1,9},{2,10},{3,11},{4,12},{5,13},{6,14},{7,15},{8,0},{9,1},... | collective-permute-start | bytes 786440 | tf_op jit(solution)/shard_map/ppermute | solution.py:430
  22.3 58.4 %collective-permute-start.2 = (f32[64,1024]{1,0:T(8,128)}, f32[64,1024]{1,0:T(8,128)S(1)}, u32[]{:S(2)}, u32[]{:S(2)}) collective-permute-start(f32[64,1024]{1,0:T(8,128)} %get-tuple-element.28), channel_id=1, source_target_pairs={{0,4},{1,5},{2,6},{3,7},{4,8},{5,9},{6,10},{7,11},{8,12},{9,13},{1... | collective-permute-start | bytes 786440 | tf_op jit(solution)/shard_map/ppermute | solution.py:430
  23.8 56.9 %collective-permute-start.4 = (f32[64,1024]{1,0:T(8,128)}, f32[64,1024]{1,0:T(8,128)S(1)}, u32[]{:S(2)}, u32[]{:S(2)}) collective-permute-start(f32[64,1024]{1,0:T(8,128)} %get-tuple-element.29), channel_id=1, source_target_pairs={{0,12},{1,13},{2,14},{3,15},{4,0},{5,1},{6,2},{7,3},{8,4},{9,5},{1... | collective-permute-start | bytes 786440 | tf_op jit(solution)/shard_map/ppermute | solution.py:430
  26.2 3.6 %collective-permute-start.1 = (f32[1,128]{1,0:T(1,128)S(1)}, f32[1,128]{1,0:T(1,128)S(1)}, u32[]{:S(2)}, u32[]{:S(2)}) collective-permute-start(f32[1,128]{1,0:T(1,128)S(1)} %broadcast_select_fusion.1), channel_id=1, source_target_pairs={{0,2},{1,3},{2,0},{3,1},{4,6},{5,7},{6,4},{7,5},{8,10},{9,11},{10,... | collective-permute-start | bytes 1544 | tf_op jit(solution)/shard_map/ppermute | solution.py:460
  80.7 17.3 %collective-permute-start.7 = (f32[1,256]{1,0:T(1,128)S(1)}, f32[1,256]{1,0:T(1,128)S(1)}, u32[]{:S(2)}, u32[]{:S(2)}) collective-permute-start(f32[1,256]{1,0:T(1,128)S(1)} %follow.1._.refs_0_), channel_id=1, source_target_pairs={{0,12},{1,13},{2,14},{3,15},{4,0},{5,1},{6,2},{7,3},{8,4},{9,5},{1... | collective-permute-start | bytes 3080 | tf_op jit(solution)/shard_map/ppermute | solution.py:477
  82.2 15.7 %collective-permute-start.6 = (f32[1,256]{1,0:T(1,128)S(1)}, f32[1,256]{1,0:T(1,128)S(1)}, u32[]{:S(2)}, u32[]{:S(2)}) collective-permute-start(f32[1,256]{1,0:T(1,128)S(1)} %follow.1._.refs_0_), channel_id=1, source_target_pairs={{0,8},{1,9},{2,10},{3,11},{4,12},{5,13},{6,14},{7,15},{8,0},{9,1},... | collective-permute-start | bytes 3080 | tf_op jit(solution)/shard_map/ppermute | solution.py:477
  87.7 10.2 %collective-permute-start.5 = (f32[1,256]{1,0:T(1,128)S(1)}, f32[1,256]{1,0:T(1,128)S(1)}, u32[]{:S(2)}, u32[]{:S(2)}) collective-permute-start(f32[1,256]{1,0:T(1,128)S(1)} %follow.1._.refs_0_), channel_id=1, source_target_pairs={{0,4},{1,5},{2,6},{3,7},{4,8},{5,9},{6,10},{7,11},{8,12},{9,13},{1... | collective-permute-start | bytes 3080 | tf_op jit(solution)/shard_map/ppermute | solution.py:477
  88.3 1.6 copy-start.1
  89.9 1.6 copy-start.11
  91.5 6.4 %copy-start.13 = (s32[3]{0:T(128)S(1)}, s32[3]{0:T(128)}, u32[]{:S(2)}) copy-start(s32[3]{0:T(128)} %pad_add_fusion.place_ref) | copy-start | bytes 40
  91.5 6.5 %copy-start.14 = (f32[8]{0:T(128)S(1)}, f32[8]{0:T(128)}, u32[]{:S(2)}) copy-start(f32[8]{0:T(128)} %table_ref.5) | copy-start | bytes 100
  98.0 7.8 %copy-start.4 = (bf16[1024,1024]{1,0:T(8,128)(2,1)S(1)}, bf16[1024,1024]{1,0:T(8,128)(2,1)}, u32[]{:S(2)}) copy-start(bf16[1024,1024]{1,0:T(8,128)(2,1)} %kernel_ref.5) | copy-start | bytes 6291460
  105.7 7.1 %collective-permute-start.9 = (f32[8,64,512]{2,1,0:T(8,128)S(1)}, f32[8,64,512]{2,1,0:T(8,128)S(1)}, u32[]{:S(2)}, u32[]{:S(2)}) collective-permute-start(f32[8,64,512]{2,1,0:T(8,128)S(1)} %get-tuple-element.38), channel_id=1, source_target_pairs={{0,1},{1,0},{2,3},{3,2},{4,5},{5,4},{6,7},{7,6},{8,9},{9,8},{10,11... | collective-permute-start | bytes 3145736 | tf_op jit(solution)/shard_map/ppermute | solution.py:493
  105.8 3.6 %copy-start.12 = (f32[64,1024]{1,0:T(8,128)S(1)}, f32[64,1024]{1,0:T(8,128)}, u32[]{:S(2)}) copy-start(f32[64,1024]{1,0:T(8,128)} %get-tuple-element.39.refs_0_) | copy-start | bytes 786436
  108.8 7.6 %collective-permute-start.8 = (f32[8,64,512]{2,1,0:T(8,128)S(1)}, f32[8,64,512]{2,1,0:T(8,128)S(1)}, u32[]{:S(2)}, u32[]{:S(2)}) collective-permute-start(f32[8,64,512]{2,1,0:T(8,128)S(1)} %get-tuple-element.34), channel_id=1, source_target_pairs={{0,1},{1,0},{2,3},{3,2},{4,5},{5,4},{6,7},{7,6},{8,9},{9,8},{10,11... | collective-permute-start | bytes 3145736 | tf_op jit(solution)/shard_map/ppermute | solution.py:493
  109.4 11.2 %collective-permute-start.10 = (f32[64,1024]{1,0:T(8,128)S(1)}, f32[64,1024]{1,0:T(8,128)S(1)}, u32[]{:S(2)}, u32[]{:S(2)}) collective-permute-start(f32[64,1024]{1,0:T(8,128)S(1)} %copy-done.12), channel_id=1, source_target_pairs={{0,2},{1,3},{2,0},{3,1},{4,6},{5,7},{6,4},{7,5},{8,10},{9,11},{10,... | collective-permute-start | bytes 786440 | tf_op jit(solution)/shard_map/ppermute | solution.py:439
  110.8 13.4 %collective-permute-start.12 = (f32[64,1024]{1,0:T(8,128)S(1)}, f32[64,1024]{1,0:T(8,128)S(1)}, u32[]{:S(2)}, u32[]{:S(2)}) collective-permute-start(f32[64,1024]{1,0:T(8,128)S(1)} %collective-permute-done.3.refs_1_.refs_2_), channel_id=1, source_target_pairs={{0,2},{1,3},{2,0},{3,1},{4,6},{5,7},{6,4},{7,5},{8,10},{9,11},{10,... | collective-permute-start | bytes 786440 | tf_op jit(solution)/shard_map/ppermute | solution.py:439
  111.4 18.4 %collective-permute-start.11 = (f32[64,1024]{1,0:T(8,128)S(1)}, f32[64,1024]{1,0:T(8,128)S(1)}, u32[]{:S(2)}, u32[]{:S(2)}) collective-permute-start(f32[64,1024]{1,0:T(8,128)S(1)} %collective-permute-done.2.refs_0_.refs_1_), channel_id=1, source_target_pairs={{0,2},{1,3},{2,0},{3,1},{4,6},{5,7},{6,4},{7,5},{8,10},{9,11},{10,... | collective-permute-start | bytes 786440 | tf_op jit(solution)/shard_map/ppermute | solution.py:439
  112.8 21.7 %collective-permute-start.13 = (f32[64,1024]{1,0:T(8,128)S(1)}, f32[64,1024]{1,0:T(8,128)S(1)}, u32[]{:S(2)}, u32[]{:S(2)}) collective-permute-start(f32[64,1024]{1,0:T(8,128)S(1)} %collective-permute-done.4.refs_2_.refs_3_), channel_id=1, source_target_pairs={{0,2},{1,3},{2,0},{3,1},{4,6},{5,7},{6,4},{7,5},{8,10},{9,11},{10,... | collective-permute-start | bytes 786440 | tf_op jit(solution)/shard_map/ppermute | solution.py:439
  113.4 3.0 %copy-start.8 = (bf16[1024,1024]{1,0:T(8,128)(2,1)S(1)}, bf16[1024,1024]{1,0:T(8,128)(2,1)}, u32[]{:S(2)}) copy-start(bf16[1024,1024]{1,0:T(8,128)(2,1)} %copy-done.7) | copy-start | bytes 6291460
  113.4 3.0 %copy-start.10 = (bf16[1024,1024]{1,0:T(8,128)(2,1)S(1)}, bf16[1024,1024]{1,0:T(8,128)(2,1)}, u32[]{:S(2)}) copy-start(bf16[1024,1024]{1,0:T(8,128)(2,1)} %copy-done.9) | copy-start | bytes 6291460
  136.8 2.7 %collective-permute-start.14 = (f32[8,64,512]{2,1,0:T(8,128)S(1)}, f32[8,64,512]{2,1,0:T(8,128)S(1)}, u32[]{:S(2)}, u32[]{:S(2)}) collective-permute-start(f32[8,64,512]{2,1,0:T(8,128)S(1)} %get-tuple-element.41), channel_id=1, source_target_pairs={{0,1},{1,0},{2,3},{3,2},{4,5},{5,4},{6,7},{7,6},{8,9},{9,8},{10,11... | collective-permute-start | bytes 3145736 | tf_op jit(solution)/shard_map/ppermute | solution.py:493
  136.9 2.6 copy-start.2
  136.9 2.6 copy-start.6
  145.1 3.7 %collective-permute-start.16 = (f32[8,64,512]{2,1,0:T(8,128)S(1)}, f32[8,64,512]{2,1,0:T(8,128)S(1)}, u32[]{:S(2)}, u32[]{:S(2)}) collective-permute-start(f32[8,64,512]{2,1,0:T(8,128)S(1)} %get-tuple-element.48), channel_id=1, source_target_pairs={{0,1},{1,0},{2,3},{3,2},{4,5},{5,4},{6,7},{7,6},{8,9},{9,8},{10,11... | collective-permute-start | bytes 3145736 | tf_op jit(solution)/shard_map/ppermute | solution.py:493
  148.3 3.4 %collective-permute-start.15 = (f32[8,64,512]{2,1,0:T(8,128)S(1)}, f32[8,64,512]{2,1,0:T(8,128)S(1)}, u32[]{:S(2)}, u32[]{:S(2)}) collective-permute-start(f32[8,64,512]{2,1,0:T(8,128)S(1)} %get-tuple-element.46), channel_id=1, source_target_pairs={{0,1},{1,0},{2,3},{3,2},{4,5},{5,4},{6,7},{7,6},{8,9},{9,8},{10,11... | collective-permute-start | bytes 3145736 | tf_op jit(solution)/shard_map/ppermute | solution.py:493
  169.7 95.8 %copy-start.3 = (f32[2,4,64,1024]{3,2,1,0:T(8,128)S(1)}, f32[2,4,64,1024]{3,2,1,0:T(8,128)}, u32[]{:S(2)}) copy-start(f32[2,4,64,1024]{3,2,1,0:T(8,128)} %right_ref.3) | copy-start | bytes 6291460
  (3 other events, 4.0 us)

commit v7 on v6

--- a/solution.py
+++ b/solution.py
@@ -146,14 +146,23 @@
     )
 
 
-def noise_kernel(shifts, place_ref, table_ref, class_ref, *out_refs):
-    planes = class_ref.shape[0]
-    for by, out_ref in zip(shifts, out_refs):
-        level = class_ref[(place_ref[2] + by) % planes]
+def noise_kernel(shifts, unit, table_ref, class_hbm, *refs):
+    out_refs, (class_ref, done) = refs[:-2], refs[-2:]
+    planes = class_hbm.shape[0]
+    plane = lax.axis_index("mode") // unit
+    copies = [
+        pltpu.make_async_copy(class_hbm.at[(plane + by) % planes], class_ref.at[at], done.at[at])
+        for at, by in enumerate(shifts)
+    ]
+    for copy in copies:
+        copy.start()
+    for at, copy in enumerate(copies):
+        copy.wait()
+        level = class_ref[at]
         noise = jnp.full(level.shape, table_ref[0], F32)
         for index in range(1, NCLASS):
             noise = jnp.where(level == index, table_ref[index], noise)
-        out_ref[...] = noise
+        out_refs[at][...] = noise
 
 
 def follow_kernel(value_ref, *refs):
@@ -216,7 +225,14 @@
     wide_refs, refs, local = refs[:-11], refs[-11:-4], refs[-4:]
     spectral_ref, weight_ref, column_ref, keep_ref, send_ref, sum_ref, scratch_ref = refs
     field_ref, turned_ref, basis_ref, done = local
-    pairs = ((field_hbm, field_ref), (turned_hbm, turned_ref), (basis_hbm, basis_ref))
+    middle = turned_ref.shape[0] // 2
+    upper, lower = pl.ds(0, middle), pl.ds(middle, middle)
+    pairs = (
+        (field_hbm, field_ref),
+        (turned_hbm.at[upper], turned_ref.at[upper]),
+        (turned_hbm.at[lower], turned_ref.at[lower]),
+        (basis_hbm, basis_ref),
+    )
     copies = [
         pltpu.make_async_copy(source, target, done.at[at])
         for at, (source, target) in enumerate(pairs)
@@ -237,12 +253,15 @@
             lanes = slice(block * part + at, block * part + at + 128)
             weight_ref[:, lanes] = 1.0 / (tall_ref[...] * wide[:, at : at + 128] + mean)
     copies[0].wait()
+    field = field_ref[...].reshape(height, width)
     copies[1].wait()
-    spectral = times_left(turned_ref[...], field_ref[...].reshape(height, width))
+    above = times_left(turned_ref[:middle], field)
+    copies[2].wait()
+    spectral = jnp.concatenate([above, times_left(turned_ref[middle:], field)], axis=0)
     weighted = spectral * weight_ref[...]
     spectral_ref[...] = spectral
     store_sums(sum_ref, [fold(spectral * weighted)])
-    copies[2].wait()
+    copies[3].wait()
     column = times_left(basis_ref[...], weighted)
     column_ref[...] = column
     split_rows(place_ref, column, scratch_ref, keep_ref, send_ref)
@@ -301,30 +320,29 @@
     return result[: field.shape[0]] + (result[field.shape[0] :] + small)
 
 
-def first_image_kernel(place_ref, keep_ref, got_ref, high_ref, low_ref, image_ref, scratch_ref):
-    image = row_image(place_ref, keep_ref, got_ref, high_ref, low_ref, scratch_ref)
-    image_ref[...] = image.reshape(image_ref.shape)
-
-
-def noise_image_kernel(place_ref, part_ref, z_ref, basis_ref, *refs):
-    noise_refs, (noise_ref, image_ref, send_ref) = refs[:-3], refs[-3:]
-    planes = len(noise_refs) // 2
+def first_image_kernel(place_ref, keep_ref, got_ref, high_ref, low_ref, z_ref, *refs):
+    parts, (image_ref, noise_ref, scratch_ref, done) = refs[:-4], refs[-4:]
+    planes = len(parts) // 2
     samples = image_ref.shape[0] // planes
+    copies = []
     for by in range(planes):
         row = (place_ref[2] + planes - by) % planes
-        for at, part in enumerate((noise_refs[by], noise_refs[planes + by])):
-            noise_ref[row * samples + (place_ref[1] + at) % samples] = part[...]
-    image_ref[...] = part_ref[...] + noise_ref[...] * z_ref[...]
-    half = send_ref.shape[2]
-    _, theirs = both_shares(place_ref, half)
+        for at, part in enumerate((parts[by], parts[planes + by])):
+            block = row * samples + (place_ref[1] + at) % samples
+            here = done.at[2 * by + at]
+            copies.append(pltpu.make_async_copy(part, noise_ref.at[block], here))
+    for copy in copies:
+        copy.start()
+    image = row_image(place_ref, keep_ref, got_ref, high_ref, low_ref, scratch_ref)
+    for copy in copies:
+        copy.wait()
+    image_ref[...] = image.reshape(image_ref.shape) + noise_ref[...] * z_ref[...]
+
+
+def return_kernel(whose, place_ref, image_ref, basis_ref, out_ref):
+    lanes = both_shares(place_ref, out_ref.shape[2])[whose]
     image = image_ref[...].reshape(-1, basis_ref.shape[0])
-    send_ref[...] = times_right(image, basis_ref[:, theirs], 0).reshape(send_ref.shape)
-
-
-def keep_kernel(place_ref, image_ref, basis_ref, keep_ref):
-    mine, _ = both_shares(place_ref, keep_ref.shape[2])
-    image = image_ref[...].reshape(-1, basis_ref.shape[0])
-    keep_ref[...] = times_right(image, basis_ref[:, mine], 0).reshape(keep_ref.shape)
+    out_ref[...] = times_right(image, basis_ref[:, lanes], 0).reshape(out_ref.shape)
 
 
 def last_image_kernel(
@@ -415,15 +433,22 @@
     core_swap = [(at, at ^ 1) for at in range(groups)]
     sample_swap = [(at, at ^ cores) for at in range(groups)]
 
+    def in_hbm(value):
+        return pltpu.with_memory_space_constraint(value, pltpu.HBM)
+
     def noise_of(shifts):
         return pl.pallas_call(
-            functools.partial(noise_kernel, shifts),
+            functools.partial(noise_kernel, shifts, unit),
             grid=(1,),
-            in_specs=[smem, smem, full(planes, rows, width)],
+            in_specs=[smem, pl.BlockSpec(memory_space=pltpu.HBM)],
             out_specs=[whole_out(rows, width)] * len(shifts),
             out_shape=[shape_of(rows, width)] * len(shifts),
+            scratch_shapes=[
+                pltpu.VMEM((len(shifts), rows, width), jnp.int32),
+                pltpu.SemaphoreType.DMA((len(shifts),)),
+            ],
             compiler_params=params(1, 56),
-        )(place, noise_table, classes)
+        )(noise_table, in_hbm(classes))
 
     def plane_shift(value, by):
         pairs = [(at, (at + by * unit) % groups) for at in range(groups)]
@@ -515,9 +540,9 @@
         (
             place,
             noise_table,
-            pltpu.with_memory_space_constraint(arrived, pltpu.HBM),
-            pltpu.with_memory_space_constraint(turned, pltpu.HBM),
-            pltpu.with_memory_space_constraint(basis_first, pltpu.HBM),
+            in_hbm(arrived),
+            in_hbm(turned),
+            in_hbm(basis_first),
             tall_eigen,
             *shifted,
         ),
@@ -531,7 +556,7 @@
             pltpu.VMEM((groups, rows, half), F32),
             pltpu.VMEM((height, height), BF16),
             pltpu.VMEM((height, height), BF16),
-            pltpu.SemaphoreType.DMA((3,)),
+            pltpu.SemaphoreType.DMA((4,)),
         ],
         18,
     )
@@ -541,14 +566,24 @@
     )
     image_got = swap(image_send)
     (z_field,) = call(row_kernel, (place, keep, got, basis_second), (whole,), flat)
-    (part,) = call(first_image_kernel, (place, image_keep, image_got, high, low), (whole,), flat)
-    noise, image, back_send = call(
-        noise_image_kernel,
-        (place, part, z_field, basis_second, *noise),
-        (whole, whole, piece),
-        None,
-    )
-    (back_keep,) = call(keep_kernel, (place, image, basis_second), (piece,), None)
+    inputs = (place, image_keep, image_got, high, low, z_field)
+    image, noise = call(
+        first_image_kernel,
+        (*inputs, *(in_hbm(value) for value in noise)),
+        (whole, whole),
+        flat,
+        [smem]
+        + [full(*value.shape) for value in inputs[1:]]
+        + [pl.BlockSpec(memory_space=pltpu.HBM)] * len(noise),
+        [pltpu.SemaphoreType.DMA((len(noise),))],
+    )
+
+    def give_back(whose):
+        kernel = functools.partial(return_kernel, whose)
+        return call(kernel, (place, image, basis_second), (piece,), None)[0]
+
+    back_send = give_back(1)
+    back_keep = give_back(0)
     back_got = swap(back_send)
 
     column, keep, send, sum_two = call(

time: 269 us -> 275 us (1.022)
  waiting for transfers between devices: 67.7 us -> 71.4 us
    ppermute x4, waiting for transfers between devices: 14 us -> 18.1 us  [paired_body(): far = [lax.ppermute(value, 'mode', sample_swap) for value in near]]
    unnamed x34 -> x46, local copies, waits for them, and re-layouts: 7.27 us -> 7.95 us
  transfers between devices with their start and end apart: 18 -> 18, of which waited for: 6 -> 7; matrix products, arithmetic and copies ran while one was open for 0% -> 0% of each run, Pallas kernels for 9% -> 8%
where the time goes in v7:
time: 275 us; the launch traced here: 274 us
  blocking collectives  108 us (39%)
  waiting for transfers between devices  71.4 us (26%)
  Pallas kernels  56.7 us (21%)
  starting transfers between devices  29 us (11%)
  local copies, waits for them, and re-layouts  7.95 us (3%)
    all_to_all x1, blocking collectives, paired_body(): lax.all_to_all(answer, 'mode', split_axis=0, concat_axis=0, axis_index_gr...  95.8 us
    ppermute x3, waiting for transfers between devices, plane_shift(): return lax.ppermute(value, 'mode', pairs)  50.4 us
    pallas_call x10, Pallas kernels, call(): pl.pallas_call(kernel, grid=(1,), in_specs=specs or [smem] + [full(*value...  38.8 us
    ppermute x4, waiting for transfers between devices, paired_body(): far = [lax.ppermute(value, 'mode', sample_swap) for value in near]  18.1 us
    all_to_all x1, blocking collectives, paired_body(): sums = lax.all_to_all(sums, 'mode', split_axis=0, concat_axis=0, tiled=True)  12.2 us
    unnamed x46, local copies, waits for them, and re-layouts  7.95 us
    ppermute x3, starting transfers between devices, paired_body(): lax.ppermute(eigen, 'mode', [(at, (at + by * unit) % groups) for at in ra...  7.67 us
    all_to_all x1, starting transfers between devices, paired_body(): lax.all_to_all(outgoing.reshape(groups, rows, half), 'mode', split_axis=0...  7.6 us
  transfers between devices with their start and end apart: 18, of which 7 were waited for; matrix products, arithmetic and copies ran while one was open for 0% of the time, Pallas kernels for 8%

profile of v7, /device:TPU:0, one launch (start us, length us, event | category | flops | bytes accessed | tf_op | source)
XLA Modules:
  0.0 274.2 jit_solution(5564950836117563737)
XLA Ops:
  0.6 6.0 %outgoing.1 = f32[4,2,2,64,512]{4,3,2,1,0:T(8,128)} custom-call(f32[2,4,64,1024]{3,2,1,0:T(8,128)} %right_ref.3, bf16[1024,1024]{1,0:T(8,128)(2,1)} %basis_ref.11), custom_call_target="tpu_custom_call" | custom-call | tf_op jit(solution)/shard_map/outgoing/pallas_call | solution.py:467
  6.7 7.6 %all-to-all-start = ((f32[16,64,512]{2,1,0:T(8,128)}), f32[16,64,512]{2,1,0:T(8,128)}, u32[]{:S(2)}, u32[]{:S(2)}) async-start(f32[16,64,512]{2,1,0:T(8,128)} %bitcast.10), calls=%async_computation | async-start | bytes 4194304 | tf_op jit(solution)/shard_map/all_to_all | solution.py:479
  14.7 2.6 shard_map.105
  17.3 2.6 collective-permute-start.3
  19.9 2.8 %shard_map.104 = (f32[64,1024]{1,0:T(8,128)}, f32[64,1024]{1,0:T(8,128)}, f32[64,1024]{1,0:T(8,128)}) custom-call(f32[8]{0:T(128)} %table_ref.5, s32[4,64,1024]{2,1,0:T(8,128)} %class_hbm.3), custom_call_target="tpu_custom_call" | custom-call | tf_op jit(solution)/shard_map/pallas_call | solution.py:440
  22.7 1.5 collective-permute-start.2
  24.2 2.4 collective-permute-start.4
  28.2 2.0 collective-permute-done.1
  30.3 50.4 %collective-permute-done.3.refs_1_.refs_2_ = f32[64,1024]{1,0:T(8,128)S(1)} collective-permute-done((f32[64,1024]{1,0:T(8,128)}, f32[64,1024]{1,0:T(8,128)S(1)}, u32[]{:S(2)}, u32[]{:S(2)}) %collective-permute-start.3) | collective-permute-done | bytes 262176 | tf_op jit(solution)/shard_map/ppermute | solution.py:455
  80.7 1.5 collective-permute-start.7
  82.2 5.5 %collective-permute-start.6 = (f32[1,256]{1,0:T(1,128)S(1)}, f32[1,256]{1,0:T(1,128)S(1)}, u32[]{:S(2)}, u32[]{:S(2)}) collective-permute-start(f32[1,256]{1,0:T(1,128)S(1)} %follow.1._.refs_0_), channel_id=1, source_target_pairs={{0,8},{1,9},{2,10},{3,11},{4,12},{5,13},{6,14},{7,15},{8,0},{9,1},... | collective-permute-start | bytes 3080 | tf_op jit(solution)/shard_map/ppermute | solution.py:502
  88.5 1.6 copy-done.1
  90.0 1.6 copy-done.11
  91.6 2.4 prepare.1
  98.1 7.6 %shard_map.106 = (f32[1024,512]{1,0:T(8,128)S(1)}, f32[1024,512]{1,0:T(8,128)S(1)}, f32[1024,512]{1,0:T(8,128)S(1)}, f32[8,64,512]{2,1,0:T(8,128)S(1)}, f32[8,64,512]{2,1,0:T(8,128)S(1)}, /*index=5*/f32[8,128]{1,0:T(8,128)S(1)}) custom-call(s32[3]{0:T(128)S(1)} %pad_add_fusion.place_ref, f32[8]{0:T(128)S(1)} %copy-done.15, ...), custom_call_target="tpu_custom_call" | custom-call | tf_op jit(solution)/shard_map/pallas_call | solution.py:521
  105.8 3.0 %shard_map.107 = (f32[8,64,512]{2,1,0:T(8,128)S(1)}, f32[8,64,512]{2,1,0:T(8,128)S(1)}) custom-call(s32[3]{0:T(128)S(1)} %pad_add_fusion.place_ref, f32[1024,512]{1,0:T(8,128)S(1)} %get-tuple-element.31.column_ref, bf16[1024,1024]{1,0:T(8,128)(2,1)S(1)} %copy-done.4), custom_call_target="tpu_custom_call" | custom-call | tf_op jit(solution)/shard_map/pallas_call | solution.py:521
  109.4 1.5 collective-permute-start.10
  113.4 3.0 %shard_map.108.z_ref = f32[8,64,1024]{2,1,0:T(8,128)S(1)} custom-call(s32[3]{0:T(128)S(1)} %pad_add_fusion.place_ref, f32[8,64,512]{2,1,0:T(8,128)S(1)} %get-tuple-element.36.keep_ref, f32[8,64,512]{2,1,0:T(8,128)S(1)} %collective-permute-done.9.got_ref, bf16[1024,1024]{1,0:T(8,128)(2,1)S(1)} %copy-done), custom_call_target="tpu_custom_call" | custom-call | tf_op jit(solution)/shard_map/pallas_call | solution.py:521
  116.4 2.1 collective-permute-done.10.refs_4_
  118.5 5.6 %collective-permute-done.12.refs_6_ = f32[64,1024]{1,0:T(8,128)S(1)} collective-permute-done((f32[64,1024]{1,0:T(8,128)S(1)}, f32[64,1024]{1,0:T(8,128)S(1)}, u32[]{:S(2)}, u32[]{:S(2)}) %collective-permute-start.12) | collective-permute-done | bytes 262176 | tf_op jit(solution)/shard_map/ppermute | solution.py:464
  124.2 5.6 %collective-permute-done.11.refs_5_ = f32[64,1024]{1,0:T(8,128)S(1)} collective-permute-done((f32[64,1024]{1,0:T(8,128)S(1)}, f32[64,1024]{1,0:T(8,128)S(1)}, u32[]{:S(2)}, u32[]{:S(2)}) %collective-permute-start.11) | collective-permute-done | bytes 262176 | tf_op jit(solution)/shard_map/ppermute | solution.py:464
  129.8 4.7 %collective-permute-done.13.refs_7_ = f32[64,1024]{1,0:T(8,128)S(1)} collective-permute-done((f32[64,1024]{1,0:T(8,128)S(1)}, f32[64,1024]{1,0:T(8,128)S(1)}, u32[]{:S(2)}, u32[]{:S(2)}) %collective-permute-start.13) | collective-permute-done | bytes 262176 | tf_op jit(solution)/shard_map/ppermute | solution.py:464
  135.2 5.9 %shard_map.109 = (f32[8,64,1024]{2,1,0:T(8,128)S(1)}, f32[8,64,1024]{2,1,0:T(8,128)S(1)}) custom-call(s32[3]{0:T(128)S(1)} %pad_add_fusion.place_ref, f32[8,64,512]{2,1,0:T(8,128)S(1)} %get-tuple-element.32.keep_ref, f32[8,64,512]{2,1,0:T(8,128)S(1)} %collective-permute-done.8.got_ref, bf16[1024,1024]{1,0:T(8,128)(2,1)S(1)} %copy-done.8, ...), custom_call_target="tpu_custom_call" | custom-call | tf_op jit(solution)/shard_map/pallas_call | solution.py:521
  141.1 1.8 shard_map.111
  143.0 1.8 shard_map.110.held_ref
  145.7 5.5 %shard_map.112 = (f32[1024,512]{1,0:T(8,128)S(1)}, f32[8,64,512]{2,1,0:T(8,128)S(1)}, f32[8,64,512]{2,1,0:T(8,128)S(1)}, f32[8,128]{1,0:T(8,128)S(1)}) custom-call(s32[3]{0:T(128)S(1)} %pad_add_fusion.place_ref, f32[8,64,512]{2,1,0:T(8,128)S(1)} %shard_map.110.held_ref, f32[8,64,512]{2,1,0:T(8,128)S(1)} %collective-permute-done.14.got_ref, ...), custom_call_target="tpu_custom_call" | custom-call | tf_op jit(solution)/shard_map/pallas_call | solution.py:521
  151.4 3.0 %shard_map.113 = (f32[8,64,512]{2,1,0:T(8,128)S(1)}, f32[8,64,512]{2,1,0:T(8,128)S(1)}) custom-call(s32[3]{0:T(128)S(1)} %pad_add_fusion.place_ref, f32[1024,512]{1,0:T(8,128)S(1)} %get-tuple-element.42.column_ref, bf16[1024,1024]{1,0:T(8,128)(2,1)S(1)} %copy-done.4), custom_call_target="tpu_custom_call" | custom-call | tf_op jit(solution)/shard_map/pallas_call | solution.py:521
  154.9 3.0 %shard_map.114.z_ref.f_ref = f32[8,64,1024]{2,1,0:T(8,128)S(1)} custom-call(s32[3]{0:T(128)S(1)} %pad_add_fusion.place_ref, f32[8,64,512]{2,1,0:T(8,128)S(1)} %get-tuple-element.45.keep_ref, f32[8,64,512]{2,1,0:T(8,128)S(1)} %collective-permute-done.16.got_ref, bf16[1024,1024]{1,0:T(8,128)(2,1)S(1)} %copy-done), custom_call_target="tpu_custom_call" | custom-call | tf_op jit(solution)/shard_map/pallas_call | solution.py:521
  157.9 4.2 %shard_map.115 = (f32[8,64,1024]{2,1,0:T(8,128)S(1)}, f32[16,8,128]{2,1,0:T(8,128)S(1)}) custom-call(s32[3]{0:T(128)S(1)} %pad_add_fusion.place_ref, f32[8,64,512]{2,1,0:T(8,128)S(1)} %get-tuple-element.43.keep_ref, f32[8,64,512]{2,1,0:T(8,128)S(1)} %collective-permute-done.15.got_ref, f32[8,64,1024]{2,1,0:T(8,128)S(1)} %shard_map.114.z_ref.f_ref, ...), custom_call_target="tpu_custom_call" | custom-call | tf_op jit(solution)/shard_map/pallas_call | solution.py:521
  162.1 12.2 %all_to_all.15.sum_ref = f32[16,8,128]{2,1,0:T(8,128)S(1)} all-to-all(f32[16,8,128]{2,1,0:T(8,128)S(1)} %get-tuple-element.50), channel_id=1, replica_groups=mesh['blocks'=2,'mode'=16] {'mode'}, dimensions={0} | all-to-all | bytes 131072 | tf_op jit(solution)/shard_map/all_to_all | solution.py:617
  175.8 95.8 %all_to_all.16.got_ref = f32[8,128,1024]{2,1,0:T(8,128)S(1)} all-to-all(f32[8,128,1024]{2,1,0:T(8,128)S(1)} %combine.1), channel_id=1, replica_groups={{0,2,4,6,8,10,12,14},{1,3,5,7,9,11,13,15},{16,18,20,22,24,26,28,30},{17..., dimensions={0} | all-to-all | bytes 8388608 | tf_op jit(solution)/shard_map/all_to_all | solution.py:630
  271.6 2.6 finish.1
  (73 shorter events, 13.8 us)
Async XLA Ops:
  6.6 7.6 %copy-start.22 = (f32[64]{0:T(128)S(1)}, f32[64]{0:T(128)}, u32[]{:S(2)}) copy-start(f32[64]{0:T(128)} %param.17) | copy-start | bytes 772
  6.7 91.4 %all-to-all-start = ((f32[16,64,512]{2,1,0:T(8,128)}), f32[16,64,512]{2,1,0:T(8,128)}, u32[]{:S(2)}, u32[]{:S(2)}) async-start(f32[16,64,512]{2,1,0:T(8,128)} %bitcast.10), calls=%async_computation | async-start | bytes 4194304 | tf_op jit(solution)/shard_map/all_to_all | solution.py:479
  14.3 74.2 %copy-start = (bf16[1024,1024]{1,0:T(8,128)(2,1)S(1)}, bf16[1024,1024]{1,0:T(8,128)(2,1)}, u32[]{:S(2)}) copy-start(bf16[1024,1024]{1,0:T(8,128)(2,1)} %basis_ref.11) | copy-start | bytes 6291460
  14.3 74.2 %copy-start.16 = (f32[1024]{0:T(1024)S(1)}, f32[1024]{0:T(1024)}, u32[]{:S(2)}) copy-start(f32[1024]{0:T(1024)} %param.16) | copy-start | bytes 12292
  14.3 12.3 %collective-permute-start = (f32[1,64]{1,0:T(1,128)S(1)}, f32[1,64]{1,0:T(1,128)S(1)}, u32[]{:S(2)}, u32[]{:S(2)}) collective-permute-start(f32[1,64]{1,0:T(1,128)S(1)} %bitcast.11), channel_id=1, source_target_pairs={{0,1},{1,0},{2,3},{3,2},{4,5},{5,4},{6,7},{7,6},{8,9},{9,8},{10,11... | collective-permute-start | bytes 776 | tf_op jit(solution)/shard_map/ppermute | solution.py:485
  17.3 63.4 %collective-permute-start.3 = (f32[64,1024]{1,0:T(8,128)}, f32[64,1024]{1,0:T(8,128)S(1)}, u32[]{:S(2)}, u32[]{:S(2)}) collective-permute-start(f32[64,1024]{1,0:T(8,128)} %shard_map.105), channel_id=1, source_target_pairs={{0,8},{1,9},{2,10},{3,11},{4,12},{5,13},{6,14},{7,15},{8,0},{9,1},... | collective-permute-start | bytes 786440 | tf_op jit(solution)/shard_map/ppermute | solution.py:455
  22.7 57.9 %collective-permute-start.2 = (f32[64,1024]{1,0:T(8,128)}, f32[64,1024]{1,0:T(8,128)S(1)}, u32[]{:S(2)}, u32[]{:S(2)}) collective-permute-start(f32[64,1024]{1,0:T(8,128)} %get-tuple-element.27), channel_id=1, source_target_pairs={{0,4},{1,5},{2,6},{3,7},{4,8},{5,9},{6,10},{7,11},{8,12},{9,13},{1... | collective-permute-start | bytes 786440 | tf_op jit(solution)/shard_map/ppermute | solution.py:455
  24.2 56.4 %collective-permute-start.4 = (f32[64,1024]{1,0:T(8,128)}, f32[64,1024]{1,0:T(8,128)S(1)}, u32[]{:S(2)}, u32[]{:S(2)}) collective-permute-start(f32[64,1024]{1,0:T(8,128)} %get-tuple-element.28), channel_id=1, source_target_pairs={{0,12},{1,13},{2,14},{3,15},{4,0},{5,1},{6,2},{7,3},{8,4},{9,5},{1... | collective-permute-start | bytes 786440 | tf_op jit(solution)/shard_map/ppermute | solution.py:455
  26.7 3.6 %collective-permute-start.1 = (f32[1,128]{1,0:T(1,128)S(1)}, f32[1,128]{1,0:T(1,128)S(1)}, u32[]{:S(2)}, u32[]{:S(2)}) collective-permute-start(f32[1,128]{1,0:T(1,128)S(1)} %broadcast_select_fusion.1), channel_id=1, source_target_pairs={{0,2},{1,3},{2,0},{3,1},{4,6},{5,7},{6,4},{7,5},{8,10},{9,11},{10,... | collective-permute-start | bytes 1544 | tf_op jit(solution)/shard_map/ppermute | solution.py:485
  80.7 30.2 %copy-start.12 = (f32[64,1024]{1,0:T(8,128)}, f32[64,1024]{1,0:T(8,128)S(1)}, u32[]{:S(2)}) copy-start(f32[64,1024]{1,0:T(8,128)S(1)} %collective-permute-done.3.refs_1_.refs_2_) | copy-start | bytes 786436
  80.7 30.7 %copy-start.13 = (f32[64,1024]{1,0:T(8,128)}, f32[64,1024]{1,0:T(8,128)S(1)}, u32[]{:S(2)}) copy-start(f32[64,1024]{1,0:T(8,128)S(1)} %collective-permute-done.2.refs_0_.refs_1_) | copy-start | bytes 786436
  80.7 32.2 %copy-start.14 = (f32[64,1024]{1,0:T(8,128)}, f32[64,1024]{1,0:T(8,128)S(1)}, u32[]{:S(2)}) copy-start(f32[64,1024]{1,0:T(8,128)S(1)} %collective-permute-done.4.refs_2_.refs_3_) | copy-start | bytes 786436
  80.7 17.3 %collective-permute-start.7 = (f32[1,256]{1,0:T(1,128)S(1)}, f32[1,256]{1,0:T(1,128)S(1)}, u32[]{:S(2)}, u32[]{:S(2)}) collective-permute-start(f32[1,256]{1,0:T(1,128)S(1)} %follow.1._.refs_0_), channel_id=1, source_target_pairs={{0,12},{1,13},{2,14},{3,15},{4,0},{5,1},{6,2},{7,3},{8,4},{9,5},{1... | collective-permute-start | bytes 3080 | tf_op jit(solution)/shard_map/ppermute | solution.py:502
  82.2 15.8 %collective-permute-start.6 = (f32[1,256]{1,0:T(1,128)S(1)}, f32[1,256]{1,0:T(1,128)S(1)}, u32[]{:S(2)}, u32[]{:S(2)}) collective-permute-start(f32[1,256]{1,0:T(1,128)S(1)} %follow.1._.refs_0_), channel_id=1, source_target_pairs={{0,8},{1,9},{2,10},{3,11},{4,12},{5,13},{6,14},{7,15},{8,0},{9,1},... | collective-permute-start | bytes 3080 | tf_op jit(solution)/shard_map/ppermute | solution.py:502
  87.7 10.3 %collective-permute-start.5 = (f32[1,256]{1,0:T(1,128)S(1)}, f32[1,256]{1,0:T(1,128)S(1)}, u32[]{:S(2)}, u32[]{:S(2)}) collective-permute-start(f32[1,256]{1,0:T(1,128)S(1)} %follow.1._.refs_0_), channel_id=1, source_target_pairs={{0,4},{1,5},{2,6},{3,7},{4,8},{5,9},{6,10},{7,11},{8,12},{9,13},{1... | collective-permute-start | bytes 3080 | tf_op jit(solution)/shard_map/ppermute | solution.py:502
  91.6 6.4 %copy-start.15 = (f32[8]{0:T(128)S(1)}, f32[8]{0:T(128)}, u32[]{:S(2)}) copy-start(f32[8]{0:T(128)} %table_ref.5) | copy-start | bytes 100
  98.1 7.7 %copy-start.4 = (bf16[1024,1024]{1,0:T(8,128)(2,1)S(1)}, bf16[1024,1024]{1,0:T(8,128)(2,1)}, u32[]{:S(2)}) copy-start(bf16[1024,1024]{1,0:T(8,128)(2,1)} %kernel_ref.5) | copy-start | bytes 6291460
  105.7 7.2 %collective-permute-start.9 = (f32[8,64,512]{2,1,0:T(8,128)S(1)}, f32[8,64,512]{2,1,0:T(8,128)S(1)}, u32[]{:S(2)}, u32[]{:S(2)}) collective-permute-start(f32[8,64,512]{2,1,0:T(8,128)S(1)} %get-tuple-element.37), channel_id=1, source_target_pairs={{0,1},{1,0},{2,3},{3,2},{4,5},{5,4},{6,7},{7,6},{8,9},{9,8},{10,11... | collective-permute-start | bytes 3145736 | tf_op jit(solution)/shard_map/ppermute | solution.py:518
  108.8 25.7 %collective-permute-start.8 = (f32[8,64,512]{2,1,0:T(8,128)S(1)}, f32[8,64,512]{2,1,0:T(8,128)S(1)}, u32[]{:S(2)}, u32[]{:S(2)}) collective-permute-start(f32[8,64,512]{2,1,0:T(8,128)S(1)} %get-tuple-element.33), channel_id=1, source_target_pairs={{0,1},{1,0},{2,3},{3,2},{4,5},{5,4},{6,7},{7,6},{8,9},{9,8},{10,11... | collective-permute-start | bytes 3145736 | tf_op jit(solution)/shard_map/ppermute | solution.py:518
  109.4 9.2 %collective-permute-start.10 = (f32[64,1024]{1,0:T(8,128)S(1)}, f32[64,1024]{1,0:T(8,128)S(1)}, u32[]{:S(2)}, u32[]{:S(2)}) collective-permute-start(f32[64,1024]{1,0:T(8,128)S(1)} %copy-done.17), channel_id=1, source_target_pairs={{0,2},{1,3},{2,0},{3,1},{4,6},{5,7},{6,4},{7,5},{8,10},{9,11},{10,... | collective-permute-start | bytes 786440 | tf_op jit(solution)/shard_map/ppermute | solution.py:464
  110.8 13.3 %collective-permute-start.12 = (f32[64,1024]{1,0:T(8,128)S(1)}, f32[64,1024]{1,0:T(8,128)S(1)}, u32[]{:S(2)}, u32[]{:S(2)}) collective-permute-start(f32[64,1024]{1,0:T(8,128)S(1)} %collective-permute-done.3.refs_1_.refs_2_), channel_id=1, source_target_pairs={{0,2},{1,3},{2,0},{3,1},{4,6},{5,7},{6,4},{7,5},{8,10},{9,11},{10,... | collective-permute-start | bytes 786440 | tf_op jit(solution)/shard_map/ppermute | solution.py:464
  111.4 18.4 %collective-permute-start.11 = (f32[64,1024]{1,0:T(8,128)S(1)}, f32[64,1024]{1,0:T(8,128)S(1)}, u32[]{:S(2)}, u32[]{:S(2)}) collective-permute-start(f32[64,1024]{1,0:T(8,128)S(1)} %collective-permute-done.2.refs_0_.refs_1_), channel_id=1, source_target_pairs={{0,2},{1,3},{2,0},{3,1},{4,6},{5,7},{6,4},{7,5},{8,10},{9,11},{10,... | collective-permute-start | bytes 786440 | tf_op jit(solution)/shard_map/ppermute | solution.py:464
  112.9 21.6 %collective-permute-start.13 = (f32[64,1024]{1,0:T(8,128)S(1)}, f32[64,1024]{1,0:T(8,128)S(1)}, u32[]{:S(2)}, u32[]{:S(2)}) collective-permute-start(f32[64,1024]{1,0:T(8,128)S(1)} %collective-permute-done.4.refs_2_.refs_3_), channel_id=1, source_target_pairs={{0,2},{1,3},{2,0},{3,1},{4,6},{5,7},{6,4},{7,5},{8,10},{9,11},{10,... | collective-permute-start | bytes 786440 | tf_op jit(solution)/shard_map/ppermute | solution.py:464
  113.4 21.8 %copy-start.8 = (bf16[1024,1024]{1,0:T(8,128)(2,1)S(1)}, bf16[1024,1024]{1,0:T(8,128)(2,1)}, u32[]{:S(2)}) copy-start(bf16[1024,1024]{1,0:T(8,128)(2,1)} %copy-done.7) | copy-start | bytes 6291460
  113.4 21.8 %copy-start.10 = (bf16[1024,1024]{1,0:T(8,128)(2,1)S(1)}, bf16[1024,1024]{1,0:T(8,128)(2,1)}, u32[]{:S(2)}) copy-start(bf16[1024,1024]{1,0:T(8,128)(2,1)} %copy-done.9) | copy-start | bytes 6291460
  118.5 16.0 %copy-start.18 = (f32[64,1024]{1,0:T(8,128)}, f32[64,1024]{1,0:T(8,128)S(1)}, u32[]{:S(2)}) copy-start(f32[64,1024]{1,0:T(8,128)S(1)} %collective-permute-done.10.refs_4_) | copy-start | bytes 786436
  124.2 10.4 %copy-start.19 = (f32[64,1024]{1,0:T(8,128)}, f32[64,1024]{1,0:T(8,128)S(1)}, u32[]{:S(2)}) copy-start(f32[64,1024]{1,0:T(8,128)S(1)} %collective-permute-done.12.refs_6_) | copy-start | bytes 786436
  129.8 4.8 %copy-start.20 = (f32[64,1024]{1,0:T(8,128)}, f32[64,1024]{1,0:T(8,128)S(1)}, u32[]{:S(2)}) copy-start(f32[64,1024]{1,0:T(8,128)S(1)} %collective-permute-done.11.refs_5_) | copy-start | bytes 786436
  142.9 2.7 collective-permute-start.14
  151.2 3.7 %collective-permute-start.16 = (f32[8,64,512]{2,1,0:T(8,128)S(1)}, f32[8,64,512]{2,1,0:T(8,128)S(1)}, u32[]{:S(2)}, u32[]{:S(2)}) collective-permute-start(f32[8,64,512]{2,1,0:T(8,128)S(1)} %get-tuple-element.46), channel_id=1, source_target_pairs={{0,1},{1,0},{2,3},{3,2},{4,5},{5,4},{6,7},{7,6},{8,9},{9,8},{10,11... | collective-permute-start | bytes 3145736 | tf_op jit(solution)/shard_map/ppermute | solution.py:518
  154.4 3.4 %collective-permute-start.15 = (f32[8,64,512]{2,1,0:T(8,128)S(1)}, f32[8,64,512]{2,1,0:T(8,128)S(1)}, u32[]{:S(2)}, u32[]{:S(2)}) collective-permute-start(f32[8,64,512]{2,1,0:T(8,128)S(1)} %get-tuple-element.44), channel_id=1, source_target_pairs={{0,1},{1,0},{2,3},{3,2},{4,5},{5,4},{6,7},{7,6},{8,9},{9,8},{10,11... | collective-permute-start | bytes 3145736 | tf_op jit(solution)/shard_map/ppermute | solution.py:518
  175.8 95.8 %copy-start.3 = (f32[2,4,64,1024]{3,2,1,0:T(8,128)S(1)}, f32[2,4,64,1024]{3,2,1,0:T(8,128)}, u32[]{:S(2)}) copy-start(f32[2,4,64,1024]{3,2,1,0:T(8,128)} %right_ref.3) | copy-start | bytes 6291460
  (9 other events, 17.0 us)

commit v8 on v7

--- a/solution.py
+++ b/solution.py
@@ -223,7 +223,7 @@
     *refs,
 ):
     wide_refs, refs, local = refs[:-11], refs[-11:-4], refs[-4:]
-    spectral_ref, weight_ref, column_ref, keep_ref, send_ref, sum_ref, scratch_ref = refs
+    start_ref, weight_ref, column_ref, keep_ref, send_ref, sum_ref, scratch_ref = refs
     field_ref, turned_ref, basis_ref, done = local
     middle = turned_ref.shape[0] // 2
     upper, lower = pl.ds(0, middle), pl.ds(middle, middle)
@@ -240,7 +240,7 @@
     for copy in copies:
         copy.start()
     mean = functools.reduce(jnp.add, [table_ref[at] for at in range(NCLASS)]) * (1.0 / NCLASS)
-    height, width = spectral_ref.shape
+    height, width = start_ref.shape
     planes = len(wide_refs)
     part = wide_refs[0].shape[1]
     for block in range(width // part):
@@ -259,7 +259,7 @@
     copies[2].wait()
     spectral = jnp.concatenate([above, times_left(turned_ref[middle:], field)], axis=0)
     weighted = spectral * weight_ref[...]
-    spectral_ref[...] = spectral
+    start_ref[...] = field
     store_sums(sum_ref, [fold(spectral * weighted)])
     copies[3].wait()
     column = times_left(basis_ref[...], weighted)
@@ -271,10 +271,12 @@
     place_ref,
     held_ref,
     got_ref,
-    before_ref,
+    start_ref,
     weight_ref,
     turned_ref,
     basis_ref,
+    own_ref,
+    other_ref,
     column_ref,
     keep_ref,
     send_ref,
@@ -284,9 +286,14 @@
     core = place_ref[0]
     scratch_ref[:, core] = held_ref[...]
     scratch_ref[:, 1 - core] = got_ref[...]
-    spectral = times_left(turned_ref[...], scratch_ref[...].reshape(column_ref.shape))
+    total = jnp.sum(own_ref[...] + other_ref[...], axis=1, keepdims=True)
+    gamma, curvature = total[0:1], total[1:2]
+    proper = (gamma > 0) & (curvature > 0)
+    step = jnp.where(proper, gamma / jnp.where(proper, curvature, 1.0), 1.0)
+    field = start_ref[...] - step * scratch_ref[...].reshape(start_ref.shape)
+    spectral = times_left(turned_ref[...], field)
     weighted = spectral * weight_ref[...]
-    store_sums(sum_ref, [fold(before_ref[...] * weighted), fold(spectral * weighted)])
+    store_sums(sum_ref, [fold(spectral * weighted), jnp.broadcast_to(step, (1, 128))])
     column = times_left(basis_ref[...], weighted)
     column_ref[...] = column
     split_rows(place_ref, column, scratch_ref, keep_ref, send_ref)
@@ -320,10 +327,10 @@
     return result[: field.shape[0]] + (result[field.shape[0] :] + small)
 
 
-def first_image_kernel(place_ref, keep_ref, got_ref, high_ref, low_ref, z_ref, *refs):
-    parts, (image_ref, noise_ref, scratch_ref, done) = refs[:-4], refs[-4:]
+def first_row_kernel(place_ref, keep_ref, got_ref, basis_ref, *refs):
+    parts, (z_ref, noise_ref, scratch_ref, done) = refs[:-4], refs[-4:]
     planes = len(parts) // 2
-    samples = image_ref.shape[0] // planes
+    samples = z_ref.shape[0] // planes
     copies = []
     for by in range(planes):
         row = (place_ref[2] + planes - by) % planes
@@ -333,10 +340,34 @@
             copies.append(pltpu.make_async_copy(part, noise_ref.at[block], here))
     for copy in copies:
         copy.start()
-    image = row_image(place_ref, keep_ref, got_ref, high_ref, low_ref, scratch_ref)
+    row_kernel(place_ref, keep_ref, got_ref, basis_ref, z_ref, scratch_ref)
     for copy in copies:
         copy.wait()
-    image_ref[...] = image.reshape(image_ref.shape) + noise_ref[...] * z_ref[...]
+
+
+def full_image(place_ref, keep_ref, got_ref, z_ref, noise_ref, high_ref, low_ref, image_ref, scratch_ref):
+    image = row_image(place_ref, keep_ref, got_ref, high_ref, low_ref, scratch_ref)
+    field = z_ref[...].reshape(image.shape)
+    image = image + noise_ref[...].reshape(image.shape) * field
+    image_ref[...] = image.reshape(image_ref.shape)
+    return fold(field * image)
+
+
+def first_image_kernel(
+    place_ref,
+    keep_ref,
+    got_ref,
+    z_ref,
+    noise_ref,
+    high_ref,
+    low_ref,
+    one_ref,
+    image_ref,
+    sum_ref,
+    scratch_ref,
+):
+    refs = (place_ref, keep_ref, got_ref, z_ref, noise_ref, high_ref, low_ref)
+    store_sums(sum_ref, [one_ref[0:1], full_image(*refs, image_ref, scratch_ref)])
 
 
 def return_kernel(whose, place_ref, image_ref, basis_ref, out_ref):
@@ -359,30 +390,39 @@
     sum_ref,
     scratch_ref,
 ):
-    image = row_image(place_ref, keep_ref, got_ref, high_ref, low_ref, scratch_ref)
-    field = z_ref[...].reshape(image.shape)
-    image = image + noise_ref[...].reshape(image.shape) * field
-    image_ref[...] = image.reshape(image_ref.shape)
-    total = jnp.concatenate(
-        [one_ref[0:1], two_ref[0:2], fold(field * image), jnp.zeros((4, 128), F32)], axis=0
-    )
-    sum_ref[...] = jnp.broadcast_to(total[None], sum_ref.shape)
-
-
-def combine_kernel(sum_ref, z_ref, image_ref, f_ref, f_image_ref, out_ref):
-    total = jnp.sum(sum_ref[...], axis=0)
-    total = jnp.sum(total, axis=1, keepdims=True)
-    g00, g01, g11, h11 = (total[at : at + 1] for at in range(4))
-    alpha = g00 / g01
-    turn = alpha * g11 / g01
-    gamma = alpha * alpha * g11 - g00
-    curvature = alpha * alpha * h11 - turn * turn * g01
-    step = gamma / curvature
-    on_z = alpha + step * turn
-    on_f = -(alpha * step)
+    refs = (place_ref, keep_ref, got_ref, z_ref, noise_ref, high_ref, low_ref)
+    last = full_image(*refs, image_ref, scratch_ref)
+    rows = [one_ref[0:2], two_ref[0:1], last, two_ref[1:2], jnp.zeros((3, 128), F32)]
+    sum_ref[...] = jnp.broadcast_to(jnp.concatenate(rows, axis=0)[None], sum_ref.shape)
+
+
+def combine_kernel(place_ref, sum_ref, z_ref, image_ref, f_ref, f_image_ref, out_ref):
+    devices, kinds, lanes = sum_ref.shape
+    pairs = devices // 2
+    total = jnp.sum(sum_ref[...], axis=2, keepdims=True)
+    total = jnp.sum(total.reshape(pairs, 2, kinds, 1), axis=1)
+    g00, g01, g11, h11, step = (total[:, at : at + 1] for at in range(5))
+    step = step * (1.0 / (2 * lanes))
+
+    def over_pairs(value):
+        return jnp.sum(value, axis=0, keepdims=True)
+
+    gamma = over_pairs(g00)
+    alpha = gamma / over_pairs(g01)
+    theta = alpha / step
+    rest = 1.0 - theta
+    gamma_new = over_pairs(rest * rest * g00 + theta * theta * g11)
+    turn = rest + gamma_new / gamma
+    curvature = over_pairs(
+        turn * turn * g01 - 2.0 * theta * turn * g11 / step + theta * theta * h11
+    )
+    alpha_new = gamma_new / curvature
+    own = lax.broadcasted_iota(jnp.int32, theta.shape, 0) == place_ref[3]
+    on_z = over_pairs(jnp.where(own, alpha + alpha_new * turn, 0.0))
+    on_f = over_pairs(jnp.where(own, alpha_new * theta, 0.0))
     share = z_ref.shape[1]
-    out_ref[:, :share, :] = on_z[None] * z_ref[...] + on_f[None] * f_ref[...]
-    out_ref[:, share:, :] = on_z[None] * image_ref[...] + on_f[None] * f_image_ref[...]
+    out_ref[:, :share, :] = on_z * z_ref[...] + on_f * f_ref[...]
+    out_ref[:, share:, :] = on_z * image_ref[...] + on_f * f_image_ref[...]
 
 
 def finish_kernel(got_ref, right_ref, solution_ref, residual_ref):
@@ -415,7 +455,7 @@
     core = index % cores
     sample = (index // cores) % samples
     plane = index // unit
-    place = jnp.stack([core, sample, plane]).astype(jnp.int32)
+    place = jnp.stack([core, sample, plane, index // cores]).astype(jnp.int32)
 
     def shape_of(*shape):
         return jax.ShapeDtypeStruct(shape, F32)
@@ -447,7 +487,7 @@
                 pltpu.VMEM((len(shifts), rows, width), jnp.int32),
                 pltpu.SemaphoreType.DMA((len(shifts),)),
             ],
-            compiler_params=params(1, 56),
+            compiler_params=params(1, 4),
         )(noise_table, in_hbm(classes))
 
     def plane_shift(value, by):
@@ -535,7 +575,7 @@
     flat = (blocks * rows, width)
     sums_shape = (8, 128)
 
-    spectral, weights, column, keep, send, sum_one = call(
+    start, weights, column, keep, send, sum_one = call(
         first_column_kernel,
         (
             place,
@@ -565,10 +605,9 @@
         column_image_kernel, (place, column, kernel_first), (piece, piece), by_rows
     )
     image_got = swap(image_send)
-    (z_field,) = call(row_kernel, (place, keep, got, basis_second), (whole,), flat)
-    inputs = (place, image_keep, image_got, high, low, z_field)
-    image, noise = call(
-        first_image_kernel,
+    inputs = (place, keep, got, basis_second)
+    z_field, noise = call(
+        first_row_kernel,
         (*inputs, *(in_hbm(value) for value in noise)),
         (whole, whole),
         flat,
@@ -577,6 +616,13 @@
         + [pl.BlockSpec(memory_space=pltpu.HBM)] * len(noise),
         [pltpu.SemaphoreType.DMA((len(noise),))],
     )
+    image, pair_sum = call(
+        first_image_kernel,
+        (place, image_keep, image_got, z_field, noise, high, low, sum_one),
+        (whole, sums_shape),
+        flat,
+    )
+    pair_other = swap(pair_sum)
 
     def give_back(whose):
         kernel = functools.partial(return_kernel, whose)
@@ -588,7 +634,17 @@
 
     column, keep, send, sum_two = call(
         next_column_kernel,
-        (place, back_keep, back_got, spectral, weights, turned, basis_first),
+        (
+            place,
+            back_keep,
+            back_got,
+            start,
+            weights,
+            turned,
+            basis_first,
+            pair_sum,
+            pair_other,
+        ),
         (tile, piece, piece, sums_shape),
         by_rows,
     )
@@ -608,7 +664,7 @@
             noise,
             high,
             low,
-            sum_one,
+            pair_sum,
             sum_two,
         ),
         (whole, (groups, 8, 128)),
@@ -621,12 +677,12 @@
     answer = pl.pallas_call(
         combine_kernel,
         grid=(4,),
-        in_specs=[full(groups, 8, 128)] + [few_spec] * 4,
+        in_specs=[smem, full(groups, 8, 128)] + [few_spec] * 4,
         out_specs=pl.BlockSpec((few, 2 * rows, width), lambda i: (i, 0, 0)),
         out_shape=shape_of(blocks, 2 * rows, width),
         compiler_params=params(1, 6),
         name="combine",
-    )(sums, z_field, image, f_field, f_image)
+    )(place, sums, z_field, image, f_field, f_image)
     answer = lax.all_to_all(
         answer,
         "mode",

time: 275 us -> 278 us (1.011)
    unnamed x46 -> x48, local copies, waits for them, and re-layouts: 7.95 us -> 8.66 us
  transfers between devices with their start and end apart: 18 -> 19, of which waited for: 7 -> 7; matrix products, arithmetic and copies ran while one was open for 0% -> 0% of each run, Pallas kernels for 8% -> 8%
where the time goes in v8:
time: 278 us
  blocking collectives  108 us (39%)
  waiting for transfers between devices  73.6 us (26%)
  Pallas kernels  55.9 us (20%)
  starting transfers between devices  30.3 us (11%)
  local copies, waits for them, and re-layouts  8.66 us (3%)
    all_to_all x1, blocking collectives, paired_body(): lax.all_to_all(answer, 'mode', split_axis=0, concat_axis=0, axis_index_gr...  95.8 us
    ppermute x3, waiting for transfers between devices, plane_shift(): return lax.ppermute(value, 'mode', pairs)  51 us
    pallas_call x10, Pallas kernels, call(): pl.pallas_call(kernel, grid=(1,), in_specs=specs or [smem] + [full(*value...  38.5 us
    ppermute x4, waiting for transfers between devices, paired_body(): far = [lax.ppermute(value, 'mode', sample_swap) for value in near]  20.2 us
    all_to_all x1, blocking collectives, paired_body(): sums = lax.all_to_all(sums, 'mode', split_axis=0, concat_axis=0, tiled=True)  12.2 us
    unnamed x48, local copies, waits for them, and re-layouts  8.66 us
    ppermute x3, starting transfers between devices, paired_body(): lax.ppermute(eigen, 'mode', [(at, (at + by * unit) % groups) for at in ra...  7.67 us
    all_to_all x1, starting transfers between devices, paired_body(): lax.all_to_all(outgoing.reshape(groups, rows, half), 'mode', split_axis=0...  7.6 us
  transfers between devices with their start and end apart: 19, of which 7 were waited for; matrix products, arithmetic and copies ran while one was open for 0% of the time, Pallas kernels for 8%

profile of v8, /device:TPU:0, one launch (start us, length us, event | category | flops | bytes accessed | tf_op | source)
XLA Modules:
  0.0 277.7 jit_solution(7617247903628860910)
XLA Ops:
  0.6 6.0 %outgoing.1 = f32[4,2,2,64,512]{4,3,2,1,0:T(8,128)} custom-call(f32[2,4,64,1024]{3,2,1,0:T(8,128)} %right_ref.3, bf16[1024,1024]{1,0:T(8,128)(2,1)} %basis_ref.11), custom_call_target="tpu_custom_call" | custom-call | tf_op jit(solution)/shard_map/outgoing/pallas_call | solution.py:507
  6.7 7.6 %all-to-all-start = ((f32[16,64,512]{2,1,0:T(8,128)}), f32[16,64,512]{2,1,0:T(8,128)}, u32[]{:S(2)}, u32[]{:S(2)}) async-start(f32[16,64,512]{2,1,0:T(8,128)} %bitcast.11), calls=%async_computation | async-start | bytes 4194304 | tf_op jit(solution)/shard_map/all_to_all | solution.py:519
  14.7 1.6 shard_map.105
  16.4 2.6 collective-permute-start.3
  19.0 2.5 shard_map.104
  23.6 2.4 collective-permute-start.4
  26.1 1.5 collective-permute-start.1
  27.6 2.0 collective-permute-done.1
  29.6 51.0 %collective-permute-done.3.refs_1_.refs_2_ = f32[64,1024]{1,0:T(8,128)S(1)} collective-permute-done((f32[64,1024]{1,0:T(8,128)S(1)}, f32[64,1024]{1,0:T(8,128)S(1)}, u32[]{:S(2)}, u32[]{:S(2)}) %collective-permute-start.3) | collective-permute-done | bytes 262176 | tf_op jit(solution)/shard_map/ppermute | solution.py:495
  80.7 1.5 collective-permute-start.7
  82.2 5.5 %collective-permute-start.6 = (f32[1,256]{1,0:T(1,128)S(1)}, f32[1,256]{1,0:T(1,128)S(1)}, u32[]{:S(2)}, u32[]{:S(2)}) collective-permute-start(f32[1,256]{1,0:T(1,128)S(1)} %follow.1._.refs_0_), channel_id=1, source_target_pairs={{0,8},{1,9},{2,10},{3,11},{4,12},{5,13},{6,14},{7,15},{8,0},{9,1},... | collective-permute-start | bytes 3080 | tf_op jit(solution)/shard_map/ppermute | solution.py:542
  88.5 1.6 copy-done.1
  90.0 1.6 copy-done.11
  91.6 2.4 prepare.1
  98.1 7.7 %shard_map.106 = (f32[1024,512]{1,0:T(8,128)S(1)}, f32[1024,512]{1,0:T(8,128)S(1)}, f32[1024,512]{1,0:T(8,128)S(1)}, f32[8,64,512]{2,1,0:T(8,128)S(1)}, f32[8,64,512]{2,1,0:T(8,128)S(1)}, /*index=5*/f32[8,128]{1,0:T(8,128)S(1)}) custom-call(s32[4]{0:T(128)S(1)} %pad_add_fusion.place_ref, f32[8]{0:T(128)S(1)} %copy-done.17, ...), custom_call_target="tpu_custom_call" | custom-call | tf_op jit(solution)/shard_map/pallas_call | solution.py:561
  105.9 3.0 %shard_map.107 = (f32[8,64,512]{2,1,0:T(8,128)S(1)}, f32[8,64,512]{2,1,0:T(8,128)S(1)}) custom-call(s32[4]{0:T(128)S(1)} %pad_add_fusion.place_ref, f32[1024,512]{1,0:T(8,128)S(1)} %get-tuple-element.33.column_ref, bf16[1024,1024]{1,0:T(8,128)(2,1)S(1)} %copy-done.4), custom_call_target="tpu_custom_call" | custom-call | tf_op jit(solution)/shard_map/pallas_call | solution.py:561
  113.0 5.7 %collective-permute-done.10.refs_4_ = f32[64,1024]{1,0:T(8,128)S(1)} collective-permute-done((f32[64,1024]{1,0:T(8,128)S(1)}, f32[64,1024]{1,0:T(8,128)S(1)}, u32[]{:S(2)}, u32[]{:S(2)}) %collective-permute-start.10) | collective-permute-done | bytes 262176 | tf_op jit(solution)/shard_map/ppermute | solution.py:504
  120.1 4.2 %collective-permute-done.12.refs_6_ = f32[64,1024]{1,0:T(8,128)S(1)} collective-permute-done((f32[64,1024]{1,0:T(8,128)S(1)}, f32[64,1024]{1,0:T(8,128)S(1)}, u32[]{:S(2)}, u32[]{:S(2)}) %collective-permute-start.12) | collective-permute-done | bytes 262176 | tf_op jit(solution)/shard_map/ppermute | solution.py:504
  124.3 5.6 %collective-permute-done.11.refs_5_ = f32[64,1024]{1,0:T(8,128)S(1)} collective-permute-done((f32[64,1024]{1,0:T(8,128)S(1)}, f32[64,1024]{1,0:T(8,128)S(1)}, u32[]{:S(2)}, u32[]{:S(2)}) %collective-permute-start.11) | collective-permute-done | bytes 262176 | tf_op jit(solution)/shard_map/ppermute | solution.py:504
  129.9 4.7 %collective-permute-done.13.refs_7_ = f32[64,1024]{1,0:T(8,128)S(1)} collective-permute-done((f32[64,1024]{1,0:T(8,128)S(1)}, f32[64,1024]{1,0:T(8,128)S(1)}, u32[]{:S(2)}, u32[]{:S(2)}) %collective-permute-start.13) | collective-permute-done | bytes 262176 | tf_op jit(solution)/shard_map/ppermute | solution.py:504
  135.3 4.1 %shard_map.108 = (f32[8,64,1024]{2,1,0:T(8,128)S(1)}, f32[8,64,1024]{2,1,0:T(8,128)S(1)}) custom-call(s32[4]{0:T(128)S(1)} %pad_add_fusion.place_ref, f32[8,64,512]{2,1,0:T(8,128)S(1)} %get-tuple-element.36.keep_ref, f32[8,64,512]{2,1,0:T(8,128)S(1)} %collective-permute-done.9.got_ref, bf16[1024,1024]{1,0:T(8,128)(2,1)S(1)} %copy-done, ...), custom_call_target="tpu_custom_call" | custom-call | tf_op jit(solution)/shard_map/pallas_call | solution.py:561
  139.5 4.4 %shard_map.109 = (f32[8,64,1024]{2,1,0:T(8,128)S(1)}, f32[8,128]{1,0:T(8,128)S(1)}) custom-call(s32[4]{0:T(128)S(1)} %pad_add_fusion.place_ref, f32[8,64,512]{2,1,0:T(8,128)S(1)} %get-tuple-element.34.keep_ref, f32[8,64,512]{2,1,0:T(8,128)S(1)} %collective-permute-done.8.got_ref, f32[8,64,1024]{2,1,0:T(8,128)S(1)} %get-tuple-element.39.z_ref, ...), custom_call_target="tpu_custom_call" | custom-call | tf_op jit(solution)/shard_map/pallas_call | solution.py:561
  143.9 1.8 shard_map.111
  146.3 1.8 shard_map.110.held_ref
  148.4 5.5 %shard_map.112 = (f32[1024,512]{1,0:T(8,128)S(1)}, f32[8,64,512]{2,1,0:T(8,128)S(1)}, f32[8,64,512]{2,1,0:T(8,128)S(1)}, f32[8,128]{1,0:T(8,128)S(1)}) custom-call(s32[4]{0:T(128)S(1)} %pad_add_fusion.place_ref, f32[8,64,512]{2,1,0:T(8,128)S(1)} %shard_map.110.held_ref, f32[8,64,512]{2,1,0:T(8,128)S(1)} %collective-permute-done.14.got_ref, ...), custom_call_target="tpu_custom_call" | custom-call | tf_op jit(solution)/shard_map/pallas_call | solution.py:561
  154.2 3.0 %shard_map.113 = (f32[8,64,512]{2,1,0:T(8,128)S(1)}, f32[8,64,512]{2,1,0:T(8,128)S(1)}) custom-call(s32[4]{0:T(128)S(1)} %pad_add_fusion.place_ref, f32[1024,512]{1,0:T(8,128)S(1)} %get-tuple-element.48.column_ref, bf16[1024,1024]{1,0:T(8,128)(2,1)S(1)} %copy-done.4), custom_call_target="tpu_custom_call" | custom-call | tf_op jit(solution)/shard_map/pallas_call | solution.py:561
  157.6 3.0 %shard_map.114.z_ref.f_ref = f32[8,64,1024]{2,1,0:T(8,128)S(1)} custom-call(s32[4]{0:T(128)S(1)} %pad_add_fusion.place_ref, f32[8,64,512]{2,1,0:T(8,128)S(1)} %get-tuple-element.51.keep_ref, f32[8,64,512]{2,1,0:T(8,128)S(1)} %collective-permute-done.17.got_ref, bf16[1024,1024]{1,0:T(8,128)(2,1)S(1)} %copy-done), custom_call_target="tpu_custom_call" | custom-call | tf_op jit(solution)/shard_map/pallas_call | solution.py:561
  160.6 4.2 %shard_map.115 = (f32[8,64,1024]{2,1,0:T(8,128)S(1)}, f32[16,8,128]{2,1,0:T(8,128)S(1)}) custom-call(s32[4]{0:T(128)S(1)} %pad_add_fusion.place_ref, f32[8,64,512]{2,1,0:T(8,128)S(1)} %get-tuple-element.49.keep_ref, f32[8,64,512]{2,1,0:T(8,128)S(1)} %collective-permute-done.16.got_ref, f32[8,64,1024]{2,1,0:T(8,128)S(1)} %shard_map.114.z_ref.f_ref, ...), custom_call_target="tpu_custom_call" | custom-call | tf_op jit(solution)/shard_map/pallas_call | solution.py:561
  164.9 12.2 %all_to_all.15.sum_ref = f32[16,8,128]{2,1,0:T(8,128)S(1)} all-to-all(f32[16,8,128]{2,1,0:T(8,128)S(1)} %get-tuple-element.54), channel_id=1, replica_groups=mesh['blocks'=2,'mode'=16] {'mode'}, dimensions={0} | all-to-all | bytes 131072 | tf_op jit(solution)/shard_map/all_to_all | solution.py:673
  177.1 2.2 combine.1
  179.3 95.8 %all_to_all.16.got_ref = f32[8,128,1024]{2,1,0:T(8,128)S(1)} all-to-all(f32[8,128,1024]{2,1,0:T(8,128)S(1)} %combine.1), channel_id=1, replica_groups={{0,2,4,6,8,10,12,14},{1,3,5,7,9,11,13,15},{16,18,20,22,24,26,28,30},{17..., dimensions={0} | all-to-all | bytes 8388608 | tf_op jit(solution)/shard_map/all_to_all | solution.py:686
  275.1 2.7 finish.1
  (77 shorter events, 15.4 us)
Async XLA Ops:
  6.6 7.6 %copy-start.23 = (f32[64]{0:T(128)S(1)}, f32[64]{0:T(128)}, u32[]{:S(2)}) copy-start(f32[64]{0:T(128)} %param.17) | copy-start | bytes 772
  6.7 8.1 %copy-start.17 = (f32[8]{0:T(128)S(1)}, f32[8]{0:T(128)}, u32[]{:S(2)}) copy-start(f32[8]{0:T(128)} %table_ref.5) | copy-start | bytes 100
  6.7 91.4 %all-to-all-start = ((f32[16,64,512]{2,1,0:T(8,128)}), f32[16,64,512]{2,1,0:T(8,128)}, u32[]{:S(2)}, u32[]{:S(2)}) async-start(f32[16,64,512]{2,1,0:T(8,128)} %bitcast.11), calls=%async_computation | async-start | bytes 4194304 | tf_op jit(solution)/shard_map/all_to_all | solution.py:519
  14.3 74.2 %copy-start = (bf16[1024,1024]{1,0:T(8,128)(2,1)S(1)}, bf16[1024,1024]{1,0:T(8,128)(2,1)}, u32[]{:S(2)}) copy-start(bf16[1024,1024]{1,0:T(8,128)(2,1)} %basis_ref.11) | copy-start | bytes 6291460
  14.3 74.2 %copy-start.18 = (f32[1024]{0:T(1024)S(1)}, f32[1024]{0:T(1024)}, u32[]{:S(2)}) copy-start(f32[1024]{0:T(1024)} %param.16) | copy-start | bytes 12292
  14.3 11.7 %collective-permute-start = (f32[1,64]{1,0:T(1,128)S(1)}, f32[1,64]{1,0:T(1,128)S(1)}, u32[]{:S(2)}, u32[]{:S(2)}) collective-permute-start(f32[1,64]{1,0:T(1,128)S(1)} %bitcast.12), channel_id=1, source_target_pairs={{0,1},{1,0},{2,3},{3,2},{4,5},{5,4},{6,7},{7,6},{8,9},{9,8},{10,11... | collective-permute-start | bytes 776 | tf_op jit(solution)/shard_map/ppermute | solution.py:525
  16.4 64.3 %collective-permute-start.3 = (f32[64,1024]{1,0:T(8,128)S(1)}, f32[64,1024]{1,0:T(8,128)S(1)}, u32[]{:S(2)}, u32[]{:S(2)}) collective-permute-start(f32[64,1024]{1,0:T(8,128)S(1)} %shard_map.105), channel_id=1, source_target_pairs={{0,8},{1,9},{2,10},{3,11},{4,12},{5,13},{6,14},{7,15},{8,0},{9,1},... | collective-permute-start | bytes 786440 | tf_op jit(solution)/shard_map/ppermute | solution.py:495
  22.2 58.5 %collective-permute-start.2 = (f32[64,1024]{1,0:T(8,128)}, f32[64,1024]{1,0:T(8,128)S(1)}, u32[]{:S(2)}, u32[]{:S(2)}) collective-permute-start(f32[64,1024]{1,0:T(8,128)} %get-tuple-element.29), channel_id=1, source_target_pairs={{0,4},{1,5},{2,6},{3,7},{4,8},{5,9},{6,10},{7,11},{8,12},{9,13},{1... | collective-permute-start | bytes 786440 | tf_op jit(solution)/shard_map/ppermute | solution.py:495
  23.6 57.0 %collective-permute-start.4 = (f32[64,1024]{1,0:T(8,128)S(1)}, f32[64,1024]{1,0:T(8,128)S(1)}, u32[]{:S(2)}, u32[]{:S(2)}) collective-permute-start(f32[64,1024]{1,0:T(8,128)S(1)} %get-tuple-element.30), channel_id=1, source_target_pairs={{0,12},{1,13},{2,14},{3,15},{4,0},{5,1},{6,2},{7,3},{8,4},{9,5},{1... | collective-permute-start | bytes 786440 | tf_op jit(solution)/shard_map/ppermute | solution.py:495
  26.1 3.6 %collective-permute-start.1 = (f32[1,128]{1,0:T(1,128)S(1)}, f32[1,128]{1,0:T(1,128)S(1)}, u32[]{:S(2)}, u32[]{:S(2)}) collective-permute-start(f32[1,128]{1,0:T(1,128)S(1)} %broadcast_select_fusion.1), channel_id=1, source_target_pairs={{0,2},{1,3},{2,0},{3,1},{4,6},{5,7},{6,4},{7,5},{8,10},{9,11},{10,... | collective-permute-start | bytes 1544 | tf_op jit(solution)/shard_map/ppermute | solution.py:525
  80.7 30.3 %copy-start.12 = (f32[64,1024]{1,0:T(8,128)}, f32[64,1024]{1,0:T(8,128)S(1)}, u32[]{:S(2)}) copy-start(f32[64,1024]{1,0:T(8,128)S(1)} %collective-permute-done.3.refs_1_.refs_2_) | copy-start | bytes 786436
  80.7 30.8 %copy-start.13 = (f32[64,1024]{1,0:T(8,128)}, f32[64,1024]{1,0:T(8,128)S(1)}, u32[]{:S(2)}) copy-start(f32[64,1024]{1,0:T(8,128)S(1)} %collective-permute-done.2.refs_0_.refs_1_) | copy-start | bytes 786436
  80.7 38.0 %copy-start.14 = (f32[64,1024]{1,0:T(8,128)}, f32[64,1024]{1,0:T(8,128)S(1)}, u32[]{:S(2)}) copy-start(f32[64,1024]{1,0:T(8,128)S(1)} %collective-permute-done.4.refs_2_.refs_3_) | copy-start | bytes 786436
  80.7 17.4 %collective-permute-start.7 = (f32[1,256]{1,0:T(1,128)S(1)}, f32[1,256]{1,0:T(1,128)S(1)}, u32[]{:S(2)}, u32[]{:S(2)}) collective-permute-start(f32[1,256]{1,0:T(1,128)S(1)} %follow.1._.refs_0_), channel_id=1, source_target_pairs={{0,12},{1,13},{2,14},{3,15},{4,0},{5,1},{6,2},{7,3},{8,4},{9,5},{1... | collective-permute-start | bytes 3080 | tf_op jit(solution)/shard_map/ppermute | solution.py:542
  82.2 15.9 %collective-permute-start.6 = (f32[1,256]{1,0:T(1,128)S(1)}, f32[1,256]{1,0:T(1,128)S(1)}, u32[]{:S(2)}, u32[]{:S(2)}) collective-permute-start(f32[1,256]{1,0:T(1,128)S(1)} %follow.1._.refs_0_), channel_id=1, source_target_pairs={{0,8},{1,9},{2,10},{3,11},{4,12},{5,13},{6,14},{7,15},{8,0},{9,1},... | collective-permute-start | bytes 3080 | tf_op jit(solution)/shard_map/ppermute | solution.py:542
  87.7 10.3 %collective-permute-start.5 = (f32[1,256]{1,0:T(1,128)S(1)}, f32[1,256]{1,0:T(1,128)S(1)}, u32[]{:S(2)}, u32[]{:S(2)}) collective-permute-start(f32[1,256]{1,0:T(1,128)S(1)} %follow.1._.refs_0_), channel_id=1, source_target_pairs={{0,4},{1,5},{2,6},{3,7},{4,8},{5,9},{6,10},{7,11},{8,12},{9,13},{1... | collective-permute-start | bytes 3080 | tf_op jit(solution)/shard_map/ppermute | solution.py:542
  98.1 7.8 %copy-start.4 = (bf16[1024,1024]{1,0:T(8,128)(2,1)S(1)}, bf16[1024,1024]{1,0:T(8,128)(2,1)}, u32[]{:S(2)}) copy-start(bf16[1024,1024]{1,0:T(8,128)(2,1)} %kernel_ref.5) | copy-start | bytes 6291460
  105.8 28.8 %collective-permute-start.9 = (f32[8,64,512]{2,1,0:T(8,128)S(1)}, f32[8,64,512]{2,1,0:T(8,128)S(1)}, u32[]{:S(2)}, u32[]{:S(2)}) collective-permute-start(f32[8,64,512]{2,1,0:T(8,128)S(1)} %get-tuple-element.37), channel_id=1, source_target_pairs={{0,1},{1,0},{2,3},{3,2},{4,5},{5,4},{6,7},{7,6},{8,9},{9,8},{10,11... | collective-permute-start | bytes 3145736 | tf_op jit(solution)/shard_map/ppermute | solution.py:558
  108.9 30.5 %collective-permute-start.8 = (f32[8,64,512]{2,1,0:T(8,128)S(1)}, f32[8,64,512]{2,1,0:T(8,128)S(1)}, u32[]{:S(2)}, u32[]{:S(2)}) collective-permute-start(f32[8,64,512]{2,1,0:T(8,128)S(1)} %get-tuple-element.35), channel_id=1, source_target_pairs={{0,1},{1,0},{2,3},{3,2},{4,5},{5,4},{6,7},{7,6},{8,9},{9,8},{10,11... | collective-permute-start | bytes 3145736 | tf_op jit(solution)/shard_map/ppermute | solution.py:558
  109.5 9.2 %collective-permute-start.10 = (f32[64,1024]{1,0:T(8,128)S(1)}, f32[64,1024]{1,0:T(8,128)S(1)}, u32[]{:S(2)}, u32[]{:S(2)}) collective-permute-start(f32[64,1024]{1,0:T(8,128)S(1)} %copy-done.16), channel_id=1, source_target_pairs={{0,2},{1,3},{2,0},{3,1},{4,6},{5,7},{6,4},{7,5},{8,10},{9,11},{10,... | collective-permute-start | bytes 786440 | tf_op jit(solution)/shard_map/ppermute | solution.py:504
  110.9 13.3 %collective-permute-start.12 = (f32[64,1024]{1,0:T(8,128)S(1)}, f32[64,1024]{1,0:T(8,128)S(1)}, u32[]{:S(2)}, u32[]{:S(2)}) collective-permute-start(f32[64,1024]{1,0:T(8,128)S(1)} %collective-permute-done.3.refs_1_.refs_2_), channel_id=1, source_target_pairs={{0,2},{1,3},{2,0},{3,1},{4,6},{5,7},{6,4},{7,5},{8,10},{9,11},{10,... | collective-permute-start | bytes 786440 | tf_op jit(solution)/shard_map/ppermute | solution.py:504
  111.5 18.4 %collective-permute-start.11 = (f32[64,1024]{1,0:T(8,128)S(1)}, f32[64,1024]{1,0:T(8,128)S(1)}, u32[]{:S(2)}, u32[]{:S(2)}) collective-permute-start(f32[64,1024]{1,0:T(8,128)S(1)} %collective-permute-done.2.refs_0_.refs_1_), channel_id=1, source_target_pairs={{0,2},{1,3},{2,0},{3,1},{4,6},{5,7},{6,4},{7,5},{8,10},{9,11},{10,... | collective-permute-start | bytes 786440 | tf_op jit(solution)/shard_map/ppermute | solution.py:504
  118.6 16.0 %copy-start.19 = (f32[64,1024]{1,0:T(8,128)}, f32[64,1024]{1,0:T(8,128)S(1)}, u32[]{:S(2)}) copy-start(f32[64,1024]{1,0:T(8,128)S(1)} %collective-permute-done.10.refs_4_) | copy-start | bytes 786436
  118.6 16.0 %collective-permute-start.13 = (f32[64,1024]{1,0:T(8,128)S(1)}, f32[64,1024]{1,0:T(8,128)S(1)}, u32[]{:S(2)}, u32[]{:S(2)}) collective-permute-start(f32[64,1024]{1,0:T(8,128)S(1)} %collective-permute-done.4.refs_2_.refs_3_), channel_id=1, source_target_pairs={{0,2},{1,3},{2,0},{3,1},{4,6},{5,7},{6,4},{7,5},{8,10},{9,11},{10,... | collective-permute-start | bytes 786440 | tf_op jit(solution)/shard_map/ppermute | solution.py:504
  124.3 10.4 %copy-start.20 = (f32[64,1024]{1,0:T(8,128)}, f32[64,1024]{1,0:T(8,128)S(1)}, u32[]{:S(2)}) copy-start(f32[64,1024]{1,0:T(8,128)S(1)} %collective-permute-done.12.refs_6_) | copy-start | bytes 786436
  129.9 4.8 %copy-start.21 = (f32[64,1024]{1,0:T(8,128)}, f32[64,1024]{1,0:T(8,128)S(1)}, u32[]{:S(2)}) copy-start(f32[64,1024]{1,0:T(8,128)S(1)} %collective-permute-done.11.refs_5_) | copy-start | bytes 786436
  135.3 4.1 %copy-start.8 = (bf16[1024,1024]{1,0:T(8,128)(2,1)S(1)}, bf16[1024,1024]{1,0:T(8,128)(2,1)}, u32[]{:S(2)}) copy-start(bf16[1024,1024]{1,0:T(8,128)(2,1)} %copy-done.7) | copy-start | bytes 6291460
  145.7 2.7 collective-permute-start.14
  145.8 2.6 collective-permute-start.15
  154.0 3.7 %collective-permute-start.17 = (f32[8,64,512]{2,1,0:T(8,128)S(1)}, f32[8,64,512]{2,1,0:T(8,128)S(1)}, u32[]{:S(2)}, u32[]{:S(2)}) collective-permute-start(f32[8,64,512]{2,1,0:T(8,128)S(1)} %get-tuple-element.52), channel_id=1, source_target_pairs={{0,1},{1,0},{2,3},{3,2},{4,5},{5,4},{6,7},{7,6},{8,9},{9,8},{10,11... | collective-permute-start | bytes 3145736 | tf_op jit(solution)/shard_map/ppermute | solution.py:558
  157.2 3.4 %collective-permute-start.16 = (f32[8,64,512]{2,1,0:T(8,128)S(1)}, f32[8,64,512]{2,1,0:T(8,128)S(1)}, u32[]{:S(2)}, u32[]{:S(2)}) collective-permute-start(f32[8,64,512]{2,1,0:T(8,128)S(1)} %get-tuple-element.50), channel_id=1, source_target_pairs={{0,1},{1,0},{2,3},{3,2},{4,5},{5,4},{6,7},{7,6},{8,9},{9,8},{10,11... | collective-permute-start | bytes 3145736 | tf_op jit(solution)/shard_map/ppermute | solution.py:558
  179.3 95.8 %copy-start.3 = (f32[2,4,64,1024]{3,2,1,0:T(8,128)S(1)}, f32[2,4,64,1024]{3,2,1,0:T(8,128)}, u32[]{:S(2)}) copy-start(f32[2,4,64,1024]{3,2,1,0:T(8,128)} %right_ref.3) | copy-start | bytes 6291460
  (11 other events, 21.6 us)

commit v9 on v8

--- a/solution.py
+++ b/solution.py
@@ -213,31 +213,41 @@
     sum_ref[...] = jnp.concatenate(sums + [jnp.zeros((rows - len(sums), 128), F32)], axis=0)
 
 
+def copy_into(pairs, done):
+    return [
+        pltpu.make_async_copy(source, target, done.at[at])
+        for at, (source, target) in enumerate(pairs)
+    ]
+
+
 def first_column_kernel(
     place_ref,
     table_ref,
     field_hbm,
     turned_hbm,
     basis_hbm,
+    kernel_hbm,
+    second_hbm,
     tall_ref,
     *refs,
 ):
-    wide_refs, refs, local = refs[:-11], refs[-11:-4], refs[-4:]
-    start_ref, weight_ref, column_ref, keep_ref, send_ref, sum_ref, scratch_ref = refs
-    field_ref, turned_ref, basis_ref, done = local
+    wide_refs, refs, outs = refs[:-13], refs[-7:], refs[-13:-7]
+    start_ref, weight_ref, column_ref, keep_ref, send_ref, sum_ref = outs
+    turned_ref, basis_ref, kernel_ref, second_ref, scratch_ref, field_ref, done = refs
     middle = turned_ref.shape[0] // 2
     upper, lower = pl.ds(0, middle), pl.ds(middle, middle)
-    pairs = (
-        (field_hbm, field_ref),
-        (turned_hbm.at[upper], turned_ref.at[upper]),
-        (turned_hbm.at[lower], turned_ref.at[lower]),
-        (basis_hbm, basis_ref),
-    )
-    copies = [
-        pltpu.make_async_copy(source, target, done.at[at])
-        for at, (source, target) in enumerate(pairs)
-    ]
-    for copy in copies:
+    copies = copy_into(
+        (
+            (field_hbm, field_ref),
+            (turned_hbm.at[upper], turned_ref.at[upper]),
+            (turned_hbm.at[lower], turned_ref.at[lower]),
+            (basis_hbm, basis_ref),
+            (kernel_hbm, kernel_ref),
+            (second_hbm, second_ref),
+        ),
+        done,
+    )
+    for copy in copies[:3]:
         copy.start()
     mean = functools.reduce(jnp.add, [table_ref[at] for at in range(NCLASS)]) * (1.0 / NCLASS)
     height, width = start_ref.shape
@@ -255,9 +265,10 @@
     copies[0].wait()
     field = field_ref[...].reshape(height, width)
     copies[1].wait()
-    above = times_left(turned_ref[:middle], field)
     copies[2].wait()
-    spectral = jnp.concatenate([above, times_left(turned_ref[middle:], field)], axis=0)
+    for copy in copies[3:]:
+        copy.start()
+    spectral = times_left(turned_ref[...], field)
     weighted = spectral * weight_ref[...]
     start_ref[...] = field
     store_sums(sum_ref, [fold(spectral * weighted)])
@@ -265,6 +276,8 @@
     column = times_left(basis_ref[...], weighted)
     column_ref[...] = column
     split_rows(place_ref, column, scratch_ref, keep_ref, send_ref)
+    copies[4].wait()
+    copies[5].wait()
 
 
 def next_column_kernel(
@@ -304,6 +317,16 @@
     split_rows(place_ref, image, scratch_ref, keep_ref, send_ref)
 
 
+def first_column_image_kernel(place_ref, column_ref, kernel_ref, high_hbm, low_hbm, *refs):
+    keep_ref, send_ref, high_ref, low_ref, scratch_ref, done = refs
+    copies = copy_into(((high_hbm, high_ref), (low_hbm, low_ref)), done)
+    for copy in copies:
+        copy.start()
+    column_image_kernel(place_ref, column_ref, kernel_ref, keep_ref, send_ref, scratch_ref)
+    for copy in copies:
+        copy.wait()
+
+
 def join_columns(place_ref, scratch_ref, keep_ref, got_ref):
     height, width = scratch_ref.shape
     mine, theirs = both_shares(place_ref, width // 2)
@@ -462,6 +485,8 @@
 
     smem = pl.BlockSpec(memory_space=pltpu.SMEM)
 
+    hbm = pl.BlockSpec(memory_space=pltpu.HBM)
+
     def full(*shape):
         return pl.BlockSpec(
             shape, lambda *at: (0,) * len(shape), pipeline_mode=pl.Buffered(1)
@@ -488,7 +513,7 @@
                 pltpu.SemaphoreType.DMA((len(shifts),)),
             ],
             compiler_params=params(1, 4),
-        )(noise_table, in_hbm(classes))
+        )(in_hbm(noise_table), in_hbm(classes))
 
     def plane_shift(value, by):
         pairs = [(at, (at + by * unit) % groups) for at in range(groups)]
@@ -557,13 +582,14 @@
     def swap(value):
         return lax.ppermute(value, "mode", core_swap)
 
-    def call(kernel, inputs, shapes, scratch_shape, specs=None, more=(), mebibytes=12):
+    def call(kernel, inputs, shapes, scratch_shape, specs=None, more=(), mebibytes=12, matrices=0):
         return pl.pallas_call(
             kernel,
             grid=(1,),
             in_specs=specs or [smem] + [full(*value.shape) for value in inputs[1:]],
-            out_specs=[whole_out(*shape) for shape in shapes],
-            out_shape=[shape_of(*shape) for shape in shapes],
+            out_specs=[whole_out(*shape) for shape in shapes]
+            + [whole_out(height, height)] * matrices,
+            out_shape=[shape_of(*shape) for shape in shapes] + [bf16_square] * matrices,
             scratch_shapes=[*([pltpu.VMEM(scratch_shape, F32)] if scratch_shape else []), *more],
             compiler_params=params(1, mebibytes),
         )(*inputs)
@@ -575,34 +601,38 @@
     flat = (blocks * rows, width)
     sums_shape = (8, 128)
 
-    start, weights, column, keep, send, sum_one = call(
+    (start, weights, column, keep, send, sum_one, turned, *squares) = call(
         first_column_kernel,
         (
             place,
             noise_table,
-            in_hbm(arrived),
-            in_hbm(turned),
-            in_hbm(basis_first),
+            *(
+                in_hbm(value)
+                for value in (arrived, turned, basis_first, kernel_first, basis_second)
+            ),
             tall_eigen,
             *shifted,
         ),
         (tile, tile, tile, piece, piece, sums_shape),
         by_rows,
         [smem, smem]
-        + [pl.BlockSpec(memory_space=pltpu.HBM)] * 3
+        + [hbm] * 5
         + [full(height, 128)]
         + [full(*value.shape) for value in shifted],
-        [
-            pltpu.VMEM((groups, rows, half), F32),
-            pltpu.VMEM((height, height), BF16),
-            pltpu.VMEM((height, height), BF16),
-            pltpu.SemaphoreType.DMA((4,)),
-        ],
-        18,
-    )
+        [pltpu.VMEM((groups, rows, half), F32), pltpu.SemaphoreType.DMA((6,))],
+        16,
+        4,
+    )
+    basis_first, kernel_first, basis_second = squares
     got = swap(send)
-    image_keep, image_send = call(
-        column_image_kernel, (place, column, kernel_first), (piece, piece), by_rows
+    image_keep, image_send, high, low = call(
+        first_column_image_kernel,
+        (place, column, kernel_first, in_hbm(high), in_hbm(low)),
+        (piece, piece),
+        by_rows,
+        [smem, full(*tile), full(height, height), hbm, hbm],
+        [pltpu.SemaphoreType.DMA((2,))],
+        matrices=2,
     )
     image_got = swap(image_send)
     inputs = (place, keep, got, basis_second)
@@ -613,7 +643,7 @@
         flat,
         [smem]
         + [full(*value.shape) for value in inputs[1:]]
-        + [pl.BlockSpec(memory_space=pltpu.HBM)] * len(noise),
+        + [hbm] * len(noise),
         [pltpu.SemaphoreType.DMA((len(noise),))],
     )
     image, pair_sum = call(
@@ -672,11 +702,11 @@
     )
     sums = lax.all_to_all(sums, "mode", split_axis=0, concat_axis=0, tiled=True)
 
-    few = blocks // 4
+    few = blocks
     few_spec = pl.BlockSpec((few, rows, width), lambda i: (i, 0, 0))
     answer = pl.pallas_call(
         combine_kernel,
-        grid=(4,),
+        grid=(1,),
         in_specs=[smem, full(groups, 8, 128)] + [few_spec] * 4,
         out_specs=pl.BlockSpec((few, 2 * rows, width), lambda i: (i, 0, 0)),
         out_shape=shape_of(blocks, 2 * rows, width),

time: 278 us -> 277 us (level)
    unnamed x48 -> x38, local copies, waits for them, and re-layouts: 8.66 us -> 8.65 us
where the time goes in v9:
time: 277 us
  blocking collectives  108 us (39%)
  waiting for transfers between devices  73.2 us (26%)
  Pallas kernels  55.4 us (20%)
  starting transfers between devices  30.4 us (11%)
  local copies, waits for them, and re-layouts  8.65 us (3%)
    all_to_all x1, blocking collectives, paired_body(): lax.all_to_all(answer, 'mode', split_axis=0, concat_axis=0, axis_index_gr...  95.8 us
    ppermute x3, waiting for transfers between devices, plane_shift(): return lax.ppermute(value, 'mode', pairs)  50.6 us
    pallas_call x10, Pallas kernels, call(): pl.pallas_call(kernel, grid=(1,), in_specs=specs or [smem] + [full(*value...  38.3 us
    ppermute x4, waiting for transfers between devices, paired_body(): far = [lax.ppermute(value, 'mode', sample_swap) for value in near]  20.2 us
    all_to_all x1, blocking collectives, paired_body(): sums = lax.all_to_all(sums, 'mode', split_axis=0, concat_axis=0, tiled=True)  12.2 us
    unnamed x38, local copies, waits for them, and re-layouts  8.65 us
    ppermute x3, starting transfers between devices, paired_body(): lax.ppermute(eigen, 'mode', [(at, (at + by * unit) % groups) for at in ra...  7.67 us
    all_to_all x1, starting transfers between devices, paired_body(): lax.all_to_all(outgoing.reshape(groups, rows, half), 'mode', split_axis=0...  7.6 us
  transfers between devices with their start and end apart: 19, of which 7 were waited for; matrix products, arithmetic and copies ran while one was open for 0% of the time, Pallas kernels for 8%

profile of v9, /device:TPU:0, one launch (start us, length us, event | category | flops | bytes accessed | tf_op | source)
XLA Modules:
  0.0 276.8 jit_solution(3152571339456082089)
XLA Ops:
  0.6 6.0 %outgoing.1 = f32[4,2,2,64,512]{4,3,2,1,0:T(8,128)} custom-call(f32[2,4,64,1024]{3,2,1,0:T(8,128)} %right_ref.3, bf16[1024,1024]{1,0:T(8,128)(2,1)} %second_hbm.1), custom_call_target="tpu_custom_call" | custom-call | tf_op jit(solution)/shard_map/outgoing/pallas_call | solution.py:532
  6.7 7.6 %all-to-all-start = ((f32[16,64,512]{2,1,0:T(8,128)}), f32[16,64,512]{2,1,0:T(8,128)}, u32[]{:S(2)}, u32[]{:S(2)}) async-start(f32[16,64,512]{2,1,0:T(8,128)} %bitcast.11), calls=%async_computation | async-start | bytes 4194304 | tf_op jit(solution)/shard_map/all_to_all | solution.py:544
  14.7 1.9 shard_map.105
  16.6 2.6 collective-permute-start.3
  19.2 2.6 shard_map.104
  24.0 2.4 collective-permute-start.4
  28.0 2.0 collective-permute-done.1
  30.0 50.6 %collective-permute-done.3.refs_1_.refs_2_ = f32[64,1024]{1,0:T(8,128)S(1)} collective-permute-done((f32[64,1024]{1,0:T(8,128)S(1)}, f32[64,1024]{1,0:T(8,128)S(1)}, u32[]{:S(2)}, u32[]{:S(2)}) %collective-permute-start.3) | collective-permute-done | bytes 262176 | tf_op jit(solution)/shard_map/ppermute | solution.py:520
  80.7 1.5 collective-permute-start.7
  82.2 5.5 %collective-permute-start.6 = (f32[1,256]{1,0:T(1,128)S(1)}, f32[1,256]{1,0:T(1,128)S(1)}, u32[]{:S(2)}, u32[]{:S(2)}) collective-permute-start(f32[1,256]{1,0:T(1,128)S(1)} %follow.1._.refs_0_), channel_id=1, source_target_pairs={{0,8},{1,9},{2,10},{3,11},{4,12},{5,13},{6,14},{7,15},{8,0},{9,1},... | collective-permute-start | bytes 3080 | tf_op jit(solution)/shard_map/ppermute | solution.py:567
  88.5 1.6 copy-done.2
  90.0 1.6 copy-done.3
  91.6 2.4 prepare.1
  98.1 7.7 %shard_map.106 = (f32[1024,512]{1,0:T(8,128)S(1)}, f32[1024,512]{1,0:T(8,128)S(1)}, f32[1024,512]{1,0:T(8,128)S(1)}, f32[8,64,512]{2,1,0:T(8,128)S(1)}, f32[8,64...) custom-call(s32[4]{0:T(128)S(1)} %pad_add_fusion.place_ref, ...), custom_call_target="tpu_custom_call" | custom-call | tf_op jit(solution)/shard_map/pallas_call | solution.py:586
  105.9 3.0 %shard_map.107 = (f32[8,64,512]{2,1,0:T(8,128)S(1)}, f32[8,64,512]{2,1,0:T(8,128)S(1)}, bf16[1024,1024]{1,0:T(8,128)(2,1)S(1)}, bf16[1024,1024]{1,0:T(8,128)(2,1)S(1)}) custom-call(s32[4]{0:T(128)S(1)} %pad_add_fusion.place_ref, f32[1024,512]{1,0:T(8,128)S(1)} %get-tuple-element.39.column_ref, bf16[1024,1024]{1,0:T(8,128)(2,1)S(1)} %get-tuple-element.40.kernel_ref, ...), custom_call_target="tpu_custom_call" | custom-call | tf_op jit(solution)/shard_map/pallas_call | solution.py:586
  113.0 5.7 %collective-permute-done.10.refs_4_ = f32[64,1024]{1,0:T(8,128)S(1)} collective-permute-done((f32[64,1024]{1,0:T(8,128)S(1)}, f32[64,1024]{1,0:T(8,128)S(1)}, u32[]{:S(2)}, u32[]{:S(2)}) %collective-permute-start.10) | collective-permute-done | bytes 262176 | tf_op jit(solution)/shard_map/ppermute | solution.py:529
  118.7 1.5 collective-permute-start.13
  120.2 4.1 %collective-permute-done.12.refs_6_ = f32[64,1024]{1,0:T(8,128)S(1)} collective-permute-done((f32[64,1024]{1,0:T(8,128)S(1)}, f32[64,1024]{1,0:T(8,128)S(1)}, u32[]{:S(2)}, u32[]{:S(2)}) %collective-permute-start.12) | collective-permute-done | bytes 262176 | tf_op jit(solution)/shard_map/ppermute | solution.py:529
  124.3 5.6 %collective-permute-done.11.refs_5_ = f32[64,1024]{1,0:T(8,128)S(1)} collective-permute-done((f32[64,1024]{1,0:T(8,128)S(1)}, f32[64,1024]{1,0:T(8,128)S(1)}, u32[]{:S(2)}, u32[]{:S(2)}) %collective-permute-start.11) | collective-permute-done | bytes 262176 | tf_op jit(solution)/shard_map/ppermute | solution.py:529
  129.9 4.7 %collective-permute-done.13.refs_7_ = f32[64,1024]{1,0:T(8,128)S(1)} collective-permute-done((f32[64,1024]{1,0:T(8,128)S(1)}, f32[64,1024]{1,0:T(8,128)S(1)}, u32[]{:S(2)}, u32[]{:S(2)}) %collective-permute-start.13) | collective-permute-done | bytes 262176 | tf_op jit(solution)/shard_map/ppermute | solution.py:529
  135.4 4.1 %shard_map.108 = (f32[8,64,1024]{2,1,0:T(8,128)S(1)}, f32[8,64,1024]{2,1,0:T(8,128)S(1)}) custom-call(s32[4]{0:T(128)S(1)} %pad_add_fusion.place_ref, f32[8,64,512]{2,1,0:T(8,128)S(1)} %get-tuple-element.45.keep_ref, f32[8,64,512]{2,1,0:T(8,128)S(1)} %collective-permute-done.9.got_ref, bf16[1024,1024]{1,0:T(8,128)(2,1)S(1)} %get-tuple-element.47.basis_ref, ...), custom_call_target="tpu_custom_call" | custom-call | tf_op jit(solution)/shard_map/pallas_call | solution.py:586
  139.5 4.3 %shard_map.109 = (f32[8,64,1024]{2,1,0:T(8,128)S(1)}, f32[8,128]{1,0:T(8,128)S(1)}) custom-call(s32[4]{0:T(128)S(1)} %pad_add_fusion.place_ref, f32[8,64,512]{2,1,0:T(8,128)S(1)} %get-tuple-element.43.keep_ref, f32[8,64,512]{2,1,0:T(8,128)S(1)} %collective-permute-done.8.got_ref, f32[8,64,1024]{2,1,0:T(8,128)S(1)} %get-tuple-element.49.z_ref, ...), custom_call_target="tpu_custom_call" | custom-call | tf_op jit(solution)/shard_map/pallas_call | solution.py:586
  143.8 1.8 shard_map.111
  146.2 1.8 shard_map.110.held_ref
  148.3 5.4 %shard_map.112 = (f32[1024,512]{1,0:T(8,128)S(1)}, f32[8,64,512]{2,1,0:T(8,128)S(1)}, f32[8,64,512]{2,1,0:T(8,128)S(1)}, f32[8,128]{1,0:T(8,128)S(1)}) custom-call(s32[4]{0:T(128)S(1)} %pad_add_fusion.place_ref, f32[8,64,512]{2,1,0:T(8,128)S(1)} %shard_map.110.held_ref, f32[8,64,512]{2,1,0:T(8,128)S(1)} %collective-permute-done.14.got_ref, ...), custom_call_target="tpu_custom_call" | custom-call | tf_op jit(solution)/shard_map/pallas_call | solution.py:586
  154.0 3.0 %shard_map.113 = (f32[8,64,512]{2,1,0:T(8,128)S(1)}, f32[8,64,512]{2,1,0:T(8,128)S(1)}) custom-call(s32[4]{0:T(128)S(1)} %pad_add_fusion.place_ref, f32[1024,512]{1,0:T(8,128)S(1)} %get-tuple-element.60.column_ref, bf16[1024,1024]{1,0:T(8,128)(2,1)S(1)} %get-tuple-element.40.kernel_ref), custom_call_target="tpu_custom_call" | custom-call | tf_op jit(solution)/shard_map/pallas_call | solution.py:586
  157.4 3.0 %shard_map.114.z_ref.f_ref = f32[8,64,1024]{2,1,0:T(8,128)S(1)} custom-call(s32[4]{0:T(128)S(1)} %pad_add_fusion.place_ref, f32[8,64,512]{2,1,0:T(8,128)S(1)} %get-tuple-element.63.keep_ref, f32[8,64,512]{2,1,0:T(8,128)S(1)} %collective-permute-done.17.got_ref, bf16[1024,1024]{1,0:T(8,128)(2,1)S(1)} %get-tuple-element.47.basis_ref), custom_call_target="tpu_custom_call" | custom-call | tf_op jit(solution)/shard_map/pallas_call | solution.py:586
  160.4 4.1 %shard_map.115 = (f32[8,64,1024]{2,1,0:T(8,128)S(1)}, f32[16,8,128]{2,1,0:T(8,128)S(1)}) custom-call(s32[4]{0:T(128)S(1)} %pad_add_fusion.place_ref, f32[8,64,512]{2,1,0:T(8,128)S(1)} %get-tuple-element.61.keep_ref, f32[8,64,512]{2,1,0:T(8,128)S(1)} %collective-permute-done.16.got_ref, f32[8,64,1024]{2,1,0:T(8,128)S(1)} %shard_map.114.z_ref.f_ref, ...), custom_call_target="tpu_custom_call" | custom-call | tf_op jit(solution)/shard_map/pallas_call | solution.py:586
  164.6 12.2 %all_to_all.15.sum_ref = f32[16,8,128]{2,1,0:T(8,128)S(1)} all-to-all(f32[16,8,128]{2,1,0:T(8,128)S(1)} %get-tuple-element.66), channel_id=1, replica_groups=mesh['blocks'=2,'mode'=16] {'mode'}, dimensions={0} | all-to-all | bytes 131072 | tf_op jit(solution)/shard_map/all_to_all | solution.py:703
  176.8 1.6 combine.1
  178.4 95.8 %all_to_all.16.got_ref = f32[8,128,1024]{2,1,0:T(8,128)S(1)} all-to-all(f32[8,128,1024]{2,1,0:T(8,128)S(1)} %combine.1), channel_id=1, replica_groups={{0,2,4,6,8,10,12,14},{1,3,5,7,9,11,13,15},{16,18,20,22,24,26,28,30},{17..., dimensions={0} | all-to-all | bytes 8388608 | tf_op jit(solution)/shard_map/all_to_all | solution.py:716
  274.2 2.6 finish.1
  (67 shorter events, 15.4 us)
Async XLA Ops:
  6.6 7.6 %copy-start.18 = (f32[64]{0:T(128)S(1)}, f32[64]{0:T(128)}, u32[]{:S(2)}) copy-start(f32[64]{0:T(128)} %param.17) | copy-start | bytes 772
  6.7 91.4 %all-to-all-start = ((f32[16,64,512]{2,1,0:T(8,128)}), f32[16,64,512]{2,1,0:T(8,128)}, u32[]{:S(2)}, u32[]{:S(2)}) async-start(f32[16,64,512]{2,1,0:T(8,128)} %bitcast.11), calls=%async_computation | async-start | bytes 4194304 | tf_op jit(solution)/shard_map/all_to_all | solution.py:544
  14.3 74.2 %copy-start = (bf16[1024,1024]{1,0:T(8,128)(2,1)S(1)}, bf16[1024,1024]{1,0:T(8,128)(2,1)}, u32[]{:S(2)}) copy-start(bf16[1024,1024]{1,0:T(8,128)(2,1)} %second_hbm.1) | copy-start | bytes 6291460
  14.3 74.2 %copy-start.13 = (f32[1024]{0:T(1024)S(1)}, f32[1024]{0:T(1024)}, u32[]{:S(2)}) copy-start(f32[1024]{0:T(1024)} %param.16) | copy-start | bytes 12292
  14.3 12.1 %collective-permute-start = (f32[1,64]{1,0:T(1,128)S(1)}, f32[1,64]{1,0:T(1,128)S(1)}, u32[]{:S(2)}, u32[]{:S(2)}) collective-permute-start(f32[1,64]{1,0:T(1,128)S(1)} %bitcast.12), channel_id=1, source_target_pairs={{0,1},{1,0},{2,3},{3,2},{4,5},{5,4},{6,7},{7,6},{8,9},{9,8},{10,11... | collective-permute-start | bytes 776 | tf_op jit(solution)/shard_map/ppermute | solution.py:550
  16.6 64.0 %collective-permute-start.3 = (f32[64,1024]{1,0:T(8,128)S(1)}, f32[64,1024]{1,0:T(8,128)S(1)}, u32[]{:S(2)}, u32[]{:S(2)}) collective-permute-start(f32[64,1024]{1,0:T(8,128)S(1)} %shard_map.105), channel_id=1, source_target_pairs={{0,8},{1,9},{2,10},{3,11},{4,12},{5,13},{6,14},{7,15},{8,0},{9,1},... | collective-permute-start | bytes 786440 | tf_op jit(solution)/shard_map/ppermute | solution.py:520
  22.5 58.1 %collective-permute-start.2 = (f32[64,1024]{1,0:T(8,128)}, f32[64,1024]{1,0:T(8,128)S(1)}, u32[]{:S(2)}, u32[]{:S(2)}) collective-permute-start(f32[64,1024]{1,0:T(8,128)} %get-tuple-element.35), channel_id=1, source_target_pairs={{0,4},{1,5},{2,6},{3,7},{4,8},{5,9},{6,10},{7,11},{8,12},{9,13},{1... | collective-permute-start | bytes 786440 | tf_op jit(solution)/shard_map/ppermute | solution.py:520
  24.0 56.7 %collective-permute-start.4 = (f32[64,1024]{1,0:T(8,128)S(1)}, f32[64,1024]{1,0:T(8,128)S(1)}, u32[]{:S(2)}, u32[]{:S(2)}) collective-permute-start(f32[64,1024]{1,0:T(8,128)S(1)} %get-tuple-element.36), channel_id=1, source_target_pairs={{0,12},{1,13},{2,14},{3,15},{4,0},{5,1},{6,2},{7,3},{8,4},{9,5},{1... | collective-permute-start | bytes 786440 | tf_op jit(solution)/shard_map/ppermute | solution.py:520
  26.4 3.6 %collective-permute-start.1 = (f32[1,128]{1,0:T(1,128)S(1)}, f32[1,128]{1,0:T(1,128)S(1)}, u32[]{:S(2)}, u32[]{:S(2)}) collective-permute-start(f32[1,128]{1,0:T(1,128)S(1)} %broadcast_select_fusion.1), channel_id=1, source_target_pairs={{0,2},{1,3},{2,0},{3,1},{4,6},{5,7},{6,4},{7,5},{8,10},{9,11},{10,... | collective-permute-start | bytes 1544 | tf_op jit(solution)/shard_map/ppermute | solution.py:550
  80.7 30.3 %copy-start.7 = (f32[64,1024]{1,0:T(8,128)}, f32[64,1024]{1,0:T(8,128)S(1)}, u32[]{:S(2)}) copy-start(f32[64,1024]{1,0:T(8,128)S(1)} %collective-permute-done.3.refs_1_.refs_2_) | copy-start | bytes 786436
  80.7 30.9 %copy-start.8 = (f32[64,1024]{1,0:T(8,128)}, f32[64,1024]{1,0:T(8,128)S(1)}, u32[]{:S(2)}) copy-start(f32[64,1024]{1,0:T(8,128)S(1)} %collective-permute-done.2.refs_0_.refs_1_) | copy-start | bytes 786436
  80.7 38.0 %copy-start.9 = (f32[64,1024]{1,0:T(8,128)}, f32[64,1024]{1,0:T(8,128)S(1)}, u32[]{:S(2)}) copy-start(f32[64,1024]{1,0:T(8,128)S(1)} %collective-permute-done.4.refs_2_.refs_3_) | copy-start | bytes 786436
  80.7 17.4 %collective-permute-start.7 = (f32[1,256]{1,0:T(1,128)S(1)}, f32[1,256]{1,0:T(1,128)S(1)}, u32[]{:S(2)}, u32[]{:S(2)}) collective-permute-start(f32[1,256]{1,0:T(1,128)S(1)} %follow.1._.refs_0_), channel_id=1, source_target_pairs={{0,12},{1,13},{2,14},{3,15},{4,0},{5,1},{6,2},{7,3},{8,4},{9,5},{1... | collective-permute-start | bytes 3080 | tf_op jit(solution)/shard_map/ppermute | solution.py:567
  82.2 15.9 %collective-permute-start.6 = (f32[1,256]{1,0:T(1,128)S(1)}, f32[1,256]{1,0:T(1,128)S(1)}, u32[]{:S(2)}, u32[]{:S(2)}) collective-permute-start(f32[1,256]{1,0:T(1,128)S(1)} %follow.1._.refs_0_), channel_id=1, source_target_pairs={{0,8},{1,9},{2,10},{3,11},{4,12},{5,13},{6,14},{7,15},{8,0},{9,1},... | collective-permute-start | bytes 3080 | tf_op jit(solution)/shard_map/ppermute | solution.py:567
  87.7 10.3 %collective-permute-start.5 = (f32[1,256]{1,0:T(1,128)S(1)}, f32[1,256]{1,0:T(1,128)S(1)}, u32[]{:S(2)}, u32[]{:S(2)}) collective-permute-start(f32[1,256]{1,0:T(1,128)S(1)} %follow.1._.refs_0_), channel_id=1, source_target_pairs={{0,4},{1,5},{2,6},{3,7},{4,8},{5,9},{6,10},{7,11},{8,12},{9,13},{1... | collective-permute-start | bytes 3080 | tf_op jit(solution)/shard_map/ppermute | solution.py:567
  88.4 1.6 copy-start.2
  91.6 6.4 %copy-start.12 = (f32[8]{0:T(128)S(1)}, f32[8]{0:T(128)}, u32[]{:S(2)}) copy-start(f32[8]{0:T(128)} %table_ref.5) | copy-start | bytes 100
  105.8 28.8 %collective-permute-start.9 = (f32[8,64,512]{2,1,0:T(8,128)S(1)}, f32[8,64,512]{2,1,0:T(8,128)S(1)}, u32[]{:S(2)}, u32[]{:S(2)}) collective-permute-start(f32[8,64,512]{2,1,0:T(8,128)S(1)} %get-tuple-element.46), channel_id=1, source_target_pairs={{0,1},{1,0},{2,3},{3,2},{4,5},{5,4},{6,7},{7,6},{8,9},{9,8},{10,11... | collective-permute-start | bytes 3145736 | tf_op jit(solution)/shard_map/ppermute | solution.py:583
  105.9 3.6 %copy-start.11 = (f32[64,1024]{1,0:T(8,128)S(1)}, f32[64,1024]{1,0:T(8,128)}, u32[]{:S(2)}) copy-start(f32[64,1024]{1,0:T(8,128)} %copy-done.10) | copy-start | bytes 786436
  109.0 30.5 %collective-permute-start.8 = (f32[8,64,512]{2,1,0:T(8,128)S(1)}, f32[8,64,512]{2,1,0:T(8,128)S(1)}, u32[]{:S(2)}, u32[]{:S(2)}) collective-permute-start(f32[8,64,512]{2,1,0:T(8,128)S(1)} %get-tuple-element.44), channel_id=1, source_target_pairs={{0,1},{1,0},{2,3},{3,2},{4,5},{5,4},{6,7},{7,6},{8,9},{9,8},{10,11... | collective-permute-start | bytes 3145736 | tf_op jit(solution)/shard_map/ppermute | solution.py:583
  109.5 9.2 %collective-permute-start.10 = (f32[64,1024]{1,0:T(8,128)S(1)}, f32[64,1024]{1,0:T(8,128)S(1)}, u32[]{:S(2)}, u32[]{:S(2)}) collective-permute-start(f32[64,1024]{1,0:T(8,128)S(1)} %copy-done.11), channel_id=1, source_target_pairs={{0,2},{1,3},{2,0},{3,1},{4,6},{5,7},{6,4},{7,5},{8,10},{9,11},{10,... | collective-permute-start | bytes 786440 | tf_op jit(solution)/shard_map/ppermute | solution.py:529
  111.0 13.3 %collective-permute-start.12 = (f32[64,1024]{1,0:T(8,128)S(1)}, f32[64,1024]{1,0:T(8,128)S(1)}, u32[]{:S(2)}, u32[]{:S(2)}) collective-permute-start(f32[64,1024]{1,0:T(8,128)S(1)} %collective-permute-done.3.refs_1_.refs_2_), channel_id=1, source_target_pairs={{0,2},{1,3},{2,0},{3,1},{4,6},{5,7},{6,4},{7,5},{8,10},{9,11},{10,... | collective-permute-start | bytes 786440 | tf_op jit(solution)/shard_map/ppermute | solution.py:529
  111.5 18.4 %collective-permute-start.11 = (f32[64,1024]{1,0:T(8,128)S(1)}, f32[64,1024]{1,0:T(8,128)S(1)}, u32[]{:S(2)}, u32[]{:S(2)}) collective-permute-start(f32[64,1024]{1,0:T(8,128)S(1)} %collective-permute-done.2.refs_0_.refs_1_), channel_id=1, source_target_pairs={{0,2},{1,3},{2,0},{3,1},{4,6},{5,7},{6,4},{7,5},{8,10},{9,11},{10,... | collective-permute-start | bytes 786440 | tf_op jit(solution)/shard_map/ppermute | solution.py:529
  118.7 16.0 %copy-start.14 = (f32[64,1024]{1,0:T(8,128)}, f32[64,1024]{1,0:T(8,128)S(1)}, u32[]{:S(2)}) copy-start(f32[64,1024]{1,0:T(8,128)S(1)} %collective-permute-done.10.refs_4_) | copy-start | bytes 786436
  118.7 16.0 %collective-permute-start.13 = (f32[64,1024]{1,0:T(8,128)S(1)}, f32[64,1024]{1,0:T(8,128)S(1)}, u32[]{:S(2)}, u32[]{:S(2)}) collective-permute-start(f32[64,1024]{1,0:T(8,128)S(1)} %collective-permute-done.4.refs_2_.refs_3_), channel_id=1, source_target_pairs={{0,2},{1,3},{2,0},{3,1},{4,6},{5,7},{6,4},{7,5},{8,10},{9,11},{10,... | collective-permute-start | bytes 786440 | tf_op jit(solution)/shard_map/ppermute | solution.py:529
  124.3 10.4 %copy-start.15 = (f32[64,1024]{1,0:T(8,128)}, f32[64,1024]{1,0:T(8,128)S(1)}, u32[]{:S(2)}) copy-start(f32[64,1024]{1,0:T(8,128)S(1)} %collective-permute-done.12.refs_6_) | copy-start | bytes 786436
  129.9 4.8 %copy-start.16 = (f32[64,1024]{1,0:T(8,128)}, f32[64,1024]{1,0:T(8,128)S(1)}, u32[]{:S(2)}) copy-start(f32[64,1024]{1,0:T(8,128)S(1)} %collective-permute-done.11.refs_5_) | copy-start | bytes 786436
  145.6 2.7 collective-permute-start.14
  145.7 2.7 collective-permute-start.15
  153.8 3.7 %collective-permute-start.17 = (f32[8,64,512]{2,1,0:T(8,128)S(1)}, f32[8,64,512]{2,1,0:T(8,128)S(1)}, u32[]{:S(2)}, u32[]{:S(2)}) collective-permute-start(f32[8,64,512]{2,1,0:T(8,128)S(1)} %get-tuple-element.64), channel_id=1, source_target_pairs={{0,1},{1,0},{2,3},{3,2},{4,5},{5,4},{6,7},{7,6},{8,9},{9,8},{10,11... | collective-permute-start | bytes 3145736 | tf_op jit(solution)/shard_map/ppermute | solution.py:583
  157.0 3.4 %collective-permute-start.16 = (f32[8,64,512]{2,1,0:T(8,128)S(1)}, f32[8,64,512]{2,1,0:T(8,128)S(1)}, u32[]{:S(2)}, u32[]{:S(2)}) collective-permute-start(f32[8,64,512]{2,1,0:T(8,128)S(1)} %get-tuple-element.62), channel_id=1, source_target_pairs={{0,1},{1,0},{2,3},{3,2},{4,5},{5,4},{6,7},{7,6},{8,9},{9,8},{10,11... | collective-permute-start | bytes 3145736 | tf_op jit(solution)/shard_map/ppermute | solution.py:583
  178.4 95.8 %copy-start.1 = (f32[2,4,64,1024]{3,2,1,0:T(8,128)S(1)}, f32[2,4,64,1024]{3,2,1,0:T(8,128)}, u32[]{:S(2)}) copy-start(f32[2,4,64,1024]{3,2,1,0:T(8,128)} %right_ref.3) | copy-start | bytes 6291460
  (6 other events, 7.1 us)

commit v10 on v9

--- a/solution.py
+++ b/solution.py
@@ -125,12 +125,19 @@
     return result[: value.shape[0]] + result[value.shape[0] :]
 
 
+def side_by_side(value):
+    return jnp.concatenate(split(value), axis=1)
+
+
+def times_both(matrix, both):
+    width = both.shape[1] // 2
+    dims = (((1,), (0,)), ((), ()))
+    result = lax.dot_general(matrix, both, dims, preferred_element_type=F32)
+    return result[:, :width] + result[:, width:]
+
+
 def times_left(matrix, value):
-    high, low = split(value)
-    dims = (((1,), (0,)), ((), ()))
-    both = jnp.concatenate([high, low], axis=1)
-    result = lax.dot_general(matrix, both, dims, preferred_element_type=F32)
-    return result[:, : value.shape[1]] + result[:, value.shape[1] :]
+    return times_both(matrix, side_by_side(value))
 
 
 def fold(value):
@@ -234,20 +241,19 @@
     wide_refs, refs, outs = refs[:-13], refs[-7:], refs[-13:-7]
     start_ref, weight_ref, column_ref, keep_ref, send_ref, sum_ref = outs
     turned_ref, basis_ref, kernel_ref, second_ref, scratch_ref, field_ref, done = refs
-    middle = turned_ref.shape[0] // 2
-    upper, lower = pl.ds(0, middle), pl.ds(middle, middle)
+    quarter = turned_ref.shape[0] // 4
+    quarters = [pl.ds(at * quarter, quarter) for at in range(4)]
     copies = copy_into(
         (
             (field_hbm, field_ref),
-            (turned_hbm.at[upper], turned_ref.at[upper]),
-            (turned_hbm.at[lower], turned_ref.at[lower]),
+            *((turned_hbm.at[rows], turned_ref.at[rows]) for rows in quarters),
             (basis_hbm, basis_ref),
             (kernel_hbm, kernel_ref),
             (second_hbm, second_ref),
         ),
         done,
     )
-    for copy in copies[:3]:
+    for copy in copies[:5]:
         copy.start()
     mean = functools.reduce(jnp.add, [table_ref[at] for at in range(NCLASS)]) * (1.0 / NCLASS)
     height, width = start_ref.shape
@@ -264,20 +270,23 @@
             weight_ref[:, lanes] = 1.0 / (tall_ref[...] * wide[:, at : at + 128] + mean)
     copies[0].wait()
     field = field_ref[...].reshape(height, width)
-    copies[1].wait()
-    copies[2].wait()
-    for copy in copies[3:]:
+    both = side_by_side(field)
+    parts = []
+    for copy, rows in zip(copies[1:5], quarters):
+        copy.wait()
+        parts.append(times_both(turned_ref[rows, :], both))
+    for copy in copies[5:]:
         copy.start()
-    spectral = times_left(turned_ref[...], field)
+    spectral = jnp.concatenate(parts, axis=0)
     weighted = spectral * weight_ref[...]
     start_ref[...] = field
     store_sums(sum_ref, [fold(spectral * weighted)])
-    copies[3].wait()
+    copies[5].wait()
     column = times_left(basis_ref[...], weighted)
     column_ref[...] = column
     split_rows(place_ref, column, scratch_ref, keep_ref, send_ref)
-    copies[4].wait()
-    copies[5].wait()
+    copies[6].wait()
+    copies[7].wait()
 
 
 def next_column_kernel(
@@ -317,9 +326,17 @@
     split_rows(place_ref, image, scratch_ref, keep_ref, send_ref)
 
 
-def first_column_image_kernel(place_ref, column_ref, kernel_ref, high_hbm, low_hbm, *refs):
-    keep_ref, send_ref, high_ref, low_ref, scratch_ref, done = refs
-    copies = copy_into(((high_hbm, high_ref), (low_hbm, low_ref)), done)
+def first_column_image_kernel(place_ref, column_ref, kernel_ref, *refs):
+    parts, (keep_ref, send_ref, noise_ref, scratch_ref, done) = refs[:-5], refs[-5:]
+    planes = len(parts) // 2
+    samples = noise_ref.shape[0] // planes
+    pairs = []
+    for by in range(planes):
+        row = (place_ref[2] + planes - by) % planes
+        for at, part in enumerate((parts[by], parts[planes + by])):
+            block = row * samples + (place_ref[1] + at) % samples
+            pairs.append((part, noise_ref.at[block]))
+    copies = copy_into(pairs, done)
     for copy in copies:
         copy.start()
     column_image_kernel(place_ref, column_ref, kernel_ref, keep_ref, send_ref, scratch_ref)
@@ -350,17 +367,9 @@
     return result[: field.shape[0]] + (result[field.shape[0] :] + small)
 
 
-def first_row_kernel(place_ref, keep_ref, got_ref, basis_ref, *refs):
-    parts, (z_ref, noise_ref, scratch_ref, done) = refs[:-4], refs[-4:]
-    planes = len(parts) // 2
-    samples = z_ref.shape[0] // planes
-    copies = []
-    for by in range(planes):
-        row = (place_ref[2] + planes - by) % planes
-        for at, part in enumerate((parts[by], parts[planes + by])):
-            block = row * samples + (place_ref[1] + at) % samples
-            here = done.at[2 * by + at]
-            copies.append(pltpu.make_async_copy(part, noise_ref.at[block], here))
+def first_row_kernel(place_ref, keep_ref, got_ref, basis_ref, high_hbm, low_hbm, *refs):
+    z_ref, high_ref, low_ref, scratch_ref, done = refs
+    copies = copy_into(((high_hbm, high_ref), (low_hbm, low_ref)), done)
     for copy in copies:
         copy.start()
     row_kernel(place_ref, keep_ref, got_ref, basis_ref, z_ref, scratch_ref)
@@ -619,32 +628,30 @@
         + [hbm] * 5
         + [full(height, 128)]
         + [full(*value.shape) for value in shifted],
-        [pltpu.VMEM((groups, rows, half), F32), pltpu.SemaphoreType.DMA((6,))],
+        [pltpu.VMEM((groups, rows, half), F32), pltpu.SemaphoreType.DMA((8,))],
         16,
         4,
     )
     basis_first, kernel_first, basis_second = squares
     got = swap(send)
-    image_keep, image_send, high, low = call(
+    image_keep, image_send, noise = call(
         first_column_image_kernel,
-        (place, column, kernel_first, in_hbm(high), in_hbm(low)),
-        (piece, piece),
+        (place, column, kernel_first, *(in_hbm(value) for value in noise)),
+        (piece, piece, whole),
         by_rows,
-        [smem, full(*tile), full(height, height), hbm, hbm],
+        [smem, full(*tile), full(height, height)] + [hbm] * len(noise),
+        [pltpu.SemaphoreType.DMA((len(noise),))],
+    )
+    image_got = swap(image_send)
+    inputs = (place, keep, got, basis_second)
+    z_field, high, low = call(
+        first_row_kernel,
+        (*inputs, in_hbm(high), in_hbm(low)),
+        (whole,),
+        flat,
+        [smem] + [full(*value.shape) for value in inputs[1:]] + [hbm] * 2,
         [pltpu.SemaphoreType.DMA((2,))],
         matrices=2,
-    )
-    image_got = swap(image_send)
-    inputs = (place, keep, got, basis_second)
-    z_field, noise = call(
-        first_row_kernel,
-        (*inputs, *(in_hbm(value) for value in noise)),
-        (whole, whole),
-        flat,
-        [smem]
-        + [full(*value.shape) for value in inputs[1:]]
-        + [hbm] * len(noise),
-        [pltpu.SemaphoreType.DMA((len(noise),))],
     )
     image, pair_sum = call(
         first_image_kernel,

time: 277 us -> 258 us (0.931)
  waiting for transfers between devices: 73.2 us -> 58.3 us
    ppermute x4, waiting for transfers between devices: 20.2 us -> 0.01 us  [paired_body(): far = [lax.ppermute(value, 'mode', sample_swap) for value in near]]
    ppermute x3, waiting for transfers between devices: 0.01 us -> 5.59 us  [paired_body(): lax.ppermute(eigen, 'mode', [(at, (at + by * unit) % groups) for at in ra...]
    unnamed x38 -> x26, local copies, waits for them, and re-layouts: 8.65 us -> 7.24 us
  transfers between devices with their start and end apart: 19 -> 19, of which waited for: 7 -> 4; matrix products, arithmetic and copies ran while one was open for 0% -> 0% of each run, Pallas kernels for 8% -> 12%
where the time goes in v10:
time: 258 us
  blocking collectives  106 us (41%)
  waiting for transfers between devices  58.3 us (23%)
  Pallas kernels  56.6 us (22%)
  starting transfers between devices  28.2 us (11%)
  local copies, waits for them, and re-layouts  7.24 us (3%)
    all_to_all x1, blocking collectives, paired_body(): lax.all_to_all(answer, 'mode', split_axis=0, concat_axis=0, axis_index_gr...  95.8 us
    ppermute x3, waiting for transfers between devices, plane_shift(): return lax.ppermute(value, 'mode', pairs)  52.3 us
    pallas_call x10, Pallas kernels, call(): pl.pallas_call(kernel, grid=(1,), in_specs=specs or [smem] + [full(*value...  39.4 us
    all_to_all x1, blocking collectives, paired_body(): sums = lax.all_to_all(sums, 'mode', split_axis=0, concat_axis=0, tiled=True)  10.4 us
    all_to_all x1, starting transfers between devices, paired_body(): lax.all_to_all(outgoing.reshape(groups, rows, half), 'mode', split_axis=0...  7.46 us
    unnamed x26, local copies, waits for them, and re-layouts  7.24 us
    ppermute x3, starting transfers between devices, plane_shift(): return lax.ppermute(value, 'mode', pairs)  6.71 us
    ppermute x3, starting transfers between devices, paired_body(): lax.ppermute(eigen, 'mode', [(at, (at + by * unit) % groups) for at in ra...  6.08 us
  transfers between devices with their start and end apart: 19, of which 4 were waited for; matrix products, arithmetic and copies ran while one was open for 0% of the time, Pallas kernels for 12%

profile of v10, /device:TPU:0, one launch (start us, length us, event | category | flops | bytes accessed | tf_op | source)
XLA Modules:
  0.0 257.8 jit_solution(16083071488440890848)
XLA Ops:
  0.6 6.0 %outgoing.1 = f32[4,2,2,64,512]{4,3,2,1,0:T(8,128)} custom-call(f32[2,4,64,1024]{3,2,1,0:T(8,128)} %right_ref.3, bf16[1024,1024]{1,0:T(8,128)(2,1)} %second_hbm.1), custom_call_target="tpu_custom_call" | custom-call | tf_op jit(solution)/shard_map/outgoing/pallas_call | solution.py:541
  6.6 7.5 %all-to-all-start = ((f32[16,64,512]{2,1,0:T(8,128)}), f32[16,64,512]{2,1,0:T(8,128)}, u32[]{:S(2)}, u32[]{:S(2)}) async-start(f32[16,64,512]{2,1,0:T(8,128)} %bitcast.11), calls=%async_computation | async-start | bytes 4194304 | tf_op jit(solution)/shard_map/all_to_all | solution.py:553
  14.2 1.9 shard_map.105
  16.1 2.8 %collective-permute-start.3 = (f32[64,1024]{1,0:T(8,128)S(1)}, f32[64,1024]{1,0:T(8,128)S(1)}, u32[]{:S(2)}, u32[]{:S(2)}) collective-permute-start(f32[64,1024]{1,0:T(8,128)S(1)} %shard_map.105), channel_id=1, source_target_pairs={{0,8},{1,9},{2,10},{3,11},{4,12},{5,13},{6,14},{7,15},{8,0},{9,1},... | collective-permute-start | bytes 786440 | tf_op jit(solution)/shard_map/ppermute | solution.py:529
  18.9 2.7 %shard_map.104 = (f32[64,1024]{1,0:T(8,128)}, f32[64,1024]{1,0:T(8,128)}, f32[64,1024]{1,0:T(8,128)S(1)}) custom-call(f32[8]{0:T(128)} %table_ref.5, s32[4,64,1024]{2,1,0:T(8,128)} %class_hbm.3), custom_call_target="tpu_custom_call" | custom-call | tf_op jit(solution)/shard_map/pallas_call | solution.py:514
  21.6 1.5 collective-permute-start.2
  23.1 2.4 collective-permute-start.4
  25.5 1.5 collective-permute-start.8
  28.2 52.3 %collective-permute-done.3.refs_1_.refs_2_ = f32[64,1024]{1,0:T(8,128)S(1)} collective-permute-done((f32[64,1024]{1,0:T(8,128)S(1)}, f32[64,1024]{1,0:T(8,128)S(1)}, u32[]{:S(2)}, u32[]{:S(2)}) %collective-permute-start.3) | collective-permute-done | bytes 262176 | tf_op jit(solution)/shard_map/ppermute | solution.py:529
  80.5 1.5 collective-permute-start.10
  82.6 1.5 collective-permute-start.11
  85.6 3.7 %collective-permute-done.7.refs_3_ = f32[1,256]{1,0:T(1,128)S(1)} collective-permute-done((f32[1,256]{1,0:T(1,128)S(1)}, f32[1,256]{1,0:T(1,128)S(1)}, u32[]{:S(2)}, u32[]{:S(2)}) %collective-permute-start.7) | collective-permute-done | bytes 1056 | tf_op jit(solution)/shard_map/ppermute | solution.py:576
  89.4 2.6 %collective-permute-start.6 = (f32[1,256]{1,0:T(1,128)S(1)}, f32[1,256]{1,0:T(1,128)S(1)}, u32[]{:S(2)}, u32[]{:S(2)}) collective-permute-start(f32[1,256]{1,0:T(1,128)S(1)} %follow.1._.refs_0_), channel_id=1, source_target_pairs={{0,8},{1,9},{2,10},{3,11},{4,12},{5,13},{6,14},{7,15},{8,0},{9,1},... | collective-permute-start | bytes 3080 | tf_op jit(solution)/shard_map/ppermute | solution.py:576
  92.0 1.9 collective-permute-done.6.refs_2_
  93.8 2.0 collective-permute-start.5
  95.9 1.6 copy-done.2
  97.5 1.6 copy-done.3
  99.1 2.4 prepare.1
  105.6 8.9 %shard_map.106 = (f32[1024,512]{1,0:T(8,128)S(1)}, f32[1024,512]{1,0:T(8,128)S(1)}, f32[1024,512]{1,0:T(8,128)S(1)}, f32[8,64,512]{2,1,0:T(8,128)S(1)}, f32[8,64...) custom-call(s32[4]{0:T(128)S(1)} %pad_add_fusion.place_ref, ...), custom_call_target="tpu_custom_call" | custom-call | tf_op jit(solution)/shard_map/pallas_call | solution.py:595
  114.7 4.0 %shard_map.107 = (f32[8,64,512]{2,1,0:T(8,128)S(1)}, f32[8,64,512]{2,1,0:T(8,128)S(1)}, f32[8,64,1024]{2,1,0:T(8,128)S(1)}) custom-call(s32[4]{0:T(128)S(1)} %pad_add_fusion.place_ref, f32[1024,512]{1,0:T(8,128)S(1)} %get-tuple-element.39.column_ref, bf16[1024,1024]{1,0:T(8,128)(2,1)S(1)} %get-tuple-element.40.kernel_ref, ...), custom_call_target="tpu_custom_call" | custom-call | tf_op jit(solution)/shard_map/pallas_call | solution.py:595
  119.2 3.0 %shard_map.108 = (f32[8,64,1024]{2,1,0:T(8,128)S(1)}, bf16[1024,1024]{1,0:T(8,128)(2,1)S(1)}, bf16[1024,1024]{1,0:T(8,128)(2,1)S(1)}) custom-call(s32[4]{0:T(128)S(1)} %pad_add_fusion.place_ref, f32[8,64,512]{2,1,0:T(8,128)S(1)} %get-tuple-element.44.keep_ref, f32[8,64,512]{2,1,0:T(8,128)S(1)} %collective-permute-done.13.got_ref, ...), custom_call_target="tpu_custom_call" | custom-call | tf_op jit(solution)/shard_map/pallas_call | solution.py:595
  122.2 4.4 %shard_map.109 = (f32[8,64,1024]{2,1,0:T(8,128)S(1)}, f32[8,128]{1,0:T(8,128)S(1)}) custom-call(s32[4]{0:T(128)S(1)} %pad_add_fusion.place_ref, f32[8,64,512]{2,1,0:T(8,128)S(1)} %get-tuple-element.42.keep_ref, f32[8,64,512]{2,1,0:T(8,128)S(1)} %collective-permute-done.12.got_ref, f32[8,64,1024]{2,1,0:T(8,128)S(1)} %get-tuple-element.49.z_ref, ...), custom_call_target="tpu_custom_call" | custom-call | tf_op jit(solution)/shard_map/pallas_call | solution.py:595
  126.6 1.8 shard_map.111
  129.0 1.8 shard_map.110.held_ref
  131.1 5.4 %shard_map.112 = (f32[1024,512]{1,0:T(8,128)S(1)}, f32[8,64,512]{2,1,0:T(8,128)S(1)}, f32[8,64,512]{2,1,0:T(8,128)S(1)}, f32[8,128]{1,0:T(8,128)S(1)}) custom-call(s32[4]{0:T(128)S(1)} %pad_add_fusion.place_ref, f32[8,64,512]{2,1,0:T(8,128)S(1)} %shard_map.110.held_ref, f32[8,64,512]{2,1,0:T(8,128)S(1)} %collective-permute-done.14.got_ref, ...), custom_call_target="tpu_custom_call" | custom-call | tf_op jit(solution)/shard_map/pallas_call | solution.py:595
  136.7 3.0 %shard_map.113 = (f32[8,64,512]{2,1,0:T(8,128)S(1)}, f32[8,64,512]{2,1,0:T(8,128)S(1)}) custom-call(s32[4]{0:T(128)S(1)} %pad_add_fusion.place_ref, f32[1024,512]{1,0:T(8,128)S(1)} %get-tuple-element.60.column_ref, bf16[1024,1024]{1,0:T(8,128)(2,1)S(1)} %get-tuple-element.40.kernel_ref), custom_call_target="tpu_custom_call" | custom-call | tf_op jit(solution)/shard_map/pallas_call | solution.py:595
  140.2 3.0 %shard_map.114.z_ref.f_ref = f32[8,64,1024]{2,1,0:T(8,128)S(1)} custom-call(s32[4]{0:T(128)S(1)} %pad_add_fusion.place_ref, f32[8,64,512]{2,1,0:T(8,128)S(1)} %get-tuple-element.63.keep_ref, f32[8,64,512]{2,1,0:T(8,128)S(1)} %collective-permute-done.17.got_ref, bf16[1024,1024]{1,0:T(8,128)(2,1)S(1)} %get-tuple-element.46.basis_ref), custom_call_target="tpu_custom_call" | custom-call | tf_op jit(solution)/shard_map/pallas_call | solution.py:595
  143.2 4.1 %shard_map.115 = (f32[8,64,1024]{2,1,0:T(8,128)S(1)}, f32[16,8,128]{2,1,0:T(8,128)S(1)}) custom-call(s32[4]{0:T(128)S(1)} %pad_add_fusion.place_ref, f32[8,64,512]{2,1,0:T(8,128)S(1)} %get-tuple-element.61.keep_ref, f32[8,64,512]{2,1,0:T(8,128)S(1)} %collective-permute-done.16.got_ref, f32[8,64,1024]{2,1,0:T(8,128)S(1)} %shard_map.114.z_ref.f_ref, ...), custom_call_target="tpu_custom_call" | custom-call | tf_op jit(solution)/shard_map/pallas_call | solution.py:595
  147.3 10.4 %all_to_all.15.sum_ref = f32[16,8,128]{2,1,0:T(8,128)S(1)} all-to-all(f32[16,8,128]{2,1,0:T(8,128)S(1)} %get-tuple-element.66), channel_id=1, replica_groups=mesh['blocks'=2,'mode'=16] {'mode'}, dimensions={0} | all-to-all | bytes 131072 | tf_op jit(solution)/shard_map/all_to_all | solution.py:710
  157.7 1.6 combine.1
  159.4 95.8 %all_to_all.16.got_ref = f32[8,128,1024]{2,1,0:T(8,128)S(1)} all-to-all(f32[8,128,1024]{2,1,0:T(8,128)S(1)} %combine.1), channel_id=1, replica_groups={{0,2,4,6,8,10,12,14},{1,3,5,7,9,11,13,15},{16,18,20,22,24,26,28,30},{17..., dimensions={0} | all-to-all | bytes 8388608 | tf_op jit(solution)/shard_map/all_to_all | solution.py:723
  255.2 2.6 %finish.1 = (f32[2,4,64,1024]{3,2,1,0:T(8,128)}, f32[2,4,64,1024]{3,2,1,0:T(8,128)}) custom-call(f32[8,128,1024]{2,1,0:T(8,128)S(1)} %all_to_all.16.got_ref, f32[2,4,64,1024]{3,2,1,0:T(8,128)S(1)} %copy-done.1), custom_call_target="tpu_custom_call" | custom-call | tf_op jit(solution)/shard_map/finish/pallas_call | solution.py:734
  (55 shorter events, 9.7 us)
Async XLA Ops:
  6.6 98.9 %all-to-all-start = ((f32[16,64,512]{2,1,0:T(8,128)}), f32[16,64,512]{2,1,0:T(8,128)}, u32[]{:S(2)}, u32[]{:S(2)}) async-start(f32[16,64,512]{2,1,0:T(8,128)} %bitcast.11), calls=%async_computation | async-start | bytes 4194304 | tf_op jit(solution)/shard_map/all_to_all | solution.py:553
  14.1 11.4 %copy-start.12 = (f32[64]{0:T(128)S(1)}, f32[64]{0:T(128)}, u32[]{:S(2)}) copy-start(f32[64]{0:T(128)} %param.17) | copy-start | bytes 772
  14.1 81.8 %copy-start = (bf16[1024,1024]{1,0:T(8,128)(2,1)S(1)}, bf16[1024,1024]{1,0:T(8,128)(2,1)}, u32[]{:S(2)}) copy-start(bf16[1024,1024]{1,0:T(8,128)(2,1)} %second_hbm.1) | copy-start | bytes 6291460
  14.1 81.8 %copy-start.11 = (f32[1024]{0:T(1024)S(1)}, f32[1024]{0:T(1024)}, u32[]{:S(2)}) copy-start(f32[1024]{0:T(1024)} %param.16) | copy-start | bytes 12292
  16.1 64.5 %collective-permute-start.3 = (f32[64,1024]{1,0:T(8,128)S(1)}, f32[64,1024]{1,0:T(8,128)S(1)}, u32[]{:S(2)}, u32[]{:S(2)}) collective-permute-start(f32[64,1024]{1,0:T(8,128)S(1)} %shard_map.105), channel_id=1, source_target_pairs={{0,8},{1,9},{2,10},{3,11},{4,12},{5,13},{6,14},{7,15},{8,0},{9,1},... | collective-permute-start | bytes 786440 | tf_op jit(solution)/shard_map/ppermute | solution.py:529
  21.6 60.4 %collective-permute-start.2 = (f32[64,1024]{1,0:T(8,128)}, f32[64,1024]{1,0:T(8,128)S(1)}, u32[]{:S(2)}, u32[]{:S(2)}) collective-permute-start(f32[64,1024]{1,0:T(8,128)} %get-tuple-element.35), channel_id=1, source_target_pairs={{0,4},{1,5},{2,6},{3,7},{4,8},{5,9},{6,10},{7,11},{8,12},{9,13},{1... | collective-permute-start | bytes 786440 | tf_op jit(solution)/shard_map/ppermute | solution.py:529
  23.1 59.4 %collective-permute-start.4 = (f32[64,1024]{1,0:T(8,128)S(1)}, f32[64,1024]{1,0:T(8,128)S(1)}, u32[]{:S(2)}, u32[]{:S(2)}) collective-permute-start(f32[64,1024]{1,0:T(8,128)S(1)} %get-tuple-element.36), channel_id=1, source_target_pairs={{0,12},{1,13},{2,14},{3,15},{4,0},{5,1},{6,2},{7,3},{8,4},{9,5},{1... | collective-permute-start | bytes 786440 | tf_op jit(solution)/shard_map/ppermute | solution.py:529
  25.5 1.5 collective-permute-start
  25.5 89.1 %collective-permute-start.8 = (f32[64,1024]{1,0:T(8,128)}, f32[64,1024]{1,0:T(8,128)}, u32[]{:S(2)}, u32[]{:S(2)}) collective-permute-start(f32[64,1024]{1,0:T(8,128)} %get-tuple-element.41.refs_0_), channel_id=1, source_target_pairs={{0,2},{1,3},{2,0},{3,1},{4,6},{5,7},{6,4},{7,5},{8,10},{9,11},{10,... | collective-permute-start | bytes 786440 | tf_op jit(solution)/shard_map/ppermute | solution.py:538
  27.0 57.1 %collective-permute-start.1 = (f32[1,128]{1,0:T(1,128)S(1)}, f32[1,128]{1,0:T(1,128)S(1)}, u32[]{:S(2)}, u32[]{:S(2)}) collective-permute-start(f32[1,128]{1,0:T(1,128)S(1)} %broadcast_select_fusion.1), channel_id=1, source_target_pairs={{0,2},{1,3},{2,0},{3,1},{4,6},{5,7},{6,4},{7,5},{8,10},{9,11},{10,... | collective-permute-start | bytes 1544 | tf_op jit(solution)/shard_map/ppermute | solution.py:559
  80.5 21.0 %copy-start.7 = (f32[64,1024]{1,0:T(8,128)}, f32[64,1024]{1,0:T(8,128)S(1)}, u32[]{:S(2)}) copy-start(f32[64,1024]{1,0:T(8,128)S(1)} %collective-permute-done.3.refs_1_.refs_2_) | copy-start | bytes 786436
  80.5 34.1 %collective-permute-start.10 = (f32[64,1024]{1,0:T(8,128)S(1)}, f32[64,1024]{1,0:T(8,128)}, u32[]{:S(2)}, u32[]{:S(2)}) collective-permute-start(f32[64,1024]{1,0:T(8,128)S(1)} %collective-permute-done.3.refs_1_.refs_2_), channel_id=1, source_target_pairs={{0,2},{1,3},{2,0},{3,1},{4,6},{5,7},{6,4},{7,5},{8,10},{9,11},{10,... | collective-permute-start | bytes 786440 | tf_op jit(solution)/shard_map/ppermute | solution.py:538
  82.0 19.5 %copy-start.8 = (f32[64,1024]{1,0:T(8,128)}, f32[64,1024]{1,0:T(8,128)S(1)}, u32[]{:S(2)}) copy-start(f32[64,1024]{1,0:T(8,128)S(1)} %collective-permute-done.2.refs_0_.refs_1_) | copy-start | bytes 786436
  82.0 32.6 %collective-permute-start.9 = (f32[64,1024]{1,0:T(8,128)S(1)}, f32[64,1024]{1,0:T(8,128)}, u32[]{:S(2)}, u32[]{:S(2)}) collective-permute-start(f32[64,1024]{1,0:T(8,128)S(1)} %collective-permute-done.2.refs_0_.refs_1_), channel_id=1, source_target_pairs={{0,2},{1,3},{2,0},{3,1},{4,6},{5,7},{6,4},{7,5},{8,10},{9,11},{10,... | collective-permute-start | bytes 786440 | tf_op jit(solution)/shard_map/ppermute | solution.py:538
  82.6 19.0 %copy-start.9 = (f32[64,1024]{1,0:T(8,128)}, f32[64,1024]{1,0:T(8,128)S(1)}, u32[]{:S(2)}) copy-start(f32[64,1024]{1,0:T(8,128)S(1)} %collective-permute-done.4.refs_2_.refs_3_) | copy-start | bytes 786436
  82.6 32.1 %collective-permute-start.11 = (f32[64,1024]{1,0:T(8,128)S(1)}, f32[64,1024]{1,0:T(8,128)}, u32[]{:S(2)}, u32[]{:S(2)}) collective-permute-start(f32[64,1024]{1,0:T(8,128)S(1)} %collective-permute-done.4.refs_2_.refs_3_), channel_id=1, source_target_pairs={{0,2},{1,3},{2,0},{3,1},{4,6},{5,7},{6,4},{7,5},{8,10},{9,11},{10,... | collective-permute-start | bytes 786440 | tf_op jit(solution)/shard_map/ppermute | solution.py:538
  84.2 5.2 %collective-permute-start.7 = (f32[1,256]{1,0:T(1,128)S(1)}, f32[1,256]{1,0:T(1,128)S(1)}, u32[]{:S(2)}, u32[]{:S(2)}) collective-permute-start(f32[1,256]{1,0:T(1,128)S(1)} %follow.1._.refs_0_), channel_id=1, source_target_pairs={{0,12},{1,13},{2,14},{3,15},{4,0},{5,1},{6,2},{7,3},{8,4},{9,5},{1... | collective-permute-start | bytes 3080 | tf_op jit(solution)/shard_map/ppermute | solution.py:576
  89.4 4.5 %collective-permute-start.6 = (f32[1,256]{1,0:T(1,128)S(1)}, f32[1,256]{1,0:T(1,128)S(1)}, u32[]{:S(2)}, u32[]{:S(2)}) collective-permute-start(f32[1,256]{1,0:T(1,128)S(1)} %follow.1._.refs_0_), channel_id=1, source_target_pairs={{0,8},{1,9},{2,10},{3,11},{4,12},{5,13},{6,14},{7,15},{8,0},{9,1},... | collective-permute-start | bytes 3080 | tf_op jit(solution)/shard_map/ppermute | solution.py:576
  93.8 11.7 %collective-permute-start.5 = (f32[1,256]{1,0:T(1,128)S(1)}, f32[1,256]{1,0:T(1,128)S(1)}, u32[]{:S(2)}, u32[]{:S(2)}) collective-permute-start(f32[1,256]{1,0:T(1,128)S(1)} %follow.1._.refs_0_), channel_id=1, source_target_pairs={{0,4},{1,5},{2,6},{3,7},{4,8},{5,9},{6,10},{7,11},{8,12},{9,13},{1... | collective-permute-start | bytes 3080 | tf_op jit(solution)/shard_map/ppermute | solution.py:576
  95.9 1.6 copy-start.2
  97.5 1.6 copy-start.3
  99.1 6.5 %copy-start.10 = (f32[8]{0:T(128)S(1)}, f32[8]{0:T(128)}, u32[]{:S(2)}) copy-start(f32[8]{0:T(128)} %table_ref.5) | copy-start | bytes 100
  101.5 1.3 copy-start.4
  102.9 1.4 copy-start.5
  104.3 1.3 copy-start.6
  114.5 4.6 %collective-permute-start.13 = (f32[8,64,512]{2,1,0:T(8,128)S(1)}, f32[8,64,512]{2,1,0:T(8,128)S(1)}, u32[]{:S(2)}, u32[]{:S(2)}) collective-permute-start(f32[8,64,512]{2,1,0:T(8,128)S(1)} %get-tuple-element.45), channel_id=1, source_target_pairs={{0,1},{1,0},{2,3},{3,2},{4,5},{5,4},{6,7},{7,6},{8,9},{9,8},{10,11... | collective-permute-start | bytes 3145736 | tf_op jit(solution)/shard_map/ppermute | solution.py:592
  118.6 3.6 %collective-permute-start.12 = (f32[8,64,512]{2,1,0:T(8,128)S(1)}, f32[8,64,512]{2,1,0:T(8,128)S(1)}, u32[]{:S(2)}, u32[]{:S(2)}) collective-permute-start(f32[8,64,512]{2,1,0:T(8,128)S(1)} %get-tuple-element.43), channel_id=1, source_target_pairs={{0,1},{1,0},{2,3},{3,2},{4,5},{5,4},{6,7},{7,6},{8,9},{9,8},{10,11... | collective-permute-start | bytes 3145736 | tf_op jit(solution)/shard_map/ppermute | solution.py:592
  128.4 2.7 %collective-permute-start.14 = (f32[8,64,512]{2,1,0:T(8,128)S(1)}, f32[8,64,512]{2,1,0:T(8,128)S(1)}, u32[]{:S(2)}, u32[]{:S(2)}) collective-permute-start(f32[8,64,512]{2,1,0:T(8,128)S(1)} %shard_map.111), channel_id=1, source_target_pairs={{0,1},{1,0},{2,3},{3,2},{4,5},{5,4},{6,7},{7,6},{8,9},{9,8},{10,11... | collective-permute-start | bytes 3145736 | tf_op jit(solution)/shard_map/ppermute | solution.py:592
  128.5 2.6 %collective-permute-start.15 = (f32[8,128]{1,0:T(8,128)S(1)}, f32[8,128]{1,0:T(8,128)S(1)}, u32[]{:S(2)}, u32[]{:S(2)}) collective-permute-start(f32[8,128]{1,0:T(8,128)S(1)} %get-tuple-element.59.own_ref.one_ref), channel_id=1, source_target_pairs={{0,1},{1,0},{2,3},{3,2},{4,5},{5,4},{6,7},{7,6},{8,9},{9,8},{10,11... | collective-permute-start | bytes 12296 | tf_op jit(solution)/shard_map/ppermute | solution.py:592
  136.5 3.7 %collective-permute-start.17 = (f32[8,64,512]{2,1,0:T(8,128)S(1)}, f32[8,64,512]{2,1,0:T(8,128)S(1)}, u32[]{:S(2)}, u32[]{:S(2)}) collective-permute-start(f32[8,64,512]{2,1,0:T(8,128)S(1)} %get-tuple-element.64), channel_id=1, source_target_pairs={{0,1},{1,0},{2,3},{3,2},{4,5},{5,4},{6,7},{7,6},{8,9},{9,8},{10,11... | collective-permute-start | bytes 3145736 | tf_op jit(solution)/shard_map/ppermute | solution.py:592
  139.7 3.4 %collective-permute-start.16 = (f32[8,64,512]{2,1,0:T(8,128)S(1)}, f32[8,64,512]{2,1,0:T(8,128)S(1)}, u32[]{:S(2)}, u32[]{:S(2)}) collective-permute-start(f32[8,64,512]{2,1,0:T(8,128)S(1)} %get-tuple-element.62), channel_id=1, source_target_pairs={{0,1},{1,0},{2,3},{3,2},{4,5},{5,4},{6,7},{7,6},{8,9},{9,8},{10,11... | collective-permute-start | bytes 3145736 | tf_op jit(solution)/shard_map/ppermute | solution.py:592
  159.4 95.8 %copy-start.1 = (f32[2,4,64,1024]{3,2,1,0:T(8,128)S(1)}, f32[2,4,64,1024]{3,2,1,0:T(8,128)}, u32[]{:S(2)}) copy-start(f32[2,4,64,1024]{3,2,1,0:T(8,128)} %right_ref.3) | copy-start | bytes 6291460

commit v11 on v9

--- a/solution.py
+++ b/solution.py
@@ -165,8 +165,12 @@
         out_refs[at][...] = noise
 
 
-def follow_kernel(value_ref, *refs):
-    refs[-1][...] = value_ref[...]
+def join_kernel(place_ref, value_ref, *refs):
+    parts, (joined_ref, out_ref) = refs[:-2], refs[-2:]
+    planes = len(parts)
+    for by, part in enumerate(parts):
+        joined_ref[(place_ref[2] + planes - by) % planes] = part[...]
+    out_ref[...] = value_ref[...]
 
 
 def prepare_kernel(
@@ -234,20 +238,17 @@
     wide_refs, refs, outs = refs[:-13], refs[-7:], refs[-13:-7]
     start_ref, weight_ref, column_ref, keep_ref, send_ref, sum_ref = outs
     turned_ref, basis_ref, kernel_ref, second_ref, scratch_ref, field_ref, done = refs
-    middle = turned_ref.shape[0] // 2
-    upper, lower = pl.ds(0, middle), pl.ds(middle, middle)
     copies = copy_into(
         (
             (field_hbm, field_ref),
-            (turned_hbm.at[upper], turned_ref.at[upper]),
-            (turned_hbm.at[lower], turned_ref.at[lower]),
+            (turned_hbm, turned_ref),
             (basis_hbm, basis_ref),
             (kernel_hbm, kernel_ref),
             (second_hbm, second_ref),
         ),
         done,
     )
-    for copy in copies[:3]:
+    for copy in copies[:2]:
         copy.start()
     mean = functools.reduce(jnp.add, [table_ref[at] for at in range(NCLASS)]) * (1.0 / NCLASS)
     height, width = start_ref.shape
@@ -265,19 +266,18 @@
     copies[0].wait()
     field = field_ref[...].reshape(height, width)
     copies[1].wait()
-    copies[2].wait()
-    for copy in copies[3:]:
+    for copy in copies[2:]:
         copy.start()
     spectral = times_left(turned_ref[...], field)
     weighted = spectral * weight_ref[...]
     start_ref[...] = field
     store_sums(sum_ref, [fold(spectral * weighted)])
-    copies[3].wait()
+    copies[2].wait()
     column = times_left(basis_ref[...], weighted)
     column_ref[...] = column
     split_rows(place_ref, column, scratch_ref, keep_ref, send_ref)
+    copies[3].wait()
     copies[4].wait()
-    copies[5].wait()
 
 
 def next_column_kernel(
@@ -350,17 +350,12 @@
     return result[: field.shape[0]] + (result[field.shape[0] :] + small)
 
 
-def first_row_kernel(place_ref, keep_ref, got_ref, basis_ref, *refs):
-    parts, (z_ref, noise_ref, scratch_ref, done) = refs[:-4], refs[-4:]
-    planes = len(parts) // 2
-    samples = z_ref.shape[0] // planes
-    copies = []
-    for by in range(planes):
-        row = (place_ref[2] + planes - by) % planes
-        for at, part in enumerate((parts[by], parts[planes + by])):
-            block = row * samples + (place_ref[1] + at) % samples
-            here = done.at[2 * by + at]
-            copies.append(pltpu.make_async_copy(part, noise_ref.at[block], here))
+def first_row_kernel(place_ref, keep_ref, got_ref, basis_ref, near_hbm, far_hbm, *refs):
+    z_ref, noise_ref, scratch_ref, done = refs
+    sample = place_ref[1]
+    copies = copy_into(
+        ((near_hbm, noise_ref.at[:, sample]), (far_hbm, noise_ref.at[:, 1 - sample])), done
+    )
     for copy in copies:
         copy.start()
     row_kernel(place_ref, keep_ref, got_ref, basis_ref, z_ref, scratch_ref)
@@ -526,8 +521,6 @@
     rest = noise_of(others)
     for by, value in zip(others, rest):
         near[by] = plane_shift(value, by) if by else value
-    far = [lax.ppermute(value, "mode", sample_swap) for value in near]
-    noise = (*near, *far)
 
     outgoing = pl.pallas_call(
         outgoing_kernel,
@@ -554,21 +547,22 @@
             jnp.concatenate([eigen, other], axis=1),
             jnp.concatenate([other, eigen], axis=1),
         )
-    eigen = pl.pallas_call(
-        follow_kernel,
-        in_specs=[pl.BlockSpec(memory_space=pltpu.VMEM)]
-        + [pl.BlockSpec(memory_space=pl.ANY)] * (planes - 1),
-        out_specs=pl.BlockSpec(memory_space=pltpu.VMEM),
-        out_shape=shape_of(*eigen.shape),
-        compiler_params=pltpu.CompilerParams(vmem_limit_bytes=1024 * 1024),
-        name="follow",
-    )(eigen, *near[1:])
+    near, eigen = pl.pallas_call(
+        join_kernel,
+        grid=(1,),
+        in_specs=[smem, full(*eigen.shape)] + [full(rows, width)] * planes,
+        out_specs=[whole_out(planes, rows, width), whole_out(*eigen.shape)],
+        out_shape=[shape_of(planes, rows, width), shape_of(*eigen.shape)],
+        compiler_params=params(1, 58),
+        name="join",
+    )(place, eigen, *near)
+    far = lax.ppermute(near, "mode", sample_swap)
     shifted = [eigen] + [
         lax.ppermute(eigen, "mode", [(at, (at + by * unit) % groups) for at in range(groups)])
         for by in range(1, planes)
     ]
     bf16_square = jax.ShapeDtypeStruct((height, height), BF16)
-    turned, high, low, tall_eigen = pl.pallas_call(
+    prepare = pl.pallas_call(
         prepare_kernel,
         grid=(1,),
         in_specs=[full(height, height), full(width, width), full(width, width), full(1, height)]
@@ -577,7 +571,10 @@
         out_shape=[bf16_square] * 3 + [shape_of(height, 128)],
         compiler_params=params(1, 24),
         name="prepare",
-    )(basis_first, basis_second, kernel_second, eigen_first.reshape(1, -1), eigen)
+    )
+    turned, high, low, tall_eigen = prepare(
+        basis_first, basis_second, kernel_second, eigen_first.reshape(1, -1), eigen
+    )
 
     def swap(value):
         return lax.ppermute(value, "mode", core_swap)
@@ -619,7 +616,7 @@
         + [hbm] * 5
         + [full(height, 128)]
         + [full(*value.shape) for value in shifted],
-        [pltpu.VMEM((groups, rows, half), F32), pltpu.SemaphoreType.DMA((6,))],
+        [pltpu.VMEM((groups, rows, half), F32), pltpu.SemaphoreType.DMA((5,))],
         16,
         4,
     )
@@ -638,13 +635,11 @@
     inputs = (place, keep, got, basis_second)
     z_field, noise = call(
         first_row_kernel,
-        (*inputs, *(in_hbm(value) for value in noise)),
-        (whole, whole),
+        (*inputs, in_hbm(near), in_hbm(far)),
+        (whole, (planes, samples, rows, width)),
         flat,
-        [smem]
-        + [full(*value.shape) for value in inputs[1:]]
-        + [hbm] * len(noise),
-        [pltpu.SemaphoreType.DMA((len(noise),))],
+        [smem] + [full(*value.shape) for value in inputs[1:]] + [hbm] * 2,
+        [pltpu.SemaphoreType.DMA((2,))],
     )
     image, pair_sum = call(
         first_image_kernel,

time: 277 us -> 256 us (0.924)
  waiting for transfers between devices: 73.2 us -> 53.3 us
  starting transfers between devices: 30.4 us -> 26.7 us
    ppermute x4 -> x1, waiting for transfers between devices: 20.2 us -> 0.83 us  [paired_body(): far = lax.ppermute(near, 'mode', sample_swap)]
    ppermute x4 -> x1, starting transfers between devices: 4.97 us -> 1.46 us  [paired_body(): far = lax.ppermute(near, 'mode', sample_swap)]
    unnamed x38 -> x32, local copies, waits for them, and re-layouts: 8.65 us -> 9.39 us
  transfers between devices with their start and end apart: 19 -> 16, of which waited for: 7 -> 4; matrix products, arithmetic and copies ran while one was open for 0% -> 1% of each run, Pallas kernels for 8% -> 12%
where the time goes in v11:
time: 256 us; the launch traced here: 255 us
  blocking collectives  107 us (42%)
  Pallas kernels  56.2 us (22%)
  waiting for transfers between devices  53.3 us (21%)
  starting transfers between devices  26.7 us (10%)
  local copies, waits for them, and re-layouts  9.39 us (4%)
    all_to_all x1, blocking collectives, paired_body(): lax.all_to_all(answer, 'mode', split_axis=0, concat_axis=0, axis_index_gr...  95.8 us
    ppermute x3, waiting for transfers between devices, plane_shift(): return lax.ppermute(value, 'mode', pairs)  50 us
    pallas_call x10, Pallas kernels, call(): pl.pallas_call(kernel, grid=(1,), in_specs=specs or [smem] + [full(*value...  37.4 us
    all_to_all x1, blocking collectives, paired_body(): sums = lax.all_to_all(sums, 'mode', split_axis=0, concat_axis=0, tiled=True)  11.7 us
    unnamed x32, local copies, waits for them, and re-layouts  9.39 us
    all_to_all x1, starting transfers between devices, paired_body(): lax.all_to_all(outgoing.reshape(groups, rows, half), 'mode', split_axis=0...  7.6 us
    ppermute x3, starting transfers between devices, paired_body(): lax.ppermute(eigen, 'mode', [(at, (at + by * unit) % groups) for at in ra...  7.53 us
    ppermute x3, starting transfers between devices, plane_shift(): return lax.ppermute(value, 'mode', pairs)  6.42 us
  transfers between devices with their start and end apart: 16, of which 4 were waited for; matrix products, arithmetic and copies ran while one was open for 1% of the time, Pallas kernels for 12%

profile of v11, /device:TPU:0, one launch (start us, length us, event | category | flops | bytes accessed | tf_op | source)
XLA Modules:
  0.0 255.3 jit_solution(8027597909583786428)
XLA Ops:
  0.6 6.0 %outgoing.1 = f32[4,2,2,64,512]{4,3,2,1,0:T(8,128)} custom-call(f32[2,4,64,1024]{3,2,1,0:T(8,128)} %right_ref.3, bf16[1024,1024]{1,0:T(8,128)(2,1)} %second_hbm.1), custom_call_target="tpu_custom_call" | custom-call | tf_op jit(solution)/shard_map/outgoing/pallas_call | solution.py:525
  6.7 7.6 %all-to-all-start = ((f32[16,64,512]{2,1,0:T(8,128)}), f32[16,64,512]{2,1,0:T(8,128)}, u32[]{:S(2)}, u32[]{:S(2)}) async-start(f32[16,64,512]{2,1,0:T(8,128)} %bitcast.11), calls=%async_computation | async-start | bytes 4194304 | tf_op jit(solution)/shard_map/all_to_all | solution.py:537
  14.7 1.9 shard_map.105
  16.6 2.6 %collective-permute-start.3 = (f32[64,1024]{1,0:T(8,128)S(1)}, f32[64,1024]{1,0:T(8,128)S(1)}, u32[]{:S(2)}, u32[]{:S(2)}) collective-permute-start(f32[64,1024]{1,0:T(8,128)S(1)} %shard_map.105), channel_id=1, source_target_pairs={{0,8},{1,9},{2,10},{3,11},{4,12},{5,13},{6,14},{7,15},{8,0},{9,1},... | collective-permute-start | bytes 786440 | tf_op jit(solution)/shard_map/ppermute | solution.py:515
  19.2 2.0 shard_map.104
  21.9 1.5 collective-permute-start.2
  23.4 2.4 collective-permute-start.4
  26.5 1.5 collective-permute-start.1
  28.0 2.0 collective-permute-done.1
  30.7 50.0 %collective-permute-done.3.refs_2_ = f32[64,1024]{1,0:T(8,128)S(1)} collective-permute-done((f32[64,1024]{1,0:T(8,128)S(1)}, f32[64,1024]{1,0:T(8,128)S(1)}, u32[]{:S(2)}, u32[]{:S(2)}) %collective-permute-start.3) | collective-permute-done | bytes 262176 | tf_op jit(solution)/shard_map/ppermute | solution.py:515
  81.5 2.3 join.1
  83.7 1.5 collective-permute-start.7
  85.2 4.9 %collective-permute-start.6 = (f32[1,256]{1,0:T(1,128)}, f32[1,256]{1,0:T(1,128)S(1)}, u32[]{:S(2)}, u32[]{:S(2)}) collective-permute-start(f32[1,256]{1,0:T(1,128)} %get-tuple-element.40._.refs_0_), channel_id=1, source_target_pairs={{0,8},{1,9},{2,10},{3,11},{4,12},{5,13},{6,14},{7,15},{8,0},{9,1},... | collective-permute-start | bytes 3080 | tf_op jit(solution)/shard_map/ppermute | solution.py:561
  91.3 1.5 collective-permute-start.10
  92.7 1.6 copy-done.2
  94.3 1.6 copy-done.3
  96.6 2.4 prepare.1
  100.3 1.4 copy-done.5
  103.0 7.8 %shard_map.106 = (f32[1024,512]{1,0:T(8,128)S(1)}, f32[1024,512]{1,0:T(8,128)S(1)}, f32[1024,512]{1,0:T(8,128)S(1)}, f32[8,64,512]{2,1,0:T(8,128)S(1)}, f32[8,64...) custom-call(s32[4]{0:T(128)S(1)} %copy-done.8, ...), custom_call_target="tpu_custom_call" | custom-call | tf_op jit(solution)/shard_map/pallas_call | solution.py:583
  110.9 3.0 %shard_map.107 = (f32[8,64,512]{2,1,0:T(8,128)S(1)}, f32[8,64,512]{2,1,0:T(8,128)S(1)}, bf16[1024,1024]{1,0:T(8,128)(2,1)S(1)}, bf16[1024,1024]{1,0:T(8,128)(2,1)S(1)}) custom-call(s32[4]{0:T(128)S(1)} %copy-done.8, f32[1024,512]{1,0:T(8,128)S(1)} %get-tuple-element.43.column_ref, bf16[1024,1024]{1,0:T(8,128)(2,1)S(1)} %get-tuple-element.44.kernel_ref, ...), custom_call_target="tpu_custom_call" | custom-call | tf_op jit(solution)/shard_map/pallas_call | solution.py:583
  115.3 3.0 %shard_map.108 = (f32[8,64,1024]{2,1,0:T(8,128)S(1)}, f32[4,2,64,1024]{3,2,1,0:T(8,128)S(1)}) custom-call(s32[4]{0:T(128)S(1)} %copy-done.8, f32[8,64,512]{2,1,0:T(8,128)S(1)} %get-tuple-element.49.keep_ref, f32[8,64,512]{2,1,0:T(8,128)S(1)} %collective-permute-done.9.got_ref, bf16[1024,1024]{1,0:T(8,128)(2,1)S(1)} %get-tuple-element.51.basis_ref, ...), custom_call_target="tpu_custom_call" | custom-call | tf_op jit(solution)/shard_map/pallas_call | solution.py:583
  118.4 4.4 %shard_map.109 = (f32[8,64,1024]{2,1,0:T(8,128)S(1)}, f32[8,128]{1,0:T(8,128)S(1)}) custom-call(s32[4]{0:T(128)S(1)} %copy-done.8, f32[8,64,512]{2,1,0:T(8,128)S(1)} %get-tuple-element.47.keep_ref, f32[8,64,512]{2,1,0:T(8,128)S(1)} %collective-permute-done.8.got_ref, f32[8,64,1024]{2,1,0:T(8,128)S(1)} %get-tuple-element.53.z_ref, ...), custom_call_target="tpu_custom_call" | custom-call | tf_op jit(solution)/shard_map/pallas_call | solution.py:583
  122.7 1.8 shard_map.111
  125.1 1.8 shard_map.110.held_ref
  127.3 5.4 %shard_map.112 = (f32[1024,512]{1,0:T(8,128)S(1)}, f32[8,64,512]{2,1,0:T(8,128)S(1)}, f32[8,64,512]{2,1,0:T(8,128)S(1)}, f32[8,128]{1,0:T(8,128)S(1)}) custom-call(s32[4]{0:T(128)S(1)} %copy-done.8, f32[8,64,512]{2,1,0:T(8,128)S(1)} %shard_map.110.held_ref, f32[8,64,512]{2,1,0:T(8,128)S(1)} %collective-permute-done.11.got_ref, ...), custom_call_target="tpu_custom_call" | custom-call | tf_op jit(solution)/shard_map/pallas_call | solution.py:583
  132.9 3.0 %shard_map.113 = (f32[8,64,512]{2,1,0:T(8,128)S(1)}, f32[8,64,512]{2,1,0:T(8,128)S(1)}) custom-call(s32[4]{0:T(128)S(1)} %copy-done.8, f32[1024,512]{1,0:T(8,128)S(1)} %get-tuple-element.64.column_ref, bf16[1024,1024]{1,0:T(8,128)(2,1)S(1)} %get-tuple-element.44.kernel_ref), custom_call_target="tpu_custom_call" | custom-call | tf_op jit(solution)/shard_map/pallas_call | solution.py:583
  136.4 3.0 %shard_map.114.z_ref.f_ref = f32[8,64,1024]{2,1,0:T(8,128)S(1)} custom-call(s32[4]{0:T(128)S(1)} %copy-done.8, f32[8,64,512]{2,1,0:T(8,128)S(1)} %get-tuple-element.67.keep_ref, f32[8,64,512]{2,1,0:T(8,128)S(1)} %collective-permute-done.14.got_ref, bf16[1024,1024]{1,0:T(8,128)(2,1)S(1)} %get-tuple-element.51.basis_ref), custom_call_target="tpu_custom_call" | custom-call | tf_op jit(solution)/shard_map/pallas_call | solution.py:583
  139.4 4.2 %shard_map.115 = (f32[8,64,1024]{2,1,0:T(8,128)S(1)}, f32[16,8,128]{2,1,0:T(8,128)S(1)}) custom-call(s32[4]{0:T(128)S(1)} %copy-done.8, f32[8,64,512]{2,1,0:T(8,128)S(1)} %get-tuple-element.65.keep_ref, f32[8,64,512]{2,1,0:T(8,128)S(1)} %collective-permute-done.13.got_ref, f32[8,64,1024]{2,1,0:T(8,128)S(1)} %shard_map.114.z_ref.f_ref, ...), custom_call_target="tpu_custom_call" | custom-call | tf_op jit(solution)/shard_map/pallas_call | solution.py:583
  143.6 11.7 %all_to_all.15.sum_ref = f32[16,8,128]{2,1,0:T(8,128)S(1)} all-to-all(f32[16,8,128]{2,1,0:T(8,128)S(1)} %get-tuple-element.70), channel_id=1, replica_groups=mesh['blocks'=2,'mode'=16] {'mode'}, dimensions={0} | all-to-all | bytes 131072 | tf_op jit(solution)/shard_map/all_to_all | solution.py:698
  155.2 1.6 combine.1
  156.9 95.8 %all_to_all.16.got_ref = f32[8,128,1024]{2,1,0:T(8,128)S(1)} all-to-all(f32[8,128,1024]{2,1,0:T(8,128)S(1)} %combine.1), channel_id=1, replica_groups={{0,2,4,6,8,10,12,14},{1,3,5,7,9,11,13,15},{16,18,20,22,24,26,28,30},{17..., dimensions={0} | all-to-all | bytes 8388608 | tf_op jit(solution)/shard_map/all_to_all | solution.py:711
  252.7 2.6 %finish.1 = (f32[2,4,64,1024]{3,2,1,0:T(8,128)}, f32[2,4,64,1024]{3,2,1,0:T(8,128)}) custom-call(f32[8,128,1024]{2,1,0:T(8,128)S(1)} %all_to_all.16.got_ref, f32[2,4,64,1024]{3,2,1,0:T(8,128)S(1)} %copy-done.1), custom_call_target="tpu_custom_call" | custom-call | tf_op jit(solution)/shard_map/finish/pallas_call | solution.py:722
  (55 shorter events, 10.9 us)
Async XLA Ops:
  6.6 7.6 %copy-start.15 = (f32[64]{0:T(128)S(1)}, f32[64]{0:T(128)}, u32[]{:S(2)}) copy-start(f32[64]{0:T(128)} %param.17) | copy-start | bytes 772
  6.7 96.4 %all-to-all-start = ((f32[16,64,512]{2,1,0:T(8,128)}), f32[16,64,512]{2,1,0:T(8,128)}, u32[]{:S(2)}, u32[]{:S(2)}) async-start(f32[16,64,512]{2,1,0:T(8,128)} %bitcast.11), calls=%async_computation | async-start | bytes 4194304 | tf_op jit(solution)/shard_map/all_to_all | solution.py:537
  14.3 78.5 %copy-start = (bf16[1024,1024]{1,0:T(8,128)(2,1)S(1)}, bf16[1024,1024]{1,0:T(8,128)(2,1)}, u32[]{:S(2)}) copy-start(bf16[1024,1024]{1,0:T(8,128)(2,1)} %second_hbm.1) | copy-start | bytes 6291460
  14.3 78.5 %copy-start.10 = (f32[1024]{0:T(1024)S(1)}, f32[1024]{0:T(1024)}, u32[]{:S(2)}) copy-start(f32[1024]{0:T(1024)} %param.16) | copy-start | bytes 12292
  14.3 12.1 %collective-permute-start = (f32[1,64]{1,0:T(1,128)S(1)}, f32[1,64]{1,0:T(1,128)S(1)}, u32[]{:S(2)}, u32[]{:S(2)}) collective-permute-start(f32[1,64]{1,0:T(1,128)S(1)} %bitcast.12), channel_id=1, source_target_pairs={{0,1},{1,0},{2,3},{3,2},{4,5},{5,4},{6,7},{7,6},{8,9},{9,8},{10,11... | collective-permute-start | bytes 776 | tf_op jit(solution)/shard_map/ppermute | solution.py:543
  16.6 64.0 %collective-permute-start.3 = (f32[64,1024]{1,0:T(8,128)S(1)}, f32[64,1024]{1,0:T(8,128)S(1)}, u32[]{:S(2)}, u32[]{:S(2)}) collective-permute-start(f32[64,1024]{1,0:T(8,128)S(1)} %shard_map.105), channel_id=1, source_target_pairs={{0,8},{1,9},{2,10},{3,11},{4,12},{5,13},{6,14},{7,15},{8,0},{9,1},... | collective-permute-start | bytes 786440 | tf_op jit(solution)/shard_map/ppermute | solution.py:515
  21.2 0.7 copy-start.7
  21.9 58.7 %collective-permute-start.2 = (f32[64,1024]{1,0:T(8,128)S(1)}, f32[64,1024]{1,0:T(8,128)S(1)}, u32[]{:S(2)}, u32[]{:S(2)}) collective-permute-start(f32[64,1024]{1,0:T(8,128)S(1)} %get-tuple-element.38), channel_id=1, source_target_pairs={{0,4},{1,5},{2,6},{3,7},{4,8},{5,9},{6,10},{7,11},{8,12},{9,13},{1... | collective-permute-start | bytes 786440 | tf_op jit(solution)/shard_map/ppermute | solution.py:515
  23.4 57.3 %collective-permute-start.4 = (f32[64,1024]{1,0:T(8,128)S(1)}, f32[64,1024]{1,0:T(8,128)}, u32[]{:S(2)}, u32[]{:S(2)}) collective-permute-start(f32[64,1024]{1,0:T(8,128)S(1)} %get-tuple-element.39), channel_id=1, source_target_pairs={{0,12},{1,13},{2,14},{3,15},{4,0},{5,1},{6,2},{7,3},{8,4},{9,5},{1... | collective-permute-start | bytes 786440 | tf_op jit(solution)/shard_map/ppermute | solution.py:515
  26.5 3.6 %collective-permute-start.1 = (f32[1,128]{1,0:T(1,128)S(1)}, f32[1,128]{1,0:T(1,128)S(1)}, u32[]{:S(2)}, u32[]{:S(2)}) collective-permute-start(f32[1,128]{1,0:T(1,128)S(1)} %broadcast_select_fusion.1), channel_id=1, source_target_pairs={{0,2},{1,3},{2,0},{3,1},{4,6},{5,7},{6,4},{7,5},{8,10},{9,11},{10,... | collective-permute-start | bytes 1544 | tf_op jit(solution)/shard_map/ppermute | solution.py:543
  80.7 0.7 copy-start.13
  80.7 0.8 copy-start.14
  83.7 19.3 %collective-permute-start.7 = (f32[1,256]{1,0:T(1,128)}, f32[1,256]{1,0:T(1,128)S(1)}, u32[]{:S(2)}, u32[]{:S(2)}) collective-permute-start(f32[1,256]{1,0:T(1,128)} %get-tuple-element.40._.refs_0_), channel_id=1, source_target_pairs={{0,12},{1,13},{2,14},{3,15},{4,0},{5,1},{6,2},{7,3},{8,4},{9,5},{1... | collective-permute-start | bytes 3080 | tf_op jit(solution)/shard_map/ppermute | solution.py:561
  85.2 17.8 %collective-permute-start.6 = (f32[1,256]{1,0:T(1,128)}, f32[1,256]{1,0:T(1,128)S(1)}, u32[]{:S(2)}, u32[]{:S(2)}) collective-permute-start(f32[1,256]{1,0:T(1,128)} %get-tuple-element.40._.refs_0_), channel_id=1, source_target_pairs={{0,8},{1,9},{2,10},{3,11},{4,12},{5,13},{6,14},{7,15},{8,0},{9,1},... | collective-permute-start | bytes 3080 | tf_op jit(solution)/shard_map/ppermute | solution.py:561
  90.1 12.9 %collective-permute-start.5 = (f32[1,256]{1,0:T(1,128)}, f32[1,256]{1,0:T(1,128)S(1)}, u32[]{:S(2)}, u32[]{:S(2)}) collective-permute-start(f32[1,256]{1,0:T(1,128)} %get-tuple-element.40._.refs_0_), channel_id=1, source_target_pairs={{0,4},{1,5},{2,6},{3,7},{4,8},{5,9},{6,10},{7,11},{8,12},{9,13},{1... | collective-permute-start | bytes 3080 | tf_op jit(solution)/shard_map/ppermute | solution.py:561
  91.3 24.1 %collective-permute-start.10 = (f32[4,64,1024]{2,1,0:T(8,128)}, f32[4,64,1024]{2,1,0:T(8,128)}, u32[]{:S(2)}, u32[]{:S(2)}) collective-permute-start(f32[4,64,1024]{2,1,0:T(8,128)} %get-tuple-element.52.near_hbm), channel_id=1, source_target_pairs={{0,2},{1,3},{2,0},{3,1},{4,6},{5,7},{6,4},{7,5},{8,10},{9,11},{10,... | collective-permute-start | bytes 3145736 | tf_op jit(solution)/shard_map/ppermute | solution.py:559
  92.7 1.6 copy-start.2
  94.3 1.6 copy-start.3
  95.9 0.7 copy-start.11
  96.6 6.4 %copy-start.8 = (s32[4]{0:T(128)S(1)}, s32[4]{0:T(128)}, u32[]{:S(2)}) copy-start(s32[4]{0:T(128)} %pad_add_fusion.place_ref) | copy-start | bytes 52
  96.6 6.5 %copy-start.9 = (f32[8]{0:T(128)S(1)}, f32[8]{0:T(128)}, u32[]{:S(2)}) copy-start(f32[8]{0:T(128)} %table_ref.5) | copy-start | bytes 100
  96.6 6.5 %copy-start.12 = (f32[1,256]{1,0:T(1,128)S(1)}, f32[1,256]{1,0:T(1,128)}, u32[]{:S(2)}) copy-start(f32[1,256]{1,0:T(1,128)} %get-tuple-element.40._.refs_0_) | copy-start | bytes 3076
  99.0 1.3 copy-start.4
  100.3 1.4 copy-start.5
  101.7 1.3 copy-start.6
  110.8 4.5 %collective-permute-start.9 = (f32[8,64,512]{2,1,0:T(8,128)S(1)}, f32[8,64,512]{2,1,0:T(8,128)S(1)}, u32[]{:S(2)}, u32[]{:S(2)}) collective-permute-start(f32[8,64,512]{2,1,0:T(8,128)S(1)} %get-tuple-element.50), channel_id=1, source_target_pairs={{0,1},{1,0},{2,3},{3,2},{4,5},{5,4},{6,7},{7,6},{8,9},{9,8},{10,11... | collective-permute-start | bytes 3145736 | tf_op jit(solution)/shard_map/ppermute | solution.py:580
  113.9 4.4 %collective-permute-start.8 = (f32[8,64,512]{2,1,0:T(8,128)S(1)}, f32[8,64,512]{2,1,0:T(8,128)S(1)}, u32[]{:S(2)}, u32[]{:S(2)}) collective-permute-start(f32[8,64,512]{2,1,0:T(8,128)S(1)} %get-tuple-element.48), channel_id=1, source_target_pairs={{0,1},{1,0},{2,3},{3,2},{4,5},{5,4},{6,7},{7,6},{8,9},{9,8},{10,11... | collective-permute-start | bytes 3145736 | tf_op jit(solution)/shard_map/ppermute | solution.py:580
  124.5 2.7 %collective-permute-start.11 = (f32[8,64,512]{2,1,0:T(8,128)S(1)}, f32[8,64,512]{2,1,0:T(8,128)S(1)}, u32[]{:S(2)}, u32[]{:S(2)}) collective-permute-start(f32[8,64,512]{2,1,0:T(8,128)S(1)} %shard_map.111), channel_id=1, source_target_pairs={{0,1},{1,0},{2,3},{3,2},{4,5},{5,4},{6,7},{7,6},{8,9},{9,8},{10,11... | collective-permute-start | bytes 3145736 | tf_op jit(solution)/shard_map/ppermute | solution.py:580
  124.6 2.7 %collective-permute-start.12 = (f32[8,128]{1,0:T(8,128)S(1)}, f32[8,128]{1,0:T(8,128)S(1)}, u32[]{:S(2)}, u32[]{:S(2)}) collective-permute-start(f32[8,128]{1,0:T(8,128)S(1)} %get-tuple-element.63.own_ref.one_ref), channel_id=1, source_target_pairs={{0,1},{1,0},{2,3},{3,2},{4,5},{5,4},{6,7},{7,6},{8,9},{9,8},{10,11... | collective-permute-start | bytes 12296 | tf_op jit(solution)/shard_map/ppermute | solution.py:580
  132.7 3.7 %collective-permute-start.14 = (f32[8,64,512]{2,1,0:T(8,128)S(1)}, f32[8,64,512]{2,1,0:T(8,128)S(1)}, u32[]{:S(2)}, u32[]{:S(2)}) collective-permute-start(f32[8,64,512]{2,1,0:T(8,128)S(1)} %get-tuple-element.68), channel_id=1, source_target_pairs={{0,1},{1,0},{2,3},{3,2},{4,5},{5,4},{6,7},{7,6},{8,9},{9,8},{10,11... | collective-permute-start | bytes 3145736 | tf_op jit(solution)/shard_map/ppermute | solution.py:580
  135.9 3.4 %collective-permute-start.13 = (f32[8,64,512]{2,1,0:T(8,128)S(1)}, f32[8,64,512]{2,1,0:T(8,128)S(1)}, u32[]{:S(2)}, u32[]{:S(2)}) collective-permute-start(f32[8,64,512]{2,1,0:T(8,128)S(1)} %get-tuple-element.66), channel_id=1, source_target_pairs={{0,1},{1,0},{2,3},{3,2},{4,5},{5,4},{6,7},{7,6},{8,9},{9,8},{10,11... | collective-permute-start | bytes 3145736 | tf_op jit(solution)/shard_map/ppermute | solution.py:580
  156.9 95.8 %copy-start.1 = (f32[2,4,64,1024]{3,2,1,0:T(8,128)S(1)}, f32[2,4,64,1024]{3,2,1,0:T(8,128)}, u32[]{:S(2)}) copy-start(f32[2,4,64,1024]{3,2,1,0:T(8,128)} %right_ref.3) | copy-start | bytes 6291460

commit v12 on v11

--- a/solution.py
+++ b/solution.py
@@ -125,12 +125,19 @@
     return result[: value.shape[0]] + result[value.shape[0] :]
 
 
+def side_by_side(value):
+    return jnp.concatenate(split(value), axis=1)
+
+
+def times_both(matrix, both):
+    width = both.shape[1] // 2
+    dims = (((1,), (0,)), ((), ()))
+    result = lax.dot_general(matrix, both, dims, preferred_element_type=F32)
+    return result[:, :width] + result[:, width:]
+
+
 def times_left(matrix, value):
-    high, low = split(value)
-    dims = (((1,), (0,)), ((), ()))
-    both = jnp.concatenate([high, low], axis=1)
-    result = lax.dot_general(matrix, both, dims, preferred_element_type=F32)
-    return result[:, : value.shape[1]] + result[:, value.shape[1] :]
+    return times_both(matrix, side_by_side(value))
 
 
 def fold(value):
@@ -174,10 +181,19 @@
 
 
 def prepare_kernel(
-    first_ref, second_ref, kernel_ref, eigen_ref, _, turned_ref, high_ref, low_ref, tall_ref
+    first_ref,
+    second_ref,
+    kernel_ref,
+    _,
+    upper_ref,
+    lower_ref,
+    high_ref,
+    low_ref,
 ):
-    turned_ref[...] = first_ref[...].T
-    tall_ref[...] = jnp.broadcast_to(eigen_ref[...], tall_ref.shape[::-1]).T
+    turned = first_ref[...].T
+    middle = upper_ref.shape[0]
+    upper_ref[...] = turned[:middle]
+    lower_ref[...] = turned[middle:]
     dims = (((1,), (0,)), ((), ()))
     product = lax.dot_general(
         kernel_ref[...], second_ref[...], dims, preferred_element_type=F32
@@ -228,20 +244,21 @@
     place_ref,
     table_ref,
     field_hbm,
-    turned_hbm,
+    lower_hbm,
     basis_hbm,
     kernel_hbm,
     second_hbm,
-    tall_ref,
+    upper_ref,
+    eigen_ref,
     *refs,
 ):
     wide_refs, refs, outs = refs[:-13], refs[-7:], refs[-13:-7]
     start_ref, weight_ref, column_ref, keep_ref, send_ref, sum_ref = outs
-    turned_ref, basis_ref, kernel_ref, second_ref, scratch_ref, field_ref, done = refs
+    lower_ref, basis_ref, kernel_ref, second_ref, scratch_ref, field_ref, done = refs
     copies = copy_into(
         (
             (field_hbm, field_ref),
-            (turned_hbm, turned_ref),
+            (lower_hbm, lower_ref),
             (basis_hbm, basis_ref),
             (kernel_hbm, kernel_ref),
             (second_hbm, second_ref),
@@ -252,6 +269,7 @@
         copy.start()
     mean = functools.reduce(jnp.add, [table_ref[at] for at in range(NCLASS)]) * (1.0 / NCLASS)
     height, width = start_ref.shape
+    tall = jnp.broadcast_to(eigen_ref[...], (128, height)).T
     planes = len(wide_refs)
     part = wide_refs[0].shape[1]
     for block in range(width // part):
@@ -262,13 +280,15 @@
             wide = jnp.where(here, wide_ref[...], wide)
         for at in range(0, part, 128):
             lanes = slice(block * part + at, block * part + at + 128)
-            weight_ref[:, lanes] = 1.0 / (tall_ref[...] * wide[:, at : at + 128] + mean)
+            weight_ref[:, lanes] = 1.0 / (tall * wide[:, at : at + 128] + mean)
     copies[0].wait()
     field = field_ref[...].reshape(height, width)
+    both = side_by_side(field)
+    above = times_both(upper_ref[...], both)
     copies[1].wait()
     for copy in copies[2:]:
         copy.start()
-    spectral = times_left(turned_ref[...], field)
+    spectral = jnp.concatenate([above, times_both(lower_ref[...], both)], axis=0)
     weighted = spectral * weight_ref[...]
     start_ref[...] = field
     store_sums(sum_ref, [fold(spectral * weighted)])
@@ -286,7 +306,8 @@
     got_ref,
     start_ref,
     weight_ref,
-    turned_ref,
+    upper_ref,
+    lower_ref,
     basis_ref,
     own_ref,
     other_ref,
@@ -304,7 +325,9 @@
     proper = (gamma > 0) & (curvature > 0)
     step = jnp.where(proper, gamma / jnp.where(proper, curvature, 1.0), 1.0)
     field = start_ref[...] - step * scratch_ref[...].reshape(start_ref.shape)
-    spectral = times_left(turned_ref[...], field)
+    both = side_by_side(field)
+    halves = [times_both(half_ref[...], both) for half_ref in (upper_ref, lower_ref)]
+    spectral = jnp.concatenate(halves, axis=0)
     weighted = spectral * weight_ref[...]
     store_sums(sum_ref, [fold(spectral * weighted), jnp.broadcast_to(step, (1, 128))])
     column = times_left(basis_ref[...], weighted)
@@ -562,31 +585,30 @@
         for by in range(1, planes)
     ]
     bf16_square = jax.ShapeDtypeStruct((height, height), BF16)
+    bf16_half = jax.ShapeDtypeStruct((height // 2, height), BF16)
     prepare = pl.pallas_call(
         prepare_kernel,
         grid=(1,),
-        in_specs=[full(height, height), full(width, width), full(width, width), full(1, height)]
+        in_specs=[full(height, height), full(width, width), full(width, width)]
         + [pl.BlockSpec(memory_space=pl.ANY)],
-        out_specs=[whole_out(height, height)] * 3 + [whole_out(height, 128)],
-        out_shape=[bf16_square] * 3 + [shape_of(height, 128)],
+        out_specs=[whole_out(height // 2, height)] * 2 + [whole_out(height, height)] * 2,
+        out_shape=[bf16_half] * 2 + [bf16_square] * 2,
         compiler_params=params(1, 24),
         name="prepare",
     )
-    turned, high, low, tall_eigen = prepare(
-        basis_first, basis_second, kernel_second, eigen_first.reshape(1, -1), eigen
-    )
+    upper, lower, high, low = prepare(basis_first, basis_second, kernel_second, eigen)
 
     def swap(value):
         return lax.ppermute(value, "mode", core_swap)
 
-    def call(kernel, inputs, shapes, scratch_shape, specs=None, more=(), mebibytes=12, matrices=0):
+    def call(kernel, inputs, shapes, scratch_shape, specs=None, more=(), mebibytes=12, matrices=()):
         return pl.pallas_call(
             kernel,
             grid=(1,),
             in_specs=specs or [smem] + [full(*value.shape) for value in inputs[1:]],
             out_specs=[whole_out(*shape) for shape in shapes]
-            + [whole_out(height, height)] * matrices,
-            out_shape=[shape_of(*shape) for shape in shapes] + [bf16_square] * matrices,
+            + [whole_out(*value.shape) for value in matrices],
+            out_shape=[shape_of(*shape) for shape in shapes] + list(matrices),
             scratch_shapes=[*([pltpu.VMEM(scratch_shape, F32)] if scratch_shape else []), *more],
             compiler_params=params(1, mebibytes),
         )(*inputs)
@@ -598,27 +620,25 @@
     flat = (blocks * rows, width)
     sums_shape = (8, 128)
 
-    (start, weights, column, keep, send, sum_one, turned, *squares) = call(
+    (start, weights, column, keep, send, sum_one, lower, *squares) = call(
         first_column_kernel,
         (
             place,
             noise_table,
-            *(
-                in_hbm(value)
-                for value in (arrived, turned, basis_first, kernel_first, basis_second)
-            ),
-            tall_eigen,
+            *(in_hbm(value) for value in (arrived, lower, basis_first, kernel_first, basis_second)),
+            upper,
+            eigen_first.reshape(1, -1),
             *shifted,
         ),
         (tile, tile, tile, piece, piece, sums_shape),
         by_rows,
         [smem, smem]
         + [hbm] * 5
-        + [full(height, 128)]
+        + [full(height // 2, height), full(1, height)]
         + [full(*value.shape) for value in shifted],
         [pltpu.VMEM((groups, rows, half), F32), pltpu.SemaphoreType.DMA((5,))],
         16,
-        4,
+        [bf16_half] + [bf16_square] * 3,
     )
     basis_first, kernel_first, basis_second = squares
     got = swap(send)
@@ -629,7 +649,7 @@
         by_rows,
         [smem, full(*tile), full(height, height), hbm, hbm],
         [pltpu.SemaphoreType.DMA((2,))],
-        matrices=2,
+        matrices=[bf16_square] * 2,
     )
     image_got = swap(image_send)
     inputs = (place, keep, got, basis_second)
@@ -665,7 +685,8 @@
             back_got,
             start,
             weights,
-            turned,
+            upper,
+            lower,
             basis_first,
             pair_sum,
             pair_other,

time: 256 us -> 256 us (level)
  no operation moved by 1% of the time
where the time goes in v12:
time: 256 us; the launch traced here: 255 us
  blocking collectives  107 us (42%)
  Pallas kernels  56 us (22%)
  waiting for transfers between devices  53.8 us (21%)
  starting transfers between devices  26.7 us (10%)
  local copies, waits for them, and re-layouts  9 us (4%)
    all_to_all x1, blocking collectives, paired_body(): lax.all_to_all(answer, 'mode', split_axis=0, concat_axis=0, axis_index_gr...  95.8 us
    ppermute x3, waiting for transfers between devices, plane_shift(): return lax.ppermute(value, 'mode', pairs)  50 us
    pallas_call x10, Pallas kernels, call(): pl.pallas_call(kernel, grid=(1,), in_specs=specs or [smem] + [full(*value...  37.2 us
    all_to_all x1, blocking collectives, paired_body(): sums = lax.all_to_all(sums, 'mode', split_axis=0, concat_axis=0, tiled=True)  11.7 us
    unnamed x32, local copies, waits for them, and re-layouts  9 us
    all_to_all x1, starting transfers between devices, paired_body(): lax.all_to_all(outgoing.reshape(groups, rows, half), 'mode', split_axis=0...  7.6 us
    ppermute x3, starting transfers between devices, paired_body(): lax.ppermute(eigen, 'mode', [(at, (at + by * unit) % groups) for at in ra...  7.53 us
    ppermute x3, starting transfers between devices, plane_shift(): return lax.ppermute(value, 'mode', pairs)  6.42 us
  transfers between devices with their start and end apart: 16, of which 4 were waited for; matrix products, arithmetic and copies ran while one was open for 1% of the time, Pallas kernels for 12%

profile of v12, /device:TPU:0, one launch (start us, length us, event | category | flops | bytes accessed | tf_op | source)
XLA Modules:
  0.0 255.3 jit_solution(13494722856407395749)
XLA Ops:
  0.6 6.0 %outgoing.1 = f32[4,2,2,64,512]{4,3,2,1,0:T(8,128)} custom-call(f32[2,4,64,1024]{3,2,1,0:T(8,128)} %right_ref.3, bf16[1024,1024]{1,0:T(8,128)(2,1)} %second_hbm.1), custom_call_target="tpu_custom_call" | custom-call | tf_op jit(solution)/shard_map/outgoing/pallas_call | solution.py:548
  6.7 7.6 %all-to-all-start = ((f32[16,64,512]{2,1,0:T(8,128)}), f32[16,64,512]{2,1,0:T(8,128)}, u32[]{:S(2)}, u32[]{:S(2)}) async-start(f32[16,64,512]{2,1,0:T(8,128)} %bitcast.11), calls=%async_computation | async-start | bytes 4194304 | tf_op jit(solution)/shard_map/all_to_all | solution.py:560
  14.7 1.9 shard_map.105
  16.6 2.6 %collective-permute-start.3 = (f32[64,1024]{1,0:T(8,128)S(1)}, f32[64,1024]{1,0:T(8,128)S(1)}, u32[]{:S(2)}, u32[]{:S(2)}) collective-permute-start(f32[64,1024]{1,0:T(8,128)S(1)} %shard_map.105), channel_id=1, source_target_pairs={{0,8},{1,9},{2,10},{3,11},{4,12},{5,13},{6,14},{7,15},{8,0},{9,1},... | collective-permute-start | bytes 786440 | tf_op jit(solution)/shard_map/ppermute | solution.py:538
  19.2 2.0 shard_map.104
  21.9 1.5 collective-permute-start.2
  23.4 2.4 collective-permute-start.4
  26.5 1.5 collective-permute-start.1
  28.0 2.0 collective-permute-done.1
  30.7 50.0 %collective-permute-done.3.refs_2_ = f32[64,1024]{1,0:T(8,128)S(1)} collective-permute-done((f32[64,1024]{1,0:T(8,128)S(1)}, f32[64,1024]{1,0:T(8,128)S(1)}, u32[]{:S(2)}, u32[]{:S(2)}) %collective-permute-start.3) | collective-permute-done | bytes 262176 | tf_op jit(solution)/shard_map/ppermute | solution.py:538
  81.5 2.3 join.1
  83.8 1.5 collective-permute-start.7
  85.2 4.9 %collective-permute-start.6 = (f32[1,256]{1,0:T(1,128)}, f32[1,256]{1,0:T(1,128)S(1)}, u32[]{:S(2)}, u32[]{:S(2)}) collective-permute-start(f32[1,256]{1,0:T(1,128)} %get-tuple-element.40._.refs_0_), channel_id=1, source_target_pairs={{0,8},{1,9},{2,10},{3,11},{4,12},{5,13},{6,14},{7,15},{8,0},{9,1},... | collective-permute-start | bytes 3080 | tf_op jit(solution)/shard_map/ppermute | solution.py:584
  91.3 1.5 collective-permute-start.10
  92.8 1.6 copy-done.2
  94.3 1.6 copy-done.3
  96.6 2.4 prepare.1
  102.7 7.6 %shard_map.106 = (f32[1024,512]{1,0:T(8,128)S(1)}, f32[1024,512]{1,0:T(8,128)S(1)}, f32[1024,512]{1,0:T(8,128)S(1)}, f32[8,64,512]{2,1,0:T(8,128)S(1)}, f32[8,64...) custom-call(s32[4]{0:T(128)S(1)} %copy-done.8, ...), custom_call_target="tpu_custom_call" | custom-call | tf_op jit(solution)/shard_map/pallas_call | solution.py:605
  110.4 3.0 %shard_map.107 = (f32[8,64,512]{2,1,0:T(8,128)S(1)}, f32[8,64,512]{2,1,0:T(8,128)S(1)}, bf16[1024,1024]{1,0:T(8,128)(2,1)S(1)}, bf16[1024,1024]{1,0:T(8,128)(2,1)S(1)}) custom-call(s32[4]{0:T(128)S(1)} %copy-done.8, f32[1024,512]{1,0:T(8,128)S(1)} %get-tuple-element.43.column_ref, bf16[1024,1024]{1,0:T(8,128)(2,1)S(1)} %get-tuple-element.44.kernel_ref, ...), custom_call_target="tpu_custom_call" | custom-call | tf_op jit(solution)/shard_map/pallas_call | solution.py:605
  114.0 1.4 collective-permute-done.10.far_hbm
  115.4 3.0 %shard_map.108 = (f32[8,64,1024]{2,1,0:T(8,128)S(1)}, f32[4,2,64,1024]{3,2,1,0:T(8,128)S(1)}) custom-call(s32[4]{0:T(128)S(1)} %copy-done.8, f32[8,64,512]{2,1,0:T(8,128)S(1)} %get-tuple-element.49.keep_ref, f32[8,64,512]{2,1,0:T(8,128)S(1)} %collective-permute-done.9.got_ref, bf16[1024,1024]{1,0:T(8,128)(2,1)S(1)} %get-tuple-element.51.basis_ref, ...), custom_call_target="tpu_custom_call" | custom-call | tf_op jit(solution)/shard_map/pallas_call | solution.py:605
  118.4 4.1 %shard_map.109 = (f32[8,64,1024]{2,1,0:T(8,128)S(1)}, f32[8,128]{1,0:T(8,128)S(1)}) custom-call(s32[4]{0:T(128)S(1)} %copy-done.8, f32[8,64,512]{2,1,0:T(8,128)S(1)} %get-tuple-element.47.keep_ref, f32[8,64,512]{2,1,0:T(8,128)S(1)} %collective-permute-done.8.got_ref, f32[8,64,1024]{2,1,0:T(8,128)S(1)} %get-tuple-element.53.z_ref, ...), custom_call_target="tpu_custom_call" | custom-call | tf_op jit(solution)/shard_map/pallas_call | solution.py:605
  122.6 2.0 shard_map.111
  125.1 1.8 shard_map.110.held_ref
  127.3 5.4 %shard_map.112 = (f32[1024,512]{1,0:T(8,128)S(1)}, f32[8,64,512]{2,1,0:T(8,128)S(1)}, f32[8,64,512]{2,1,0:T(8,128)S(1)}, f32[8,128]{1,0:T(8,128)S(1)}) custom-call(s32[4]{0:T(128)S(1)} %copy-done.8, f32[8,64,512]{2,1,0:T(8,128)S(1)} %shard_map.110.held_ref, f32[8,64,512]{2,1,0:T(8,128)S(1)} %collective-permute-done.11.got_ref, ...), custom_call_target="tpu_custom_call" | custom-call | tf_op jit(solution)/shard_map/pallas_call | solution.py:605
  132.9 3.0 %shard_map.113 = (f32[8,64,512]{2,1,0:T(8,128)S(1)}, f32[8,64,512]{2,1,0:T(8,128)S(1)}) custom-call(s32[4]{0:T(128)S(1)} %copy-done.8, f32[1024,512]{1,0:T(8,128)S(1)} %get-tuple-element.64.column_ref, bf16[1024,1024]{1,0:T(8,128)(2,1)S(1)} %get-tuple-element.44.kernel_ref), custom_call_target="tpu_custom_call" | custom-call | tf_op jit(solution)/shard_map/pallas_call | solution.py:605
  136.4 3.0 %shard_map.114.z_ref.f_ref = f32[8,64,1024]{2,1,0:T(8,128)S(1)} custom-call(s32[4]{0:T(128)S(1)} %copy-done.8, f32[8,64,512]{2,1,0:T(8,128)S(1)} %get-tuple-element.67.keep_ref, f32[8,64,512]{2,1,0:T(8,128)S(1)} %collective-permute-done.14.got_ref, bf16[1024,1024]{1,0:T(8,128)(2,1)S(1)} %get-tuple-element.51.basis_ref), custom_call_target="tpu_custom_call" | custom-call | tf_op jit(solution)/shard_map/pallas_call | solution.py:605
  139.4 4.2 %shard_map.115 = (f32[8,64,1024]{2,1,0:T(8,128)S(1)}, f32[16,8,128]{2,1,0:T(8,128)S(1)}) custom-call(s32[4]{0:T(128)S(1)} %copy-done.8, f32[8,64,512]{2,1,0:T(8,128)S(1)} %get-tuple-element.65.keep_ref, f32[8,64,512]{2,1,0:T(8,128)S(1)} %collective-permute-done.13.got_ref, f32[8,64,1024]{2,1,0:T(8,128)S(1)} %shard_map.114.z_ref.f_ref, ...), custom_call_target="tpu_custom_call" | custom-call | tf_op jit(solution)/shard_map/pallas_call | solution.py:605
  143.6 11.7 %all_to_all.15.sum_ref = f32[16,8,128]{2,1,0:T(8,128)S(1)} all-to-all(f32[16,8,128]{2,1,0:T(8,128)S(1)} %get-tuple-element.70), channel_id=1, replica_groups=mesh['blocks'=2,'mode'=16] {'mode'}, dimensions={0} | all-to-all | bytes 131072 | tf_op jit(solution)/shard_map/all_to_all | solution.py:719
  155.3 1.6 combine.1
  156.9 95.8 %all_to_all.16.got_ref = f32[8,128,1024]{2,1,0:T(8,128)S(1)} all-to-all(f32[8,128,1024]{2,1,0:T(8,128)S(1)} %combine.1), channel_id=1, replica_groups={{0,2,4,6,8,10,12,14},{1,3,5,7,9,11,13,15},{16,18,20,22,24,26,28,30},{17..., dimensions={0} | all-to-all | bytes 8388608 | tf_op jit(solution)/shard_map/all_to_all | solution.py:732
  252.7 2.6 %finish.1 = (f32[2,4,64,1024]{3,2,1,0:T(8,128)}, f32[2,4,64,1024]{3,2,1,0:T(8,128)}) custom-call(f32[8,128,1024]{2,1,0:T(8,128)S(1)} %all_to_all.16.got_ref, f32[2,4,64,1024]{3,2,1,0:T(8,128)S(1)} %copy-done.1), custom_call_target="tpu_custom_call" | custom-call | tf_op jit(solution)/shard_map/finish/pallas_call | solution.py:743
  (55 shorter events, 11.0 us)
Async XLA Ops:
  6.6 7.6 %copy-start.15 = (f32[64]{0:T(128)S(1)}, f32[64]{0:T(128)}, u32[]{:S(2)}) copy-start(f32[64]{0:T(128)} %param.17) | copy-start | bytes 772
  6.7 96.0 %all-to-all-start = ((f32[16,64,512]{2,1,0:T(8,128)}), f32[16,64,512]{2,1,0:T(8,128)}, u32[]{:S(2)}, u32[]{:S(2)}) async-start(f32[16,64,512]{2,1,0:T(8,128)} %bitcast.11), calls=%async_computation | async-start | bytes 4194304 | tf_op jit(solution)/shard_map/all_to_all | solution.py:560
  14.3 78.5 %copy-start = (bf16[1024,1024]{1,0:T(8,128)(2,1)S(1)}, bf16[1024,1024]{1,0:T(8,128)(2,1)}, u32[]{:S(2)}) copy-start(bf16[1024,1024]{1,0:T(8,128)(2,1)} %second_hbm.1) | copy-start | bytes 6291460
  14.3 12.1 %collective-permute-start = (f32[1,64]{1,0:T(1,128)S(1)}, f32[1,64]{1,0:T(1,128)S(1)}, u32[]{:S(2)}, u32[]{:S(2)}) collective-permute-start(f32[1,64]{1,0:T(1,128)S(1)} %bitcast.12), channel_id=1, source_target_pairs={{0,1},{1,0},{2,3},{3,2},{4,5},{5,4},{6,7},{7,6},{8,9},{9,8},{10,11... | collective-permute-start | bytes 776 | tf_op jit(solution)/shard_map/ppermute | solution.py:566
  16.6 64.1 %collective-permute-start.3 = (f32[64,1024]{1,0:T(8,128)S(1)}, f32[64,1024]{1,0:T(8,128)S(1)}, u32[]{:S(2)}, u32[]{:S(2)}) collective-permute-start(f32[64,1024]{1,0:T(8,128)S(1)} %shard_map.105), channel_id=1, source_target_pairs={{0,8},{1,9},{2,10},{3,11},{4,12},{5,13},{6,14},{7,15},{8,0},{9,1},... | collective-permute-start | bytes 786440 | tf_op jit(solution)/shard_map/ppermute | solution.py:538
  21.2 0.7 copy-start.7
  21.9 58.7 %collective-permute-start.2 = (f32[64,1024]{1,0:T(8,128)S(1)}, f32[64,1024]{1,0:T(8,128)S(1)}, u32[]{:S(2)}, u32[]{:S(2)}) collective-permute-start(f32[64,1024]{1,0:T(8,128)S(1)} %get-tuple-element.38), channel_id=1, source_target_pairs={{0,4},{1,5},{2,6},{3,7},{4,8},{5,9},{6,10},{7,11},{8,12},{9,13},{1... | collective-permute-start | bytes 786440 | tf_op jit(solution)/shard_map/ppermute | solution.py:538
  23.4 57.3 %collective-permute-start.4 = (f32[64,1024]{1,0:T(8,128)S(1)}, f32[64,1024]{1,0:T(8,128)}, u32[]{:S(2)}, u32[]{:S(2)}) collective-permute-start(f32[64,1024]{1,0:T(8,128)S(1)} %get-tuple-element.39), channel_id=1, source_target_pairs={{0,12},{1,13},{2,14},{3,15},{4,0},{5,1},{6,2},{7,3},{8,4},{9,5},{1... | collective-permute-start | bytes 786440 | tf_op jit(solution)/shard_map/ppermute | solution.py:538
  26.5 3.6 %collective-permute-start.1 = (f32[1,128]{1,0:T(1,128)S(1)}, f32[1,128]{1,0:T(1,128)S(1)}, u32[]{:S(2)}, u32[]{:S(2)}) collective-permute-start(f32[1,128]{1,0:T(1,128)S(1)} %broadcast_select_fusion.1), channel_id=1, source_target_pairs={{0,2},{1,3},{2,0},{3,1},{4,6},{5,7},{6,4},{7,5},{8,10},{9,11},{10,... | collective-permute-start | bytes 1544 | tf_op jit(solution)/shard_map/ppermute | solution.py:566
  80.7 0.7 copy-start.13
  80.7 0.8 copy-start.14
  83.8 18.9 %collective-permute-start.7 = (f32[1,256]{1,0:T(1,128)}, f32[1,256]{1,0:T(1,128)S(1)}, u32[]{:S(2)}, u32[]{:S(2)}) collective-permute-start(f32[1,256]{1,0:T(1,128)} %get-tuple-element.40._.refs_0_), channel_id=1, source_target_pairs={{0,12},{1,13},{2,14},{3,15},{4,0},{5,1},{6,2},{7,3},{8,4},{9,5},{1... | collective-permute-start | bytes 3080 | tf_op jit(solution)/shard_map/ppermute | solution.py:584
  85.2 17.4 %collective-permute-start.6 = (f32[1,256]{1,0:T(1,128)}, f32[1,256]{1,0:T(1,128)S(1)}, u32[]{:S(2)}, u32[]{:S(2)}) collective-permute-start(f32[1,256]{1,0:T(1,128)} %get-tuple-element.40._.refs_0_), channel_id=1, source_target_pairs={{0,8},{1,9},{2,10},{3,11},{4,12},{5,13},{6,14},{7,15},{8,0},{9,1},... | collective-permute-start | bytes 3080 | tf_op jit(solution)/shard_map/ppermute | solution.py:584
  90.1 12.5 %collective-permute-start.5 = (f32[1,256]{1,0:T(1,128)}, f32[1,256]{1,0:T(1,128)S(1)}, u32[]{:S(2)}, u32[]{:S(2)}) collective-permute-start(f32[1,256]{1,0:T(1,128)} %get-tuple-element.40._.refs_0_), channel_id=1, source_target_pairs={{0,4},{1,5},{2,6},{3,7},{4,8},{5,9},{6,10},{7,11},{8,12},{9,13},{1... | collective-permute-start | bytes 3080 | tf_op jit(solution)/shard_map/ppermute | solution.py:584
  91.3 24.1 %collective-permute-start.10 = (f32[4,64,1024]{2,1,0:T(8,128)}, f32[4,64,1024]{2,1,0:T(8,128)}, u32[]{:S(2)}, u32[]{:S(2)}) collective-permute-start(f32[4,64,1024]{2,1,0:T(8,128)} %get-tuple-element.52.near_hbm), channel_id=1, source_target_pairs={{0,2},{1,3},{2,0},{3,1},{4,6},{5,7},{6,4},{7,5},{8,10},{9,11},{10,... | collective-permute-start | bytes 3145736 | tf_op jit(solution)/shard_map/ppermute | solution.py:582
  92.8 1.6 copy-start.2
  94.3 1.6 copy-start.3
  95.9 0.7 copy-start.11
  96.6 6.1 %copy-start.8 = (s32[4]{0:T(128)S(1)}, s32[4]{0:T(128)}, u32[]{:S(2)}) copy-start(s32[4]{0:T(128)} %pad_add_fusion.place_ref) | copy-start | bytes 52
  96.6 6.1 %copy-start.9 = (f32[8]{0:T(128)S(1)}, f32[8]{0:T(128)}, u32[]{:S(2)}) copy-start(f32[8]{0:T(128)} %table_ref.5) | copy-start | bytes 100
  96.6 6.1 %copy-start.10 = (f32[1024]{0:T(1024)S(1)}, f32[1024]{0:T(1024)}, u32[]{:S(2)}) copy-start(f32[1024]{0:T(1024)} %param.16) | copy-start | bytes 12292
  96.6 6.1 %copy-start.12 = (f32[1,256]{1,0:T(1,128)S(1)}, f32[1,256]{1,0:T(1,128)}, u32[]{:S(2)}) copy-start(f32[1,256]{1,0:T(1,128)} %get-tuple-element.40._.refs_0_) | copy-start | bytes 3076
  99.0 1.3 copy-start.4
  100.3 1.3 copy-start.5
  101.7 1.0 copy-start.6
  110.3 5.1 %collective-permute-start.9 = (f32[8,64,512]{2,1,0:T(8,128)S(1)}, f32[8,64,512]{2,1,0:T(8,128)S(1)}, u32[]{:S(2)}, u32[]{:S(2)}) collective-permute-start(f32[8,64,512]{2,1,0:T(8,128)S(1)} %get-tuple-element.50), channel_id=1, source_target_pairs={{0,1},{1,0},{2,3},{3,2},{4,5},{5,4},{6,7},{7,6},{8,9},{9,8},{10,11... | collective-permute-start | bytes 3145736 | tf_op jit(solution)/shard_map/ppermute | solution.py:602
  113.4 5.0 %collective-permute-start.8 = (f32[8,64,512]{2,1,0:T(8,128)S(1)}, f32[8,64,512]{2,1,0:T(8,128)S(1)}, u32[]{:S(2)}, u32[]{:S(2)}) collective-permute-start(f32[8,64,512]{2,1,0:T(8,128)S(1)} %get-tuple-element.48), channel_id=1, source_target_pairs={{0,1},{1,0},{2,3},{3,2},{4,5},{5,4},{6,7},{7,6},{8,9},{9,8},{10,11... | collective-permute-start | bytes 3145736 | tf_op jit(solution)/shard_map/ppermute | solution.py:602
  124.6 2.7 %collective-permute-start.11 = (f32[8,64,512]{2,1,0:T(8,128)S(1)}, f32[8,64,512]{2,1,0:T(8,128)S(1)}, u32[]{:S(2)}, u32[]{:S(2)}) collective-permute-start(f32[8,64,512]{2,1,0:T(8,128)S(1)} %shard_map.111), channel_id=1, source_target_pairs={{0,1},{1,0},{2,3},{3,2},{4,5},{5,4},{6,7},{7,6},{8,9},{9,8},{10,11... | collective-permute-start | bytes 3145736 | tf_op jit(solution)/shard_map/ppermute | solution.py:602
  124.6 2.7 %collective-permute-start.12 = (f32[8,128]{1,0:T(8,128)S(1)}, f32[8,128]{1,0:T(8,128)S(1)}, u32[]{:S(2)}, u32[]{:S(2)}) collective-permute-start(f32[8,128]{1,0:T(8,128)S(1)} %get-tuple-element.63.own_ref.one_ref), channel_id=1, source_target_pairs={{0,1},{1,0},{2,3},{3,2},{4,5},{5,4},{6,7},{7,6},{8,9},{9,8},{10,11... | collective-permute-start | bytes 12296 | tf_op jit(solution)/shard_map/ppermute | solution.py:602
  132.7 3.7 %collective-permute-start.14 = (f32[8,64,512]{2,1,0:T(8,128)S(1)}, f32[8,64,512]{2,1,0:T(8,128)S(1)}, u32[]{:S(2)}, u32[]{:S(2)}) collective-permute-start(f32[8,64,512]{2,1,0:T(8,128)S(1)} %get-tuple-element.68), channel_id=1, source_target_pairs={{0,1},{1,0},{2,3},{3,2},{4,5},{5,4},{6,7},{7,6},{8,9},{9,8},{10,11... | collective-permute-start | bytes 3145736 | tf_op jit(solution)/shard_map/ppermute | solution.py:602
  136.0 3.4 %collective-permute-start.13 = (f32[8,64,512]{2,1,0:T(8,128)S(1)}, f32[8,64,512]{2,1,0:T(8,128)S(1)}, u32[]{:S(2)}, u32[]{:S(2)}) collective-permute-start(f32[8,64,512]{2,1,0:T(8,128)S(1)} %get-tuple-element.66), channel_id=1, source_target_pairs={{0,1},{1,0},{2,3},{3,2},{4,5},{5,4},{6,7},{7,6},{8,9},{9,8},{10,11... | collective-permute-start | bytes 3145736 | tf_op jit(solution)/shard_map/ppermute | solution.py:602
  156.9 95.8 %copy-start.1 = (f32[2,4,64,1024]{3,2,1,0:T(8,128)S(1)}, f32[2,4,64,1024]{3,2,1,0:T(8,128)}, u32[]{:S(2)}) copy-start(f32[2,4,64,1024]{3,2,1,0:T(8,128)} %right_ref.3) | copy-start | bytes 6291460

commit v13 on v12

--- a/solution.py
+++ b/solution.py
@@ -283,11 +283,11 @@
             weight_ref[:, lanes] = 1.0 / (tall * wide[:, at : at + 128] + mean)
     copies[0].wait()
     field = field_ref[...].reshape(height, width)
+    for copy in copies[2:]:
+        copy.start()
     both = side_by_side(field)
     above = times_both(upper_ref[...], both)
     copies[1].wait()
-    for copy in copies[2:]:
-        copy.start()
     spectral = jnp.concatenate([above, times_both(lower_ref[...], both)], axis=0)
     weighted = spectral * weight_ref[...]
     start_ref[...] = field
@@ -310,7 +310,6 @@
     lower_ref,
     basis_ref,
     own_ref,
-    other_ref,
     column_ref,
     keep_ref,
     send_ref,
@@ -318,9 +317,10 @@
     scratch_ref,
 ):
     core = place_ref[0]
+    tall = got_ref.shape[0] - own_ref.shape[0]
     scratch_ref[:, core] = held_ref[...]
-    scratch_ref[:, 1 - core] = got_ref[...]
-    total = jnp.sum(own_ref[...] + other_ref[...], axis=1, keepdims=True)
+    scratch_ref[:, 1 - core] = got_ref[:tall, :].reshape(held_ref.shape)
+    total = jnp.sum(own_ref[...] + got_ref[tall:, :128], axis=1, keepdims=True)
     gamma, curvature = total[0:1], total[1:2]
     proper = (gamma > 0) & (curvature > 0)
     step = jnp.where(proper, gamma / jnp.where(proper, curvature, 1.0), 1.0)
@@ -411,10 +411,23 @@
     store_sums(sum_ref, [one_ref[0:1], full_image(*refs, image_ref, scratch_ref)])
 
 
-def return_kernel(whose, place_ref, image_ref, basis_ref, out_ref):
-    lanes = both_shares(place_ref, out_ref.shape[2])[whose]
+def returned(place_ref, image_ref, basis_ref, whose, half):
+    lanes = both_shares(place_ref, half)[whose]
     image = image_ref[...].reshape(-1, basis_ref.shape[0])
-    out_ref[...] = times_right(image, basis_ref[:, lanes], 0).reshape(out_ref.shape)
+    return times_right(image, basis_ref[:, lanes], 0)
+
+
+def return_theirs_kernel(place_ref, image_ref, basis_ref, sum_ref, out_ref):
+    part = returned(place_ref, image_ref, basis_ref, 1, out_ref.shape[1])
+    out_ref[: part.shape[0], :] = part
+    out_ref[part.shape[0] :, :] = jnp.concatenate(
+        [sum_ref[...]] * (out_ref.shape[1] // 128), axis=1
+    )
+
+
+def return_mine_kernel(place_ref, image_ref, basis_ref, out_ref):
+    part = returned(place_ref, image_ref, basis_ref, 0, out_ref.shape[2])
+    out_ref[...] = part.reshape(out_ref.shape)
 
 
 def last_image_kernel(
@@ -667,14 +680,11 @@
         (whole, sums_shape),
         flat,
     )
-    pair_other = swap(pair_sum)
-
-    def give_back(whose):
-        kernel = functools.partial(return_kernel, whose)
-        return call(kernel, (place, image, basis_second), (piece,), None)[0]
-
-    back_send = give_back(1)
-    back_keep = give_back(0)
+
+    (back_send,) = call(
+        return_theirs_kernel, (place, image, basis_second, pair_sum), ((flat[0] + 8, half),), None
+    )
+    (back_keep,) = call(return_mine_kernel, (place, image, basis_second), (piece,), None)
     back_got = swap(back_send)
 
     column, keep, send, sum_two = call(
@@ -689,7 +699,6 @@
             lower,
             basis_first,
             pair_sum,
-            pair_other,
         ),
         (tile, piece, piece, sums_shape),
         by_rows,

time: 256 us -> 256 us (level)
  transfers between devices with their start and end apart: 16 -> 15, of which waited for: 4 -> 4; matrix products, arithmetic and copies ran while one was open for 1% -> 1% of each run, Pallas kernels for 12% -> 12%
where the time goes in v13:
time: 256 us; the launch traced here: 255 us
  blocking collectives  107 us (42%)
  Pallas kernels  55.8 us (22%)
  waiting for transfers between devices  54.6 us (21%)
  starting transfers between devices  26.2 us (10%)
  local copies, waits for them, and re-layouts  9 us (4%)
    all_to_all x1, blocking collectives, paired_body(): lax.all_to_all(answer, 'mode', split_axis=0, concat_axis=0, axis_index_gr...  95.8 us
    ppermute x3, waiting for transfers between devices, plane_shift(): return lax.ppermute(value, 'mode', pairs)  50.1 us
    pallas_call x10, Pallas kernels, call(): pl.pallas_call(kernel, grid=(1,), in_specs=specs or [smem] + [full(*value...  36.9 us
    all_to_all x1, blocking collectives, paired_body(): sums = lax.all_to_all(sums, 'mode', split_axis=0, concat_axis=0, tiled=True)  11.7 us
    unnamed x32, local copies, waits for them, and re-layouts  9 us
    all_to_all x1, starting transfers between devices, paired_body(): lax.all_to_all(outgoing.reshape(groups, rows, half), 'mode', split_axis=0...  7.6 us
    ppermute x3, starting transfers between devices, paired_body(): lax.ppermute(eigen, 'mode', [(at, (at + by * unit) % groups) for at in ra...  7.53 us
    ppermute x3, starting transfers between devices, plane_shift(): return lax.ppermute(value, 'mode', pairs)  6.42 us
  transfers between devices with their start and end apart: 15, of which 4 were waited for; matrix products, arithmetic and copies ran while one was open for 1% of the time, Pallas kernels for 12%

profile of v13, /device:TPU:0, one launch (start us, length us, event | category | flops | bytes accessed | tf_op | source)
XLA Modules:
  0.0 255.3 jit_solution(15103115151884977826)
XLA Ops:
  0.6 6.0 %outgoing.1 = f32[4,2,2,64,512]{4,3,2,1,0:T(8,128)} custom-call(f32[2,4,64,1024]{3,2,1,0:T(8,128)} %right_ref.3, bf16[1024,1024]{1,0:T(8,128)(2,1)} %second_hbm.1), custom_call_target="tpu_custom_call" | custom-call | tf_op jit(solution)/shard_map/outgoing/pallas_call | solution.py:561
  6.7 7.6 %all-to-all-start = ((f32[16,64,512]{2,1,0:T(8,128)}), f32[16,64,512]{2,1,0:T(8,128)}, u32[]{:S(2)}, u32[]{:S(2)}) async-start(f32[16,64,512]{2,1,0:T(8,128)} %bitcast.11), calls=%async_computation | async-start | bytes 4194304 | tf_op jit(solution)/shard_map/all_to_all | solution.py:573
  14.7 1.9 shard_map.105
  16.6 2.6 %collective-permute-start.3 = (f32[64,1024]{1,0:T(8,128)S(1)}, f32[64,1024]{1,0:T(8,128)S(1)}, u32[]{:S(2)}, u32[]{:S(2)}) collective-permute-start(f32[64,1024]{1,0:T(8,128)S(1)} %shard_map.105), channel_id=1, source_target_pairs={{0,8},{1,9},{2,10},{3,11},{4,12},{5,13},{6,14},{7,15},{8,0},{9,1},... | collective-permute-start | bytes 786440 | tf_op jit(solution)/shard_map/ppermute | solution.py:551
  19.2 2.0 shard_map.104
  21.9 1.5 collective-permute-start.2
  23.4 2.4 collective-permute-start.4
  26.5 1.5 collective-permute-start.1
  28.0 2.0 collective-permute-done.1
  30.6 50.1 %collective-permute-done.3.refs_2_ = f32[64,1024]{1,0:T(8,128)S(1)} collective-permute-done((f32[64,1024]{1,0:T(8,128)S(1)}, f32[64,1024]{1,0:T(8,128)S(1)}, u32[]{:S(2)}, u32[]{:S(2)}) %collective-permute-start.3) | collective-permute-done | bytes 262176 | tf_op jit(solution)/shard_map/ppermute | solution.py:551
  81.5 2.3 join.1
  83.8 1.5 collective-permute-start.7
  85.2 4.9 %collective-permute-start.6 = (f32[1,256]{1,0:T(1,128)}, f32[1,256]{1,0:T(1,128)S(1)}, u32[]{:S(2)}, u32[]{:S(2)}) collective-permute-start(f32[1,256]{1,0:T(1,128)} %get-tuple-element.40._.refs_0_), channel_id=1, source_target_pairs={{0,8},{1,9},{2,10},{3,11},{4,12},{5,13},{6,14},{7,15},{8,0},{9,1},... | collective-permute-start | bytes 3080 | tf_op jit(solution)/shard_map/ppermute | solution.py:597
  91.3 1.5 collective-permute-start.10
  92.8 1.6 copy-done.2
  94.4 1.6 copy-done.3
  96.6 2.4 prepare.1
  102.7 7.4 %shard_map.106 = (f32[1024,512]{1,0:T(8,128)S(1)}, f32[1024,512]{1,0:T(8,128)S(1)}, f32[1024,512]{1,0:T(8,128)S(1)}, f32[8,64,512]{2,1,0:T(8,128)S(1)}, f32[8,64...) custom-call(s32[4]{0:T(128)S(1)} %copy-done.8, ...), custom_call_target="tpu_custom_call" | custom-call | tf_op jit(solution)/shard_map/pallas_call | solution.py:618
  110.2 3.0 %shard_map.107 = (f32[8,64,512]{2,1,0:T(8,128)S(1)}, f32[8,64,512]{2,1,0:T(8,128)S(1)}, bf16[1024,1024]{1,0:T(8,128)(2,1)S(1)}, bf16[1024,1024]{1,0:T(8,128)(2,1)S(1)}) custom-call(s32[4]{0:T(128)S(1)} %copy-done.8, f32[1024,512]{1,0:T(8,128)S(1)} %get-tuple-element.43.column_ref, bf16[1024,1024]{1,0:T(8,128)(2,1)S(1)} %get-tuple-element.44.kernel_ref, ...), custom_call_target="tpu_custom_call" | custom-call | tf_op jit(solution)/shard_map/pallas_call | solution.py:618
  113.8 1.6 collective-permute-done.10.far_hbm
  115.4 3.0 %shard_map.108 = (f32[8,64,1024]{2,1,0:T(8,128)S(1)}, f32[4,2,64,1024]{3,2,1,0:T(8,128)S(1)}) custom-call(s32[4]{0:T(128)S(1)} %copy-done.8, f32[8,64,512]{2,1,0:T(8,128)S(1)} %get-tuple-element.49.keep_ref, f32[8,64,512]{2,1,0:T(8,128)S(1)} %collective-permute-done.9.got_ref, bf16[1024,1024]{1,0:T(8,128)(2,1)S(1)} %get-tuple-element.51.basis_ref, ...), custom_call_target="tpu_custom_call" | custom-call | tf_op jit(solution)/shard_map/pallas_call | solution.py:618
  118.4 4.1 %shard_map.109 = (f32[8,64,1024]{2,1,0:T(8,128)S(1)}, f32[8,128]{1,0:T(8,128)S(1)}) custom-call(s32[4]{0:T(128)S(1)} %copy-done.8, f32[8,64,512]{2,1,0:T(8,128)S(1)} %get-tuple-element.47.keep_ref, f32[8,64,512]{2,1,0:T(8,128)S(1)} %collective-permute-done.8.got_ref, f32[8,64,1024]{2,1,0:T(8,128)S(1)} %get-tuple-element.53.z_ref, ...), custom_call_target="tpu_custom_call" | custom-call | tf_op jit(solution)/shard_map/pallas_call | solution.py:618
  122.6 2.0 shard_map.111
  124.7 1.8 shard_map.110.held_ref
  127.3 5.4 %shard_map.112 = (f32[1024,512]{1,0:T(8,128)S(1)}, f32[8,64,512]{2,1,0:T(8,128)S(1)}, f32[8,64,512]{2,1,0:T(8,128)S(1)}, f32[8,128]{1,0:T(8,128)S(1)}) custom-call(s32[4]{0:T(128)S(1)} %copy-done.8, f32[8,64,512]{2,1,0:T(8,128)S(1)} %shard_map.110.held_ref, f32[520,512]{1,0:T(8,128)S(1)} %collective-permute-done.11.got_ref, ...), custom_call_target="tpu_custom_call" | custom-call | tf_op jit(solution)/shard_map/pallas_call | solution.py:618
  133.0 3.0 %shard_map.113 = (f32[8,64,512]{2,1,0:T(8,128)S(1)}, f32[8,64,512]{2,1,0:T(8,128)S(1)}) custom-call(s32[4]{0:T(128)S(1)} %copy-done.8, f32[1024,512]{1,0:T(8,128)S(1)} %get-tuple-element.64.column_ref, bf16[1024,1024]{1,0:T(8,128)(2,1)S(1)} %get-tuple-element.44.kernel_ref), custom_call_target="tpu_custom_call" | custom-call | tf_op jit(solution)/shard_map/pallas_call | solution.py:618
  136.4 3.0 %shard_map.114.z_ref.f_ref = f32[8,64,1024]{2,1,0:T(8,128)S(1)} custom-call(s32[4]{0:T(128)S(1)} %copy-done.8, f32[8,64,512]{2,1,0:T(8,128)S(1)} %get-tuple-element.67.keep_ref, f32[8,64,512]{2,1,0:T(8,128)S(1)} %collective-permute-done.13.got_ref, bf16[1024,1024]{1,0:T(8,128)(2,1)S(1)} %get-tuple-element.51.basis_ref), custom_call_target="tpu_custom_call" | custom-call | tf_op jit(solution)/shard_map/pallas_call | solution.py:618
  139.4 4.1 %shard_map.115 = (f32[8,64,1024]{2,1,0:T(8,128)S(1)}, f32[16,8,128]{2,1,0:T(8,128)S(1)}) custom-call(s32[4]{0:T(128)S(1)} %copy-done.8, f32[8,64,512]{2,1,0:T(8,128)S(1)} %get-tuple-element.65.keep_ref, f32[8,64,512]{2,1,0:T(8,128)S(1)} %collective-permute-done.12.got_ref, f32[8,64,1024]{2,1,0:T(8,128)S(1)} %shard_map.114.z_ref.f_ref, ...), custom_call_target="tpu_custom_call" | custom-call | tf_op jit(solution)/shard_map/pallas_call | solution.py:618
  143.6 11.7 %all_to_all.15.sum_ref = f32[16,8,128]{2,1,0:T(8,128)S(1)} all-to-all(f32[16,8,128]{2,1,0:T(8,128)S(1)} %get-tuple-element.70), channel_id=1, replica_groups=mesh['blocks'=2,'mode'=16] {'mode'}, dimensions={0} | all-to-all | bytes 131072 | tf_op jit(solution)/shard_map/all_to_all | solution.py:728
  155.3 1.6 combine.1
  156.9 95.8 %all_to_all.16.got_ref = f32[8,128,1024]{2,1,0:T(8,128)S(1)} all-to-all(f32[8,128,1024]{2,1,0:T(8,128)S(1)} %combine.1), channel_id=1, replica_groups={{0,2,4,6,8,10,12,14},{1,3,5,7,9,11,13,15},{16,18,20,22,24,26,28,30},{17..., dimensions={0} | all-to-all | bytes 8388608 | tf_op jit(solution)/shard_map/all_to_all | solution.py:741
  252.7 2.6 %finish.1 = (f32[2,4,64,1024]{3,2,1,0:T(8,128)}, f32[2,4,64,1024]{3,2,1,0:T(8,128)}) custom-call(f32[8,128,1024]{2,1,0:T(8,128)S(1)} %all_to_all.16.got_ref, f32[2,4,64,1024]{3,2,1,0:T(8,128)S(1)} %copy-done.1), custom_call_target="tpu_custom_call" | custom-call | tf_op jit(solution)/shard_map/finish/pallas_call | solution.py:752
  (53 shorter events, 11.0 us)
Async XLA Ops:
  6.6 7.6 %copy-start.15 = (f32[64]{0:T(128)S(1)}, f32[64]{0:T(128)}, u32[]{:S(2)}) copy-start(f32[64]{0:T(128)} %param.17) | copy-start | bytes 772
  6.7 96.0 %all-to-all-start = ((f32[16,64,512]{2,1,0:T(8,128)}), f32[16,64,512]{2,1,0:T(8,128)}, u32[]{:S(2)}, u32[]{:S(2)}) async-start(f32[16,64,512]{2,1,0:T(8,128)} %bitcast.11), calls=%async_computation | async-start | bytes 4194304 | tf_op jit(solution)/shard_map/all_to_all | solution.py:573
  14.3 78.5 %copy-start = (bf16[1024,1024]{1,0:T(8,128)(2,1)S(1)}, bf16[1024,1024]{1,0:T(8,128)(2,1)}, u32[]{:S(2)}) copy-start(bf16[1024,1024]{1,0:T(8,128)(2,1)} %second_hbm.1) | copy-start | bytes 6291460
  14.3 12.1 %collective-permute-start = (f32[1,64]{1,0:T(1,128)S(1)}, f32[1,64]{1,0:T(1,128)S(1)}, u32[]{:S(2)}, u32[]{:S(2)}) collective-permute-start(f32[1,64]{1,0:T(1,128)S(1)} %bitcast.12), channel_id=1, source_target_pairs={{0,1},{1,0},{2,3},{3,2},{4,5},{5,4},{6,7},{7,6},{8,9},{9,8},{10,11... | collective-permute-start | bytes 776 | tf_op jit(solution)/shard_map/ppermute | solution.py:579
  16.6 64.1 %collective-permute-start.3 = (f32[64,1024]{1,0:T(8,128)S(1)}, f32[64,1024]{1,0:T(8,128)S(1)}, u32[]{:S(2)}, u32[]{:S(2)}) collective-permute-start(f32[64,1024]{1,0:T(8,128)S(1)} %shard_map.105), channel_id=1, source_target_pairs={{0,8},{1,9},{2,10},{3,11},{4,12},{5,13},{6,14},{7,15},{8,0},{9,1},... | collective-permute-start | bytes 786440 | tf_op jit(solution)/shard_map/ppermute | solution.py:551
  21.2 0.7 copy-start.7
  21.9 58.7 %collective-permute-start.2 = (f32[64,1024]{1,0:T(8,128)S(1)}, f32[64,1024]{1,0:T(8,128)S(1)}, u32[]{:S(2)}, u32[]{:S(2)}) collective-permute-start(f32[64,1024]{1,0:T(8,128)S(1)} %get-tuple-element.38), channel_id=1, source_target_pairs={{0,4},{1,5},{2,6},{3,7},{4,8},{5,9},{6,10},{7,11},{8,12},{9,13},{1... | collective-permute-start | bytes 786440 | tf_op jit(solution)/shard_map/ppermute | solution.py:551
  23.4 57.3 %collective-permute-start.4 = (f32[64,1024]{1,0:T(8,128)S(1)}, f32[64,1024]{1,0:T(8,128)}, u32[]{:S(2)}, u32[]{:S(2)}) collective-permute-start(f32[64,1024]{1,0:T(8,128)S(1)} %get-tuple-element.39), channel_id=1, source_target_pairs={{0,12},{1,13},{2,14},{3,15},{4,0},{5,1},{6,2},{7,3},{8,4},{9,5},{1... | collective-permute-start | bytes 786440 | tf_op jit(solution)/shard_map/ppermute | solution.py:551
  26.5 3.6 %collective-permute-start.1 = (f32[1,128]{1,0:T(1,128)S(1)}, f32[1,128]{1,0:T(1,128)S(1)}, u32[]{:S(2)}, u32[]{:S(2)}) collective-permute-start(f32[1,128]{1,0:T(1,128)S(1)} %broadcast_select_fusion.1), channel_id=1, source_target_pairs={{0,2},{1,3},{2,0},{3,1},{4,6},{5,7},{6,4},{7,5},{8,10},{9,11},{10,... | collective-permute-start | bytes 1544 | tf_op jit(solution)/shard_map/ppermute | solution.py:579
  80.7 0.7 copy-start.13
  80.7 0.8 copy-start.14
  83.8 18.9 %collective-permute-start.7 = (f32[1,256]{1,0:T(1,128)}, f32[1,256]{1,0:T(1,128)S(1)}, u32[]{:S(2)}, u32[]{:S(2)}) collective-permute-start(f32[1,256]{1,0:T(1,128)} %get-tuple-element.40._.refs_0_), channel_id=1, source_target_pairs={{0,12},{1,13},{2,14},{3,15},{4,0},{5,1},{6,2},{7,3},{8,4},{9,5},{1... | collective-permute-start | bytes 3080 | tf_op jit(solution)/shard_map/ppermute | solution.py:597
  85.2 17.4 %collective-permute-start.6 = (f32[1,256]{1,0:T(1,128)}, f32[1,256]{1,0:T(1,128)S(1)}, u32[]{:S(2)}, u32[]{:S(2)}) collective-permute-start(f32[1,256]{1,0:T(1,128)} %get-tuple-element.40._.refs_0_), channel_id=1, source_target_pairs={{0,8},{1,9},{2,10},{3,11},{4,12},{5,13},{6,14},{7,15},{8,0},{9,1},... | collective-permute-start | bytes 3080 | tf_op jit(solution)/shard_map/ppermute | solution.py:597
  90.1 12.5 %collective-permute-start.5 = (f32[1,256]{1,0:T(1,128)}, f32[1,256]{1,0:T(1,128)S(1)}, u32[]{:S(2)}, u32[]{:S(2)}) collective-permute-start(f32[1,256]{1,0:T(1,128)} %get-tuple-element.40._.refs_0_), channel_id=1, source_target_pairs={{0,4},{1,5},{2,6},{3,7},{4,8},{5,9},{6,10},{7,11},{8,12},{9,13},{1... | collective-permute-start | bytes 3080 | tf_op jit(solution)/shard_map/ppermute | solution.py:597
  91.3 24.1 %collective-permute-start.10 = (f32[4,64,1024]{2,1,0:T(8,128)}, f32[4,64,1024]{2,1,0:T(8,128)}, u32[]{:S(2)}, u32[]{:S(2)}) collective-permute-start(f32[4,64,1024]{2,1,0:T(8,128)} %get-tuple-element.52.near_hbm), channel_id=1, source_target_pairs={{0,2},{1,3},{2,0},{3,1},{4,6},{5,7},{6,4},{7,5},{8,10},{9,11},{10,... | collective-permute-start | bytes 3145736 | tf_op jit(solution)/shard_map/ppermute | solution.py:595
  92.8 1.6 copy-start.2
  94.4 1.6 copy-start.3
  96.0 0.7 copy-start.11
  96.6 6.1 %copy-start.8 = (s32[4]{0:T(128)S(1)}, s32[4]{0:T(128)}, u32[]{:S(2)}) copy-start(s32[4]{0:T(128)} %pad_add_fusion.place_ref) | copy-start | bytes 52
  96.6 6.1 %copy-start.9 = (f32[8]{0:T(128)S(1)}, f32[8]{0:T(128)}, u32[]{:S(2)}) copy-start(f32[8]{0:T(128)} %table_ref.5) | copy-start | bytes 100
  96.6 6.1 %copy-start.10 = (f32[1024]{0:T(1024)S(1)}, f32[1024]{0:T(1024)}, u32[]{:S(2)}) copy-start(f32[1024]{0:T(1024)} %param.16) | copy-start | bytes 12292
  96.6 6.1 %copy-start.12 = (f32[1,256]{1,0:T(1,128)S(1)}, f32[1,256]{1,0:T(1,128)}, u32[]{:S(2)}) copy-start(f32[1,256]{1,0:T(1,128)} %get-tuple-element.40._.refs_0_) | copy-start | bytes 3076
  99.0 1.3 copy-start.4
  100.3 1.3 copy-start.5
  101.7 1.0 copy-start.6
  110.1 5.3 %collective-permute-start.9 = (f32[8,64,512]{2,1,0:T(8,128)S(1)}, f32[8,64,512]{2,1,0:T(8,128)S(1)}, u32[]{:S(2)}, u32[]{:S(2)}) collective-permute-start(f32[8,64,512]{2,1,0:T(8,128)S(1)} %get-tuple-element.50), channel_id=1, source_target_pairs={{0,1},{1,0},{2,3},{3,2},{4,5},{5,4},{6,7},{7,6},{8,9},{9,8},{10,11... | collective-permute-start | bytes 3145736 | tf_op jit(solution)/shard_map/ppermute | solution.py:615
  113.2 5.2 %collective-permute-start.8 = (f32[8,64,512]{2,1,0:T(8,128)S(1)}, f32[8,64,512]{2,1,0:T(8,128)S(1)}, u32[]{:S(2)}, u32[]{:S(2)}) collective-permute-start(f32[8,64,512]{2,1,0:T(8,128)S(1)} %get-tuple-element.48), channel_id=1, source_target_pairs={{0,1},{1,0},{2,3},{3,2},{4,5},{5,4},{6,7},{7,6},{8,9},{9,8},{10,11... | collective-permute-start | bytes 3145736 | tf_op jit(solution)/shard_map/ppermute | solution.py:615
  124.6 2.7 %collective-permute-start.11 = (f32[520,512]{1,0:T(8,128)S(1)}, f32[520,512]{1,0:T(8,128)S(1)}, u32[]{:S(2)}, u32[]{:S(2)}) collective-permute-start(f32[520,512]{1,0:T(8,128)S(1)} %shard_map.111), channel_id=1, source_target_pairs={{0,1},{1,0},{2,3},{3,2},{4,5},{5,4},{6,7},{7,6},{8,9},{9,8},{10,11... | collective-permute-start | bytes 3194888 | tf_op jit(solution)/shard_map/ppermute | solution.py:615
  132.8 3.7 %collective-permute-start.13 = (f32[8,64,512]{2,1,0:T(8,128)S(1)}, f32[8,64,512]{2,1,0:T(8,128)S(1)}, u32[]{:S(2)}, u32[]{:S(2)}) collective-permute-start(f32[8,64,512]{2,1,0:T(8,128)S(1)} %get-tuple-element.68), channel_id=1, source_target_pairs={{0,1},{1,0},{2,3},{3,2},{4,5},{5,4},{6,7},{7,6},{8,9},{9,8},{10,11... | collective-permute-start | bytes 3145736 | tf_op jit(solution)/shard_map/ppermute | solution.py:615
  136.0 3.5 %collective-permute-start.12 = (f32[8,64,512]{2,1,0:T(8,128)S(1)}, f32[8,64,512]{2,1,0:T(8,128)S(1)}, u32[]{:S(2)}, u32[]{:S(2)}) collective-permute-start(f32[8,64,512]{2,1,0:T(8,128)S(1)} %get-tuple-element.66), channel_id=1, source_target_pairs={{0,1},{1,0},{2,3},{3,2},{4,5},{5,4},{6,7},{7,6},{8,9},{9,8},{10,11... | collective-permute-start | bytes 3145736 | tf_op jit(solution)/shard_map/ppermute | solution.py:615
  156.9 95.8 %copy-start.1 = (f32[2,4,64,1024]{3,2,1,0:T(8,128)S(1)}, f32[2,4,64,1024]{3,2,1,0:T(8,128)}, u32[]{:S(2)}) copy-start(f32[2,4,64,1024]{3,2,1,0:T(8,128)} %right_ref.3) | copy-start | bytes 6291460

commit v14 on v13

--- a/solution.py
+++ b/solution.py
@@ -153,30 +153,39 @@
     )
 
 
+def look_up(table_ref, level):
+    noise = jnp.full(level.shape, table_ref[0], F32)
+    for index in range(1, NCLASS):
+        noise = jnp.where(level == index, table_ref[index], noise)
+    return noise
+
+
+def pick_kernel(by, unit, class_hbm, out_ref, done):
+    plane = lax.axis_index("mode") // unit
+    copy = pltpu.make_async_copy(class_hbm.at[(plane + by) % class_hbm.shape[0]], out_ref, done)
+    copy.start()
+    copy.wait()
+
+
 def noise_kernel(shifts, unit, table_ref, class_hbm, *refs):
     out_refs, (class_ref, done) = refs[:-2], refs[-2:]
     planes = class_hbm.shape[0]
     plane = lax.axis_index("mode") // unit
-    copies = [
-        pltpu.make_async_copy(class_hbm.at[(plane + by) % planes], class_ref.at[at], done.at[at])
-        for at, by in enumerate(shifts)
-    ]
+    pairs = [(class_hbm.at[(plane + by) % planes], class_ref.at[at]) for at, by in enumerate(shifts)]
+    copies = copy_into(pairs, done)
     for copy in copies:
         copy.start()
     for at, copy in enumerate(copies):
         copy.wait()
-        level = class_ref[at]
-        noise = jnp.full(level.shape, table_ref[0], F32)
-        for index in range(1, NCLASS):
-            noise = jnp.where(level == index, table_ref[index], noise)
-        out_refs[at][...] = noise
-
-
-def join_kernel(place_ref, value_ref, *refs):
+        out_refs[at][...] = look_up(table_ref, class_ref[at])
+
+
+def join_kernel(ahead, place_ref, table_ref, value_ref, *refs):
     parts, (joined_ref, out_ref) = refs[:-2], refs[-2:]
     planes = len(parts)
     for by, part in enumerate(parts):
-        joined_ref[(place_ref[2] + planes - by) % planes] = part[...]
+        noise = look_up(table_ref, part[...]) if by == ahead else part[...]
+        joined_ref[(place_ref[2] + planes - by) % planes] = noise
     out_ref[...] = value_ref[...]
 
 
@@ -553,7 +562,16 @@
     ahead = planes // 2
     others = [by for by in range(planes) if by != ahead]
     near = [None] * planes
-    near[ahead] = plane_shift(noise_of([ahead])[0], ahead)
+    picked = pl.pallas_call(
+        functools.partial(pick_kernel, ahead, unit),
+        in_specs=[hbm],
+        out_specs=pl.BlockSpec(memory_space=pltpu.VMEM),
+        out_shape=jax.ShapeDtypeStruct((rows, width), jnp.int32),
+        scratch_shapes=[pltpu.SemaphoreType.DMA],
+        compiler_params=pltpu.CompilerParams(vmem_limit_bytes=1024 * 1024),
+        name="pick",
+    )(in_hbm(classes))
+    near[ahead] = plane_shift(picked, ahead)
     rest = noise_of(others)
     for by, value in zip(others, rest):
         near[by] = plane_shift(value, by) if by else value
@@ -584,14 +602,14 @@
             jnp.concatenate([other, eigen], axis=1),
         )
     near, eigen = pl.pallas_call(
-        join_kernel,
+        functools.partial(join_kernel, ahead),
         grid=(1,),
-        in_specs=[smem, full(*eigen.shape)] + [full(rows, width)] * planes,
+        in_specs=[smem, smem, full(*eigen.shape)] + [full(rows, width)] * planes,
         out_specs=[whole_out(planes, rows, width), whole_out(*eigen.shape)],
         out_shape=[shape_of(planes, rows, width), shape_of(*eigen.shape)],
         compiler_params=params(1, 58),
         name="join",
-    )(place, eigen, *near)
+    )(place, noise_table, eigen, *near)
     far = lax.ppermute(near, "mode", sample_swap)
     shifted = [eigen] + [
         lax.ppermute(eigen, "mode", [(at, (at + by * unit) % groups) for at in range(groups)])

time: 256 us -> 256 us (level)
  transfers between devices with their start and end apart: 15 -> 15, of which waited for: 4 -> 4; matrix products, arithmetic and copies ran while one was open for 1% -> 1% of each run, Pallas kernels for 12% -> 11%
where the time goes in v14:
time: 256 us; the launch traced here: 255 us
  blocking collectives  107 us (42%)
  waiting for transfers between devices  55.4 us (22%)
  Pallas kernels  55.1 us (22%)
  starting transfers between devices  26.2 us (10%)
  local copies, waits for them, and re-layouts  9 us (4%)
    all_to_all x1, blocking collectives, paired_body(): lax.all_to_all(answer, 'mode', split_axis=0, concat_axis=0, axis_index_gr...  95.8 us
    ppermute x3, waiting for transfers between devices, plane_shift(): return lax.ppermute(value, 'mode', pairs)  50.8 us
    pallas_call x10, Pallas kernels, call(): pl.pallas_call(kernel, grid=(1,), in_specs=specs or [smem] + [full(*value...  36.9 us
    all_to_all x1, blocking collectives, paired_body(): sums = lax.all_to_all(sums, 'mode', split_axis=0, concat_axis=0, tiled=True)  11.7 us
    unnamed x32, local copies, waits for them, and re-layouts  9 us
    all_to_all x1, starting transfers between devices, paired_body(): lax.all_to_all(outgoing.reshape(groups, rows, half), 'mode', split_axis=0...  7.6 us
    ppermute x3, starting transfers between devices, paired_body(): lax.ppermute(eigen, 'mode', [(at, (at + by * unit) % groups) for at in ra...  7.53 us
    ppermute x3, starting transfers between devices, plane_shift(): return lax.ppermute(value, 'mode', pairs)  6.34 us
  transfers between devices with their start and end apart: 15, of which 4 were waited for; matrix products, arithmetic and copies ran while one was open for 1% of the time, Pallas kernels for 11%

profile of v14, /device:TPU:0, one launch (start us, length us, event | category | flops | bytes accessed | tf_op | source)
XLA Modules:
  0.0 255.4 jit_solution(6996399865247550368)
XLA Ops:
  0.6 6.0 %outgoing.1 = f32[4,2,2,64,512]{4,3,2,1,0:T(8,128)} custom-call(f32[2,4,64,1024]{3,2,1,0:T(8,128)} %right_ref.3, bf16[1024,1024]{1,0:T(8,128)(2,1)} %second_hbm.1), custom_call_target="tpu_custom_call" | custom-call | tf_op jit(solution)/shard_map/outgoing/pallas_call | solution.py:579
  6.7 7.6 %all-to-all-start = ((f32[16,64,512]{2,1,0:T(8,128)}), f32[16,64,512]{2,1,0:T(8,128)}, u32[]{:S(2)}, u32[]{:S(2)}) async-start(f32[16,64,512]{2,1,0:T(8,128)} %bitcast.11), calls=%async_computation | async-start | bytes 4194304 | tf_op jit(solution)/shard_map/all_to_all | solution.py:591
  15.9 2.5 collective-permute-start.3
  18.4 2.0 shard_map.104
  21.1 1.5 collective-permute-start.2
  22.6 2.4 collective-permute-start.4
  25.7 1.5 collective-permute-start.1
  27.2 2.1 collective-permute-done.1
  29.8 50.8 %collective-permute-done.3.refs_2_ = s32[64,1024]{1,0:T(8,128)S(1)} collective-permute-done((s32[64,1024]{1,0:T(8,128)S(1)}, s32[64,1024]{1,0:T(8,128)S(1)}, u32[]{:S(2)}, u32[]{:S(2)}) %collective-permute-start.3) | collective-permute-done | bytes 262176 | tf_op jit(solution)/shard_map/ppermute | solution.py:560
  81.5 2.4 join.1
  83.9 1.5 collective-permute-start.7
  85.3 4.9 %collective-permute-start.6 = (f32[1,256]{1,0:T(1,128)}, f32[1,256]{1,0:T(1,128)S(1)}, u32[]{:S(2)}, u32[]{:S(2)}) collective-permute-start(f32[1,256]{1,0:T(1,128)} %get-tuple-element.40._.refs_0_), channel_id=1, source_target_pairs={{0,8},{1,9},{2,10},{3,11},{4,12},{5,13},{6,14},{7,15},{8,0},{9,1},... | collective-permute-start | bytes 3080 | tf_op jit(solution)/shard_map/ppermute | solution.py:615
  91.4 1.5 collective-permute-start.10
  92.9 1.6 copy-done.2
  94.5 1.6 copy-done.3
  96.7 2.4 prepare.1
  100.4 1.3 copy-done.5
  102.8 7.4 %shard_map.105 = (f32[1024,512]{1,0:T(8,128)S(1)}, f32[1024,512]{1,0:T(8,128)S(1)}, f32[1024,512]{1,0:T(8,128)S(1)}, f32[8,64,512]{2,1,0:T(8,128)S(1)}, f32[8,64...) custom-call(s32[4]{0:T(128)S(1)} %copy-done.8, ...), custom_call_target="tpu_custom_call" | custom-call | tf_op jit(solution)/shard_map/pallas_call | solution.py:636
  110.3 3.0 %shard_map.106 = (f32[8,64,512]{2,1,0:T(8,128)S(1)}, f32[8,64,512]{2,1,0:T(8,128)S(1)}, bf16[1024,1024]{1,0:T(8,128)(2,1)S(1)}, bf16[1024,1024]{1,0:T(8,128)(2,1)S(1)}) custom-call(s32[4]{0:T(128)S(1)} %copy-done.8, f32[1024,512]{1,0:T(8,128)S(1)} %get-tuple-element.43.column_ref, bf16[1024,1024]{1,0:T(8,128)(2,1)S(1)} %get-tuple-element.44.kernel_ref, ...), custom_call_target="tpu_custom_call" | custom-call | tf_op jit(solution)/shard_map/pallas_call | solution.py:636
  113.9 1.6 collective-permute-done.10.far_hbm
  115.5 3.0 %shard_map.107 = (f32[8,64,1024]{2,1,0:T(8,128)S(1)}, f32[4,2,64,1024]{3,2,1,0:T(8,128)S(1)}) custom-call(s32[4]{0:T(128)S(1)} %copy-done.8, f32[8,64,512]{2,1,0:T(8,128)S(1)} %get-tuple-element.49.keep_ref, f32[8,64,512]{2,1,0:T(8,128)S(1)} %collective-permute-done.9.got_ref, bf16[1024,1024]{1,0:T(8,128)(2,1)S(1)} %get-tuple-element.51.basis_ref, ...), custom_call_target="tpu_custom_call" | custom-call | tf_op jit(solution)/shard_map/pallas_call | solution.py:636
  118.5 4.1 %shard_map.108 = (f32[8,64,1024]{2,1,0:T(8,128)S(1)}, f32[8,128]{1,0:T(8,128)S(1)}) custom-call(s32[4]{0:T(128)S(1)} %copy-done.8, f32[8,64,512]{2,1,0:T(8,128)S(1)} %get-tuple-element.47.keep_ref, f32[8,64,512]{2,1,0:T(8,128)S(1)} %collective-permute-done.8.got_ref, f32[8,64,1024]{2,1,0:T(8,128)S(1)} %get-tuple-element.53.z_ref, ...), custom_call_target="tpu_custom_call" | custom-call | tf_op jit(solution)/shard_map/pallas_call | solution.py:636
  122.7 2.0 shard_map.110
  124.7 1.8 shard_map.109.held_ref
  127.4 5.4 %shard_map.111 = (f32[1024,512]{1,0:T(8,128)S(1)}, f32[8,64,512]{2,1,0:T(8,128)S(1)}, f32[8,64,512]{2,1,0:T(8,128)S(1)}, f32[8,128]{1,0:T(8,128)S(1)}) custom-call(s32[4]{0:T(128)S(1)} %copy-done.8, f32[8,64,512]{2,1,0:T(8,128)S(1)} %shard_map.109.held_ref, f32[520,512]{1,0:T(8,128)S(1)} %collective-permute-done.11.got_ref, ...), custom_call_target="tpu_custom_call" | custom-call | tf_op jit(solution)/shard_map/pallas_call | solution.py:636
  133.0 3.0 %shard_map.112 = (f32[8,64,512]{2,1,0:T(8,128)S(1)}, f32[8,64,512]{2,1,0:T(8,128)S(1)}) custom-call(s32[4]{0:T(128)S(1)} %copy-done.8, f32[1024,512]{1,0:T(8,128)S(1)} %get-tuple-element.64.column_ref, bf16[1024,1024]{1,0:T(8,128)(2,1)S(1)} %get-tuple-element.44.kernel_ref), custom_call_target="tpu_custom_call" | custom-call | tf_op jit(solution)/shard_map/pallas_call | solution.py:636
  136.5 3.0 %shard_map.113.z_ref.f_ref = f32[8,64,1024]{2,1,0:T(8,128)S(1)} custom-call(s32[4]{0:T(128)S(1)} %copy-done.8, f32[8,64,512]{2,1,0:T(8,128)S(1)} %get-tuple-element.67.keep_ref, f32[8,64,512]{2,1,0:T(8,128)S(1)} %collective-permute-done.13.got_ref, bf16[1024,1024]{1,0:T(8,128)(2,1)S(1)} %get-tuple-element.51.basis_ref), custom_call_target="tpu_custom_call" | custom-call | tf_op jit(solution)/shard_map/pallas_call | solution.py:636
  139.5 4.1 %shard_map.114 = (f32[8,64,1024]{2,1,0:T(8,128)S(1)}, f32[16,8,128]{2,1,0:T(8,128)S(1)}) custom-call(s32[4]{0:T(128)S(1)} %copy-done.8, f32[8,64,512]{2,1,0:T(8,128)S(1)} %get-tuple-element.65.keep_ref, f32[8,64,512]{2,1,0:T(8,128)S(1)} %collective-permute-done.12.got_ref, f32[8,64,1024]{2,1,0:T(8,128)S(1)} %shard_map.113.z_ref.f_ref, ...), custom_call_target="tpu_custom_call" | custom-call | tf_op jit(solution)/shard_map/pallas_call | solution.py:636
  143.6 11.7 %all_to_all.15.sum_ref = f32[16,8,128]{2,1,0:T(8,128)S(1)} all-to-all(f32[16,8,128]{2,1,0:T(8,128)S(1)} %get-tuple-element.70), channel_id=1, replica_groups=mesh['blocks'=2,'mode'=16] {'mode'}, dimensions={0} | all-to-all | bytes 131072 | tf_op jit(solution)/shard_map/all_to_all | solution.py:746
  155.3 1.6 combine.1
  157.0 95.8 %all_to_all.16.got_ref = f32[8,128,1024]{2,1,0:T(8,128)S(1)} all-to-all(f32[8,128,1024]{2,1,0:T(8,128)S(1)} %combine.1), channel_id=1, replica_groups={{0,2,4,6,8,10,12,14},{1,3,5,7,9,11,13,15},{16,18,20,22,24,26,28,30},{17..., dimensions={0} | all-to-all | bytes 8388608 | tf_op jit(solution)/shard_map/all_to_all | solution.py:759
  252.8 2.6 %finish.1 = (f32[2,4,64,1024]{3,2,1,0:T(8,128)}, f32[2,4,64,1024]{3,2,1,0:T(8,128)}) custom-call(f32[8,128,1024]{2,1,0:T(8,128)S(1)} %all_to_all.16.got_ref, f32[2,4,64,1024]{3,2,1,0:T(8,128)S(1)} %copy-done.1), custom_call_target="tpu_custom_call" | custom-call | tf_op jit(solution)/shard_map/finish/pallas_call | solution.py:770
  (53 shorter events, 10.8 us)
Async XLA Ops:
  6.6 7.6 %copy-start.15 = (f32[64]{0:T(128)S(1)}, f32[64]{0:T(128)}, u32[]{:S(2)}) copy-start(f32[64]{0:T(128)} %param.17) | copy-start | bytes 772
  6.7 96.1 %all-to-all-start = ((f32[16,64,512]{2,1,0:T(8,128)}), f32[16,64,512]{2,1,0:T(8,128)}, u32[]{:S(2)}, u32[]{:S(2)}) async-start(f32[16,64,512]{2,1,0:T(8,128)} %bitcast.11), calls=%async_computation | async-start | bytes 4194304 | tf_op jit(solution)/shard_map/all_to_all | solution.py:591
  14.3 78.6 %copy-start = (bf16[1024,1024]{1,0:T(8,128)(2,1)S(1)}, bf16[1024,1024]{1,0:T(8,128)(2,1)}, u32[]{:S(2)}) copy-start(bf16[1024,1024]{1,0:T(8,128)(2,1)} %second_hbm.1) | copy-start | bytes 6291460
  14.3 11.3 %collective-permute-start = (f32[1,64]{1,0:T(1,128)S(1)}, f32[1,64]{1,0:T(1,128)S(1)}, u32[]{:S(2)}, u32[]{:S(2)}) collective-permute-start(f32[1,64]{1,0:T(1,128)S(1)} %bitcast.12), channel_id=1, source_target_pairs={{0,1},{1,0},{2,3},{3,2},{4,5},{5,4},{6,7},{7,6},{8,9},{9,8},{10,11... | collective-permute-start | bytes 776 | tf_op jit(solution)/shard_map/ppermute | solution.py:597
  15.9 64.8 %collective-permute-start.3 = (s32[64,1024]{1,0:T(8,128)S(1)}, s32[64,1024]{1,0:T(8,128)S(1)}, u32[]{:S(2)}, u32[]{:S(2)}) collective-permute-start(s32[64,1024]{1,0:T(8,128)S(1)} %pick.1), channel_id=1, source_target_pairs={{0,8},{1,9},{2,10},{3,11},{4,12},{5,13},{6,14},{7,15},{8,0},{9,1},... | collective-permute-start | bytes 786440 | tf_op jit(solution)/shard_map/ppermute | solution.py:560
  20.4 0.7 copy-start.7
  21.1 59.6 %collective-permute-start.2 = (f32[64,1024]{1,0:T(8,128)S(1)}, f32[64,1024]{1,0:T(8,128)S(1)}, u32[]{:S(2)}, u32[]{:S(2)}) collective-permute-start(f32[64,1024]{1,0:T(8,128)S(1)} %get-tuple-element.38), channel_id=1, source_target_pairs={{0,4},{1,5},{2,6},{3,7},{4,8},{5,9},{6,10},{7,11},{8,12},{9,13},{1... | collective-permute-start | bytes 786440 | tf_op jit(solution)/shard_map/ppermute | solution.py:560
  22.6 58.1 %collective-permute-start.4 = (f32[64,1024]{1,0:T(8,128)S(1)}, f32[64,1024]{1,0:T(8,128)}, u32[]{:S(2)}, u32[]{:S(2)}) collective-permute-start(f32[64,1024]{1,0:T(8,128)S(1)} %get-tuple-element.39), channel_id=1, source_target_pairs={{0,12},{1,13},{2,14},{3,15},{4,0},{5,1},{6,2},{7,3},{8,4},{9,5},{1... | collective-permute-start | bytes 786440 | tf_op jit(solution)/shard_map/ppermute | solution.py:560
  25.7 3.6 %collective-permute-start.1 = (f32[1,128]{1,0:T(1,128)S(1)}, f32[1,128]{1,0:T(1,128)S(1)}, u32[]{:S(2)}, u32[]{:S(2)}) collective-permute-start(f32[1,128]{1,0:T(1,128)S(1)} %broadcast_select_fusion.1), channel_id=1, source_target_pairs={{0,2},{1,3},{2,0},{3,1},{4,6},{5,7},{6,4},{7,5},{8,10},{9,11},{10,... | collective-permute-start | bytes 1544 | tf_op jit(solution)/shard_map/ppermute | solution.py:597
  80.7 0.7 copy-start.13
  80.7 0.8 copy-start.14
  83.9 18.9 %collective-permute-start.7 = (f32[1,256]{1,0:T(1,128)}, f32[1,256]{1,0:T(1,128)S(1)}, u32[]{:S(2)}, u32[]{:S(2)}) collective-permute-start(f32[1,256]{1,0:T(1,128)} %get-tuple-element.40._.refs_0_), channel_id=1, source_target_pairs={{0,12},{1,13},{2,14},{3,15},{4,0},{5,1},{6,2},{7,3},{8,4},{9,5},{1... | collective-permute-start | bytes 3080 | tf_op jit(solution)/shard_map/ppermute | solution.py:615
  85.3 17.4 %collective-permute-start.6 = (f32[1,256]{1,0:T(1,128)}, f32[1,256]{1,0:T(1,128)S(1)}, u32[]{:S(2)}, u32[]{:S(2)}) collective-permute-start(f32[1,256]{1,0:T(1,128)} %get-tuple-element.40._.refs_0_), channel_id=1, source_target_pairs={{0,8},{1,9},{2,10},{3,11},{4,12},{5,13},{6,14},{7,15},{8,0},{9,1},... | collective-permute-start | bytes 3080 | tf_op jit(solution)/shard_map/ppermute | solution.py:615
  90.2 12.5 %collective-permute-start.5 = (f32[1,256]{1,0:T(1,128)}, f32[1,256]{1,0:T(1,128)S(1)}, u32[]{:S(2)}, u32[]{:S(2)}) collective-permute-start(f32[1,256]{1,0:T(1,128)} %get-tuple-element.40._.refs_0_), channel_id=1, source_target_pairs={{0,4},{1,5},{2,6},{3,7},{4,8},{5,9},{6,10},{7,11},{8,12},{9,13},{1... | collective-permute-start | bytes 3080 | tf_op jit(solution)/shard_map/ppermute | solution.py:615
  91.4 24.1 %collective-permute-start.10 = (f32[4,64,1024]{2,1,0:T(8,128)}, f32[4,64,1024]{2,1,0:T(8,128)}, u32[]{:S(2)}, u32[]{:S(2)}) collective-permute-start(f32[4,64,1024]{2,1,0:T(8,128)} %get-tuple-element.52.near_hbm), channel_id=1, source_target_pairs={{0,2},{1,3},{2,0},{3,1},{4,6},{5,7},{6,4},{7,5},{8,10},{9,11},{10,... | collective-permute-start | bytes 3145736 | tf_op jit(solution)/shard_map/ppermute | solution.py:613
  92.9 1.6 copy-start.2
  94.5 1.6 copy-start.3
  96.0 0.7 copy-start.11
  96.7 6.1 %copy-start.8 = (s32[4]{0:T(128)S(1)}, s32[4]{0:T(128)}, u32[]{:S(2)}) copy-start(s32[4]{0:T(128)} %pad_add_fusion.place_ref) | copy-start | bytes 52
  96.7 6.1 %copy-start.9 = (f32[8]{0:T(128)S(1)}, f32[8]{0:T(128)}, u32[]{:S(2)}) copy-start(f32[8]{0:T(128)} %table_ref.5) | copy-start | bytes 100
  96.7 6.1 %copy-start.10 = (f32[1024]{0:T(1024)S(1)}, f32[1024]{0:T(1024)}, u32[]{:S(2)}) copy-start(f32[1024]{0:T(1024)} %param.16) | copy-start | bytes 12292
  96.7 6.1 %copy-start.12 = (f32[1,256]{1,0:T(1,128)S(1)}, f32[1,256]{1,0:T(1,128)}, u32[]{:S(2)}) copy-start(f32[1,256]{1,0:T(1,128)} %get-tuple-element.40._.refs_0_) | copy-start | bytes 3076
  99.1 1.3 copy-start.4
  100.4 1.3 copy-start.5
  101.8 1.0 copy-start.6
  110.2 5.3 %collective-permute-start.9 = (f32[8,64,512]{2,1,0:T(8,128)S(1)}, f32[8,64,512]{2,1,0:T(8,128)S(1)}, u32[]{:S(2)}, u32[]{:S(2)}) collective-permute-start(f32[8,64,512]{2,1,0:T(8,128)S(1)} %get-tuple-element.50), channel_id=1, source_target_pairs={{0,1},{1,0},{2,3},{3,2},{4,5},{5,4},{6,7},{7,6},{8,9},{9,8},{10,11... | collective-permute-start | bytes 3145736 | tf_op jit(solution)/shard_map/ppermute | solution.py:633
  113.3 5.2 %collective-permute-start.8 = (f32[8,64,512]{2,1,0:T(8,128)S(1)}, f32[8,64,512]{2,1,0:T(8,128)S(1)}, u32[]{:S(2)}, u32[]{:S(2)}) collective-permute-start(f32[8,64,512]{2,1,0:T(8,128)S(1)} %get-tuple-element.48), channel_id=1, source_target_pairs={{0,1},{1,0},{2,3},{3,2},{4,5},{5,4},{6,7},{7,6},{8,9},{9,8},{10,11... | collective-permute-start | bytes 3145736 | tf_op jit(solution)/shard_map/ppermute | solution.py:633
  124.6 2.7 %collective-permute-start.11 = (f32[520,512]{1,0:T(8,128)S(1)}, f32[520,512]{1,0:T(8,128)S(1)}, u32[]{:S(2)}, u32[]{:S(2)}) collective-permute-start(f32[520,512]{1,0:T(8,128)S(1)} %shard_map.110), channel_id=1, source_target_pairs={{0,1},{1,0},{2,3},{3,2},{4,5},{5,4},{6,7},{7,6},{8,9},{9,8},{10,11... | collective-permute-start | bytes 3194888 | tf_op jit(solution)/shard_map/ppermute | solution.py:633
  132.8 3.7 %collective-permute-start.13 = (f32[8,64,512]{2,1,0:T(8,128)S(1)}, f32[8,64,512]{2,1,0:T(8,128)S(1)}, u32[]{:S(2)}, u32[]{:S(2)}) collective-permute-start(f32[8,64,512]{2,1,0:T(8,128)S(1)} %get-tuple-element.68), channel_id=1, source_target_pairs={{0,1},{1,0},{2,3},{3,2},{4,5},{5,4},{6,7},{7,6},{8,9},{9,8},{10,11... | collective-permute-start | bytes 3145736 | tf_op jit(solution)/shard_map/ppermute | solution.py:633
  136.0 3.4 %collective-permute-start.12 = (f32[8,64,512]{2,1,0:T(8,128)S(1)}, f32[8,64,512]{2,1,0:T(8,128)S(1)}, u32[]{:S(2)}, u32[]{:S(2)}) collective-permute-start(f32[8,64,512]{2,1,0:T(8,128)S(1)} %get-tuple-element.66), channel_id=1, source_target_pairs={{0,1},{1,0},{2,3},{3,2},{4,5},{5,4},{6,7},{7,6},{8,9},{9,8},{10,11... | collective-permute-start | bytes 3145736 | tf_op jit(solution)/shard_map/ppermute | solution.py:633
  157.0 95.8 %copy-start.1 = (f32[2,4,64,1024]{3,2,1,0:T(8,128)S(1)}, f32[2,4,64,1024]{3,2,1,0:T(8,128)}, u32[]{:S(2)}) copy-start(f32[2,4,64,1024]{3,2,1,0:T(8,128)} %right_ref.3) | copy-start | bytes 6291460

commit v15 on v14

--- a/solution.py
+++ b/solution.py
@@ -264,9 +264,12 @@
     wide_refs, refs, outs = refs[:-13], refs[-7:], refs[-13:-7]
     start_ref, weight_ref, column_ref, keep_ref, send_ref, sum_ref = outs
     lower_ref, basis_ref, kernel_ref, second_ref, scratch_ref, field_ref, done = refs
+    groups = field_ref.shape[0]
+    first, second = pl.ds(0, groups // 2), pl.ds(groups // 2, groups // 2)
     copies = copy_into(
         (
-            (field_hbm, field_ref),
+            (field_hbm.at[first], field_ref.at[first]),
+            (field_hbm.at[second], field_ref.at[second]),
             (lower_hbm, lower_ref),
             (basis_hbm, basis_ref),
             (kernel_hbm, kernel_ref),
@@ -274,7 +277,7 @@
         ),
         done,
     )
-    for copy in copies[:2]:
+    for copy in copies[:3]:
         copy.start()
     mean = functools.reduce(jnp.add, [table_ref[at] for at in range(NCLASS)]) * (1.0 / NCLASS)
     height, width = start_ref.shape
@@ -290,23 +293,27 @@
         for at in range(0, part, 128):
             lanes = slice(block * part + at, block * part + at + 128)
             weight_ref[:, lanes] = 1.0 / (tall * wide[:, at : at + 128] + mean)
+    middle = height // 2
     copies[0].wait()
-    field = field_ref[...].reshape(height, width)
-    for copy in copies[2:]:
+    start = side_by_side(field_ref[: groups // 2].reshape(middle, width))
+    above = times_both(upper_ref[:, :middle], start)
+    copies[1].wait()
+    for copy in copies[3:]:
         copy.start()
-    both = side_by_side(field)
-    above = times_both(upper_ref[...], both)
-    copies[1].wait()
-    spectral = jnp.concatenate([above, times_both(lower_ref[...], both)], axis=0)
+    end = side_by_side(field_ref[groups // 2 :].reshape(middle, width))
+    above = above + times_both(upper_ref[:, middle:], end)
+    copies[2].wait()
+    below = times_both(lower_ref[...], jnp.concatenate([start, end], axis=0))
+    spectral = jnp.concatenate([above, below], axis=0)
     weighted = spectral * weight_ref[...]
-    start_ref[...] = field
+    start_ref[...] = field_ref[...].reshape(height, width)
     store_sums(sum_ref, [fold(spectral * weighted)])
-    copies[2].wait()
+    copies[3].wait()
     column = times_left(basis_ref[...], weighted)
     column_ref[...] = column
     split_rows(place_ref, column, scratch_ref, keep_ref, send_ref)
-    copies[3].wait()
     copies[4].wait()
+    copies[5].wait()
 
 
 def next_column_kernel(
@@ -667,7 +674,7 @@
         + [hbm] * 5
         + [full(height // 2, height), full(1, height)]
         + [full(*value.shape) for value in shifted],
-        [pltpu.VMEM((groups, rows, half), F32), pltpu.SemaphoreType.DMA((5,))],
+        [pltpu.VMEM((groups, rows, half), F32), pltpu.SemaphoreType.DMA((6,))],
         16,
         [bf16_half] + [bf16_square] * 3,
     )

time: 256 us -> 256 us (level)
  no operation moved by 1% of the time
where the time goes in v15:
time: 256 us; the launch traced here: 255 us
  blocking collectives  107 us (42%)
  waiting for transfers between devices  55.8 us (22%)
  Pallas kernels  54.8 us (21%)
  starting transfers between devices  26.2 us (10%)
  local copies, waits for them, and re-layouts  9 us (4%)
    all_to_all x1, blocking collectives, paired_body(): lax.all_to_all(answer, 'mode', split_axis=0, concat_axis=0, axis_index_gr...  95.8 us
    ppermute x3, waiting for transfers between devices, plane_shift(): return lax.ppermute(value, 'mode', pairs)  50.8 us
    pallas_call x10, Pallas kernels, call(): pl.pallas_call(kernel, grid=(1,), in_specs=specs or [smem] + [full(*value...  36.6 us
    all_to_all x1, blocking collectives, paired_body(): sums = lax.all_to_all(sums, 'mode', split_axis=0, concat_axis=0, tiled=True)  11.7 us
    unnamed x32, local copies, waits for them, and re-layouts  9 us
    all_to_all x1, starting transfers between devices, paired_body(): lax.all_to_all(outgoing.reshape(groups, rows, half), 'mode', split_axis=0...  7.6 us
    ppermute x3, starting transfers between devices, paired_body(): lax.ppermute(eigen, 'mode', [(at, (at + by * unit) % groups) for at in ra...  7.53 us
    ppermute x3, starting transfers between devices, plane_shift(): return lax.ppermute(value, 'mode', pairs)  6.34 us
  transfers between devices with their start and end apart: 15, of which 4 were waited for; matrix products, arithmetic and copies ran while one was open for 1% of the time, Pallas kernels for 11%

profile of v15, /device:TPU:0, one launch (start us, length us, event | category | flops | bytes accessed | tf_op | source)
XLA Modules:
  0.0 255.4 jit_solution(12579746566630423927)
XLA Ops:
  0.6 6.0 %outgoing.1 = f32[4,2,2,64,512]{4,3,2,1,0:T(8,128)} custom-call(f32[2,4,64,1024]{3,2,1,0:T(8,128)} %right_ref.3, bf16[1024,1024]{1,0:T(8,128)(2,1)} %second_hbm.1), custom_call_target="tpu_custom_call" | custom-call | tf_op jit(solution)/shard_map/outgoing/pallas_call | solution.py:586
  6.7 7.6 %all-to-all-start = ((f32[16,64,512]{2,1,0:T(8,128)}), f32[16,64,512]{2,1,0:T(8,128)}, u32[]{:S(2)}, u32[]{:S(2)}) async-start(f32[16,64,512]{2,1,0:T(8,128)} %bitcast.11), calls=%async_computation | async-start | bytes 4194304 | tf_op jit(solution)/shard_map/all_to_all | solution.py:598
  15.9 2.5 collective-permute-start.3
  18.4 2.0 shard_map.104
  21.1 1.5 collective-permute-start.2
  22.6 2.4 collective-permute-start.4
  25.7 1.5 collective-permute-start.1
  27.2 2.1 collective-permute-done.1
  29.8 50.8 %collective-permute-done.3.refs_2_ = s32[64,1024]{1,0:T(8,128)S(1)} collective-permute-done((s32[64,1024]{1,0:T(8,128)S(1)}, s32[64,1024]{1,0:T(8,128)S(1)}, u32[]{:S(2)}, u32[]{:S(2)}) %collective-permute-start.3) | collective-permute-done | bytes 262176 | tf_op jit(solution)/shard_map/ppermute | solution.py:567
  81.5 2.4 join.1
  83.9 1.5 collective-permute-start.7
  85.3 4.9 %collective-permute-start.6 = (f32[1,256]{1,0:T(1,128)}, f32[1,256]{1,0:T(1,128)S(1)}, u32[]{:S(2)}, u32[]{:S(2)}) collective-permute-start(f32[1,256]{1,0:T(1,128)} %get-tuple-element.40._.refs_0_), channel_id=1, source_target_pairs={{0,8},{1,9},{2,10},{3,11},{4,12},{5,13},{6,14},{7,15},{8,0},{9,1},... | collective-permute-start | bytes 3080 | tf_op jit(solution)/shard_map/ppermute | solution.py:622
  91.4 1.5 collective-permute-start.10
  92.9 1.6 copy-done.2
  94.5 1.6 copy-done.3
  96.7 2.4 prepare.1
  100.4 1.3 copy-done.5
  102.8 7.1 %shard_map.105 = (f32[1024,512]{1,0:T(8,128)S(1)}, f32[1024,512]{1,0:T(8,128)S(1)}, f32[1024,512]{1,0:T(8,128)S(1)}, f32[8,64,512]{2,1,0:T(8,128)S(1)}, f32[8,64...) custom-call(s32[4]{0:T(128)S(1)} %copy-done.8, ...), custom_call_target="tpu_custom_call" | custom-call | tf_op jit(solution)/shard_map/pallas_call | solution.py:643
  109.9 3.0 %shard_map.106 = (f32[8,64,512]{2,1,0:T(8,128)S(1)}, f32[8,64,512]{2,1,0:T(8,128)S(1)}, bf16[1024,1024]{1,0:T(8,128)(2,1)S(1)}, bf16[1024,1024]{1,0:T(8,128)(2,1)S(1)}) custom-call(s32[4]{0:T(128)S(1)} %copy-done.8, f32[1024,512]{1,0:T(8,128)S(1)} %get-tuple-element.43.column_ref, bf16[1024,1024]{1,0:T(8,128)(2,1)S(1)} %get-tuple-element.44.kernel_ref, ...), custom_call_target="tpu_custom_call" | custom-call | tf_op jit(solution)/shard_map/pallas_call | solution.py:643
  113.5 1.9 collective-permute-done.10.far_hbm
  115.5 3.0 %shard_map.107 = (f32[8,64,1024]{2,1,0:T(8,128)S(1)}, f32[4,2,64,1024]{3,2,1,0:T(8,128)S(1)}) custom-call(s32[4]{0:T(128)S(1)} %copy-done.8, f32[8,64,512]{2,1,0:T(8,128)S(1)} %get-tuple-element.49.keep_ref, f32[8,64,512]{2,1,0:T(8,128)S(1)} %collective-permute-done.9.got_ref, bf16[1024,1024]{1,0:T(8,128)(2,1)S(1)} %get-tuple-element.51.basis_ref, ...), custom_call_target="tpu_custom_call" | custom-call | tf_op jit(solution)/shard_map/pallas_call | solution.py:643
  118.5 4.1 %shard_map.108 = (f32[8,64,1024]{2,1,0:T(8,128)S(1)}, f32[8,128]{1,0:T(8,128)S(1)}) custom-call(s32[4]{0:T(128)S(1)} %copy-done.8, f32[8,64,512]{2,1,0:T(8,128)S(1)} %get-tuple-element.47.keep_ref, f32[8,64,512]{2,1,0:T(8,128)S(1)} %collective-permute-done.8.got_ref, f32[8,64,1024]{2,1,0:T(8,128)S(1)} %get-tuple-element.53.z_ref, ...), custom_call_target="tpu_custom_call" | custom-call | tf_op jit(solution)/shard_map/pallas_call | solution.py:643
  122.7 2.0 shard_map.110
  124.7 1.8 shard_map.109.held_ref
  127.4 5.4 %shard_map.111 = (f32[1024,512]{1,0:T(8,128)S(1)}, f32[8,64,512]{2,1,0:T(8,128)S(1)}, f32[8,64,512]{2,1,0:T(8,128)S(1)}, f32[8,128]{1,0:T(8,128)S(1)}) custom-call(s32[4]{0:T(128)S(1)} %copy-done.8, f32[8,64,512]{2,1,0:T(8,128)S(1)} %shard_map.109.held_ref, f32[520,512]{1,0:T(8,128)S(1)} %collective-permute-done.11.got_ref, ...), custom_call_target="tpu_custom_call" | custom-call | tf_op jit(solution)/shard_map/pallas_call | solution.py:643
  133.0 3.0 %shard_map.112 = (f32[8,64,512]{2,1,0:T(8,128)S(1)}, f32[8,64,512]{2,1,0:T(8,128)S(1)}) custom-call(s32[4]{0:T(128)S(1)} %copy-done.8, f32[1024,512]{1,0:T(8,128)S(1)} %get-tuple-element.64.column_ref, bf16[1024,1024]{1,0:T(8,128)(2,1)S(1)} %get-tuple-element.44.kernel_ref), custom_call_target="tpu_custom_call" | custom-call | tf_op jit(solution)/shard_map/pallas_call | solution.py:643
  136.5 3.0 %shard_map.113.z_ref.f_ref = f32[8,64,1024]{2,1,0:T(8,128)S(1)} custom-call(s32[4]{0:T(128)S(1)} %copy-done.8, f32[8,64,512]{2,1,0:T(8,128)S(1)} %get-tuple-element.67.keep_ref, f32[8,64,512]{2,1,0:T(8,128)S(1)} %collective-permute-done.13.got_ref, bf16[1024,1024]{1,0:T(8,128)(2,1)S(1)} %get-tuple-element.51.basis_ref), custom_call_target="tpu_custom_call" | custom-call | tf_op jit(solution)/shard_map/pallas_call | solution.py:643
  139.5 4.1 %shard_map.114 = (f32[8,64,1024]{2,1,0:T(8,128)S(1)}, f32[16,8,128]{2,1,0:T(8,128)S(1)}) custom-call(s32[4]{0:T(128)S(1)} %copy-done.8, f32[8,64,512]{2,1,0:T(8,128)S(1)} %get-tuple-element.65.keep_ref, f32[8,64,512]{2,1,0:T(8,128)S(1)} %collective-permute-done.12.got_ref, f32[8,64,1024]{2,1,0:T(8,128)S(1)} %shard_map.113.z_ref.f_ref, ...), custom_call_target="tpu_custom_call" | custom-call | tf_op jit(solution)/shard_map/pallas_call | solution.py:643
  143.7 11.7 %all_to_all.15.sum_ref = f32[16,8,128]{2,1,0:T(8,128)S(1)} all-to-all(f32[16,8,128]{2,1,0:T(8,128)S(1)} %get-tuple-element.70), channel_id=1, replica_groups=mesh['blocks'=2,'mode'=16] {'mode'}, dimensions={0} | all-to-all | bytes 131072 | tf_op jit(solution)/shard_map/all_to_all | solution.py:753
  155.3 1.6 combine.1
  157.0 95.8 %all_to_all.16.got_ref = f32[8,128,1024]{2,1,0:T(8,128)S(1)} all-to-all(f32[8,128,1024]{2,1,0:T(8,128)S(1)} %combine.1), channel_id=1, replica_groups={{0,2,4,6,8,10,12,14},{1,3,5,7,9,11,13,15},{16,18,20,22,24,26,28,30},{17..., dimensions={0} | all-to-all | bytes 8388608 | tf_op jit(solution)/shard_map/all_to_all | solution.py:766
  252.8 2.6 %finish.1 = (f32[2,4,64,1024]{3,2,1,0:T(8,128)}, f32[2,4,64,1024]{3,2,1,0:T(8,128)}) custom-call(f32[8,128,1024]{2,1,0:T(8,128)S(1)} %all_to_all.16.got_ref, f32[2,4,64,1024]{3,2,1,0:T(8,128)S(1)} %copy-done.1), custom_call_target="tpu_custom_call" | custom-call | tf_op jit(solution)/shard_map/finish/pallas_call | solution.py:777
  (53 shorter events, 10.8 us)
Async XLA Ops:
  6.6 7.6 %copy-start.15 = (f32[64]{0:T(128)S(1)}, f32[64]{0:T(128)}, u32[]{:S(2)}) copy-start(f32[64]{0:T(128)} %param.17) | copy-start | bytes 772
  6.7 96.1 %all-to-all-start = ((f32[16,64,512]{2,1,0:T(8,128)}), f32[16,64,512]{2,1,0:T(8,128)}, u32[]{:S(2)}, u32[]{:S(2)}) async-start(f32[16,64,512]{2,1,0:T(8,128)} %bitcast.11), calls=%async_computation | async-start | bytes 4194304 | tf_op jit(solution)/shard_map/all_to_all | solution.py:598
  14.3 78.6 %copy-start = (bf16[1024,1024]{1,0:T(8,128)(2,1)S(1)}, bf16[1024,1024]{1,0:T(8,128)(2,1)}, u32[]{:S(2)}) copy-start(bf16[1024,1024]{1,0:T(8,128)(2,1)} %second_hbm.1) | copy-start | bytes 6291460
  14.3 11.3 %collective-permute-start = (f32[1,64]{1,0:T(1,128)S(1)}, f32[1,64]{1,0:T(1,128)S(1)}, u32[]{:S(2)}, u32[]{:S(2)}) collective-permute-start(f32[1,64]{1,0:T(1,128)S(1)} %bitcast.12), channel_id=1, source_target_pairs={{0,1},{1,0},{2,3},{3,2},{4,5},{5,4},{6,7},{7,6},{8,9},{9,8},{10,11... | collective-permute-start | bytes 776 | tf_op jit(solution)/shard_map/ppermute | solution.py:604
  15.9 64.8 %collective-permute-start.3 = (s32[64,1024]{1,0:T(8,128)S(1)}, s32[64,1024]{1,0:T(8,128)S(1)}, u32[]{:S(2)}, u32[]{:S(2)}) collective-permute-start(s32[64,1024]{1,0:T(8,128)S(1)} %pick.1), channel_id=1, source_target_pairs={{0,8},{1,9},{2,10},{3,11},{4,12},{5,13},{6,14},{7,15},{8,0},{9,1},... | collective-permute-start | bytes 786440 | tf_op jit(solution)/shard_map/ppermute | solution.py:567
  20.4 0.7 copy-start.7
  21.1 59.6 %collective-permute-start.2 = (f32[64,1024]{1,0:T(8,128)S(1)}, f32[64,1024]{1,0:T(8,128)S(1)}, u32[]{:S(2)}, u32[]{:S(2)}) collective-permute-start(f32[64,1024]{1,0:T(8,128)S(1)} %get-tuple-element.38), channel_id=1, source_target_pairs={{0,4},{1,5},{2,6},{3,7},{4,8},{5,9},{6,10},{7,11},{8,12},{9,13},{1... | collective-permute-start | bytes 786440 | tf_op jit(solution)/shard_map/ppermute | solution.py:567
  22.6 58.1 %collective-permute-start.4 = (f32[64,1024]{1,0:T(8,128)S(1)}, f32[64,1024]{1,0:T(8,128)}, u32[]{:S(2)}, u32[]{:S(2)}) collective-permute-start(f32[64,1024]{1,0:T(8,128)S(1)} %get-tuple-element.39), channel_id=1, source_target_pairs={{0,12},{1,13},{2,14},{3,15},{4,0},{5,1},{6,2},{7,3},{8,4},{9,5},{1... | collective-permute-start | bytes 786440 | tf_op jit(solution)/shard_map/ppermute | solution.py:567
  25.7 3.6 %collective-permute-start.1 = (f32[1,128]{1,0:T(1,128)S(1)}, f32[1,128]{1,0:T(1,128)S(1)}, u32[]{:S(2)}, u32[]{:S(2)}) collective-permute-start(f32[1,128]{1,0:T(1,128)S(1)} %broadcast_select_fusion.1), channel_id=1, source_target_pairs={{0,2},{1,3},{2,0},{3,1},{4,6},{5,7},{6,4},{7,5},{8,10},{9,11},{10,... | collective-permute-start | bytes 1544 | tf_op jit(solution)/shard_map/ppermute | solution.py:604
  80.7 0.7 copy-start.13
  80.7 0.8 copy-start.14
  83.9 18.9 %collective-permute-start.7 = (f32[1,256]{1,0:T(1,128)}, f32[1,256]{1,0:T(1,128)S(1)}, u32[]{:S(2)}, u32[]{:S(2)}) collective-permute-start(f32[1,256]{1,0:T(1,128)} %get-tuple-element.40._.refs_0_), channel_id=1, source_target_pairs={{0,12},{1,13},{2,14},{3,15},{4,0},{5,1},{6,2},{7,3},{8,4},{9,5},{1... | collective-permute-start | bytes 3080 | tf_op jit(solution)/shard_map/ppermute | solution.py:622
  85.3 17.4 %collective-permute-start.6 = (f32[1,256]{1,0:T(1,128)}, f32[1,256]{1,0:T(1,128)S(1)}, u32[]{:S(2)}, u32[]{:S(2)}) collective-permute-start(f32[1,256]{1,0:T(1,128)} %get-tuple-element.40._.refs_0_), channel_id=1, source_target_pairs={{0,8},{1,9},{2,10},{3,11},{4,12},{5,13},{6,14},{7,15},{8,0},{9,1},... | collective-permute-start | bytes 3080 | tf_op jit(solution)/shard_map/ppermute | solution.py:622
  90.2 12.5 %collective-permute-start.5 = (f32[1,256]{1,0:T(1,128)}, f32[1,256]{1,0:T(1,128)S(1)}, u32[]{:S(2)}, u32[]{:S(2)}) collective-permute-start(f32[1,256]{1,0:T(1,128)} %get-tuple-element.40._.refs_0_), channel_id=1, source_target_pairs={{0,4},{1,5},{2,6},{3,7},{4,8},{5,9},{6,10},{7,11},{8,12},{9,13},{1... | collective-permute-start | bytes 3080 | tf_op jit(solution)/shard_map/ppermute | solution.py:622
  91.4 24.1 %collective-permute-start.10 = (f32[4,64,1024]{2,1,0:T(8,128)}, f32[4,64,1024]{2,1,0:T(8,128)}, u32[]{:S(2)}, u32[]{:S(2)}) collective-permute-start(f32[4,64,1024]{2,1,0:T(8,128)} %get-tuple-element.52.near_hbm), channel_id=1, source_target_pairs={{0,2},{1,3},{2,0},{3,1},{4,6},{5,7},{6,4},{7,5},{8,10},{9,11},{10,... | collective-permute-start | bytes 3145736 | tf_op jit(solution)/shard_map/ppermute | solution.py:620
  92.9 1.6 copy-start.2
  94.5 1.6 copy-start.3
  96.0 0.7 copy-start.11
  96.7 6.1 %copy-start.8 = (s32[4]{0:T(128)S(1)}, s32[4]{0:T(128)}, u32[]{:S(2)}) copy-start(s32[4]{0:T(128)} %pad_add_fusion.place_ref) | copy-start | bytes 52
  96.7 6.1 %copy-start.9 = (f32[8]{0:T(128)S(1)}, f32[8]{0:T(128)}, u32[]{:S(2)}) copy-start(f32[8]{0:T(128)} %table_ref.5) | copy-start | bytes 100
  96.7 6.1 %copy-start.10 = (f32[1024]{0:T(1024)S(1)}, f32[1024]{0:T(1024)}, u32[]{:S(2)}) copy-start(f32[1024]{0:T(1024)} %param.16) | copy-start | bytes 12292
  96.7 6.1 %copy-start.12 = (f32[1,256]{1,0:T(1,128)S(1)}, f32[1,256]{1,0:T(1,128)}, u32[]{:S(2)}) copy-start(f32[1,256]{1,0:T(1,128)} %get-tuple-element.40._.refs_0_) | copy-start | bytes 3076
  99.1 1.3 copy-start.4
  100.4 1.3 copy-start.5
  101.8 1.0 copy-start.6
  109.9 5.6 %collective-permute-start.9 = (f32[8,64,512]{2,1,0:T(8,128)S(1)}, f32[8,64,512]{2,1,0:T(8,128)S(1)}, u32[]{:S(2)}, u32[]{:S(2)}) collective-permute-start(f32[8,64,512]{2,1,0:T(8,128)S(1)} %get-tuple-element.50), channel_id=1, source_target_pairs={{0,1},{1,0},{2,3},{3,2},{4,5},{5,4},{6,7},{7,6},{8,9},{9,8},{10,11... | collective-permute-start | bytes 3145736 | tf_op jit(solution)/shard_map/ppermute | solution.py:640
  113.0 5.5 %collective-permute-start.8 = (f32[8,64,512]{2,1,0:T(8,128)S(1)}, f32[8,64,512]{2,1,0:T(8,128)S(1)}, u32[]{:S(2)}, u32[]{:S(2)}) collective-permute-start(f32[8,64,512]{2,1,0:T(8,128)S(1)} %get-tuple-element.48), channel_id=1, source_target_pairs={{0,1},{1,0},{2,3},{3,2},{4,5},{5,4},{6,7},{7,6},{8,9},{9,8},{10,11... | collective-permute-start | bytes 3145736 | tf_op jit(solution)/shard_map/ppermute | solution.py:640
  124.6 2.7 %collective-permute-start.11 = (f32[520,512]{1,0:T(8,128)S(1)}, f32[520,512]{1,0:T(8,128)S(1)}, u32[]{:S(2)}, u32[]{:S(2)}) collective-permute-start(f32[520,512]{1,0:T(8,128)S(1)} %shard_map.110), channel_id=1, source_target_pairs={{0,1},{1,0},{2,3},{3,2},{4,5},{5,4},{6,7},{7,6},{8,9},{9,8},{10,11... | collective-permute-start | bytes 3194888 | tf_op jit(solution)/shard_map/ppermute | solution.py:640
  132.8 3.7 %collective-permute-start.13 = (f32[8,64,512]{2,1,0:T(8,128)S(1)}, f32[8,64,512]{2,1,0:T(8,128)S(1)}, u32[]{:S(2)}, u32[]{:S(2)}) collective-permute-start(f32[8,64,512]{2,1,0:T(8,128)S(1)} %get-tuple-element.68), channel_id=1, source_target_pairs={{0,1},{1,0},{2,3},{3,2},{4,5},{5,4},{6,7},{7,6},{8,9},{9,8},{10,11... | collective-permute-start | bytes 3145736 | tf_op jit(solution)/shard_map/ppermute | solution.py:640
  136.1 3.5 %collective-permute-start.12 = (f32[8,64,512]{2,1,0:T(8,128)S(1)}, f32[8,64,512]{2,1,0:T(8,128)S(1)}, u32[]{:S(2)}, u32[]{:S(2)}) collective-permute-start(f32[8,64,512]{2,1,0:T(8,128)S(1)} %get-tuple-element.66), channel_id=1, source_target_pairs={{0,1},{1,0},{2,3},{3,2},{4,5},{5,4},{6,7},{7,6},{8,9},{9,8},{10,11... | collective-permute-start | bytes 3145736 | tf_op jit(solution)/shard_map/ppermute | solution.py:640
  157.0 95.8 %copy-start.1 = (f32[2,4,64,1024]{3,2,1,0:T(8,128)S(1)}, f32[2,4,64,1024]{3,2,1,0:T(8,128)}, u32[]{:S(2)}) copy-start(f32[2,4,64,1024]{3,2,1,0:T(8,128)} %right_ref.3) | copy-start | bytes 6291460

commit v16 on v15

--- a/solution.py
+++ b/solution.py
@@ -495,12 +495,18 @@
     out_ref[:, share:, :] = on_z * image_ref[...] + on_f * f_image_ref[...]
 
 
-def finish_kernel(got_ref, right_ref, solution_ref, residual_ref):
-    samples = got_ref.shape[0]
-    rows = got_ref.shape[1] // 2
-    for sample in range(samples):
-        solution_ref[sample, 0] = got_ref[sample, :rows, :]
-        residual_ref[sample, 0] = right_ref[sample, 0] - got_ref[sample, rows:, :]
+def finish_kernel(got_ref, right_ref, solution_hbm, residual_hbm, residual_ref, done):
+    samples, _, rows, _ = right_ref.shape
+    kept = [(got_ref.at[:, at, :rows], solution_hbm.at[at]) for at in range(samples)]
+    made = [(residual_ref.at[at], residual_hbm.at[at]) for at in range(samples)]
+    copies = copy_into(kept + made, done)
+    for copy in copies[:samples]:
+        copy.start()
+    for at in range(samples):
+        residual_ref[at] = right_ref[at] - got_ref[:, at, rows:]
+        copies[samples + at].start()
+    for copy in copies:
+        copy.wait()
 
 
 def paired_body(
@@ -566,7 +572,7 @@
         pairs = [(at, (at + by * unit) % groups) for at in range(groups)]
         return lax.ppermute(value, "mode", pairs)
 
-    ahead = planes // 2
+    ahead = 1
     others = [by for by in range(planes) if by != ahead]
     near = [None] * planes
     picked = pl.pallas_call(
@@ -772,17 +778,18 @@
         tiled=True,
     )
 
-    block = pl.BlockSpec((samples, 1, rows, width), lambda p: (0, p, 0, 0))
+    answer = answer.reshape(planes, samples, 2 * rows, width)
     return tuple(
         pl.pallas_call(
             finish_kernel,
-            grid=(planes,),
-            in_specs=[
-                pl.BlockSpec((samples, 2 * rows, width), lambda p: (p, 0, 0)),
-                block,
+            grid=(1,),
+            in_specs=[full(*answer.shape), full(*right_side.shape)],
+            out_specs=[hbm, hbm],
+            out_shape=[shape_of(*right_side.shape)] * 2,
+            scratch_shapes=[
+                pltpu.VMEM(right_side.shape, F32),
+                pltpu.SemaphoreType.DMA((2 * samples,)),
             ],
-            out_specs=[block, block],
-            out_shape=[shape_of(*right_side.shape)] * 2,
             compiler_params=params(1, 10),
             name="finish",
         )(answer, right_side)

time: 256 us -> 256 us (level)
  transfers between devices with their start and end apart: 15 -> 15, of which waited for: 4 -> 5; matrix products, arithmetic and copies ran while one was open for 1% -> 1% of each run, Pallas kernels for 11% -> 11%
where the time goes in v16:
time: 256 us; the launch traced here: 255 us
  blocking collectives  108 us (42%)
  waiting for transfers between devices  56.9 us (22%)
  Pallas kernels  54.3 us (21%)
  starting transfers between devices  24.8 us (10%)
  local copies, waits for them, and re-layouts  8.89 us (3%)
    all_to_all x1, blocking collectives, paired_body(): lax.all_to_all(answer, 'mode', split_axis=0, concat_axis=0, axis_index_gr...  95.8 us
    ppermute x3, waiting for transfers between devices, plane_shift(): return lax.ppermute(value, 'mode', pairs)  51.8 us
    pallas_call x10, Pallas kernels, call(): pl.pallas_call(kernel, grid=(1,), in_specs=specs or [smem] + [full(*value...  36.6 us
    all_to_all x1, blocking collectives, paired_body(): sums = lax.all_to_all(sums, 'mode', split_axis=0, concat_axis=0, tiled=True)  12.2 us
    unnamed x32, local copies, waits for them, and re-layouts  8.89 us
    all_to_all x1, starting transfers between devices, paired_body(): lax.all_to_all(outgoing.reshape(groups, rows, half), 'mode', split_axis=0...  7.6 us
    ppermute x3, starting transfers between devices, paired_body(): lax.ppermute(eigen, 'mode', [(at, (at + by * unit) % groups) for at in ra...  7.07 us
    pallas_call x1, Pallas kernels, paired_body(): pl.pallas_call(outgoing_kernel, grid=(planes,), in_specs=[pl.BlockSpec((s...  6.02 us
  transfers between devices with their start and end apart: 15, of which 5 were waited for; matrix products, arithmetic and copies ran while one was open for 1% of the time, Pallas kernels for 11%

profile of v16, /device:TPU:0, one launch (start us, length us, event | category | flops | bytes accessed | tf_op | source)
XLA Modules:
  0.0 255.3 jit_solution(8422937085695419258)
XLA Ops:
  0.6 6.0 %outgoing.1 = f32[4,2,2,64,512]{4,3,2,1,0:T(8,128)} custom-call(f32[2,4,64,1024]{3,2,1,0:T(8,128)} %right_ref.3, bf16[1024,1024]{1,0:T(8,128)(2,1)} %second_hbm.1), custom_call_target="tpu_custom_call" | custom-call | tf_op jit(solution)/shard_map/outgoing/pallas_call | solution.py:592
  6.7 7.6 %all-to-all-start = ((f32[16,64,512]{2,1,0:T(8,128)}), f32[16,64,512]{2,1,0:T(8,128)}, u32[]{:S(2)}, u32[]{:S(2)}) async-start(f32[16,64,512]{2,1,0:T(8,128)} %bitcast.13), calls=%async_computation | async-start | bytes 4194304 | tf_op jit(solution)/shard_map/all_to_all | solution.py:604
  15.9 1.6 collective-permute-start.2
  17.5 2.0 shard_map.104
  20.2 2.4 collective-permute-start.3
  22.6 1.5 collective-permute-start.4
  24.8 1.5 collective-permute-start.1
  26.3 2.0 collective-permute-done.1
  28.9 30.4 %collective-permute-done.2.refs_1_ = s32[64,1024]{1,0:T(8,128)S(1)} collective-permute-done((s32[64,1024]{1,0:T(8,128)S(1)}, s32[64,1024]{1,0:T(8,128)S(1)}, u32[]{:S(2)}, u32[]{:S(2)}) %collective-permute-start.2) | collective-permute-done | bytes 262176 | tf_op jit(solution)/shard_map/ppermute | solution.py:573
  59.2 21.4 %collective-permute-done.3.refs_2_ = f32[64,1024]{1,0:T(8,128)S(1)} collective-permute-done((f32[64,1024]{1,0:T(8,128)S(1)}, f32[64,1024]{1,0:T(8,128)S(1)}, u32[]{:S(2)}, u32[]{:S(2)}) %collective-permute-start.3) | collective-permute-done | bytes 262176 | tf_op jit(solution)/shard_map/ppermute | solution.py:573
  81.4 2.4 join.1
  83.8 6.5 %collective-permute-start.7 = (f32[1,256]{1,0:T(1,128)}, f32[1,256]{1,0:T(1,128)S(1)}, u32[]{:S(2)}, u32[]{:S(2)}) collective-permute-start(f32[1,256]{1,0:T(1,128)} %get-tuple-element.40._.refs_0_), channel_id=1, source_target_pairs={{0,12},{1,13},{2,14},{3,15},{4,0},{5,1},{6,2},{7,3},{8,4},{9,5},{1... | collective-permute-start | bytes 3080 | tf_op jit(solution)/shard_map/ppermute | solution.py:628
  90.8 1.5 collective-permute-start.10
  92.3 1.6 copy-done.2
  93.9 1.6 copy-done.3
  96.2 2.4 prepare.1
  99.9 1.3 copy-done.5
  102.3 7.1 %shard_map.105 = (f32[1024,512]{1,0:T(8,128)S(1)}, f32[1024,512]{1,0:T(8,128)S(1)}, f32[1024,512]{1,0:T(8,128)S(1)}, f32[8,64,512]{2,1,0:T(8,128)S(1)}, f32[8,64...) custom-call(s32[4]{0:T(128)S(1)} %copy-done.8, ...), custom_call_target="tpu_custom_call" | custom-call | tf_op jit(solution)/shard_map/pallas_call | solution.py:649
  109.4 3.0 %shard_map.106 = (f32[8,64,512]{2,1,0:T(8,128)S(1)}, f32[8,64,512]{2,1,0:T(8,128)S(1)}, bf16[1024,1024]{1,0:T(8,128)(2,1)S(1)}, bf16[1024,1024]{1,0:T(8,128)(2,1)S(1)}) custom-call(s32[4]{0:T(128)S(1)} %copy-done.8, f32[1024,512]{1,0:T(8,128)S(1)} %get-tuple-element.43.column_ref, bf16[1024,1024]{1,0:T(8,128)(2,1)S(1)} %get-tuple-element.44.kernel_ref, ...), custom_call_target="tpu_custom_call" | custom-call | tf_op jit(solution)/shard_map/pallas_call | solution.py:649
  113.0 2.2 collective-permute-done.10.far_hbm
  115.2 3.0 %shard_map.107 = (f32[8,64,1024]{2,1,0:T(8,128)S(1)}, f32[4,2,64,1024]{3,2,1,0:T(8,128)S(1)}) custom-call(s32[4]{0:T(128)S(1)} %copy-done.8, f32[8,64,512]{2,1,0:T(8,128)S(1)} %get-tuple-element.49.keep_ref, f32[8,64,512]{2,1,0:T(8,128)S(1)} %collective-permute-done.9.got_ref, bf16[1024,1024]{1,0:T(8,128)(2,1)S(1)} %get-tuple-element.51.basis_ref, ...), custom_call_target="tpu_custom_call" | custom-call | tf_op jit(solution)/shard_map/pallas_call | solution.py:649
  118.2 4.1 %shard_map.108 = (f32[8,64,1024]{2,1,0:T(8,128)S(1)}, f32[8,128]{1,0:T(8,128)S(1)}) custom-call(s32[4]{0:T(128)S(1)} %copy-done.8, f32[8,64,512]{2,1,0:T(8,128)S(1)} %get-tuple-element.47.keep_ref, f32[8,64,512]{2,1,0:T(8,128)S(1)} %collective-permute-done.8.got_ref, f32[8,64,1024]{2,1,0:T(8,128)S(1)} %get-tuple-element.53.z_ref, ...), custom_call_target="tpu_custom_call" | custom-call | tf_op jit(solution)/shard_map/pallas_call | solution.py:649
  122.4 2.0 shard_map.110
  124.4 1.8 shard_map.109.held_ref
  127.1 5.4 %shard_map.111 = (f32[1024,512]{1,0:T(8,128)S(1)}, f32[8,64,512]{2,1,0:T(8,128)S(1)}, f32[8,64,512]{2,1,0:T(8,128)S(1)}, f32[8,128]{1,0:T(8,128)S(1)}) custom-call(s32[4]{0:T(128)S(1)} %copy-done.8, f32[8,64,512]{2,1,0:T(8,128)S(1)} %shard_map.109.held_ref, f32[520,512]{1,0:T(8,128)S(1)} %collective-permute-done.11.got_ref, ...), custom_call_target="tpu_custom_call" | custom-call | tf_op jit(solution)/shard_map/pallas_call | solution.py:649
  132.7 3.0 %shard_map.112 = (f32[8,64,512]{2,1,0:T(8,128)S(1)}, f32[8,64,512]{2,1,0:T(8,128)S(1)}) custom-call(s32[4]{0:T(128)S(1)} %copy-done.8, f32[1024,512]{1,0:T(8,128)S(1)} %get-tuple-element.64.column_ref, bf16[1024,1024]{1,0:T(8,128)(2,1)S(1)} %get-tuple-element.44.kernel_ref), custom_call_target="tpu_custom_call" | custom-call | tf_op jit(solution)/shard_map/pallas_call | solution.py:649
  136.2 3.0 %shard_map.113.z_ref.f_ref = f32[8,64,1024]{2,1,0:T(8,128)S(1)} custom-call(s32[4]{0:T(128)S(1)} %copy-done.8, f32[8,64,512]{2,1,0:T(8,128)S(1)} %get-tuple-element.67.keep_ref, f32[8,64,512]{2,1,0:T(8,128)S(1)} %collective-permute-done.13.got_ref, bf16[1024,1024]{1,0:T(8,128)(2,1)S(1)} %get-tuple-element.51.basis_ref), custom_call_target="tpu_custom_call" | custom-call | tf_op jit(solution)/shard_map/pallas_call | solution.py:649
  139.2 4.1 %shard_map.114 = (f32[8,64,1024]{2,1,0:T(8,128)S(1)}, f32[16,8,128]{2,1,0:T(8,128)S(1)}) custom-call(s32[4]{0:T(128)S(1)} %copy-done.8, f32[8,64,512]{2,1,0:T(8,128)S(1)} %get-tuple-element.65.keep_ref, f32[8,64,512]{2,1,0:T(8,128)S(1)} %collective-permute-done.12.got_ref, f32[8,64,1024]{2,1,0:T(8,128)S(1)} %shard_map.113.z_ref.f_ref, ...), custom_call_target="tpu_custom_call" | custom-call | tf_op jit(solution)/shard_map/pallas_call | solution.py:649
  143.4 12.2 %all_to_all.15.sum_ref = f32[16,8,128]{2,1,0:T(8,128)S(1)} all-to-all(f32[16,8,128]{2,1,0:T(8,128)S(1)} %get-tuple-element.70), channel_id=1, replica_groups=mesh['blocks'=2,'mode'=16] {'mode'}, dimensions={0} | all-to-all | bytes 131072 | tf_op jit(solution)/shard_map/all_to_all | solution.py:759
  155.6 1.6 combine.1
  157.3 95.8 %all_to_all.16 = f32[8,128,1024]{2,1,0:T(8,128)S(1)} all-to-all(f32[8,128,1024]{2,1,0:T(8,128)S(1)} %combine.1), channel_id=1, replica_groups={{0,2,4,6,8,10,12,14},{1,3,5,7,9,11,13,15},{16,18,20,22,24,26,28,30},{17..., dimensions={0} | all-to-all | bytes 8388608 | tf_op jit(solution)/shard_map/all_to_all | solution.py:772
  253.1 2.0 finish.1
  (53 shorter events, 10.1 us)
Async XLA Ops:
  6.6 7.6 %copy-start.15 = (f32[64]{0:T(128)S(1)}, f32[64]{0:T(128)}, u32[]{:S(2)}) copy-start(f32[64]{0:T(128)} %param.17) | copy-start | bytes 772
  6.7 95.6 %all-to-all-start = ((f32[16,64,512]{2,1,0:T(8,128)}), f32[16,64,512]{2,1,0:T(8,128)}, u32[]{:S(2)}, u32[]{:S(2)}) async-start(f32[16,64,512]{2,1,0:T(8,128)} %bitcast.13), calls=%async_computation | async-start | bytes 4194304 | tf_op jit(solution)/shard_map/all_to_all | solution.py:604
  14.3 78.0 %copy-start = (bf16[1024,1024]{1,0:T(8,128)(2,1)S(1)}, bf16[1024,1024]{1,0:T(8,128)(2,1)}, u32[]{:S(2)}) copy-start(bf16[1024,1024]{1,0:T(8,128)(2,1)} %second_hbm.1) | copy-start | bytes 6291460
  14.3 10.4 %collective-permute-start = (f32[1,64]{1,0:T(1,128)S(1)}, f32[1,64]{1,0:T(1,128)S(1)}, u32[]{:S(2)}, u32[]{:S(2)}) collective-permute-start(f32[1,64]{1,0:T(1,128)S(1)} %bitcast.14), channel_id=1, source_target_pairs={{0,1},{1,0},{2,3},{3,2},{4,5},{5,4},{6,7},{7,6},{8,9},{9,8},{10,11... | collective-permute-start | bytes 776 | tf_op jit(solution)/shard_map/ppermute | solution.py:610
  15.9 43.4 %collective-permute-start.2 = (s32[64,1024]{1,0:T(8,128)S(1)}, s32[64,1024]{1,0:T(8,128)S(1)}, u32[]{:S(2)}, u32[]{:S(2)}) collective-permute-start(s32[64,1024]{1,0:T(8,128)S(1)} %pick.1), channel_id=1, source_target_pairs={{0,4},{1,5},{2,6},{3,7},{4,8},{5,9},{6,10},{7,11},{8,12},{9,13},{1... | collective-permute-start | bytes 786440 | tf_op jit(solution)/shard_map/ppermute | solution.py:573
  19.5 0.7 copy-start.7
  20.2 60.5 %collective-permute-start.3 = (f32[64,1024]{1,0:T(8,128)S(1)}, f32[64,1024]{1,0:T(8,128)S(1)}, u32[]{:S(2)}, u32[]{:S(2)}) collective-permute-start(f32[64,1024]{1,0:T(8,128)S(1)} %get-tuple-element.38), channel_id=1, source_target_pairs={{0,8},{1,9},{2,10},{3,11},{4,12},{5,13},{6,14},{7,15},{8,0},{9,1},... | collective-permute-start | bytes 786440 | tf_op jit(solution)/shard_map/ppermute | solution.py:573
  22.6 58.1 %collective-permute-start.4 = (f32[64,1024]{1,0:T(8,128)S(1)}, f32[64,1024]{1,0:T(8,128)}, u32[]{:S(2)}, u32[]{:S(2)}) collective-permute-start(f32[64,1024]{1,0:T(8,128)S(1)} %get-tuple-element.39), channel_id=1, source_target_pairs={{0,12},{1,13},{2,14},{3,15},{4,0},{5,1},{6,2},{7,3},{8,4},{9,5},{1... | collective-permute-start | bytes 786440 | tf_op jit(solution)/shard_map/ppermute | solution.py:573
  24.8 3.6 %collective-permute-start.1 = (f32[1,128]{1,0:T(1,128)S(1)}, f32[1,128]{1,0:T(1,128)S(1)}, u32[]{:S(2)}, u32[]{:S(2)}) collective-permute-start(f32[1,128]{1,0:T(1,128)S(1)} %broadcast_select_fusion.1), channel_id=1, source_target_pairs={{0,2},{1,3},{2,0},{3,1},{4,6},{5,7},{6,4},{7,5},{8,10},{9,11},{10,... | collective-permute-start | bytes 1544 | tf_op jit(solution)/shard_map/ppermute | solution.py:610
  59.2 21.4 %copy-start.13 = (s32[64,1024]{1,0:T(8,128)}, s32[64,1024]{1,0:T(8,128)S(1)}, u32[]{:S(2)}) copy-start(s32[64,1024]{1,0:T(8,128)S(1)} %collective-permute-done.2.refs_1_) | copy-start | bytes 786436
  80.7 0.7 copy-start.14
  83.8 18.4 %collective-permute-start.7 = (f32[1,256]{1,0:T(1,128)}, f32[1,256]{1,0:T(1,128)S(1)}, u32[]{:S(2)}, u32[]{:S(2)}) collective-permute-start(f32[1,256]{1,0:T(1,128)} %get-tuple-element.40._.refs_0_), channel_id=1, source_target_pairs={{0,12},{1,13},{2,14},{3,15},{4,0},{5,1},{6,2},{7,3},{8,4},{9,5},{1... | collective-permute-start | bytes 3080 | tf_op jit(solution)/shard_map/ppermute | solution.py:628
  90.3 11.9 %collective-permute-start.6 = (f32[1,256]{1,0:T(1,128)}, f32[1,256]{1,0:T(1,128)S(1)}, u32[]{:S(2)}, u32[]{:S(2)}) collective-permute-start(f32[1,256]{1,0:T(1,128)} %get-tuple-element.40._.refs_0_), channel_id=1, source_target_pairs={{0,8},{1,9},{2,10},{3,11},{4,12},{5,13},{6,14},{7,15},{8,0},{9,1},... | collective-permute-start | bytes 3080 | tf_op jit(solution)/shard_map/ppermute | solution.py:628
  90.3 11.9 %collective-permute-start.5 = (f32[1,256]{1,0:T(1,128)}, f32[1,256]{1,0:T(1,128)S(1)}, u32[]{:S(2)}, u32[]{:S(2)}) collective-permute-start(f32[1,256]{1,0:T(1,128)} %get-tuple-element.40._.refs_0_), channel_id=1, source_target_pairs={{0,4},{1,5},{2,6},{3,7},{4,8},{5,9},{6,10},{7,11},{8,12},{9,13},{1... | collective-permute-start | bytes 3080 | tf_op jit(solution)/shard_map/ppermute | solution.py:628
  90.8 24.4 %collective-permute-start.10 = (f32[4,64,1024]{2,1,0:T(8,128)}, f32[4,64,1024]{2,1,0:T(8,128)}, u32[]{:S(2)}, u32[]{:S(2)}) collective-permute-start(f32[4,64,1024]{2,1,0:T(8,128)} %get-tuple-element.52.near_hbm), channel_id=1, source_target_pairs={{0,2},{1,3},{2,0},{3,1},{4,6},{5,7},{6,4},{7,5},{8,10},{9,11},{10,... | collective-permute-start | bytes 3145736 | tf_op jit(solution)/shard_map/ppermute | solution.py:626
  92.3 1.6 copy-start.2
  93.9 1.6 copy-start.3
  95.5 0.7 copy-start.11
  96.2 6.1 %copy-start.8 = (s32[4]{0:T(128)S(1)}, s32[4]{0:T(128)}, u32[]{:S(2)}) copy-start(s32[4]{0:T(128)} %pad_add_fusion.place_ref) | copy-start | bytes 52
  96.2 6.1 %copy-start.9 = (f32[8]{0:T(128)S(1)}, f32[8]{0:T(128)}, u32[]{:S(2)}) copy-start(f32[8]{0:T(128)} %table_ref.5) | copy-start | bytes 100
  96.2 6.1 %copy-start.10 = (f32[1024]{0:T(1024)S(1)}, f32[1024]{0:T(1024)}, u32[]{:S(2)}) copy-start(f32[1024]{0:T(1024)} %param.16) | copy-start | bytes 12292
  96.2 6.1 %copy-start.12 = (f32[1,256]{1,0:T(1,128)S(1)}, f32[1,256]{1,0:T(1,128)}, u32[]{:S(2)}) copy-start(f32[1,256]{1,0:T(1,128)} %get-tuple-element.40._.refs_0_) | copy-start | bytes 3076
  98.6 1.3 copy-start.4
  99.9 1.3 copy-start.5
  101.2 1.0 copy-start.6
  109.3 5.9 %collective-permute-start.9 = (f32[8,64,512]{2,1,0:T(8,128)S(1)}, f32[8,64,512]{2,1,0:T(8,128)S(1)}, u32[]{:S(2)}, u32[]{:S(2)}) collective-permute-start(f32[8,64,512]{2,1,0:T(8,128)S(1)} %get-tuple-element.50), channel_id=1, source_target_pairs={{0,1},{1,0},{2,3},{3,2},{4,5},{5,4},{6,7},{7,6},{8,9},{9,8},{10,11... | collective-permute-start | bytes 3145736 | tf_op jit(solution)/shard_map/ppermute | solution.py:646
  112.4 5.8 %collective-permute-start.8 = (f32[8,64,512]{2,1,0:T(8,128)S(1)}, f32[8,64,512]{2,1,0:T(8,128)S(1)}, u32[]{:S(2)}, u32[]{:S(2)}) collective-permute-start(f32[8,64,512]{2,1,0:T(8,128)S(1)} %get-tuple-element.48), channel_id=1, source_target_pairs={{0,1},{1,0},{2,3},{3,2},{4,5},{5,4},{6,7},{7,6},{8,9},{9,8},{10,11... | collective-permute-start | bytes 3145736 | tf_op jit(solution)/shard_map/ppermute | solution.py:646
  124.4 2.7 %collective-permute-start.11 = (f32[520,512]{1,0:T(8,128)S(1)}, f32[520,512]{1,0:T(8,128)S(1)}, u32[]{:S(2)}, u32[]{:S(2)}) collective-permute-start(f32[520,512]{1,0:T(8,128)S(1)} %shard_map.110), channel_id=1, source_target_pairs={{0,1},{1,0},{2,3},{3,2},{4,5},{5,4},{6,7},{7,6},{8,9},{9,8},{10,11... | collective-permute-start | bytes 3194888 | tf_op jit(solution)/shard_map/ppermute | solution.py:646
  132.5 3.7 %collective-permute-start.13 = (f32[8,64,512]{2,1,0:T(8,128)S(1)}, f32[8,64,512]{2,1,0:T(8,128)S(1)}, u32[]{:S(2)}, u32[]{:S(2)}) collective-permute-start(f32[8,64,512]{2,1,0:T(8,128)S(1)} %get-tuple-element.68), channel_id=1, source_target_pairs={{0,1},{1,0},{2,3},{3,2},{4,5},{5,4},{6,7},{7,6},{8,9},{9,8},{10,11... | collective-permute-start | bytes 3145736 | tf_op jit(solution)/shard_map/ppermute | solution.py:646
  135.8 3.4 %collective-permute-start.12 = (f32[8,64,512]{2,1,0:T(8,128)S(1)}, f32[8,64,512]{2,1,0:T(8,128)S(1)}, u32[]{:S(2)}, u32[]{:S(2)}) collective-permute-start(f32[8,64,512]{2,1,0:T(8,128)S(1)} %get-tuple-element.66), channel_id=1, source_target_pairs={{0,1},{1,0},{2,3},{3,2},{4,5},{5,4},{6,7},{7,6},{8,9},{9,8},{10,11... | collective-permute-start | bytes 3145736 | tf_op jit(solution)/shard_map/ppermute | solution.py:646
  157.3 95.8 %copy-start.1 = (f32[2,4,64,1024]{3,2,1,0:T(8,128)S(1)}, f32[2,4,64,1024]{3,2,1,0:T(8,128)}, u32[]{:S(2)}) copy-start(f32[2,4,64,1024]{3,2,1,0:T(8,128)} %right_ref.3) | copy-start | bytes 6291460
